TPU v7x, 32 devices: a whole 2x2x4 slice. The times are simulated.
32 devices in a mesh: ckpt: 2 (over y), lat: 4 (over z), col: 4 (over x, core).
Axes of the slice: x: 2, y: 2, z: 4, core: 2. Of those that a mesh axis runs over, the one named last changes fastest.
Arguments:
- code_ids: int32 [1024, 64], P(('ckpt', 'lat')), parts along dimension 0, may hold values from 0 to 32767, as said below
- code_vals: float32 [1024, 64], P(('ckpt', 'lat')), parts along dimension 0, may hold values from 0.2 to 5
- decoder: bfloat16 [65536, 5120], P(('ckpt', 'lat'), 'col'), parts along dimension 0, may hold values from -0.375 to 0.375
- dec_bias: bfloat16 [10240], P(('ckpt', 'col')), parts along dimension 0, may hold values from -3 to 3
- ln_gain: float32 [10240], P(('ckpt', 'col')), parts along dimension 0, may hold values from 0.5 to 1.5
- ln_bias: float32 [10240], P(('ckpt', 'col')), parts along dimension 0, may hold values from -2.5 to 2.5
- w_qkv: bfloat16 [10240, 3, 4096], P(('ckpt', 'col'), None, 'lat'), parts along dimension 0, may hold values from -0.078125 to 0.078125
- cache_kv: bfloat16 [2, 3072, 4096], P(None, ('ckpt', 'col'), 'lat'), parts along dimension 1
- positions: int32 [1024], P('ckpt'), parts along dimension 0, may hold values from 0 to 511, each once
- w_out: bfloat16 [8192, 5120], P(('ckpt', 'lat'), 'col'), parts along dimension 0, may hold values from -0.09375 to 0.09375
Outputs:
- layer_out: bfloat16 [1024, 5120], P(('ckpt', 'lat'), 'col'), parts along dimension 0
There are 2 independent parts, one for each index of `ckpt`. A program takes and returns all parts, laid end to end along the dimension named above; each array names one. Nothing has to cross between parts.
Inputs may be any that keep to these rules, and one draw needn't show every extreme that they name: `code_ids`: the ids within a row are distinct.
All inputs are finite; a program needn't handle non-finite values.
Results may differ from a plain program's by a relative error of at most 0.0085.
The roundings to bfloat16 on the way count: a program that leaves them out, or rounds other values in their place, can miss the bound.
Values may be sent and summed in bfloat16 or wider, within the bound.
No kernel may reach another device: no remote copies, remote signals or barrier semaphores. Data moves between devices by JAX's collectives and lax.ppermute only.
A program may use at most 128 MiB of HBM per device.

v0:
```python
import math

import jax
import jax.numpy as jnp
from jax import lax
from jax.sharding import PartitionSpec as P

D = 5120
HEAD = 128


def normalize(values, sums, gain, shift):
    row_mean = sums[0] / D
    row_var = sums[1] / D - row_mean * row_mean
    inverse = 1.0 / jnp.sqrt(row_var + 1e-05)
    return ((values - row_mean[:, None]) * inverse[:, None] * gain + shift).astype(jnp.bfloat16)


def attend_block(queries, keys, values, query_pos, key_pos):
    heads = queries.shape[1] // HEAD
    query_heads = queries.reshape(queries.shape[0], heads, HEAD)
    key_heads = keys.reshape(keys.shape[0], heads, HEAD)
    value_heads = values.reshape(values.shape[0], heads, HEAD)
    scores = jnp.einsum(
        "qhe,khe->hqk", query_heads, key_heads, preferred_element_type=jnp.float32
    ) * (1.0 / math.sqrt(HEAD))
    visible = key_pos[None, None, :] <= query_pos[None, :, None]
    scores = jnp.where(visible, scores, -1e30)
    highest = jnp.max(scores, axis=-1, keepdims=True)
    expo = jnp.exp(scores - highest)
    probs = (expo / jnp.sum(expo, axis=-1, keepdims=True)).astype(jnp.bfloat16)
    mixed = jnp.einsum("hqk,khe->qhe", probs, value_heads, preferred_element_type=jnp.float32)
    return mixed.reshape(queries.shape[0], heads * HEAD).astype(jnp.bfloat16)


def densify(local_ids, weights_all, shard_latents):
    total_rows = local_ids.shape[0]
    block_rows = math.gcd(total_rows, 32)
    block_count = total_rows // block_rows
    lanes = jnp.arange(shard_latents, dtype=jnp.int32)
    id_blocks = local_ids.reshape(block_count, block_rows, local_ids.shape[1])
    weight_blocks = weights_all.reshape(block_count, block_rows, weights_all.shape[1])

    def one_block(pair):
        ids_block, weight_block = pair
        match = ids_block[:, :, None] == lanes[None, None, :]
        picked = jnp.where(match, weight_block[:, :, None], jnp.zeros((), jnp.bfloat16))
        return jnp.sum(picked, axis=1, dtype=jnp.bfloat16)

    dense_blocks = lax.map(one_block, (id_blocks, weight_blocks))
    return dense_blocks.reshape(total_rows, shard_latents)


def body(
    code_ids, code_vals, decoder, dec_bias, ln_gain, ln_bias, w_qkv, cache_kv, positions, w_out
):
    lat_index = lax.axis_index("lat")
    col_total = lax.axis_size("col")
    col_index = lax.axis_index("col")
    ids_all, weights_all = (
        lax.all_gather(code_ids, "lat", axis=0, tiled=True),
        lax.all_gather(code_vals.astype(jnp.bfloat16), "lat", axis=0, tiled=True),
    )
    total_rows = ids_all.shape[0]
    shard_latents = decoder.shape[0]
    local_ids = ids_all - lat_index * shard_latents
    inside = (local_ids >= 0) & (local_ids < shard_latents)
    local_ids = jnp.where(inside, local_ids, shard_latents)
    dense_codes = densify(local_ids, weights_all, shard_latents)
    col_rows = total_rows // col_total
    bias_decoded = dec_bias.astype(jnp.float32)
    block = dense_codes
    residual = (
        lax.psum_scatter(
            jnp.dot(block, decoder, preferred_element_type=jnp.float32),
            "lat",
            scatter_dimension=0,
            tiled=True,
        )
        + bias_decoded
    )
    sums = lax.psum((jnp.sum(residual, axis=1), jnp.sum(residual * residual, axis=1)), "col")
    normed = lax.all_gather(normalize(residual, sums, ln_gain, ln_bias), "lat", axis=0, tiled=True)
    head_width = w_qkv.shape[2]
    w_flat = w_qkv.reshape(w_qkv.shape[0], 3 * head_width)
    block = normed
    own_rows = lax.psum_scatter(
        jnp.dot(block, w_flat, preferred_element_type=jnp.float32),
        "col",
        scatter_dimension=0,
        tiled=True,
    ).astype(jnp.bfloat16)
    queries = own_rows[:, :head_width]
    new_kv = lax.all_gather(own_rows[:, head_width:], "col", axis=0, tiled=True)
    context = lax.all_gather(cache_kv, "col", axis=1, tiled=True)
    cached_len = context.shape[1]
    keys = jnp.concatenate([context[0], new_kv[:, :head_width]], axis=0)
    values = jnp.concatenate([context[1], new_kv[:, head_width:]], axis=0)
    key_pos = jnp.concatenate([jnp.arange(cached_len, dtype=jnp.int32), cached_len + positions])
    query_pos = cached_len + lax.dynamic_slice_in_dim(positions, col_index * col_rows, col_rows, 0)
    attended = attend_block(queries, keys, values, query_pos, key_pos)
    gathered = lax.all_gather(attended, "col", axis=0, tiled=True)
    block = gathered
    branch_out = lax.psum_scatter(
        jnp.dot(block, w_out, preferred_element_type=jnp.float32).astype(jnp.bfloat16),
        "lat",
        scatter_dimension=0,
        tiled=True,
    ).astype(jnp.float32)
    return (residual + branch_out).astype(jnp.bfloat16)


def solution(mesh):
    return jax.shard_map(
        body,
        mesh=mesh,
        in_specs=(
            P(("ckpt", "lat"), None),
            P(("ckpt", "lat"), None),
            P(("ckpt", "lat"), "col"),
            P(("ckpt", "col")),
            P(("ckpt", "col")),
            P(("ckpt", "col")),
            P(("ckpt", "col"), None, "lat"),
            P(None, ("ckpt", "col"), "lat"),
            P("ckpt"),
            P(("ckpt", "lat"), "col"),
        ),
        out_specs=P(("ckpt", "lat"), "col"),
        check_vma=False,
    )
```

profile of v0, /device:TPU:8, one launch (start us, length us, event | category | flops | bytes accessed | tf_op | source)
XLA Modules:
  0.0 561.9 jit_solution(10485041958467285273)
XLA Ops:
  6.5 14.2 %all_gather.18 = s32[512,64]{0,1:T(8,128)S(1)} all-gather(s32[128,64]{0,1:T(8,128)} %param.12), channel_id=1, replica_groups=mesh['ckpt'=2,'lat'=4,'col'=4] {'lat'}, dimensions={0}, use_global_device_ids=true | all-gather | bytes 163840 | tf_op jit(solution)/shard_map/all_gather | solution.py:61
  21.7 12.2 %all_gather.19 = bf16[512,64]{0,1:T(8,128)(2,1)S(1)} all-gather(bf16[128,64]{0,1:T(8,128)(2,1)S(1)} %convert_element_type.33), channel_id=1, replica_groups=mesh['ckpt'=2,'lat'=4,'col'=4] {'lat'}, dimensions={0}, use_global_device_ids=true | all-gather | bytes 81920 | tf_op jit(solution)/shard_map/all_gather | solution.py:62
  34.0 196.1 %while.11 = (s32[]{:T(128)}, bf16[16,32,8192]{2,1,0:T(8,128)(2,1)}, s32[16,32,64]{2,1,0:T(8,128)S(1)}, bf16[16,32,64]{2,1,0:T(8,128)(2,1)S(1)}, s32[]{:T(128)}) while((s32[]{:T(128)}, bf16[16,32,8192]{2,1,0:T(8,128)(2,1)}, s32[16,32,64]{2,1,0:T(8,128)S(1)}, bf16[16,32,64]{2,1,0:T(8,128)(2,1)S(1)}, s32[]{:T(128)}) %tuple.44), condition=%wide.region_2.3_spmd.clone, body=%wide.region_0.2_spmd.clone.sunk | while | flops 50069504 | bytes 1610309 | solution.py:50
  34.1 11.4 %fusion.38 = bf16[32,8192]{1,0:T(8,128)(2,1)S(1)} fusion(s32[32,64]{1,0:T(8,128)S(1)} %dynamic-slice_bitcast_fusion.4, bf16[32,64]{1,0:T(8,128)(2,1)S(1)} %dynamic-slice_bitcast_fusion.5), kind=kLoop, calls=%fused_computation.3.clone.1 | loop fusion | flops 50069504 | bytes 536576 | tf_op jit(solution)/shard_map/while/body/eval_jaxpr/reduce_sum | solution.py:48
  46.3 11.4 %fusion.38 = bf16[32,8192]{1,0:T(8,128)(2,1)S(1)} fusion(s32[32,64]{1,0:T(8,128)S(1)} %dynamic-slice_bitcast_fusion.4, bf16[32,64]{1,0:T(8,128)(2,1)S(1)} %dynamic-slice_bitcast_fusion.5), kind=kLoop, calls=%fused_computation.3.clone.1 | loop fusion | flops 50069504 | bytes 536576 | tf_op jit(solution)/shard_map/while/body/eval_jaxpr/reduce_sum | solution.py:48
  58.5 11.4 %fusion.38 = bf16[32,8192]{1,0:T(8,128)(2,1)S(1)} fusion(s32[32,64]{1,0:T(8,128)S(1)} %dynamic-slice_bitcast_fusion.4, bf16[32,64]{1,0:T(8,128)(2,1)S(1)} %dynamic-slice_bitcast_fusion.5), kind=kLoop, calls=%fused_computation.3.clone.1 | loop fusion | flops 50069504 | bytes 536576 | tf_op jit(solution)/shard_map/while/body/eval_jaxpr/reduce_sum | solution.py:48
  69.9 0.9 bitcast_dynamic-update-slice_fusion.2
  70.8 11.4 %fusion.38 = bf16[32,8192]{1,0:T(8,128)(2,1)S(1)} fusion(s32[32,64]{1,0:T(8,128)S(1)} %dynamic-slice_bitcast_fusion.4, bf16[32,64]{1,0:T(8,128)(2,1)S(1)} %dynamic-slice_bitcast_fusion.5), kind=kLoop, calls=%fused_computation.3.clone.1 | loop fusion | flops 50069504 | bytes 536576 | tf_op jit(solution)/shard_map/while/body/eval_jaxpr/reduce_sum | solution.py:48
  83.0 11.4 %fusion.38 = bf16[32,8192]{1,0:T(8,128)(2,1)S(1)} fusion(s32[32,64]{1,0:T(8,128)S(1)} %dynamic-slice_bitcast_fusion.4, bf16[32,64]{1,0:T(8,128)(2,1)S(1)} %dynamic-slice_bitcast_fusion.5), kind=kLoop, calls=%fused_computation.3.clone.1 | loop fusion | flops 50069504 | bytes 536576 | tf_op jit(solution)/shard_map/while/body/eval_jaxpr/reduce_sum | solution.py:48
  95.3 11.4 %fusion.38 = bf16[32,8192]{1,0:T(8,128)(2,1)S(1)} fusion(s32[32,64]{1,0:T(8,128)S(1)} %dynamic-slice_bitcast_fusion.4, bf16[32,64]{1,0:T(8,128)(2,1)S(1)} %dynamic-slice_bitcast_fusion.5), kind=kLoop, calls=%fused_computation.3.clone.1 | loop fusion | flops 50069504 | bytes 536576 | tf_op jit(solution)/shard_map/while/body/eval_jaxpr/reduce_sum | solution.py:48
  107.5 11.4 %fusion.38 = bf16[32,8192]{1,0:T(8,128)(2,1)S(1)} fusion(s32[32,64]{1,0:T(8,128)S(1)} %dynamic-slice_bitcast_fusion.4, bf16[32,64]{1,0:T(8,128)(2,1)S(1)} %dynamic-slice_bitcast_fusion.5), kind=kLoop, calls=%fused_computation.3.clone.1 | loop fusion | flops 50069504 | bytes 536576 | tf_op jit(solution)/shard_map/while/body/eval_jaxpr/reduce_sum | solution.py:48
  119.8 11.4 %fusion.38 = bf16[32,8192]{1,0:T(8,128)(2,1)S(1)} fusion(s32[32,64]{1,0:T(8,128)S(1)} %dynamic-slice_bitcast_fusion.4, bf16[32,64]{1,0:T(8,128)(2,1)S(1)} %dynamic-slice_bitcast_fusion.5), kind=kLoop, calls=%fused_computation.3.clone.1 | loop fusion | flops 50069504 | bytes 536576 | tf_op jit(solution)/shard_map/while/body/eval_jaxpr/reduce_sum | solution.py:48
  132.0 11.4 %fusion.38 = bf16[32,8192]{1,0:T(8,128)(2,1)S(1)} fusion(s32[32,64]{1,0:T(8,128)S(1)} %dynamic-slice_bitcast_fusion.4, bf16[32,64]{1,0:T(8,128)(2,1)S(1)} %dynamic-slice_bitcast_fusion.5), kind=kLoop, calls=%fused_computation.3.clone.1 | loop fusion | flops 50069504 | bytes 536576 | tf_op jit(solution)/shard_map/while/body/eval_jaxpr/reduce_sum | solution.py:48
  144.3 11.4 %fusion.38 = bf16[32,8192]{1,0:T(8,128)(2,1)S(1)} fusion(s32[32,64]{1,0:T(8,128)S(1)} %dynamic-slice_bitcast_fusion.4, bf16[32,64]{1,0:T(8,128)(2,1)S(1)} %dynamic-slice_bitcast_fusion.5), kind=kLoop, calls=%fused_computation.3.clone.1 | loop fusion | flops 50069504 | bytes 536576 | tf_op jit(solution)/shard_map/while/body/eval_jaxpr/reduce_sum | solution.py:48
  156.5 11.4 %fusion.38 = bf16[32,8192]{1,0:T(8,128)(2,1)S(1)} fusion(s32[32,64]{1,0:T(8,128)S(1)} %dynamic-slice_bitcast_fusion.4, bf16[32,64]{1,0:T(8,128)(2,1)S(1)} %dynamic-slice_bitcast_fusion.5), kind=kLoop, calls=%fused_computation.3.clone.1 | loop fusion | flops 50069504 | bytes 536576 | tf_op jit(solution)/shard_map/while/body/eval_jaxpr/reduce_sum | solution.py:48
  167.9 0.9 bitcast_dynamic-update-slice_fusion.2
  168.8 11.4 %fusion.38 = bf16[32,8192]{1,0:T(8,128)(2,1)S(1)} fusion(s32[32,64]{1,0:T(8,128)S(1)} %dynamic-slice_bitcast_fusion.4, bf16[32,64]{1,0:T(8,128)(2,1)S(1)} %dynamic-slice_bitcast_fusion.5), kind=kLoop, calls=%fused_computation.3.clone.1 | loop fusion | flops 50069504 | bytes 536576 | tf_op jit(solution)/shard_map/while/body/eval_jaxpr/reduce_sum | solution.py:48
  181.0 11.4 %fusion.38 = bf16[32,8192]{1,0:T(8,128)(2,1)S(1)} fusion(s32[32,64]{1,0:T(8,128)S(1)} %dynamic-slice_bitcast_fusion.4, bf16[32,64]{1,0:T(8,128)(2,1)S(1)} %dynamic-slice_bitcast_fusion.5), kind=kLoop, calls=%fused_computation.3.clone.1 | loop fusion | flops 50069504 | bytes 536576 | tf_op jit(solution)/shard_map/while/body/eval_jaxpr/reduce_sum | solution.py:48
  193.3 11.4 %fusion.38 = bf16[32,8192]{1,0:T(8,128)(2,1)S(1)} fusion(s32[32,64]{1,0:T(8,128)S(1)} %dynamic-slice_bitcast_fusion.4, bf16[32,64]{1,0:T(8,128)(2,1)S(1)} %dynamic-slice_bitcast_fusion.5), kind=kLoop, calls=%fused_computation.3.clone.1 | loop fusion | flops 50069504 | bytes 536576 | tf_op jit(solution)/shard_map/while/body/eval_jaxpr/reduce_sum | solution.py:48
  205.5 11.4 %fusion.38 = bf16[32,8192]{1,0:T(8,128)(2,1)S(1)} fusion(s32[32,64]{1,0:T(8,128)S(1)} %dynamic-slice_bitcast_fusion.4, bf16[32,64]{1,0:T(8,128)(2,1)S(1)} %dynamic-slice_bitcast_fusion.5), kind=kLoop, calls=%fused_computation.3.clone.1 | loop fusion | flops 50069504 | bytes 536576 | tf_op jit(solution)/shard_map/while/body/eval_jaxpr/reduce_sum | solution.py:48
  217.8 11.4 %fusion.38 = bf16[32,8192]{1,0:T(8,128)(2,1)S(1)} fusion(s32[32,64]{1,0:T(8,128)S(1)} %dynamic-slice_bitcast_fusion.4, bf16[32,64]{1,0:T(8,128)(2,1)S(1)} %dynamic-slice_bitcast_fusion.5), kind=kLoop, calls=%fused_computation.3.clone.1 | loop fusion | flops 50069504 | bytes 536576 | tf_op jit(solution)/shard_map/while/body/eval_jaxpr/reduce_sum | solution.py:48
  229.2 0.9 bitcast_dynamic-update-slice_fusion.2
  230.1 18.0 %fusion.29 = f32[512,1280]{1,0:T(8,128)} fusion(bf16[512,8192]{1,0:T(8,128)(2,1)} %bitcast.48, bf16[8192,1280]{1,0:T(8,128)(2,1)} %param.14), kind=kOutput, calls=%fused_computation.48 | convolution fusion | flops 10737418240 | bytes 31981568 | tf_op jit(solution)/shard_map/dot_general | solution.py:75
  248.2 51.1 %reduce-scatter.4.cloned.1.call-done = f32[128,1280]{1,0:T(8,128)} async-done(((f32[512,1280]{1,0:T(8,128)}), f32[128,1280]{1,0:T(8,128)}) %reduce-scatter.4.cloned.1.call-update) | async-done | bytes 655376 | tf_op jit(solution)/shard_map/reduce_scatter | solution.py:74
  299.3 1.3 add_reduce_fusion
  300.5 6.5 %all-reduce = (f32[128]{0:T(128)S(1)}, f32[128]{0:T(128)S(1)}) all-reduce(f32[128]{0:T(128)S(1)} %get-tuple-element.44, f32[128]{0:T(128)S(1)} %get-tuple-element.43), channel_id=1, replica_groups=mesh['ckpt'=2,'lat'=4,'col'=4] {'col'}, use_global_device_ids=true, to_apply=%region_7.8 | all-reduce | flops 256 | bytes 2048 | tf_op jit(solution)/shard_map/psum | solution.py:82
  307.0 2.0 add_convert_fusion.1
  309.1 10.9 %copy.28 = bf16[1280,3,1024]{0,2,1:T(8,128)(2,1)} copy(bf16[1280,3,1024]{2,0,1:T(8,128)(2,1)} %param.18) | data formatting | bytes 15728640 | tf_op args[6]
  320.0 21.2 %all-gather.7.cloned.1.call-done = bf16[512,1280]{1,0:T(8,128)(2,1)} async-done(((bf16[128,1280]{1,0:T(8,128)(2,1)}), bf16[512,1280]{1,0:T(8,128)(2,1)}) %all-gather.7.cloned.1.call-update) | async-done | bytes 1310736 | tf_op jit(solution)/shard_map/all_gather | solution.py:83
  341.2 10.6 %fusion.30 = f32[512,3072]{1,0:T(8,128)} fusion(bf16[512,1280]{1,0:T(8,128)(2,1)} %all-gather.7.cloned.1.call-done, bf16[1280,3072]{0,1:T(8,128)(2,1)} %bitcast.41), kind=kOutput, calls=%fused_computation.49 | convolution fusion | flops 4026531840 | bytes 15466496 | tf_op jit(solution)/shard_map/dot_general | solution.py:88
  351.8 2.6 copy.27
  354.5 55.5 %reduce-scatter.6.cloned.1.call-done = f32[128,3072]{1,0:T(8,128)} async-done(((f32[512,3072]{1,0:T(8,128)}), f32[128,3072]{1,0:T(8,128)}) %reduce-scatter.6.cloned.1.call-update) | async-done | bytes 1572880 | tf_op jit(solution)/shard_map/reduce_scatter | solution.py:87
  410.0 1.5 convert_element_type.36
  412.7 0.9 broadcast_compare_fusion
  413.6 44.2 %all-gather.5.cloned.1.call-done = bf16[2,1536,1024]{1,2,0:T(8,128)(2,1)} async-done(((bf16[2,384,1024]{1,2,0:T(8,128)(2,1)}), bf16[2,1536,1024]{1,2,0:T(8,128)(2,1)}) %all-gather.5.cloned.1.call-update) | async-done | bytes 6291472 | tf_op jit(solution)/shard_map/all_gather | solution.py:95
  457.8 5.9 %fusion.26 = (bf16[1,1536,1024]{1,2,0:T(8,128)(2,1)}, bf16[1,1536,1024]{1,2,0:T(8,128)(2,1)}) fusion(bf16[2,1536,1024]{1,2,0:T(8,128)(2,1)} %all-gather.5.cloned.1.call-done), kind=kLoop, calls=%fused_computation.45 | loop fusion | bytes 12582912 | tf_op jit(solution)/shard_map/slice | solution.py:98
  463.8 4.7 copy.30
  468.5 13.5 %all-gather.9.cloned.1.call-done = bf16[512,2048]{1,0:T(8,128)(2,1)} async-done(((bf16[128,2048]{1,0:T(8,128)(2,1)}), bf16[512,2048]{1,0:T(8,128)(2,1)}) %all-gather.9.cloned.1.call-update) | async-done | bytes 2097168 | tf_op jit(solution)/shard_map/all_gather | solution.py:94
  481.9 2.7 fusion.27
  484.7 1.2 copy.41
  485.8 2.3 copy.33
  488.1 3.5 fusion.10
  491.7 5.8 %fusion.28 = (f32[8,128]{1,0:T(8,128)S(1)}, f32[8,128,2048]{2,1,0:T(8,128)}) fusion(f32[8,128,2048]{2,1,0:T(8,128)S(1)} %fusion.10, pred[128,2048]{1,0:T(8,128)(4,1)S(1)} %copy-done.4), kind=kOutput, calls=%fused_computation.47 | output fusion | flops 12584959 | bytes 17043456 | tf_op jit(solution)/shard_map/sub | solution.py:30
  497.4 5.5 fusion.17
  503.0 16.9 %all-gather.11.cloned.1.call-done = bf16[512,1024]{0,1:T(8,128)(2,1)} async-done(((bf16[128,1024]{0,1:T(8,128)(2,1)}), bf16[512,1024]{0,1:T(8,128)(2,1)}) %all-gather.11.cloned.1.call-update) | async-done | bytes 1048592 | tf_op jit(solution)/shard_map/all_gather | solution.py:102
  519.9 3.9 convolution_convert_fusion
  523.8 29.5 %reduce-scatter.8.cloned.1.call-done = bf16[128,1280]{1,0:T(8,128)(2,1)} async-done(((bf16[512,1280]{1,0:T(8,128)(2,1)}), bf16[128,1280]{1,0:T(8,128)(2,1)}) %reduce-scatter.8.cloned.1.call-update) | async-done | bytes 327696 | tf_op jit(solution)/shard_map/reduce_scatter | solution.py:104
  553.3 1.8 add_convert_fusion
  (89 shorter events, 13.5 us)
Async XLA Ops:
  6.5 513.4 %copy-start = (bf16[1024,1280]{1,0:T(8,128)(2,1)S(1)}, bf16[1024,1280]{1,0:T(8,128)(2,1)}, u32[]{:S(2)}) copy-start(bf16[1024,1280]{1,0:T(8,128)(2,1)} %param.21) | copy-start | bytes 7864324
  6.5 292.7 %reduce-scatter.4.cloned.1.call-start = ((), (), s32[]{:S(2)}) async-start(), calls=%async_computation.3 | async-start | bytes 3276800 | tf_op jit(solution)/shard_map/reduce_scatter | solution.py:74
  230.1 18.1 %copy-start.7 = (bf16[1280]{0:T(1024)(128)(2,1)S(1)}, bf16[1280]{0:T(1024)(128)(2,1)}, u32[]{:S(2)}) copy-start(bf16[1280]{0:T(1024)(128)(2,1)} %param.15) | copy-start | bytes 7684
  230.1 77.0 %copy-start.5 = (f32[1280]{0:T(1024)S(1)}, f32[1280]{0:T(1024)}, u32[]{:S(2)}) copy-start(f32[1280]{0:T(1024)} %param.17) | copy-start | bytes 15364
  230.1 77.0 %copy-start.6 = (f32[1280]{0:T(1024)S(1)}, f32[1280]{0:T(1024)}, u32[]{:S(2)}) copy-start(f32[1280]{0:T(1024)} %param.16) | copy-start | bytes 15364
  248.1 93.1 %all-gather.7.cloned.1.call-start = ((), (), s32[]{:S(2)}) async-start(), calls=%async_computation.5 | async-start | bytes 1638400 | tf_op jit(solution)/shard_map/all_gather | solution.py:83
  309.1 101.0 %reduce-scatter.6.cloned.1.call-start = ((), (), s32[]{:S(2)}) async-start(), calls=%async_computation.6 | async-start | bytes 7864320 | tf_op jit(solution)/shard_map/reduce_scatter | solution.py:87
  351.8 60.9 %copy-start.8 = (s32[512]{0:T(512)S(1)}, s32[512]{0:T(512)}, u32[]{:S(2)}) copy-start(s32[512]{0:T(512)} %param.20) | copy-start | bytes 6148
  351.8 106.1 %all-gather.5.cloned.1.call-start = ((), (), s32[]{:S(2)}) async-start(), calls=%async_computation.4 | async-start | bytes 7864320 | tf_op jit(solution)/shard_map/all_gather | solution.py:95
  354.4 127.5 %all-gather.9.cloned.1.call-start = ((), (), s32[]{:S(2)}) async-start(), calls=%async_computation.7 | async-start | bytes 2621440 | tf_op jit(solution)/shard_map/all_gather | solution.py:94
  412.4 107.5 %all-gather.11.cloned.1.call-start = ((), (), s32[]{:S(2)}) async-start(), calls=%async_computation.8 | async-start | bytes 1310720 | tf_op jit(solution)/shard_map/all_gather | solution.py:102
  488.1 3.5 copy-start.4
  491.6 5.8 %copy-start.2 = (bf16[1,1536,1024]{1,2,0:T(8,128)(2,1)S(1)}, bf16[1,1536,1024]{1,2,0:T(8,128)(2,1)}, u32[]{:S(2)}) copy-start(bf16[1,1536,1024]{1,2,0:T(8,128)(2,1)} %get-tuple-element.55) | copy-start | bytes 9437188
  491.6 5.8 %copy-start.3 = (bf16[512,1024]{0,1:T(8,128)(2,1)S(1)}, bf16[512,1024]{0,1:T(8,128)(2,1)}, u32[]{:S(2)}) copy-start(bf16[512,1024]{0,1:T(8,128)(2,1)} %copy.33) | copy-start | bytes 3145732
  497.4 55.9 %copy-start.1 = (f32[128,1280]{1,0:T(8,128)S(1)}, f32[128,1280]{1,0:T(8,128)}, u32[]{:S(2)}) copy-start(f32[128,1280]{1,0:T(8,128)} %reduce-scatter.4.cloned.1.call-done) | copy-start | bytes 1966084
  502.9 50.4 %reduce-scatter.8.cloned.1.call-start = ((), (), s32[]{:S(2)}) async-start(), calls=%async_computation.9 | async-start | bytes 1638400 | tf_op jit(solution)/shard_map/reduce_scatter | solution.py:104
Sparse Core Ops, SparseCore 0:
  248.2 51.0 reduce-scatter.3
  309.2 31.9 all-gather.6
  351.9 58.0 reduce-scatter.5
  411.5 46.2 all-gather.4
  459.3 22.5 all-gather.8
  503.1 16.8 all-gather.10
  524.0 29.3 reduce-scatter.7
where the time goes:
time: 566 us; the launch traced here: 562 us
  waiting for transfers between devices  232 us (41%)
  other arithmetic  196 us (35%)
  local copies, waits for them, and re-layouts  45 us (8%)
  matrix products  41.5 us (7%)
  blocking collectives  32.9 us (6%)
  between operations  13.6 us (2%)
    reduce_sum x16, other arithmetic, one_block(): return jnp.sum(picked, axis=1, dtype=jnp.bfloat16)  182 us
    reduce_scatter x1, waiting for transfers between devices, body(): lax.psum_scatter(jnp.dot(block, w_flat, preferred_element_type=jnp.float3...  55.5 us
    reduce_scatter x1, waiting for transfers between devices, body(): lax.psum_scatter(jnp.dot(block, decoder, preferred_element_type=jnp.float...  51.1 us
    all_gather x1, waiting for transfers between devices, body(): context = lax.all_gather(cache_kv, 'col', axis=1, tiled=True)  44.2 us
    reduce_scatter x1, waiting for transfers between devices, body(): lax.psum_scatter(jnp.dot(block, w_out, preferred_element_type=jnp.float32...  29.5 us
    all_gather x1, waiting for transfers between devices, body(): lax.all_gather(normalize(residual, sums, ln_gain, ln_bias), 'lat', axis=0...  21.2 us
    dot_general x1, matrix products, body(): jnp.dot(block, decoder, preferred_element_type=jnp.float32)  18 us
    all_gather x1, waiting for transfers between devices, body(): gathered = lax.all_gather(attended, 'col', axis=0, tiled=True)  16.9 us
  transfers between devices with their start and end apart: 7, of which 7 were waited for; matrix products, arithmetic and copies ran while one was open for 5% of the time, Pallas kernels for 0%

commit v1 on v0

v1 whole, which is shorter than its diff:
```python
import functools
import math

import jax
import jax.numpy as jnp
from jax import lax
from jax.experimental import pallas as pl
from jax.experimental.pallas import tpu as pltpu
from jax.sharding import PartitionSpec as P

D = 5120
HEAD = 128
GROUP = 8
VMEM_BYTES = 48 * 1024 * 1024


def densify_kernel(base_ref, ids_ref, vals_ref, out_ref, *, topk, latents, lanes):
    groups, width = ids_ref.shape
    high = latents // lanes
    base = base_ref[0]
    row_of = lax.broadcasted_iota(jnp.int32, (1, width), 1) // topk
    sub = lax.broadcasted_iota(jnp.int32, (high * GROUP, width), 0)
    low_sub = lax.broadcasted_iota(jnp.int32, (lanes, width), 0)

    def one_group(g):
        local = ids_ref[pl.ds(g, 1), :].astype(jnp.int32) - base
        inside = (local >= 0) & (local < latents)
        key = jnp.where(inside, (local // lanes) * GROUP + row_of, -1)
        low = jnp.where(inside, local % lanes, -1)
        vals = vals_ref[pl.ds(g, 1), :]
        left = jnp.where(key == sub, vals, 0.0).astype(jnp.bfloat16)
        right = jnp.where(low == low_sub, 1.0, 0.0).astype(jnp.bfloat16)
        dense = lax.dot_general(
            left, right, (((1,), (1,)), ((), ())), preferred_element_type=jnp.float32
        )
        return dense.reshape(high, GROUP, lanes)

    def pair(i, carry):
        both = jnp.concatenate([one_group(2 * i), one_group(2 * i + 1)], axis=1)
        both = both.astype(jnp.bfloat16)
        rows = pl.ds(pl.multiple_of(i * 2 * GROUP, 2 * GROUP), 2 * GROUP)
        for h in range(high):
            out_ref[rows, h * lanes : (h + 1) * lanes] = both[h]
        return carry

    lax.fori_loop(0, groups // 2, pair, 0)


def densify(ids, vals, base, topk, latents):
    groups, width = ids.shape
    lanes = 256 if latents % 256 == 0 else 128
    rows = groups * GROUP
    return pl.pallas_call(
        functools.partial(densify_kernel, topk=topk, latents=latents, lanes=lanes),
        out_shape=jax.ShapeDtypeStruct((rows, latents), jnp.bfloat16),
        in_specs=[
            pl.BlockSpec(memory_space=pltpu.SMEM),
            pl.BlockSpec(memory_space=pltpu.VMEM),
            pl.BlockSpec(memory_space=pltpu.VMEM),
        ],
        out_specs=pl.BlockSpec(memory_space=pltpu.VMEM),
        compiler_params=pltpu.CompilerParams(vmem_limit_bytes=VMEM_BYTES),
        cost_estimate=pl.CostEstimate(
            flops=2 * groups * GROUP * latents * width,
            bytes_accessed=rows * latents * 2,
            transcendentals=0,
        ),
        name="densify",
    )(base, ids, vals)


def decode_kernel(*refs):
    codes, weights, out = refs[:-2], refs[-2], refs[-1]
    block = jnp.concatenate([c[...] for c in codes], axis=0)
    part = jnp.dot(block, weights[...], preferred_element_type=jnp.float32)

    @pl.when(pl.program_id(0) == 0)
    def _():
        out[...] = part

    @pl.when(pl.program_id(0) > 0)
    def _():
        out[...] += part


def decode(codes, decoder):
    rows, latents = codes[0].shape
    columns = decoder.shape[1]
    depth = math.gcd(latents, 1024)
    total = rows * len(codes)
    return pl.pallas_call(
        decode_kernel,
        out_shape=jax.ShapeDtypeStruct((total, columns), jnp.float32),
        grid=(latents // depth,),
        in_specs=[pl.BlockSpec((rows, depth), lambda k: (0, k)) for _ in codes]
        + [pl.BlockSpec((depth, columns), lambda k: (k, 0))],
        out_specs=pl.BlockSpec((total, columns), lambda k: (0, 0)),
        compiler_params=pltpu.CompilerParams(
            dimension_semantics=("arbitrary",), vmem_limit_bytes=VMEM_BYTES
        ),
        cost_estimate=pl.CostEstimate(
            flops=2 * total * latents * columns,
            bytes_accessed=latents * (total + columns) * 2 + total * columns * 4,
            transcendentals=0,
        ),
        name="decode",
    )(*codes, decoder)


def attend_kernel(*refs, heads, slots, slot):
    query_pos, key_pos = refs[0], refs[1]
    new = refs[2 : 2 + slots]
    cached = refs[2 + slots : -1]
    out = refs[-1]
    width = heads * HEAD
    hidden = key_pos[...] > query_pos[...]
    for h in range(heads):
        here = slice(h * HEAD, (h + 1) * HEAD)
        keys = [c[0, :, here] for c in cached] + [
            n[:, width + h * HEAD : width + (h + 1) * HEAD] for n in new
        ]
        values = [c[1, :, here] for c in cached] + [
            n[:, 2 * width + h * HEAD : 2 * width + (h + 1) * HEAD] for n in new
        ]
        keys = jnp.concatenate(keys, axis=0)
        values = jnp.concatenate(values, axis=0)
        scores = lax.dot_general(
            new[slot][:, here], keys, (((1,), (1,)), ((), ())), preferred_element_type=jnp.float32
        ) * (1.0 / math.sqrt(HEAD))
        cut = scores.shape[1] - hidden.shape[1]
        old, fresh = scores[:, :cut], jnp.where(hidden, -1e30, scores[:, cut:])
        highest = jnp.maximum(
            jnp.max(old, axis=1, keepdims=True), jnp.max(fresh, axis=1, keepdims=True)
        )
        old, fresh = jnp.exp(old - highest), jnp.exp(fresh - highest)
        total = jnp.sum(old, axis=1, keepdims=True) + jnp.sum(fresh, axis=1, keepdims=True)
        scale = 1.0 / total
        probs = jnp.concatenate(
            [(old * scale).astype(jnp.bfloat16), (fresh * scale).astype(jnp.bfloat16)], axis=1
        )
        mixed = jnp.dot(probs, values, preferred_element_type=jnp.float32)
        out[:, here] = mixed.astype(jnp.bfloat16)


def attend(query_pos, key_pos, new, cached, slot, heads):
    rows = new[0].shape[0]
    keys = rows * len(new) + sum(c.shape[1] for c in cached)
    vmem = pl.BlockSpec(memory_space=pltpu.VMEM)
    return pl.pallas_call(
        functools.partial(attend_kernel, heads=heads, slots=len(new), slot=slot),
        out_shape=jax.ShapeDtypeStruct((rows, heads * HEAD), jnp.bfloat16),
        in_specs=[vmem] * (2 + len(new) + len(cached)),
        out_specs=vmem,
        compiler_params=pltpu.CompilerParams(vmem_limit_bytes=VMEM_BYTES),
        cost_estimate=pl.CostEstimate(
            flops=4 * rows * keys * heads * HEAD,
            bytes_accessed=keys * heads * HEAD * 4,
            transcendentals=rows * keys * heads,
        ),
        name="attend",
    )(query_pos, key_pos, *new, *cached)


PAIRS = [(0, 1), (1, 0), (2, 3), (3, 2)]
INWARD = [(0, 1), (3, 2)]
MIDDLE = [(1, 2), (2, 1)]
OUTWARD = [(1, 0), (2, 3)]


def line_slots(index):
    low = index < 2
    return [index, index ^ 1, jnp.where(low, 2, 1), jnp.where(low, 3, 0)]


def line_gather(own, outer):
    near = lax.ppermute(own, "lat", PAIRS)
    across = lax.ppermute(own, "lat", MIDDLE)
    far = lax.ppermute(near, "lat", MIDDLE)
    across_out = lax.ppermute(across, "lat", OUTWARD)
    far_out = lax.ppermute(far, "lat", OUTWARD)
    return [own, near, jnp.where(outer, across_out, across), jnp.where(outer, far_out, far)]


def line_sum(parts, encode, decode_sent):
    in_far = lax.ppermute(encode(parts[3]), "lat", INWARD)
    in_across = lax.ppermute(encode(parts[2]), "lat", INWARD)
    far = lax.ppermute(encode(parts[3] + decode_sent(in_far)), "lat", MIDDLE)
    across = lax.ppermute(encode(parts[2] + decode_sent(in_across)), "lat", MIDDLE)
    near = lax.ppermute(encode(parts[1] + decode_sent(far)), "lat", PAIRS)
    return parts[0] + decode_sent(across) + decode_sent(near)


def swap(value, distance, size):
    return lax.ppermute(value, "col", [(i, i ^ distance) for i in range(size)])


def normalize(values, sums, gain, shift):
    row_mean = sums[0] / D
    row_var = sums[1] / D - row_mean * row_mean
    inverse = 1.0 / jnp.sqrt(row_var + 1e-05)
    return ((values - row_mean[:, None]) * inverse[:, None] * gain + shift).astype(jnp.bfloat16)


SCALE = 256.0


def to_half(value):
    return (value * SCALE).astype(jnp.float16)


def from_half(value):
    return value.astype(jnp.float32) * (1.0 / SCALE)


def line_body(
    code_ids, code_vals, decoder, dec_bias, ln_gain, ln_bias, w_qkv, cache_kv, positions, w_out
):
    lat = lax.axis_index("lat")
    col = lax.axis_index("col")
    cols = lax.axis_size("col")
    rows, topk = code_ids.shape
    latents, columns = decoder.shape
    head_width = w_qkv.shape[2]
    own_width = head_width // cols
    heads = own_width // HEAD
    outer = (lat == 0) | (lat == 3)
    slots = line_slots(lat)

    packed = jnp.concatenate(
        [
            code_ids.reshape(rows // GROUP, GROUP * topk).astype(jnp.float32),
            code_vals.astype(jnp.bfloat16)
            .astype(jnp.float32)
            .reshape(rows // GROUP, GROUP * topk),
        ],
        axis=1,
    )
    packed = line_gather(packed, outer)
    base = (lat * latents).reshape(1)

    def cache_of(j):
        start = (col ^ j) * own_width
        return lax.dynamic_slice_in_dim(cache_kv, start, own_width, 2)

    sent = swap(jnp.stack([cache_of(1), cache_of(3)]), 1, cols)
    other = swap(jnp.stack([cache_of(2), sent[1]]), 2, cols)
    cached = [cache_of(0), sent[0], other[0], other[1]]

    weights = jnp.concatenate(
        [
            lax.dynamic_slice_in_dim(w_qkv, (col ^ j) * own_width, own_width, 2).reshape(
                w_qkv.shape[0], 3 * own_width
            )
            for j in (1, 3, 0, 2)
        ],
        axis=1,
    )
    out_weights = jnp.concatenate(
        [
            lax.dynamic_slice_in_dim(w_out, (col ^ j) * own_width, own_width, 0)
            for j in (0, 2, 1, 3)
        ],
        axis=0,
    )
    key_pos = jnp.concatenate(
        [lax.dynamic_slice_in_dim(positions, s * rows, rows, 0) for s in slots]
    )

    codes = [
        densify(p[:, : GROUP * topk], p[:, GROUP * topk :], base, topk, latents) for p in packed
    ]
    far = decode([codes[3], codes[2]], decoder)
    near = decode([codes[1], codes[0]], decoder)
    parts = [near[rows:], near[:rows], far[rows:], far[:rows]]
    residual = line_sum(parts, to_half, from_half) + dec_bias.astype(jnp.float32)

    sums = jnp.stack([jnp.sum(residual, axis=1), jnp.sum(residual * residual, axis=1)])
    sums = sums + swap(sums, 1, cols)
    sums = sums + swap(sums, 2, cols)
    normed = line_gather(normalize(residual, sums, ln_gain, ln_bias), outer)

    half = weights.shape[1] // 2
    quarter = half // 2

    def project(block):
        away = jnp.dot(block, weights[:, :half], preferred_element_type=jnp.float32)
        keep = jnp.dot(block, weights[:, half:], preferred_element_type=jnp.float32)
        keep = keep + swap(away.astype(jnp.float16), 1, cols).astype(jnp.float32)
        came = swap(keep[:, quarter:].astype(jnp.float16), 2, cols).astype(jnp.float32)
        return (keep[:, :quarter] + came).astype(jnp.bfloat16)

    qkv = [project(block) for block in normed]

    branch = [None] * 4
    for slot in (3, 2, 1, 0):
        query_pos = key_pos[slot * rows : (slot + 1) * rows].reshape(rows, 1)
        mixed = attend(query_pos, key_pos.reshape(1, -1), qkv, cached, slot, heads)
        mixed = jnp.concatenate([mixed, swap(mixed, 2, cols)], axis=1)
        mixed = jnp.concatenate([mixed, swap(mixed, 1, cols)], axis=1)
        branch[slot] = jnp.dot(mixed, out_weights, preferred_element_type=jnp.float32)
    added = line_sum(
        branch, lambda v: v.astype(jnp.bfloat16), lambda v: v.astype(jnp.float32)
    )
    return (residual + added).astype(jnp.bfloat16)


def attend_block(queries, keys, values, query_pos, key_pos):
    heads = queries.shape[1] // HEAD
    query_heads = queries.reshape(queries.shape[0], heads, HEAD)
    key_heads = keys.reshape(keys.shape[0], heads, HEAD)
    value_heads = values.reshape(values.shape[0], heads, HEAD)
    scores = jnp.einsum(
        "qhe,khe->hqk", query_heads, key_heads, preferred_element_type=jnp.float32
    ) * (1.0 / math.sqrt(HEAD))
    visible = key_pos[None, None, :] <= query_pos[None, :, None]
    scores = jnp.where(visible, scores, -1e30)
    highest = jnp.max(scores, axis=-1, keepdims=True)
    expo = jnp.exp(scores - highest)
    probs = (expo / jnp.sum(expo, axis=-1, keepdims=True)).astype(jnp.bfloat16)
    mixed = jnp.einsum("hqk,khe->qhe", probs, value_heads, preferred_element_type=jnp.float32)
    return mixed.reshape(queries.shape[0], heads * HEAD).astype(jnp.bfloat16)


def general_body(
    code_ids, code_vals, decoder, dec_bias, ln_gain, ln_bias, w_qkv, cache_kv, positions, w_out
):
    lat_index = lax.axis_index("lat")
    col_total = lax.axis_size("col")
    col_index = lax.axis_index("col")
    rows, topk = code_ids.shape
    shard_latents = decoder.shape[0]
    packed = jnp.concatenate(
        [
            code_ids.reshape(rows // GROUP, GROUP * topk).astype(jnp.float32),
            code_vals.astype(jnp.bfloat16)
            .astype(jnp.float32)
            .reshape(rows // GROUP, GROUP * topk),
        ],
        axis=1,
    )
    packed = lax.all_gather(packed, "lat", axis=0, tiled=True)
    base = (lat_index * shard_latents).reshape(1)
    dense_codes = densify(
        packed[:, : GROUP * topk], packed[:, GROUP * topk :], base, topk, shard_latents
    )
    total_rows = dense_codes.shape[0]
    col_rows = total_rows // col_total
    residual = lax.psum_scatter(
        jnp.dot(dense_codes, decoder, preferred_element_type=jnp.float32),
        "lat",
        scatter_dimension=0,
        tiled=True,
    ) + dec_bias.astype(jnp.float32)
    sums = lax.psum((jnp.sum(residual, axis=1), jnp.sum(residual * residual, axis=1)), "col")
    normed = lax.all_gather(normalize(residual, sums, ln_gain, ln_bias), "lat", axis=0, tiled=True)
    head_width = w_qkv.shape[2]
    w_flat = w_qkv.reshape(w_qkv.shape[0], 3 * head_width)
    own_rows = lax.psum_scatter(
        jnp.dot(normed, w_flat, preferred_element_type=jnp.float32),
        "col",
        scatter_dimension=0,
        tiled=True,
    ).astype(jnp.bfloat16)
    queries = own_rows[:, :head_width]
    new_kv = lax.all_gather(own_rows[:, head_width:], "col", axis=0, tiled=True)
    context = lax.all_gather(cache_kv, "col", axis=1, tiled=True)
    cached_len = context.shape[1]
    keys = jnp.concatenate([context[0], new_kv[:, :head_width]], axis=0)
    values = jnp.concatenate([context[1], new_kv[:, head_width:]], axis=0)
    key_pos = jnp.concatenate([jnp.arange(cached_len, dtype=jnp.int32), cached_len + positions])
    query_pos = cached_len + lax.dynamic_slice_in_dim(positions, col_index * col_rows, col_rows, 0)
    attended = attend_block(queries, keys, values, query_pos, key_pos)
    gathered = lax.all_gather(attended, "col", axis=0, tiled=True)
    branch_out = lax.psum_scatter(
        jnp.dot(gathered, w_out, preferred_element_type=jnp.float32).astype(jnp.bfloat16),
        "lat",
        scatter_dimension=0,
        tiled=True,
    ).astype(jnp.float32)
    return (residual + branch_out).astype(jnp.bfloat16)


def solution(mesh):
    def program(*args):
        lats, cols = mesh.shape["lat"], mesh.shape["col"]
        heads = args[6].shape[2] // HEAD // lats
        fits = lats == 4 and cols == 4 and heads % cols == 0
        return jax.shard_map(
            line_body if fits else general_body,
            mesh=mesh,
            in_specs=(
                P(("ckpt", "lat"), None),
                P(("ckpt", "lat"), None),
                P(("ckpt", "lat"), "col"),
                P(("ckpt", "col")),
                P(("ckpt", "col")),
                P(("ckpt", "col")),
                P(("ckpt", "col"), None, "lat"),
                P(None, ("ckpt", "col"), "lat"),
                P("ckpt"),
                P(("ckpt", "lat"), "col"),
            ),
            out_specs=P(("ckpt", "lat"), "col"),
            check_vma=False,
        )(*args)

    return program
```

time: 566 us -> 208 us (0.37)
  other arithmetic: 196 us -> 5.05 us
  waiting for transfers between devices: 232 us -> 61.5 us
  starting transfers between devices: 0.43 us -> 50.6 us
  Pallas kernels: 0 us -> 43 us
  blocking collectives: 32.9 us -> 0 us
  matrix products: 41.5 us -> 16.3 us
  local copies, waits for them, and re-layouts: 45 us -> 27.2 us
  between operations: 13.6 us -> 0.87 us
    reduce_sum x17 -> x1, other arithmetic: 184 us -> 1.27 us  [line_body(): jnp.sum(residual, axis=1)]
    reduce_scatter x3 -> x0, waiting for transfers between devices: 136 us -> none  [the longest x1 55.5 us: body(): lax.psum_scatter(jnp.dot(block, w_flat, preferred_element_type=jnp.float3...]
    all_gather x4 -> x0, waiting for transfers between devices: 95.8 us -> none  [the longest x1 44.2 us: body(): context = lax.all_gather(cache_kv, 'col', axis=1, tiled=True)]
    ppermute x0 -> x40, waiting for transfers between devices: none -> 61.5 us  [the longest x20 32.6 us: swap(): return lax.ppermute(value, 'col', [(i, i ^ distance) for i in range(size)])]
    ppermute x0 -> x40, starting transfers between devices: none -> 50.6 us  [the longest x20 13.5 us: swap(): return lax.ppermute(value, 'col', [(i, i ^ distance) for i in range(size)])]
    pallas_call x0 -> x10, Pallas kernels: none -> 43 us  [the longest x2 24.9 us: decode(): pl.pallas_call(decode_kernel, out_shape=jax.ShapeDtypeStruct((total, colu...]
    all_gather x2 -> x0, blocking collectives: 26.4 us -> none  [the longest x1 14.2 us: body(): lax.all_gather(code_ids, 'lat', axis=0, tiled=True)]
    dot_general x5 -> x12, matrix products: 41.5 us -> 16.3 us  [the longest x4 7.87 us: project(): away = jnp.dot(block, weights[:, :half], preferred_element_type=jnp.float32)]
  transfers between devices with their start and end apart: 7 -> 40, of which waited for: 7 -> 19; matrix products, arithmetic and copies ran while one was open for 5% -> 22% of each run, Pallas kernels for 0% -> 20%
where the time goes in v1:
time: 208 us; the launch traced here: 205 us
  waiting for transfers between devices  61.5 us (30%)
  starting transfers between devices  50.6 us (24%)
  Pallas kernels  43 us (21%)
  local copies, waits for them, and re-layouts  27.2 us (13%)
  matrix products  16.3 us (8%)
  other arithmetic  5.05 us (2%)
    ppermute x20, waiting for transfers between devices, swap(): return lax.ppermute(value, 'col', [(i, i ^ distance) for i in range(size)])  32.6 us
    pallas_call x2, Pallas kernels, decode(): pl.pallas_call(decode_kernel, out_shape=jax.ShapeDtypeStruct((total, colu...  24.9 us
    ppermute x2, waiting for transfers between devices, line_sum(): in_far = lax.ppermute(encode(parts[3]), 'lat', INWARD)  14.6 us
    unnamed x35, local copies, waits for them, and re-layouts  14.5 us
    ppermute x20, starting transfers between devices, swap(): return lax.ppermute(value, 'col', [(i, i ^ distance) for i in range(size)])  13.5 us
    pallas_call x4, Pallas kernels, densify(): pl.pallas_call(functools.partial(densify_kernel, topk=topk, latents=laten...  11.7 us
    ppermute x2, starting transfers between devices, line_gather(): across = lax.ppermute(own, 'lat', MIDDLE)  8.5 us
    ppermute x2, waiting for transfers between devices, line_sum(): in_across = lax.ppermute(encode(parts[2]), 'lat', INWARD)  8.17 us
  transfers between devices with their start and end apart: 40, of which 19 were waited for; matrix products, arithmetic and copies ran while one was open for 22% of the time, Pallas kernels for 20%

profile of v1, /device:TPU:8, one launch (start us, length us, event | category | flops | bytes accessed | tf_op | source)
XLA Modules:
  0.0 204.5 jit_solution(10527323840082984521)
XLA Ops:
  1.9 5.0 %collective-permute-start.3 = (f32[16,1024]{1,0:T(8,128)S(1)}, f32[16,1024]{1,0:T(8,128)S(1)}, u32[]{:S(2)}, u32[]{:S(2)}) collective-permute-start(f32[16,1024]{1,0:T(8,128)S(1)} %constant_dynamic-update-slice_fusion), channel_id=1, source_target_pairs={{4,8},{8,4},{5,9},{9,5},{6,10},{10,6},{7,11},{11,7},{20,24},{24,20... | collective-permute-start | bytes 196616 | tf_op jit(solution)/shard_map/ppermute | solution.py:177
  7.0 2.2 %dynamic-slice_bitcast_fusion = (bf16[1,2,384,256]{3,2,1,0:T(8,128)(2,1)}, bf16[1,2,384,256]{3,2,1,0:T(8,128)(2,1)S(1)}, bf16[2,384,256]{2,1,0:T(8,128)(2,1)S(1)}, bf16[1,2,384,256]{3,2,1,0:T(8,128)(2,1)S(1)}) fusion(bf16[2,384,1024]{2,1,0:T(8,128)(2,1)} %param.17, s32[]{:T(128)S(6)} %select_n.73, s32[]{:T(128)S(6)} %select_n.74, s32[]{:T(128)S(6)} %select_n.72, ...), kind=kLoop, calls=%fused_computation.48 | loop fusion | bytes 3145744 | tf_op jit(solution)/shard_map/stack | solution.py:246
  11.5 3.9 %collective-permute-start.1 = (f32[16,1024]{1,0:T(8,128)S(1)}, f32[16,1024]{1,0:T(8,128)S(1)}, u32[]{:S(2)}, u32[]{:S(2)}) collective-permute-start(f32[16,1024]{1,0:T(8,128)S(1)} %collective-permute-done), channel_id=1, source_target_pairs={{4,8},{8,4},{5,9},{9,5},{6,10},{10,6},{7,11},{11,7},{20,24},{24,20... | collective-permute-start | bytes 196616 | tf_op jit(solution)/shard_map/ppermute | solution.py:178
  15.5 2.7 %collective-permute-done.1 = f32[16,1024]{1,0:T(8,128)S(1)} collective-permute-done((f32[16,1024]{1,0:T(8,128)S(1)}, f32[16,1024]{1,0:T(8,128)S(1)}, u32[]{:S(2)}, u32[]{:S(2)}) %collective-permute-start.1) | collective-permute-done | bytes 65568 | tf_op jit(solution)/shard_map/ppermute | solution.py:178
  19.4 2.9 %densify.7.refs_1_ = bf16[128,8192]{1,0:T(8,128)(2,1)S(1)} custom-call(s32[1]{0:T(128)} %bitcast.base_ref, f32[16,512]{1,0:T(8,128)S(1)} %get-tuple-element.29.ids_ref, f32[16,512]{1,0:T(8,128)S(1)} %get-tuple-element.28.vals_ref), custom_call_target="tpu_custom_call" | custom-call | flops 1073741824 | bytes 2097152 | tf_op jit(solution)/shard_map/densify/pallas_call | solution.py:53
  22.4 2.9 %densify.6.refs_0_ = bf16[128,8192]{1,0:T(8,128)(2,1)S(1)} custom-call(s32[1]{0:T(128)} %bitcast.base_ref, f32[16,512]{1,0:T(8,128)S(1)} %get-tuple-element.31.ids_ref, f32[16,512]{1,0:T(8,128)S(1)} %get-tuple-element.30.vals_ref), custom_call_target="tpu_custom_call" | custom-call | flops 1073741824 | bytes 2097152 | tf_op jit(solution)/shard_map/densify/pallas_call | solution.py:53
  25.3 12.4 %decode.3 = f32[256,1280]{1,0:T(8,128)S(1)} custom-call(bf16[128,8192]{1,0:T(8,128)(2,1)S(1)} %densify.6.refs_0_, bf16[128,8192]{1,0:T(8,128)(2,1)S(1)} %densify.7.refs_1_, bf16[8192,1280]{1,0:T(8,128)(2,1)} %refs_2_.3), custom_call_target="tpu_custom_call" | custom-call | flops 5368709120 | bytes 26476544 | tf_op jit(solution)/shard_map/decode/pallas_call | solution.py:91
  40.5 2.9 %densify.5.refs_1_ = bf16[128,8192]{1,0:T(8,128)(2,1)S(1)} custom-call(s32[1]{0:T(128)} %bitcast.base_ref, f32[16,512]{1,0:T(8,128)S(1)} %convert_element_type.131.ids_ref, f32[16,512]{1,0:T(8,128)S(1)} %reshape.77.vals_ref), custom_call_target="tpu_custom_call" | custom-call | flops 1073741824 | bytes 2097152 | tf_op jit(solution)/shard_map/densify/pallas_call | solution.py:53
  43.4 2.9 %densify.4.refs_0_ = bf16[128,8192]{1,0:T(8,128)(2,1)S(1)} custom-call(s32[1]{0:T(128)} %bitcast.base_ref, f32[16,512]{1,0:T(8,128)S(1)} %get-tuple-element.33.ids_ref, f32[16,512]{1,0:T(8,128)S(1)} %get-tuple-element.32.vals_ref), custom_call_target="tpu_custom_call" | custom-call | flops 1073741824 | bytes 2097152 | tf_op jit(solution)/shard_map/densify/pallas_call | solution.py:53
  46.4 4.0 %collective-permute-done.5 = f16[128,1280]{1,0:T(8,128)(2,1)S(1)} collective-permute-done((f16[128,1280]{1,0:T(8,128)(2,1)S(1)}, f16[128,1280]{1,0:T(8,128)(2,1)S(1)}, u32[]{:S(2)}, u32[]{:S(2)}) %collective-permute-start.5) | collective-permute-done | bytes 327712 | tf_op jit(solution)/shard_map/ppermute | solution.py:186
  50.4 5.9 %collective-permute-done.7 = f16[128,1280]{1,0:T(8,128)(2,1)S(1)} collective-permute-done((f16[128,1280]{1,0:T(8,128)(2,1)S(1)}, f16[128,1280]{1,0:T(8,128)(2,1)S(1)}, u32[]{:S(2)}, u32[]{:S(2)}) %collective-permute-start.7) | collective-permute-done | bytes 327712 | tf_op jit(solution)/shard_map/ppermute | solution.py:185
  56.6 3.5 %collective-permute-start.8 = (f16[128,1280]{1,0:T(8,128)(2,1)S(1)}, f16[128,1280]{1,0:T(8,128)(2,1)S(1)}, u32[]{:S(2)}, u32[]{:S(2)}) collective-permute-start(f16[128,1280]{1,0:T(8,128)(2,1)S(1)} %get-tuple-element.21), channel_id=1, source_target_pairs={{4,8},{8,4},{5,9},{9,5},{6,10},{10,6},{7,11},{11,7},{20,24},{24,20... | collective-permute-start | bytes 983048 | tf_op jit(solution)/shard_map/ppermute | solution.py:187
  60.1 12.4 %decode.2 = f32[256,1280]{1,0:T(8,128)S(1)} custom-call(bf16[128,8192]{1,0:T(8,128)(2,1)S(1)} %densify.4.refs_0_, bf16[128,8192]{1,0:T(8,128)(2,1)S(1)} %densify.5.refs_1_, bf16[8192,1280]{1,0:T(8,128)(2,1)} %refs_2_.3), custom_call_target="tpu_custom_call" | custom-call | flops 5368709120 | bytes 26476544 | tf_op jit(solution)/shard_map/decode/pallas_call | solution.py:91
  72.5 2.4 %collective-permute-start.6 = (f16[128,1280]{1,0:T(8,128)(2,1)S(1)}, f16[128,1280]{1,0:T(8,128)(2,1)S(1)}, u32[]{:S(2)}, u32[]{:S(2)}) collective-permute-start(f16[128,1280]{1,0:T(8,128)(2,1)S(1)} %get-tuple-element.20), channel_id=1, source_target_pairs={{4,8},{8,4},{5,9},{9,5},{6,10},{10,6},{7,11},{11,7},{20,24},{24,20... | collective-permute-start | bytes 983048 | tf_op jit(solution)/shard_map/ppermute | solution.py:188
  75.1 6.8 %constant_dynamic-slice_fusion.8 = (bf16[1280,3,256]{2,0,1:T(8,128)(2,1)}, bf16[1280,3,256]{2,0,1:T(8,128)(2,1)}, bf16[1280,3,256]{2,0,1:T(8,128)(2,1)}, bf16[1280,3,256]{2,0,1:T(8,128)(2,1)}) fusion(bf16[1280,3,1024]{2,0,1:T(8,128)(2,1)} %param.16, s32[]{:T(128)S(6)} %select_n.72, s32[]{:T(128)S(6)} %select_n.74, s32[]{:T(128)S(6)} %select_n.73, ...), kind=kLoop, calls=%fused_computation.92 | loop fusion | bytes 15728656 | tf_op jit(solution)/shard_map/dynamic_slice | solution.py:251
  84.7 4.0 %copy.30 = bf16[1280,3,256]{0,2,1:T(8,128)(2,1)} copy(bf16[1280,3,256]{2,0,1:T(8,128)(2,1)} %get-tuple-element.11) | data formatting | bytes 3932160
  88.7 4.1 %copy.29 = bf16[1280,3,256]{0,2,1:T(8,128)(2,1)} copy(bf16[1280,3,256]{2,0,1:T(8,128)(2,1)} %get-tuple-element.9) | data formatting | bytes 3932160
  92.8 4.0 %copy.27 = bf16[1280,3,256]{0,2,1:T(8,128)(2,1)} copy(bf16[1280,3,256]{2,0,1:T(8,128)(2,1)} %get-tuple-element.8) | data formatting | bytes 3932160
  96.8 2.3 %copy.28 = bf16[1280,3,256]{0,2,1:T(8,128)(2,1)} copy(bf16[1280,3,256]{2,0,1:T(8,128)(2,1)S(1)} %copy-done) | data formatting | bytes 3932160
  99.3 1.6 collective-permute-start.11
  103.9 3.5 %collective-permute-start.17 = (bf16[128,1280]{1,0:T(8,128)(2,1)S(1)}, bf16[128,1280]{1,0:T(8,128)(2,1)S(1)}, u32[]{:S(2)}, u32[]{:S(2)}) collective-permute-start(bf16[128,1280]{1,0:T(8,128)(2,1)S(1)} %add_convert_fusion.2), channel_id=1, source_target_pairs={{4,8},{8,4},{5,9},{9,5},{6,10},{10,6},{7,11},{11,7},{20,24},{24,20... | collective-permute-start | bytes 983048 | tf_op jit(solution)/shard_map/ppermute | solution.py:177
  107.4 3.7 %convolution_convert_fusion.3 = f16[128,1536]{1,0:T(8,128)(2,1)S(1)} fusion(bf16[128,1280]{1,0:T(8,128)(2,1)S(1)} %add_convert_fusion.2, bf16[1280,768]{0,1:T(8,128)(2,1)} %bitcast.50, bf16[1280,768]{0,1:T(8,128)(2,1)} %bitcast.54), kind=kOutput, calls=%fused_computation.13 | convolution fusion | flops 511377408 | bytes 4653056 | tf_op jit(solution)/shard_map/dot_general | solution.py:286
  111.3 1.6 collective-permute-start.26
  114.5 2.4 %collective-permute-start.21 = (bf16[128,1280]{1,0:T(8,128)(2,1)S(1)}, bf16[128,1280]{1,0:T(8,128)(2,1)S(1)}, u32[]{:S(2)}, u32[]{:S(2)}) collective-permute-start(bf16[128,1280]{1,0:T(8,128)(2,1)S(1)} %collective-permute-done.14), channel_id=1, source_target_pairs={{4,8},{8,4},{5,9},{9,5},{6,10},{10,6},{7,11},{11,7},{20,24},{24,20... | collective-permute-start | bytes 983048 | tf_op jit(solution)/shard_map/ppermute | solution.py:178
  119.7 1.5 collective-permute-start.13
  121.3 10.4 %collective-permute-done.26 = bf16[2,2,384,256]{3,2,1,0:T(8,128)(2,1)S(1)} collective-permute-done((bf16[2,2,384,256]{3,2,1,0:T(8,128)(2,1)S(1)}, bf16[2,2,384,256]{3,2,1,0:T(8,128)(2,1)S(1)}, u32[]{:S(2)}, u32[]{:S(2)}) %collective-permute-start.26) | collective-permute-done | bytes 786464 | tf_op jit(solution)/shard_map/ppermute | solution.py:194
  131.7 3.8 %collective-permute-done.13 = f16[128,768]{1,0:T(8,128)(2,1)S(1)} collective-permute-done((f16[128,768]{1,0:T(8,128)(2,1)S(1)}, f16[128,768]{1,0:T(8,128)(2,1)S(1)}, u32[]{:S(2)}, u32[]{:S(2)}) %collective-permute-start.13) | collective-permute-done | bytes 196640 | tf_op jit(solution)/shard_map/ppermute | solution.py:194
  135.6 1.5 collective-permute-start.22
  137.1 1.4 convolution_add_fusion.4
  138.5 1.6 collective-permute-start.16
  141.5 3.5 %collective-permute-done.16 = f16[128,768]{1,0:T(8,128)(2,1)S(1)} collective-permute-done((f16[128,768]{1,0:T(8,128)(2,1)S(1)}, f16[128,768]{1,0:T(8,128)(2,1)S(1)}, u32[]{:S(2)}, u32[]{:S(2)}) %collective-permute-start.16) | collective-permute-done | bytes 196640 | tf_op jit(solution)/shard_map/ppermute | solution.py:194
  145.1 1.4 convolution_convert_fusion
  148.1 1.6 collective-permute-start.20
  151.7 4.2 %collective-permute-done.20 = f16[128,768]{1,0:T(8,128)(2,1)S(1)} collective-permute-done((f16[128,768]{1,0:T(8,128)(2,1)S(1)}, f16[128,768]{1,0:T(8,128)(2,1)S(1)}, u32[]{:S(2)}, u32[]{:S(2)}) %collective-permute-start.20) | collective-permute-done | bytes 196640 | tf_op jit(solution)/shard_map/ppermute | solution.py:194
  155.9 3.7 %collective-permute-done.24 = f16[128,768]{1,0:T(8,128)(2,1)S(1)} collective-permute-done((f16[128,768]{1,0:T(8,128)(2,1)S(1)}, f16[128,768]{1,0:T(8,128)(2,1)S(1)}, u32[]{:S(2)}, u32[]{:S(2)}) %collective-permute-start.24) | collective-permute-done | bytes 196640 | tf_op jit(solution)/shard_map/ppermute | solution.py:194
  159.7 1.6 attend.7
  161.3 1.6 collective-permute-start.35
  162.9 1.5 constant_dynamic-slice_fusion.3
  164.8 1.6 attend.5
  167.1 1.6 attend.6
  168.7 1.6 collective-permute-start.33
  175.2 8.6 %collective-permute-done.37 = bf16[128,1280]{1,0:T(8,128)(2,1)S(1)} collective-permute-done((bf16[128,1280]{1,0:T(8,128)(2,1)S(1)}, bf16[128,1280]{1,0:T(8,128)(2,1)S(1)}, u32[]{:S(2)}, u32[]{:S(2)}) %collective-permute-start.37) | collective-permute-done | bytes 327712 | tf_op jit(solution)/shard_map/ppermute | solution.py:185
  183.9 2.4 %collective-permute-start.38 = (bf16[128,1280]{1,0:T(8,128)(2,1)S(1)}, bf16[128,1280]{1,0:T(8,128)(2,1)S(1)}, u32[]{:S(2)}, u32[]{:S(2)}) collective-permute-start(bf16[128,1280]{1,0:T(8,128)(2,1)S(1)} %add_convert_fusion), channel_id=1, source_target_pairs={{4,8},{8,4},{5,9},{9,5},{6,10},{10,6},{7,11},{11,7},{20,24},{24,20... | collective-permute-start | bytes 983048 | tf_op jit(solution)/shard_map/ppermute | solution.py:187
  186.3 4.2 %collective-permute-done.31 = bf16[128,1280]{1,0:T(8,128)(2,1)S(1)} collective-permute-done((bf16[128,1280]{1,0:T(8,128)(2,1)S(1)}, bf16[128,1280]{1,0:T(8,128)(2,1)S(1)}, u32[]{:S(2)}, u32[]{:S(2)}) %collective-permute-start.31) | collective-permute-done | bytes 327712 | tf_op jit(solution)/shard_map/ppermute | solution.py:186
  190.5 2.6 %collective-permute-start.32 = (bf16[128,1280]{1,0:T(8,128)(2,1)S(1)}, bf16[128,1280]{1,0:T(8,128)(2,1)S(1)}, u32[]{:S(2)}, u32[]{:S(2)}) collective-permute-start(bf16[128,1280]{1,0:T(8,128)(2,1)S(1)} %add_convert_fusion.1), channel_id=1, source_target_pairs={{4,8},{8,4},{5,9},{9,5},{6,10},{10,6},{7,11},{11,7},{20,24},{24,20... | collective-permute-start | bytes 983048 | tf_op jit(solution)/shard_map/ppermute | solution.py:188
  193.1 1.6 collective-permute-done.38
  195.3 1.6 attend.4
  197.5 3.7 %collective-permute-done.27 = bf16[128,256]{1,0:T(8,128)(2,1)S(1)} collective-permute-done((bf16[128,256]{1,0:T(8,128)(2,1)S(1)}, bf16[128,256]{1,0:T(8,128)(2,1)S(1)}, u32[]{:S(2)}, u32[]{:S(2)}) %collective-permute-start.27) | collective-permute-done | bytes 65568 | tf_op jit(solution)/shard_map/ppermute | solution.py:194
  (139 shorter events, 34.9 us)
Async XLA Ops:
  1.9 9.6 %collective-permute-start = (f32[16,1024]{1,0:T(8,128)S(1)}, f32[16,1024]{1,0:T(8,128)S(1)}, u32[]{:S(2)}, u32[]{:S(2)}) collective-permute-start(f32[16,1024]{1,0:T(8,128)S(1)} %constant_dynamic-update-slice_fusion), channel_id=1, source_target_pairs={{0,4},{4,0},{8,12},{12,8},{1,5},{5,1},{9,13},{13,9},{2,6},{6,2},{1... | collective-permute-start | bytes 196616 | tf_op jit(solution)/shard_map/ppermute | solution.py:176
  1.9 7.3 %collective-permute-start.3 = (f32[16,1024]{1,0:T(8,128)S(1)}, f32[16,1024]{1,0:T(8,128)S(1)}, u32[]{:S(2)}, u32[]{:S(2)}) collective-permute-start(f32[16,1024]{1,0:T(8,128)S(1)} %constant_dynamic-update-slice_fusion), channel_id=1, source_target_pairs={{4,8},{8,4},{5,9},{9,5},{6,10},{10,6},{7,11},{11,7},{20,24},{24,20... | collective-permute-start | bytes 196616 | tf_op jit(solution)/shard_map/ppermute | solution.py:177
  9.2 6.2 %collective-permute-start.4 = (f32[16,1024]{1,0:T(8,128)S(1)}, f32[16,1024]{1,0:T(8,128)S(1)}, u32[]{:S(2)}, u32[]{:S(2)}) collective-permute-start(f32[16,1024]{1,0:T(8,128)S(1)} %collective-permute-done.3), channel_id=1, source_target_pairs={{4,0},{8,12},{5,1},{9,13},{6,2},{10,14},{7,3},{11,15},{20,16},{24,... | collective-permute-start | bytes 196616 | tf_op jit(solution)/shard_map/ppermute | solution.py:179
  11.5 89.3 %collective-permute-start.25 = (bf16[2,2,384,256]{3,2,1,0:T(8,128)(2,1)}, bf16[2,2,384,256]{3,2,1,0:T(8,128)(2,1)}, u32[]{:S(2)}, u32[]{:S(2)}) collective-permute-start(bf16[2,2,384,256]{3,2,1,0:T(8,128)(2,1)} %pad_maximum_fusion.3), channel_id=1, source_target_pairs={{0,1},{1,0},{2,3},{3,2},{4,5},{5,4},{6,7},{7,6},{8,9},{9,8},{10,11... | collective-permute-start | bytes 2359304 | tf_op jit(solution)/shard_map/ppermute | solution.py:194
  11.5 6.6 %collective-permute-start.1 = (f32[16,1024]{1,0:T(8,128)S(1)}, f32[16,1024]{1,0:T(8,128)S(1)}, u32[]{:S(2)}, u32[]{:S(2)}) collective-permute-start(f32[16,1024]{1,0:T(8,128)S(1)} %collective-permute-done), channel_id=1, source_target_pairs={{4,8},{8,4},{5,9},{9,5},{6,10},{10,6},{7,11},{11,7},{20,24},{24,20... | collective-permute-start | bytes 196616 | tf_op jit(solution)/shard_map/ppermute | solution.py:178
  18.2 4.2 %collective-permute-start.2 = (f32[16,1024]{1,0:T(8,128)S(1)}, f32[16,1024]{1,0:T(8,128)S(1)}, u32[]{:S(2)}, u32[]{:S(2)}) collective-permute-start(f32[16,1024]{1,0:T(8,128)S(1)} %collective-permute-done.1), channel_id=1, source_target_pairs={{4,0},{8,12},{5,1},{9,13},{6,2},{10,14},{7,3},{11,15},{20,16},{24,... | collective-permute-start | bytes 196616 | tf_op jit(solution)/shard_map/ppermute | solution.py:180
  37.9 12.5 %collective-permute-start.5 = (f16[128,1280]{1,0:T(8,128)(2,1)S(1)}, f16[128,1280]{1,0:T(8,128)(2,1)S(1)}, u32[]{:S(2)}, u32[]{:S(2)}) collective-permute-start(f16[128,1280]{1,0:T(8,128)(2,1)S(1)} %get-tuple-element.22), channel_id=1, source_target_pairs={{0,4},{12,8},{1,5},{13,9},{2,6},{14,10},{3,7},{15,11},{16,20},{28,... | collective-permute-start | bytes 983048 | tf_op jit(solution)/shard_map/ppermute | solution.py:186
  39.2 17.1 %collective-permute-start.7 = (f16[128,1280]{1,0:T(8,128)(2,1)S(1)}, f16[128,1280]{1,0:T(8,128)(2,1)S(1)}, u32[]{:S(2)}, u32[]{:S(2)}) collective-permute-start(f16[128,1280]{1,0:T(8,128)(2,1)S(1)} %get-tuple-element.23), channel_id=1, source_target_pairs={{0,4},{12,8},{1,5},{13,9},{2,6},{14,10},{3,7},{15,11},{16,20},{28,... | collective-permute-start | bytes 983048 | tf_op jit(solution)/shard_map/ppermute | solution.py:185
  56.6 18.3 %collective-permute-start.8 = (f16[128,1280]{1,0:T(8,128)(2,1)S(1)}, f16[128,1280]{1,0:T(8,128)(2,1)S(1)}, u32[]{:S(2)}, u32[]{:S(2)}) collective-permute-start(f16[128,1280]{1,0:T(8,128)(2,1)S(1)} %get-tuple-element.21), channel_id=1, source_target_pairs={{4,8},{8,4},{5,9},{9,5},{6,10},{10,6},{7,11},{11,7},{20,24},{24,20... | collective-permute-start | bytes 983048 | tf_op jit(solution)/shard_map/ppermute | solution.py:187
  72.5 10.1 %collective-permute-start.6 = (f16[128,1280]{1,0:T(8,128)(2,1)S(1)}, f16[128,1280]{1,0:T(8,128)(2,1)S(1)}, u32[]{:S(2)}, u32[]{:S(2)}) collective-permute-start(f16[128,1280]{1,0:T(8,128)(2,1)S(1)} %get-tuple-element.20), channel_id=1, source_target_pairs={{4,8},{8,4},{5,9},{9,5},{6,10},{10,6},{7,11},{11,7},{20,24},{24,20... | collective-permute-start | bytes 983048 | tf_op jit(solution)/shard_map/ppermute | solution.py:188
  75.0 6.9 %copy-start.13 = (bf16[1280]{0:T(1024)(128)(2,1)S(1)}, bf16[1280]{0:T(1024)(128)(2,1)}, u32[]{:S(2)}) copy-start(bf16[1280]{0:T(1024)(128)(2,1)} %param.13) | copy-start | bytes 7684
  75.1 8.3 %collective-permute-start.9 = (f16[128,1280]{1,0:T(8,128)(2,1)S(1)}, f16[128,1280]{1,0:T(8,128)(2,1)}, u32[]{:S(2)}, u32[]{:S(2)}) collective-permute-start(f16[128,1280]{1,0:T(8,128)(2,1)S(1)} %fusion.5), channel_id=1, source_target_pairs={{0,4},{4,0},{8,12},{12,8},{1,5},{5,1},{9,13},{13,9},{2,6},{6,2},{1... | collective-permute-start | bytes 983048 | tf_op jit(solution)/shard_map/ppermute | solution.py:189
  84.6 14.6 %collective-permute-start.10 = (f32[2,128]{1,0:T(2,128)S(1)}, f32[2,128]{1,0:T(2,128)S(1)}, u32[]{:S(2)}, u32[]{:S(2)}) collective-permute-start(f32[2,128]{1,0:T(2,128)S(1)} %pad_maximum_fusion.9), channel_id=1, source_target_pairs={{0,1},{1,0},{2,3},{3,2},{4,5},{5,4},{6,7},{7,6},{8,9},{9,8},{10,11... | collective-permute-start | bytes 3080 | tf_op jit(solution)/shard_map/ppermute | solution.py:194
  88.7 8.1 %copy-start = (bf16[1280,3,256]{2,0,1:T(8,128)(2,1)S(1)}, bf16[1280,3,256]{2,0,1:T(8,128)(2,1)}, u32[]{:S(2)}) copy-start(bf16[1280,3,256]{2,0,1:T(8,128)(2,1)} %get-tuple-element.10) | copy-start | bytes 5898244
  92.8 10.2 %copy-start.11 = (f32[1280]{0:T(1024)S(1)}, f32[1280]{0:T(1024)}, u32[]{:S(2)}) copy-start(f32[1280]{0:T(1024)} %param.15) | copy-start | bytes 15364
  92.8 10.2 %copy-start.12 = (f32[1280]{0:T(1024)S(1)}, f32[1280]{0:T(1024)}, u32[]{:S(2)}) copy-start(f32[1280]{0:T(1024)} %param.14) | copy-start | bytes 15364
  99.3 3.6 %collective-permute-start.11 = (f32[2,128]{1,0:T(2,128)S(1)}, f32[2,128]{1,0:T(2,128)S(1)}, u32[]{:S(2)}, u32[]{:S(2)}) collective-permute-start(f32[2,128]{1,0:T(2,128)S(1)} %fusion.40), channel_id=1, source_target_pairs={{0,2},{1,3},{2,0},{3,1},{4,6},{5,7},{6,4},{7,5},{8,10},{9,11},{10,... | collective-permute-start | bytes 3080 | tf_op jit(solution)/shard_map/ppermute | solution.py:194
  103.1 8.0 %copy-start.6 = (bf16[1,2,384,256]{3,2,1,0:T(8,128)(2,1)S(1)}, bf16[1,2,384,256]{3,2,1,0:T(8,128)(2,1)}, u32[]{:S(2)}) copy-start(bf16[1,2,384,256]{3,2,1,0:T(8,128)(2,1)} %get-tuple-element.16) | copy-start | bytes 1179652
  103.2 9.7 %collective-permute-start.14 = (bf16[128,1280]{1,0:T(8,128)(2,1)S(1)}, bf16[128,1280]{1,0:T(8,128)(2,1)S(1)}, u32[]{:S(2)}, u32[]{:S(2)}) collective-permute-start(bf16[128,1280]{1,0:T(8,128)(2,1)S(1)} %add_convert_fusion.2), channel_id=1, source_target_pairs={{0,4},{4,0},{8,12},{12,8},{1,5},{5,1},{9,13},{13,9},{2,6},{6,2},{1... | collective-permute-start | bytes 983048 | tf_op jit(solution)/shard_map/ppermute | solution.py:176
  103.9 13.0 %collective-permute-start.17 = (bf16[128,1280]{1,0:T(8,128)(2,1)S(1)}, bf16[128,1280]{1,0:T(8,128)(2,1)S(1)}, u32[]{:S(2)}, u32[]{:S(2)}) collective-permute-start(bf16[128,1280]{1,0:T(8,128)(2,1)S(1)} %add_convert_fusion.2), channel_id=1, source_target_pairs={{4,8},{8,4},{5,9},{9,5},{6,10},{10,6},{7,11},{11,7},{20,24},{24,20... | collective-permute-start | bytes 983048 | tf_op jit(solution)/shard_map/ppermute | solution.py:177
  111.1 7.2 %collective-permute-start.12 = (f16[128,1536]{1,0:T(8,128)(2,1)S(1)}, f16[128,1536]{1,0:T(8,128)(2,1)S(1)}, u32[]{:S(2)}, u32[]{:S(2)}) collective-permute-start(f16[128,1536]{1,0:T(8,128)(2,1)S(1)} %convolution_convert_fusion.3), channel_id=1, source_target_pairs={{0,1},{1,0},{2,3},{3,2},{4,5},{5,4},{6,7},{7,6},{8,9},{9,8},{10,11... | collective-permute-start | bytes 1179656 | tf_op jit(solution)/shard_map/ppermute | solution.py:194
  111.3 7.0 %copy-start.2 = (bf16[1280,3,256]{0,2,1:T(8,128)(2,1)S(1)}, bf16[1280,3,256]{0,2,1:T(8,128)(2,1)}, u32[]{:S(2)}) copy-start(bf16[1280,3,256]{0,2,1:T(8,128)(2,1)} %copy.27) | copy-start | bytes 5898244
  111.3 7.0 %copy-start.3 = (bf16[1280,3,256]{0,2,1:T(8,128)(2,1)S(1)}, bf16[1280,3,256]{0,2,1:T(8,128)(2,1)}, u32[]{:S(2)}) copy-start(bf16[1280,3,256]{0,2,1:T(8,128)(2,1)} %copy.28) | copy-start | bytes 5898244
  111.3 20.4 %collective-permute-start.26 = (bf16[2,2,384,256]{3,2,1,0:T(8,128)(2,1)S(1)}, bf16[2,2,384,256]{3,2,1,0:T(8,128)(2,1)S(1)}, u32[]{:S(2)}, u32[]{:S(2)}) collective-permute-start(bf16[2,2,384,256]{3,2,1,0:T(8,128)(2,1)S(1)} %pad_maximum_fusion.4), channel_id=1, source_target_pairs={{0,2},{1,3},{2,0},{3,1},{4,6},{5,7},{6,4},{7,5},{8,10},{9,11},{10,... | collective-permute-start | bytes 2359304 | tf_op jit(solution)/shard_map/ppermute | solution.py:194
  114.3 22.8 %collective-permute-start.15 = (f16[128,1536]{1,0:T(8,128)(2,1)S(1)}, f16[128,1536]{1,0:T(8,128)(2,1)S(1)}, u32[]{:S(2)}, u32[]{:S(2)}) collective-permute-start(f16[128,1536]{1,0:T(8,128)(2,1)S(1)} %convolution_convert_fusion.2), channel_id=1, source_target_pairs={{0,1},{1,0},{2,3},{3,2},{4,5},{5,4},{6,7},{7,6},{8,9},{9,8},{10,11... | collective-permute-start | bytes 1179656 | tf_op jit(solution)/shard_map/ppermute | solution.py:194
  114.5 21.0 %collective-permute-start.21 = (bf16[128,1280]{1,0:T(8,128)(2,1)S(1)}, bf16[128,1280]{1,0:T(8,128)(2,1)S(1)}, u32[]{:S(2)}, u32[]{:S(2)}) collective-permute-start(bf16[128,1280]{1,0:T(8,128)(2,1)S(1)} %collective-permute-done.14), channel_id=1, source_target_pairs={{4,8},{8,4},{5,9},{9,5},{6,10},{10,6},{7,11},{11,7},{20,24},{24,20... | collective-permute-start | bytes 983048 | tf_op jit(solution)/shard_map/ppermute | solution.py:178
  117.0 23.1 %collective-permute-start.18 = (bf16[128,1280]{1,0:T(8,128)(2,1)S(1)}, bf16[128,1280]{1,0:T(8,128)(2,1)S(1)}, u32[]{:S(2)}, u32[]{:S(2)}) collective-permute-start(bf16[128,1280]{1,0:T(8,128)(2,1)S(1)} %collective-permute-done.17), channel_id=1, source_target_pairs={{4,0},{8,12},{5,1},{9,13},{6,2},{10,14},{7,3},{11,15},{20,16},{24,... | collective-permute-start | bytes 983048 | tf_op jit(solution)/shard_map/ppermute | solution.py:179
  119.7 15.7 %collective-permute-start.13 = (f16[128,768]{1,0:T(8,128)(2,1)S(1)}, f16[128,768]{1,0:T(8,128)(2,1)S(1)}, u32[]{:S(2)}, u32[]{:S(2)}) collective-permute-start(f16[128,768]{1,0:T(8,128)(2,1)S(1)} %slice_convert_fusion.3), channel_id=1, source_target_pairs={{0,2},{1,3},{2,0},{3,1},{4,6},{5,7},{6,4},{7,5},{8,10},{9,11},{10,... | collective-permute-start | bytes 589832 | tf_op jit(solution)/shard_map/ppermute | solution.py:194
  135.6 9.6 %collective-permute-start.22 = (bf16[128,1280]{1,0:T(8,128)(2,1)S(1)}, bf16[128,1280]{1,0:T(8,128)(2,1)S(1)}, u32[]{:S(2)}, u32[]{:S(2)}) collective-permute-start(bf16[128,1280]{1,0:T(8,128)(2,1)S(1)} %collective-permute-done.21), channel_id=1, source_target_pairs={{4,0},{8,12},{5,1},{9,13},{6,2},{10,14},{7,3},{11,15},{20,16},{24,... | collective-permute-start | bytes 983048 | tf_op jit(solution)/shard_map/ppermute | solution.py:180
  138.5 6.6 %collective-permute-start.16 = (f16[128,768]{1,0:T(8,128)(2,1)S(1)}, f16[128,768]{1,0:T(8,128)(2,1)S(1)}, u32[]{:S(2)}, u32[]{:S(2)}) collective-permute-start(f16[128,768]{1,0:T(8,128)(2,1)S(1)} %slice_convert_fusion.2), channel_id=1, source_target_pairs={{0,2},{1,3},{2,0},{3,1},{4,6},{5,7},{6,4},{7,5},{8,10},{9,11},{10,... | collective-permute-start | bytes 589832 | tf_op jit(solution)/shard_map/ppermute | solution.py:194
  141.5 5.2 %collective-permute-start.19 = (f16[128,1536]{1,0:T(8,128)(2,1)S(1)}, f16[128,1536]{1,0:T(8,128)(2,1)S(1)}, u32[]{:S(2)}, u32[]{:S(2)}) collective-permute-start(f16[128,1536]{1,0:T(8,128)(2,1)S(1)} %convolution_convert_fusion.1), channel_id=1, source_target_pairs={{0,1},{1,0},{2,3},{3,2},{4,5},{5,4},{6,7},{7,6},{8,9},{9,8},{10,11... | collective-permute-start | bytes 1179656 | tf_op jit(solution)/shard_map/ppermute | solution.py:194
  146.6 3.1 %collective-permute-start.23 = (f16[128,1536]{1,0:T(8,128)(2,1)S(1)}, f16[128,1536]{1,0:T(8,128)(2,1)S(1)}, u32[]{:S(2)}, u32[]{:S(2)}) collective-permute-start(f16[128,1536]{1,0:T(8,128)(2,1)S(1)} %convolution_convert_fusion), channel_id=1, source_target_pairs={{0,1},{1,0},{2,3},{3,2},{4,5},{5,4},{6,7},{7,6},{8,9},{9,8},{10,11... | collective-permute-start | bytes 1179656 | tf_op jit(solution)/shard_map/ppermute | solution.py:194
  148.1 7.8 %collective-permute-start.20 = (f16[128,768]{1,0:T(8,128)(2,1)S(1)}, f16[128,768]{1,0:T(8,128)(2,1)S(1)}, u32[]{:S(2)}, u32[]{:S(2)}) collective-permute-start(f16[128,768]{1,0:T(8,128)(2,1)S(1)} %slice_convert_fusion.1), channel_id=1, source_target_pairs={{0,2},{1,3},{2,0},{3,1},{4,6},{5,7},{6,4},{7,5},{8,10},{9,11},{10,... | collective-permute-start | bytes 589832 | tf_op jit(solution)/shard_map/ppermute | solution.py:194
  151.1 11.8 %copy-start.1 = (bf16[1024,1280]{1,0:T(8,128)(2,1)S(1)}, bf16[1024,1280]{1,0:T(8,128)(2,1)}, u32[]{:S(2)}) copy-start(bf16[1024,1280]{1,0:T(8,128)(2,1)} %param.19) | copy-start | bytes 7864324
  151.1 8.6 %collective-permute-start.24 = (f16[128,768]{1,0:T(8,128)(2,1)S(1)}, f16[128,768]{1,0:T(8,128)(2,1)S(1)}, u32[]{:S(2)}, u32[]{:S(2)}) collective-permute-start(f16[128,768]{1,0:T(8,128)(2,1)S(1)} %slice_convert_fusion), channel_id=1, source_target_pairs={{0,2},{1,3},{2,0},{3,1},{4,6},{5,7},{6,4},{7,5},{8,10},{9,11},{10,... | collective-permute-start | bytes 589832 | tf_op jit(solution)/shard_map/ppermute | solution.py:194
  161.3 5.7 %collective-permute-start.35 = (bf16[128,256]{1,0:T(8,128)(2,1)S(1)}, bf16[128,256]{1,0:T(8,128)(2,1)S(1)}, u32[]{:S(2)}, u32[]{:S(2)}) collective-permute-start(bf16[128,256]{1,0:T(8,128)(2,1)S(1)} %attend.7), channel_id=1, source_target_pairs={{0,2},{1,3},{2,0},{3,1},{4,6},{5,7},{6,4},{7,5},{8,10},{9,11},{10,... | collective-permute-start | bytes 196616 | tf_op jit(solution)/shard_map/ppermute | solution.py:194
  166.4 4.3 %collective-permute-start.29 = (bf16[128,256]{1,0:T(8,128)(2,1)S(1)}, bf16[128,256]{1,0:T(8,128)(2,1)S(1)}, u32[]{:S(2)}, u32[]{:S(2)}) collective-permute-start(bf16[128,256]{1,0:T(8,128)(2,1)S(1)} %attend.5), channel_id=1, source_target_pairs={{0,2},{1,3},{2,0},{3,1},{4,6},{5,7},{6,4},{7,5},{8,10},{9,11},{10,... | collective-permute-start | bytes 196616 | tf_op jit(solution)/shard_map/ppermute | solution.py:194
  167.0 3.8 %collective-permute-start.36 = (bf16[128,512]{1,0:T(8,128)(2,1)S(1)}, bf16[128,512]{1,0:T(8,128)(2,1)S(1)}, u32[]{:S(2)}, u32[]{:S(2)}) collective-permute-start(bf16[128,512]{1,0:T(8,128)(2,1)S(1)} %pad_maximum_fusion.8), channel_id=1, source_target_pairs={{0,1},{1,0},{2,3},{3,2},{4,5},{5,4},{6,7},{7,6},{8,9},{9,8},{10,11... | collective-permute-start | bytes 393224 | tf_op jit(solution)/shard_map/ppermute | solution.py:194
  168.7 4.6 %collective-permute-start.33 = (bf16[128,256]{1,0:T(8,128)(2,1)S(1)}, bf16[128,256]{1,0:T(8,128)(2,1)S(1)}, u32[]{:S(2)}, u32[]{:S(2)}) collective-permute-start(bf16[128,256]{1,0:T(8,128)(2,1)S(1)} %attend.6), channel_id=1, source_target_pairs={{0,2},{1,3},{2,0},{3,1},{4,6},{5,7},{6,4},{7,5},{8,10},{9,11},{10,... | collective-permute-start | bytes 196616 | tf_op jit(solution)/shard_map/ppermute | solution.py:194
  170.7 2.6 %collective-permute-start.30 = (bf16[128,512]{1,0:T(8,128)(2,1)S(1)}, bf16[128,512]{1,0:T(8,128)(2,1)S(1)}, u32[]{:S(2)}, u32[]{:S(2)}) collective-permute-start(bf16[128,512]{1,0:T(8,128)(2,1)S(1)} %pad_maximum_fusion.6), channel_id=1, source_target_pairs={{0,1},{1,0},{2,3},{3,2},{4,5},{5,4},{6,7},{7,6},{8,9},{9,8},{10,11... | collective-permute-start | bytes 393224 | tf_op jit(solution)/shard_map/ppermute | solution.py:194
  171.4 12.4 %collective-permute-start.37 = (bf16[128,1280]{1,0:T(8,128)(2,1)S(1)}, bf16[128,1280]{1,0:T(8,128)(2,1)S(1)}, u32[]{:S(2)}, u32[]{:S(2)}) collective-permute-start(bf16[128,1280]{1,0:T(8,128)(2,1)S(1)} %get-tuple-element.38), channel_id=1, source_target_pairs={{0,4},{12,8},{1,5},{13,9},{2,6},{14,10},{3,7},{15,11},{16,20},{28,... | collective-permute-start | bytes 983048 | tf_op jit(solution)/shard_map/ppermute | solution.py:185
  173.3 19.8 %collective-permute-start.34 = (bf16[128,512]{1,0:T(8,128)(2,1)S(1)}, bf16[128,512]{1,0:T(8,128)(2,1)S(1)}, u32[]{:S(2)}, u32[]{:S(2)}) collective-permute-start(bf16[128,512]{1,0:T(8,128)(2,1)S(1)} %pad_maximum_fusion.7), channel_id=1, source_target_pairs={{0,1},{1,0},{2,3},{3,2},{4,5},{5,4},{6,7},{7,6},{8,9},{9,8},{10,11... | collective-permute-start | bytes 393224 | tf_op jit(solution)/shard_map/ppermute | solution.py:194
  173.9 16.5 %collective-permute-start.31 = (bf16[128,1280]{1,0:T(8,128)(2,1)S(1)}, bf16[128,1280]{1,0:T(8,128)(2,1)S(1)}, u32[]{:S(2)}, u32[]{:S(2)}) collective-permute-start(bf16[128,1280]{1,0:T(8,128)(2,1)S(1)} %get-tuple-element.40), channel_id=1, source_target_pairs={{0,4},{12,8},{1,5},{13,9},{2,6},{14,10},{3,7},{15,11},{16,20},{28,... | collective-permute-start | bytes 983048 | tf_op jit(solution)/shard_map/ppermute | solution.py:186
  183.9 10.8 %collective-permute-start.38 = (bf16[128,1280]{1,0:T(8,128)(2,1)S(1)}, bf16[128,1280]{1,0:T(8,128)(2,1)S(1)}, u32[]{:S(2)}, u32[]{:S(2)}) collective-permute-start(bf16[128,1280]{1,0:T(8,128)(2,1)S(1)} %add_convert_fusion), channel_id=1, source_target_pairs={{4,8},{8,4},{5,9},{9,5},{6,10},{10,6},{7,11},{11,7},{20,24},{24,20... | collective-permute-start | bytes 983048 | tf_op jit(solution)/shard_map/ppermute | solution.py:187
  190.5 12.2 %collective-permute-start.32 = (bf16[128,1280]{1,0:T(8,128)(2,1)S(1)}, bf16[128,1280]{1,0:T(8,128)(2,1)S(1)}, u32[]{:S(2)}, u32[]{:S(2)}) collective-permute-start(bf16[128,1280]{1,0:T(8,128)(2,1)S(1)} %add_convert_fusion.1), channel_id=1, source_target_pairs={{4,8},{8,4},{5,9},{9,5},{6,10},{10,6},{7,11},{11,7},{20,24},{24,20... | collective-permute-start | bytes 983048 | tf_op jit(solution)/shard_map/ppermute | solution.py:188
  195.2 8.0 %collective-permute-start.39 = (bf16[128,1280]{1,0:T(8,128)(2,1)S(1)}, bf16[128,1280]{1,0:T(8,128)(2,1)S(1)}, u32[]{:S(2)}, u32[]{:S(2)}) collective-permute-start(bf16[128,1280]{1,0:T(8,128)(2,1)S(1)} %fusion.3), channel_id=1, source_target_pairs={{0,4},{4,0},{8,12},{12,8},{1,5},{5,1},{9,13},{13,9},{2,6},{6,2},{1... | collective-permute-start | bytes 983048 | tf_op jit(solution)/shard_map/ppermute | solution.py:189
  196.9 4.3 %collective-permute-start.27 = (bf16[128,256]{1,0:T(8,128)(2,1)S(1)}, bf16[128,256]{1,0:T(8,128)(2,1)S(1)}, u32[]{:S(2)}, u32[]{:S(2)}) collective-permute-start(bf16[128,256]{1,0:T(8,128)(2,1)S(1)} %attend.4), channel_id=1, source_target_pairs={{0,2},{1,3},{2,0},{3,1},{4,6},{5,7},{6,4},{7,5},{8,10},{9,11},{10,... | collective-permute-start | bytes 196616 | tf_op jit(solution)/shard_map/ppermute | solution.py:194
  201.2 1.4 collective-permute-start.28
  (7 other events, 42.1 us)

commit v2 on v1

--- a/solution.py
+++ b/solution.py
@@ -11,103 +11,112 @@
 D = 5120
 HEAD = 128
 GROUP = 8
-VMEM_BYTES = 48 * 1024 * 1024
-
-
-def densify_kernel(base_ref, ids_ref, vals_ref, out_ref, *, topk, latents, lanes):
-    groups, width = ids_ref.shape
+VMEM_BYTES = 20 * 1024 * 1024
+
+
+def densify_kernel(base_ref, *refs, topk, latents, lanes):
+    packed, out_ref = refs[:-1], refs[-1]
+    groups, width = packed[0].shape[0], packed[0].shape[1] // 2
     high = latents // lanes
     base = base_ref[0]
     row_of = lax.broadcasted_iota(jnp.int32, (1, width), 1) // topk
     sub = lax.broadcasted_iota(jnp.int32, (high * GROUP, width), 0)
+    sub = sub.astype(jnp.float32).astype(jnp.bfloat16)
     low_sub = lax.broadcasted_iota(jnp.int32, (lanes, width), 0)
-
-    def one_group(g):
-        local = ids_ref[pl.ds(g, 1), :].astype(jnp.int32) - base
+    low_sub = low_sub.astype(jnp.float32).astype(jnp.bfloat16)
+    one, zero = jnp.ones((), jnp.bfloat16), jnp.zeros((), jnp.bfloat16)
+
+    def half(value):
+        return value.astype(jnp.float32).astype(jnp.bfloat16)
+
+    def one_group(ref, g):
+        local = ref[pl.ds(g, 1), :width].astype(jnp.int32) - base
         inside = (local >= 0) & (local < latents)
-        key = jnp.where(inside, (local // lanes) * GROUP + row_of, -1)
-        low = jnp.where(inside, local % lanes, -1)
-        vals = vals_ref[pl.ds(g, 1), :]
-        left = jnp.where(key == sub, vals, 0.0).astype(jnp.bfloat16)
-        right = jnp.where(low == low_sub, 1.0, 0.0).astype(jnp.bfloat16)
+        key = half(jnp.where(inside, (local // lanes) * GROUP + row_of, -1))
+        low = half(jnp.where(inside, local % lanes, -1))
+        vals = ref[pl.ds(g, 1), width:].astype(jnp.bfloat16)
+        left = jnp.where(key == sub, vals, zero)
+        right = jnp.where(low == low_sub, one, zero)
         dense = lax.dot_general(
             left, right, (((1,), (1,)), ((), ())), preferred_element_type=jnp.float32
         )
         return dense.reshape(high, GROUP, lanes)
 
-    def pair(i, carry):
-        both = jnp.concatenate([one_group(2 * i), one_group(2 * i + 1)], axis=1)
-        both = both.astype(jnp.bfloat16)
-        rows = pl.ds(pl.multiple_of(i * 2 * GROUP, 2 * GROUP), 2 * GROUP)
-        for h in range(high):
-            out_ref[rows, h * lanes : (h + 1) * lanes] = both[h]
-        return carry
-
-    lax.fori_loop(0, groups // 2, pair, 0)
-
-
-def densify(ids, vals, base, topk, latents):
-    groups, width = ids.shape
+    for at, ref in enumerate(packed):
+
+        def pair(i, carry, at=at, ref=ref):
+            both = jnp.concatenate([one_group(ref, 2 * i), one_group(ref, 2 * i + 1)], axis=1)
+            both = both.astype(jnp.bfloat16)
+            start = pl.multiple_of(i * 2 * GROUP, 2 * GROUP) + at * groups * GROUP
+            for h in range(high):
+                out_ref[pl.ds(start, 2 * GROUP), h * lanes : (h + 1) * lanes] = both[h]
+            return carry
+
+        lax.fori_loop(0, groups // 2, pair, 0)
+
+
+def densify(packed, base, topk, latents):
+    groups, width = packed[0].shape
     lanes = 256 if latents % 256 == 0 else 128
-    rows = groups * GROUP
+    rows = groups * GROUP * len(packed)
     return pl.pallas_call(
         functools.partial(densify_kernel, topk=topk, latents=latents, lanes=lanes),
         out_shape=jax.ShapeDtypeStruct((rows, latents), jnp.bfloat16),
-        in_specs=[
-            pl.BlockSpec(memory_space=pltpu.SMEM),
-            pl.BlockSpec(memory_space=pltpu.VMEM),
-            pl.BlockSpec(memory_space=pltpu.VMEM),
-        ],
+        in_specs=[pl.BlockSpec(memory_space=pltpu.SMEM)]
+        + [pl.BlockSpec(memory_space=pltpu.VMEM) for _ in packed],
         out_specs=pl.BlockSpec(memory_space=pltpu.VMEM),
         compiler_params=pltpu.CompilerParams(vmem_limit_bytes=VMEM_BYTES),
         cost_estimate=pl.CostEstimate(
-            flops=2 * groups * GROUP * latents * width,
-            bytes_accessed=rows * latents * 2,
-            transcendentals=0,
+            flops=rows * latents * width, bytes_accessed=rows * latents * 2, transcendentals=0
         ),
         name="densify",
-    )(base, ids, vals)
-
-
-def decode_kernel(*refs):
-    codes, weights, out = refs[:-2], refs[-2], refs[-1]
-    block = jnp.concatenate([c[...] for c in codes], axis=0)
-    part = jnp.dot(block, weights[...], preferred_element_type=jnp.float32)
-
-    @pl.when(pl.program_id(0) == 0)
-    def _():
-        out[...] = part
-
-    @pl.when(pl.program_id(0) > 0)
-    def _():
-        out[...] += part
-
-
-def decode(codes, decoder):
-    rows, latents = codes[0].shape
-    columns = decoder.shape[1]
-    depth = math.gcd(latents, 1024)
-    total = rows * len(codes)
+    )(base, *packed)
+
+
+def copy_kernel(order_ref, from_ref, to_ref):
+    to_ref[...] = from_ref[...].reshape(to_ref.shape)
+
+
+def select_columns(weights, order, width):
+    kinds, depth = weights.shape[:2]
+    count = order.shape[0]
     return pl.pallas_call(
-        decode_kernel,
-        out_shape=jax.ShapeDtypeStruct((total, columns), jnp.float32),
-        grid=(latents // depth,),
-        in_specs=[pl.BlockSpec((rows, depth), lambda k: (0, k)) for _ in codes]
-        + [pl.BlockSpec((depth, columns), lambda k: (k, 0))],
-        out_specs=pl.BlockSpec((total, columns), lambda k: (0, 0)),
-        compiler_params=pltpu.CompilerParams(
-            dimension_semantics=("arbitrary",), vmem_limit_bytes=VMEM_BYTES
-        ),
+        copy_kernel,
+        out_shape=jax.ShapeDtypeStruct((depth, count * kinds * width), weights.dtype),
+        grid_spec=pltpu.PrefetchScalarGridSpec(
+            num_scalar_prefetch=1,
+            grid=(count, kinds),
+            in_specs=[pl.BlockSpec((1, depth, width), lambda j, t, order: (t, 0, order[j]))],
+            out_specs=pl.BlockSpec((depth, width), lambda j, t, order: (0, j * kinds + t)),
+        ),
+        compiler_params=pltpu.CompilerParams(vmem_limit_bytes=VMEM_BYTES),
         cost_estimate=pl.CostEstimate(
-            flops=2 * total * latents * columns,
-            bytes_accessed=latents * (total + columns) * 2 + total * columns * 4,
-            transcendentals=0,
-        ),
-        name="decode",
-    )(*codes, decoder)
-
-
-def attend_kernel(*refs, heads, slots, slot):
+            flops=0, bytes_accessed=4 * depth * count * kinds * width, transcendentals=0
+        ),
+        name="select_columns",
+    )(order, weights)
+
+
+def select_rows(weights, order, height):
+    columns, count = weights.shape[1], order.shape[0]
+    return pl.pallas_call(
+        copy_kernel,
+        out_shape=jax.ShapeDtypeStruct((count * height, columns), weights.dtype),
+        grid_spec=pltpu.PrefetchScalarGridSpec(
+            num_scalar_prefetch=1,
+            grid=(count,),
+            in_specs=[pl.BlockSpec((height, columns), lambda j, order: (order[j], 0))],
+            out_specs=pl.BlockSpec((height, columns), lambda j, order: (j, 0)),
+        ),
+        compiler_params=pltpu.CompilerParams(vmem_limit_bytes=VMEM_BYTES),
+        cost_estimate=pl.CostEstimate(
+            flops=0, bytes_accessed=4 * count * height * columns, transcendentals=0
+        ),
+        name="select_rows",
+    )(order, weights)
+
+
+def attend_kernel(*refs, heads, slots, group):
     query_pos, key_pos = refs[0], refs[1]
     new = refs[2 : 2 + slots]
     cached = refs[2 + slots : -1]
@@ -125,7 +134,7 @@
         keys = jnp.concatenate(keys, axis=0)
         values = jnp.concatenate(values, axis=0)
         scores = lax.dot_general(
-            new[slot][:, here], keys, (((1,), (1,)), ((), ())), preferred_element_type=jnp.float32
+            jnp.concatenate([new[s][:, here] for s in group], axis=0), keys, (((1,), (1,)), ((), ())), preferred_element_type=jnp.float32
         ) * (1.0 / math.sqrt(HEAD))
         cut = scores.shape[1] - hidden.shape[1]
         old, fresh = scores[:, :cut], jnp.where(hidden, -1e30, scores[:, cut:])
@@ -142,12 +151,13 @@
         out[:, here] = mixed.astype(jnp.bfloat16)
 
 
-def attend(query_pos, key_pos, new, cached, slot, heads):
-    rows = new[0].shape[0]
-    keys = rows * len(new) + sum(c.shape[1] for c in cached)
+def attend(query_pos, key_pos, new, cached, group, heads):
+    slot_rows = new[0].shape[0]
+    rows = slot_rows * len(group)
+    keys = slot_rows * len(new) + sum(c.shape[1] for c in cached)
     vmem = pl.BlockSpec(memory_space=pltpu.VMEM)
     return pl.pallas_call(
-        functools.partial(attend_kernel, heads=heads, slots=len(new), slot=slot),
+        functools.partial(attend_kernel, heads=heads, slots=len(new), group=group),
         out_shape=jax.ShapeDtypeStruct((rows, heads * HEAD), jnp.bfloat16),
         in_specs=[vmem] * (2 + len(new) + len(cached)),
         out_specs=vmem,
@@ -184,8 +194,14 @@
 def line_sum(parts, encode, decode_sent):
     in_far = lax.ppermute(encode(parts[3]), "lat", INWARD)
     in_across = lax.ppermute(encode(parts[2]), "lat", INWARD)
-    far = lax.ppermute(encode(parts[3] + decode_sent(in_far)), "lat", MIDDLE)
-    across = lax.ppermute(encode(parts[2] + decode_sent(in_across)), "lat", MIDDLE)
+    return line_end(parts, in_far, in_across, encode, decode_sent)
+
+
+def line_end(parts, in_far, in_across, encode, decode_sent):
+    far = encode(parts[3] + decode_sent(in_far))
+    second, far = lax.optimization_barrier((parts[2], far))
+    far = lax.ppermute(far, "lat", MIDDLE)
+    across = lax.ppermute(encode(second + decode_sent(in_across)), "lat", MIDDLE)
     near = lax.ppermute(encode(parts[1] + decode_sent(far)), "lat", PAIRS)
     return parts[0] + decode_sent(across) + decode_sent(near)
 
@@ -199,6 +215,13 @@
     row_var = sums[1] / D - row_mean * row_mean
     inverse = 1.0 / jnp.sqrt(row_var + 1e-05)
     return ((values - row_mean[:, None]) * inverse[:, None] * gain + shift).astype(jnp.bfloat16)
+
+
+def pack(code_ids, code_vals):
+    rows, topk = code_ids.shape
+    vals = code_vals.astype(jnp.bfloat16).astype(jnp.float32)
+    shape = (rows // GROUP, GROUP * topk)
+    return jnp.concatenate([code_ids.astype(jnp.float32).reshape(shape), vals.reshape(shape)], axis=1)
 
 
 SCALE = 256.0
@@ -225,16 +248,9 @@
     heads = own_width // HEAD
     outer = (lat == 0) | (lat == 3)
     slots = line_slots(lat)
-
-    packed = jnp.concatenate(
-        [
-            code_ids.reshape(rows // GROUP, GROUP * topk).astype(jnp.float32),
-            code_vals.astype(jnp.bfloat16)
-            .astype(jnp.float32)
-            .reshape(rows // GROUP, GROUP * topk),
-        ],
-        axis=1,
-    )
+    hold = lax.optimization_barrier
+
+    packed = pack(code_ids, code_vals)
     packed = line_gather(packed, outer)
     base = (lat * latents).reshape(1)
 
@@ -244,60 +260,60 @@
 
     sent = swap(jnp.stack([cache_of(1), cache_of(3)]), 1, cols)
     other = swap(jnp.stack([cache_of(2), sent[1]]), 2, cols)
-    cached = [cache_of(0), sent[0], other[0], other[1]]
-
-    weights = jnp.concatenate(
-        [
-            lax.dynamic_slice_in_dim(w_qkv, (col ^ j) * own_width, own_width, 2).reshape(
-                w_qkv.shape[0], 3 * own_width
-            )
-            for j in (1, 3, 0, 2)
-        ],
-        axis=1,
-    )
-    out_weights = jnp.concatenate(
-        [
-            lax.dynamic_slice_in_dim(w_out, (col ^ j) * own_width, own_width, 0)
-            for j in (0, 2, 1, 3)
-        ],
-        axis=0,
-    )
+
+    weights = w_qkv.transpose(1, 0, 2)
+    away_weights = select_columns(weights, jnp.stack([col ^ 1, col ^ 3]), own_width)
+    keep_weights = select_columns(weights, jnp.stack([col, col ^ 2]), own_width)
+    out_weights = select_rows(w_out, jnp.stack([col, col ^ 2, col ^ 1, col ^ 3]), own_width)
     key_pos = jnp.concatenate(
         [lax.dynamic_slice_in_dim(positions, s * rows, rows, 0) for s in slots]
     )
-
-    codes = [
-        densify(p[:, : GROUP * topk], p[:, GROUP * topk :], base, topk, latents) for p in packed
-    ]
-    far = decode([codes[3], codes[2]], decoder)
-    near = decode([codes[1], codes[0]], decoder)
+    query_pos = key_pos.reshape(-1, 1)
+
+    near_packed, away_weights, keep_weights, out_weights = hold(
+        (packed[:2], away_weights, keep_weights, out_weights)
+    )
+    codes_far = densify([packed[3], packed[2]], base, topk, latents)
+    codes_near = densify([near_packed[1], near_packed[0]], base, topk, latents)
+    far = jnp.dot(codes_far, decoder, preferred_element_type=jnp.float32)
+    codes_near, other, query_pos = hold((codes_near, other, query_pos))
+    cached = [cache_of(0), sent[0], other[0], other[1]]
+    in_far = lax.ppermute(to_half(far[:rows]), "lat", INWARD)
+    in_across = lax.ppermute(to_half(far[rows:]), "lat", INWARD)
+    near = jnp.dot(codes_near, decoder, preferred_element_type=jnp.float32)
+    near, in_far = hold((near, in_far))
     parts = [near[rows:], near[:rows], far[rows:], far[:rows]]
-    residual = line_sum(parts, to_half, from_half) + dec_bias.astype(jnp.float32)
+    residual = line_end(parts, in_far, in_across, to_half, from_half)
+    residual = residual + dec_bias.astype(jnp.float32)
 
     sums = jnp.stack([jnp.sum(residual, axis=1), jnp.sum(residual * residual, axis=1)])
     sums = sums + swap(sums, 1, cols)
     sums = sums + swap(sums, 2, cols)
     normed = line_gather(normalize(residual, sums, ln_gain, ln_bias), outer)
 
-    half = weights.shape[1] // 2
-    quarter = half // 2
-
-    def project(block):
-        away = jnp.dot(block, weights[:, :half], preferred_element_type=jnp.float32)
-        keep = jnp.dot(block, weights[:, half:], preferred_element_type=jnp.float32)
-        keep = keep + swap(away.astype(jnp.float16), 1, cols).astype(jnp.float32)
+    quarter = keep_weights.shape[1] // 2
+
+    def project(block, after):
+        block, _ = hold((block, after))
+        away = jnp.dot(block, away_weights, preferred_element_type=jnp.float32).astype(jnp.float16)
+        keep = jnp.dot(block, keep_weights, preferred_element_type=jnp.float32)
+        keep = keep + swap(away, 1, cols).astype(jnp.float32)
         came = swap(keep[:, quarter:].astype(jnp.float16), 2, cols).astype(jnp.float32)
-        return (keep[:, :quarter] + came).astype(jnp.bfloat16)
-
-    qkv = [project(block) for block in normed]
+        return (keep[:, :quarter] + came).astype(jnp.bfloat16), away
+
+    pair, sent = project(jnp.concatenate(normed[:2], axis=0), normed[0])
+    third, sent = project(normed[2], sent)
+    fourth, sent = project(normed[3], sent)
+    qkv = [pair[:rows], pair[rows:], third, fourth]
 
     branch = [None] * 4
-    for slot in (3, 2, 1, 0):
-        query_pos = key_pos[slot * rows : (slot + 1) * rows].reshape(rows, 1)
-        mixed = attend(query_pos, key_pos.reshape(1, -1), qkv, cached, slot, heads)
+    for group in ((3, 2), (1, 0)):
+        pos = jnp.concatenate([query_pos[g * rows : (g + 1) * rows] for g in group], axis=0)
+        mixed = attend(pos, key_pos.reshape(1, -1), qkv, cached, group, heads)
         mixed = jnp.concatenate([mixed, swap(mixed, 2, cols)], axis=1)
         mixed = jnp.concatenate([mixed, swap(mixed, 1, cols)], axis=1)
-        branch[slot] = jnp.dot(mixed, out_weights, preferred_element_type=jnp.float32)
+        product = jnp.dot(mixed, out_weights, preferred_element_type=jnp.float32)
+        branch[group[0]], branch[group[1]] = product[:rows], product[rows:]
     added = line_sum(
         branch, lambda v: v.astype(jnp.bfloat16), lambda v: v.astype(jnp.float32)
     )
@@ -329,20 +345,9 @@
     col_index = lax.axis_index("col")
     rows, topk = code_ids.shape
     shard_latents = decoder.shape[0]
-    packed = jnp.concatenate(
-        [
-            code_ids.reshape(rows // GROUP, GROUP * topk).astype(jnp.float32),
-            code_vals.astype(jnp.bfloat16)
-            .astype(jnp.float32)
-            .reshape(rows // GROUP, GROUP * topk),
-        ],
-        axis=1,
-    )
-    packed = lax.all_gather(packed, "lat", axis=0, tiled=True)
+    packed = lax.all_gather(pack(code_ids, code_vals), "lat", axis=0, tiled=True)
     base = (lat_index * shard_latents).reshape(1)
-    dense_codes = densify(
-        packed[:, : GROUP * topk], packed[:, GROUP * topk :], base, topk, shard_latents
-    )
+    dense_codes = densify([packed], base, topk, shard_latents)
     total_rows = dense_codes.shape[0]
     col_rows = total_rows // col_total
     residual = lax.psum_scatter(

time: 208 us -> 212 us (1.019)
  waiting for transfers between devices: 61.5 us -> 90.2 us
  Pallas kernels: 43 us -> 20.6 us
  local copies, waits for them, and re-layouts: 27.2 us -> 12.7 us
  matrix products: 16.3 us -> 30.4 us
    ppermute x6 -> x8, waiting for transfers between devices: 3.45 us -> 24.3 us  [the longest x2 10.5 us: line_end(): lax.ppermute(encode(second + decode_sent(in_across)), 'lat', MIDDLE)]
    pallas_call x2 -> x3, Pallas kernels: 24.9 us -> 4.35 us  [the longest x2 3.56 us: select_columns(): pl.pallas_call(copy_kernel, out_shape=jax.ShapeDtypeStruct((depth, count...]
    dot_general x12 -> x10, matrix products: 16.3 us -> 30.4 us  [the longest x1 9.89 us: line_body(): near = jnp.dot(codes_near, decoder, preferred_element_type=jnp.float32)]
    ppermute x2, waiting for transfers between devices: 0.01 us -> 8.34 us  [line_gather(): far_out = lax.ppermute(far, 'lat', OUTWARD)]
    dynamic_slice x2 -> x1, local copies, waits for them, and re-layouts: 8.31 us -> 1.48 us  [cache_of(): return lax.dynamic_slice_in_dim(cache_kv, start, own_width, 2)]
    ppermute x6 -> x8, starting transfers between devices: 11 us -> 17 us  [the longest x2 7.31 us: line_end(): lax.ppermute(encode(second + decode_sent(in_across)), 'lat', MIDDLE)]
    ppermute x2 -> x1, waiting for transfers between devices: 14.6 us -> 8.91 us  [line_sum(): in_far = lax.ppermute(encode(parts[3]), 'lat', INWARD)]
    ppermute x2 -> x1, waiting for transfers between devices: 8.17 us -> 2.92 us  [line_sum(): in_across = lax.ppermute(encode(parts[2]), 'lat', INWARD)]
  transfers between devices with their start and end apart: 40 -> 34, of which waited for: 19 -> 22; matrix products, arithmetic and copies ran while one was open for 22% -> 16% of each run, Pallas kernels for 20% -> 9%
where the time goes in v2:
time: 212 us; the launch traced here: 210 us
  waiting for transfers between devices  90.2 us (43%)
  starting transfers between devices  49.9 us (24%)
  matrix products  30.4 us (14%)
  Pallas kernels  20.6 us (10%)
  local copies, waits for them, and re-layouts  12.7 us (6%)
  other arithmetic  5.38 us (3%)
    ppermute x14, waiting for transfers between devices, swap(): return lax.ppermute(value, 'col', [(i, i ^ distance) for i in range(size)])  31.6 us
    pallas_call x2, Pallas kernels, densify(): pl.pallas_call(functools.partial(densify_kernel, topk=topk, latents=laten...  11.4 us
    ppermute x14, starting transfers between devices, swap(): return lax.ppermute(value, 'col', [(i, i ^ distance) for i in range(size)])  10.6 us
    ppermute x2, waiting for transfers between devices, line_end(): lax.ppermute(encode(second + decode_sent(in_across)), 'lat', MIDDLE)  10.5 us
    unnamed x25, local copies, waits for them, and re-layouts  10.3 us
    dot_general x1, matrix products, line_body(): near = jnp.dot(codes_near, decoder, preferred_element_type=jnp.float32)  9.89 us
    dot_general x1, matrix products, line_body(): far = jnp.dot(codes_far, decoder, preferred_element_type=jnp.float32)  9.89 us
    ppermute x1, waiting for transfers between devices, line_sum(): in_far = lax.ppermute(encode(parts[3]), 'lat', INWARD)  8.91 us
  transfers between devices with their start and end apart: 34, of which 22 were waited for; matrix products, arithmetic and copies ran while one was open for 16% of the time, Pallas kernels for 9%

profile of v2, /device:TPU:8, one launch (start us, length us, event | category | flops | bytes accessed | tf_op | source)
XLA Modules:
  0.0 210.0 jit_solution(663209107499768272)
XLA Ops:
  1.9 5.0 %collective-permute-start.5 = (f32[16,1024]{1,0:T(8,128)S(1)}, f32[16,1024]{1,0:T(8,128)S(1)}, u32[]{:S(2)}, u32[]{:S(2)}) collective-permute-start(f32[16,1024]{1,0:T(8,128)S(1)} %constant_dynamic-update-slice_fusion.refs_1_), channel_id=1, source_target_pairs={{4,8},{8,4},{5,9},{9,5},{6,10},{10,6},{7,11},{11,7},{20,24},{24,20... | collective-permute-start | bytes 196616 | tf_op jit(solution)/shard_map/ppermute | solution.py:187
  8.8 3.2 %copy-done.4 = bf16[1280,3,1024]{2,0,1:T(8,128)(2,1)S(1)} copy-done((bf16[1280,3,1024]{2,0,1:T(8,128)(2,1)S(1)}, bf16[1280,3,1024]{2,0,1:T(8,128)(2,1)}, u32[]{:S(2)}) %copy-start.4) | copy-done | bytes 7864344
  12.1 1.8 select_columns.2
  13.9 1.9 copy-done.2
  15.8 1.8 select_columns.3
  17.6 1.9 copy-done
  19.4 1.7 copy-done.5
  22.0 1.6 copy-done.6
  23.6 1.9 collective-permute-start.3
  26.9 5.7 %densify.2 = bf16[256,8192]{1,0:T(8,128)(2,1)S(1)} custom-call(s32[1]{0:T(128)} %bitcast.base_ref, f32[16,1024]{1,0:T(8,128)S(1)} %collective-permute-done.refs_0_, f32[16,1024]{1,0:T(8,128)S(1)} %constant_dynamic-update-slice_fusion.refs_1_), custom_call_target="tpu_custom_call" | custom-call | flops 2147483648 | bytes 4194304 | tf_op jit(solution)/shard_map/densify/pallas_call | solution.py:62
  33.9 2.2 %collective-permute-done.4 = f32[16,1024]{1,0:T(8,128)S(1)} collective-permute-done((f32[16,1024]{1,0:T(8,128)S(1)}, f32[16,1024]{1,0:T(8,128)S(1)}, u32[]{:S(2)}, u32[]{:S(2)}) %collective-permute-start.4) | collective-permute-done | bytes 65568 | tf_op jit(solution)/shard_map/ppermute | solution.py:190
  36.2 5.7 %densify.3 = bf16[256,8192]{1,0:T(8,128)(2,1)S(1)} custom-call(s32[1]{0:T(128)} %bitcast.base_ref, f32[16,1024]{1,0:T(8,128)S(1)} %broadcast_select_fusion.3.refs_0_, f32[16,1024]{1,0:T(8,128)S(1)} %broadcast_select_fusion.2.refs_1_), custom_call_target="tpu_custom_call" | custom-call | flops 2147483648 | bytes 4194304 | tf_op jit(solution)/shard_map/densify/pallas_call | solution.py:62
  42.1 1.6 collective-permute-start.2
  43.6 9.9 %fusion.30 = f32[256,1280]{1,0:T(8,128)S(1)} fusion(bf16[256,8192]{1,0:T(8,128)(2,1)S(1)} %densify.3, bf16[8192,1280]{1,0:T(8,128)(2,1)} %param.12), kind=kOutput, calls=%fused_computation.84 | convolution fusion | flops 5368709120 | bytes 26476544 | tf_op jit(solution)/shard_map/dot_general | solution.py:278
  54.9 6.6 %collective-permute-done.2 = bf16[2,2,384,256]{3,2,1,0:T(8,128)(2,1)S(1)} collective-permute-done((bf16[2,2,384,256]{3,2,1,0:T(8,128)(2,1)S(1)}, bf16[2,2,384,256]{3,2,1,0:T(8,128)(2,1)S(1)}, u32[]{:S(2)}, u32[]{:S(2)}) %collective-permute-start.2) | collective-permute-done | bytes 786464 | tf_op jit(solution)/shard_map/ppermute | solution.py:210
  61.5 9.9 %fusion.29 = f32[256,1280]{1,0:T(8,128)S(1)} fusion(bf16[256,8192]{1,0:T(8,128)(2,1)S(1)} %densify.2, bf16[8192,1280]{1,0:T(8,128)(2,1)} %param.12), kind=kOutput, calls=%fused_computation.83 | convolution fusion | flops 5368709120 | bytes 26476544 | tf_op jit(solution)/shard_map/dot_general | solution.py:283
  71.6 3.3 %collective-permute-start.10 = (f16[128,1280]{1,0:T(8,128)(2,1)S(1)}, f16[128,1280]{1,0:T(8,128)(2,1)S(1)}, u32[]{:S(2)}, u32[]{:S(2)}) collective-permute-start(f16[128,1280]{1,0:T(8,128)(2,1)S(1)} %get-tuple-element.28), channel_id=1, source_target_pairs={{4,8},{8,4},{5,9},{9,5},{6,10},{10,6},{7,11},{11,7},{20,24},{24,20... | collective-permute-start | bytes 983048 | tf_op jit(solution)/shard_map/ppermute | solution.py:203
  76.2 6.0 %collective-permute-done.10 = f16[128,1280]{1,0:T(8,128)(2,1)S(1)} collective-permute-done((f16[128,1280]{1,0:T(8,128)(2,1)S(1)}, f16[128,1280]{1,0:T(8,128)(2,1)S(1)}, u32[]{:S(2)}, u32[]{:S(2)}) %collective-permute-start.10) | collective-permute-done | bytes 327712 | tf_op jit(solution)/shard_map/ppermute | solution.py:203
  82.4 3.9 %collective-permute-done.8 = f16[128,1280]{1,0:T(8,128)(2,1)S(1)} collective-permute-done((f16[128,1280]{1,0:T(8,128)(2,1)S(1)}, f16[128,1280]{1,0:T(8,128)(2,1)S(1)}, u32[]{:S(2)}, u32[]{:S(2)}) %collective-permute-start.8) | collective-permute-done | bytes 327712 | tf_op jit(solution)/shard_map/ppermute | solution.py:282
  86.4 3.6 %collective-permute-start.9 = (f16[128,1280]{1,0:T(8,128)(2,1)S(1)}, f16[128,1280]{1,0:T(8,128)(2,1)S(1)}, u32[]{:S(2)}, u32[]{:S(2)}) collective-permute-start(f16[128,1280]{1,0:T(8,128)(2,1)S(1)} %multiply_convert_fusion.1), channel_id=1, source_target_pairs={{4,8},{8,4},{5,9},{9,5},{6,10},{10,6},{7,11},{11,7},{20,24},{24,20... | collective-permute-start | bytes 983048 | tf_op jit(solution)/shard_map/ppermute | solution.py:204
  90.1 1.6 collective-permute-done.11
  91.8 3.6 %collective-permute-done.9 = f16[128,1280]{1,0:T(8,128)(2,1)S(1)} collective-permute-done((f16[128,1280]{1,0:T(8,128)(2,1)S(1)}, f16[128,1280]{1,0:T(8,128)(2,1)S(1)}, u32[]{:S(2)}, u32[]{:S(2)}) %collective-permute-start.9) | collective-permute-done | bytes 327712 | tf_op jit(solution)/shard_map/ppermute | solution.py:204
  96.9 1.6 collective-permute-start.13
  98.6 2.0 collective-permute-done.13
  100.9 3.6 %collective-permute-start.17 = (bf16[128,1280]{1,0:T(8,128)(2,1)S(1)}, bf16[128,1280]{1,0:T(8,128)(2,1)}, u32[]{:S(2)}, u32[]{:S(2)}) collective-permute-start(bf16[128,1280]{1,0:T(8,128)(2,1)S(1)} %add_convert_fusion.2), channel_id=1, source_target_pairs={{4,8},{8,4},{5,9},{9,5},{6,10},{10,6},{7,11},{11,7},{20,24},{24,20... | collective-permute-start | bytes 983048 | tf_op jit(solution)/shard_map/ppermute | solution.py:187
  104.7 4.8 %collective-permute-done.14 = bf16[128,1280]{1,0:T(8,128)(2,1)S(1)} collective-permute-done((bf16[128,1280]{1,0:T(8,128)(2,1)S(1)}, bf16[128,1280]{1,0:T(8,128)(2,1)S(1)}, u32[]{:S(2)}, u32[]{:S(2)}) %collective-permute-start.14) | collective-permute-done | bytes 327712 | tf_op jit(solution)/shard_map/ppermute | solution.py:186
  109.5 2.0 collective-permute-done.17
  112.8 3.3 %convolution_convert_fusion = f16[256,1536]{1,0:T(8,128)(2,1)S(1)} fusion(bf16[256,1280]{1,0:T(8,128)(2,1)S(1)} %pad_maximum_fusion.2, bf16[1280,1536]{1,0:T(8,128)(2,1)} %copy-done.2), kind=kOutput, calls=%fused_computation.1 | convolution fusion | flops 1007026176 | bytes 5373952 | tf_op jit(solution)/shard_map/dot_general | solution.py:298
  116.2 3.6 %collective-permute-start.21 = (bf16[128,1280]{1,0:T(8,128)(2,1)S(1)}, bf16[128,1280]{1,0:T(8,128)(2,1)S(1)}, u32[]{:S(2)}, u32[]{:S(2)}) collective-permute-start(bf16[128,1280]{1,0:T(8,128)(2,1)S(1)} %collective-permute-done.14), channel_id=1, source_target_pairs={{4,8},{8,4},{5,9},{9,5},{6,10},{10,6},{7,11},{11,7},{20,24},{24,20... | collective-permute-start | bytes 983048 | tf_op jit(solution)/shard_map/ppermute | solution.py:188
  120.9 7.3 %collective-permute-done.21 = bf16[128,1280]{1,0:T(8,128)(2,1)S(1)} collective-permute-done((bf16[128,1280]{1,0:T(8,128)(2,1)S(1)}, bf16[128,1280]{1,0:T(8,128)(2,1)S(1)}, u32[]{:S(2)}, u32[]{:S(2)}) %collective-permute-start.21) | collective-permute-done | bytes 327712 | tf_op jit(solution)/shard_map/ppermute | solution.py:188
  130.5 6.1 %collective-permute-done.22 = bf16[128,1280]{1,0:T(8,128)(2,1)S(1)} collective-permute-done((bf16[128,1280]{1,0:T(8,128)(2,1)S(1)}, bf16[128,1280]{1,0:T(8,128)(2,1)S(1)}, u32[]{:S(2)}, u32[]{:S(2)}) %collective-permute-start.22) | collective-permute-done | bytes 327712 | tf_op jit(solution)/shard_map/ppermute | solution.py:190
  138.1 1.6 collective-permute-start.20
  141.5 4.4 %collective-permute-done.20 = f16[128,768]{1,0:T(8,128)(2,1)S(1)} collective-permute-done((f16[128,768]{1,0:T(8,128)(2,1)S(1)}, f16[128,768]{1,0:T(8,128)(2,1)S(1)}, u32[]{:S(2)}, u32[]{:S(2)}) %collective-permute-start.20) | collective-permute-done | bytes 196640 | tf_op jit(solution)/shard_map/ppermute | solution.py:210
  146.7 1.6 collective-permute-start.24
  148.3 6.1 %collective-permute-done.16 = f16[256,768]{1,0:T(8,128)(2,1)S(1)} collective-permute-done((f16[256,768]{1,0:T(8,128)(2,1)S(1)}, f16[256,768]{1,0:T(8,128)(2,1)S(1)}, u32[]{:S(2)}, u32[]{:S(2)}) %collective-permute-start.16) | collective-permute-done | bytes 393248 | tf_op jit(solution)/shard_map/ppermute | solution.py:210
  154.4 3.7 %collective-permute-done.24 = f16[128,768]{1,0:T(8,128)(2,1)S(1)} collective-permute-done((f16[128,768]{1,0:T(8,128)(2,1)S(1)}, f16[128,768]{1,0:T(8,128)(2,1)S(1)}, u32[]{:S(2)}, u32[]{:S(2)}) %collective-permute-start.24) | collective-permute-done | bytes 196640 | tf_op jit(solution)/shard_map/ppermute | solution.py:210
  158.2 2.4 %attend.3 = bf16[256,256]{1,0:T(8,128)(2,1)S(1)} custom-call(s32[256,1]{1,0:T(8,128)S(1)} %copy.22.refs_0_, s32[1,512]{1,0:T(1,128)S(1)} %bitcast.53, bf16[128,768]{1,0:T(8,128)(2,1)S(1)} %get-tuple-element.58.refs_2_, bf16[128,768]{1,0:T(8,128)(2,1)S(1)} %get-tuple-element.57.refs_3_, bf16[128,768]{1,0:T(8,128)(2,1)S(1)} %fusion.18.refs_4_, ...), custom_call_target="tpu_custom_call" | custom-call | flops 536870912 | bytes 2097152 | tf_op jit(solution)/shard_map/attend/pallas_call | solution.py:159
  160.6 1.6 collective-permute-start.27
  162.3 3.4 %collective-permute-done.27 = bf16[256,256]{1,0:T(8,128)(2,1)S(1)} collective-permute-done((bf16[256,256]{1,0:T(8,128)(2,1)S(1)}, bf16[256,256]{1,0:T(8,128)(2,1)S(1)}, u32[]{:S(2)}, u32[]{:S(2)}) %collective-permute-start.27) | collective-permute-done | bytes 131104 | tf_op jit(solution)/shard_map/ppermute | solution.py:210
  165.8 2.4 %attend.2 = bf16[256,256]{1,0:T(8,128)(2,1)S(1)} custom-call(s32[256,1]{1,0:T(8,128)S(1)} %copy.21.refs_0_, s32[1,512]{1,0:T(1,128)S(1)} %bitcast.54, bf16[128,768]{1,0:T(8,128)(2,1)S(1)} %get-tuple-element.58.refs_2_, bf16[128,768]{1,0:T(8,128)(2,1)S(1)} %get-tuple-element.57.refs_3_, bf16[128,768]{1,0:T(8,128)(2,1)S(1)} %fusion.18.refs_4_, ...), custom_call_target="tpu_custom_call" | custom-call | flops 536870912 | bytes 2097152 | tf_op jit(solution)/shard_map/attend/pallas_call | solution.py:159
  168.3 1.6 collective-permute-start.25
  169.9 4.4 %collective-permute-done.25 = bf16[256,256]{1,0:T(8,128)(2,1)S(1)} collective-permute-done((bf16[256,256]{1,0:T(8,128)(2,1)S(1)}, bf16[256,256]{1,0:T(8,128)(2,1)S(1)}, u32[]{:S(2)}, u32[]{:S(2)}) %collective-permute-start.25) | collective-permute-done | bytes 131104 | tf_op jit(solution)/shard_map/ppermute | solution.py:210
  174.3 2.6 %fusion.11 = f32[256,1280]{1,0:T(8,128)S(1)} fusion(bf16[1024,1280]{1,0:T(8,128)(2,1)} %copy-done.6, bf16[256,512]{1,0:T(8,128)(2,1)S(1)} %collective-permute-done.28, bf16[256,256]{1,0:T(8,128)(2,1)S(1)} %collective-permute-done.27, bf16[256,256]{1,0:T(8,128)(2,1)S(1)} %attend.3), kind=kOutput, calls=%fused_computation.35 | convolution fusion | flops 672661504 | bytes 4456448 | tf_op jit(solution)/shard_map/dot_general | solution.py:315
  180.5 8.9 %collective-permute-done.29 = bf16[128,1280]{1,0:T(8,128)(2,1)S(1)} collective-permute-done((bf16[128,1280]{1,0:T(8,128)(2,1)S(1)}, bf16[128,1280]{1,0:T(8,128)(2,1)S(1)}, u32[]{:S(2)}, u32[]{:S(2)}) %collective-permute-start.29) | collective-permute-done | bytes 327712 | tf_op jit(solution)/shard_map/ppermute | solution.py:195
  189.5 3.7 %collective-permute-start.32 = (bf16[128,1280]{1,0:T(8,128)(2,1)S(1)}, bf16[128,1280]{1,0:T(8,128)(2,1)S(1)}, u32[]{:S(2)}, u32[]{:S(2)}) collective-permute-start(bf16[128,1280]{1,0:T(8,128)(2,1)S(1)} %get-tuple-element.38), channel_id=1, source_target_pairs={{4,8},{8,4},{5,9},{9,5},{6,10},{10,6},{7,11},{11,7},{20,24},{24,20... | collective-permute-start | bytes 983048 | tf_op jit(solution)/shard_map/ppermute | solution.py:203
  193.2 2.9 %collective-permute-done.30 = bf16[128,1280]{1,0:T(8,128)(2,1)S(1)} collective-permute-done((bf16[128,1280]{1,0:T(8,128)(2,1)S(1)}, bf16[128,1280]{1,0:T(8,128)(2,1)S(1)}, u32[]{:S(2)}, u32[]{:S(2)}) %collective-permute-start.30) | collective-permute-done | bytes 327712 | tf_op jit(solution)/shard_map/ppermute | solution.py:196
  196.2 3.7 %collective-permute-start.31 = (bf16[128,1280]{1,0:T(8,128)(2,1)S(1)}, bf16[128,1280]{1,0:T(8,128)(2,1)S(1)}, u32[]{:S(2)}, u32[]{:S(2)}) collective-permute-start(bf16[128,1280]{1,0:T(8,128)(2,1)S(1)} %add_convert_fusion), channel_id=1, source_target_pairs={{4,8},{8,4},{5,9},{9,5},{6,10},{10,6},{7,11},{11,7},{20,24},{24,20... | collective-permute-start | bytes 983048 | tf_op jit(solution)/shard_map/ppermute | solution.py:204
  200.7 6.9 %collective-permute-done.31 = bf16[128,1280]{1,0:T(8,128)(2,1)S(1)} collective-permute-done((bf16[128,1280]{1,0:T(8,128)(2,1)S(1)}, bf16[128,1280]{1,0:T(8,128)(2,1)S(1)}, u32[]{:S(2)}, u32[]{:S(2)}) %collective-permute-start.31) | collective-permute-done | bytes 327712 | tf_op jit(solution)/shard_map/ppermute | solution.py:204
  (114 shorter events, 28.6 us)
Async XLA Ops:
  1.9 21.7 %collective-permute-start = (f32[16,1024]{1,0:T(8,128)S(1)}, f32[16,1024]{1,0:T(8,128)S(1)}, u32[]{:S(2)}, u32[]{:S(2)}) collective-permute-start(f32[16,1024]{1,0:T(8,128)S(1)} %constant_dynamic-update-slice_fusion.refs_1_), channel_id=1, source_target_pairs={{0,4},{4,0},{8,12},{12,8},{1,5},{5,1},{9,13},{13,9},{2,6},{6,2},{1... | collective-permute-start | bytes 196616 | tf_op jit(solution)/shard_map/ppermute | solution.py:186
  1.9 23.6 %collective-permute-start.5 = (f32[16,1024]{1,0:T(8,128)S(1)}, f32[16,1024]{1,0:T(8,128)S(1)}, u32[]{:S(2)}, u32[]{:S(2)}) collective-permute-start(f32[16,1024]{1,0:T(8,128)S(1)} %constant_dynamic-update-slice_fusion.refs_1_), channel_id=1, source_target_pairs={{4,8},{8,4},{5,9},{9,5},{6,10},{10,6},{7,11},{11,7},{20,24},{24,20... | collective-permute-start | bytes 196616 | tf_op jit(solution)/shard_map/ppermute | solution.py:187
  8.6 33.3 %collective-permute-start.1 = (bf16[2,2,384,256]{3,2,1,0:T(8,128)(2,1)S(1)}, bf16[2,2,384,256]{3,2,1,0:T(8,128)(2,1)S(1)}, u32[]{:S(2)}, u32[]{:S(2)}) collective-permute-start(bf16[2,2,384,256]{3,2,1,0:T(8,128)(2,1)S(1)} %pad_maximum_fusion), channel_id=1, source_target_pairs={{0,1},{1,0},{2,3},{3,2},{4,5},{5,4},{6,7},{7,6},{8,9},{9,8},{10,11... | collective-permute-start | bytes 2359304 | tf_op jit(solution)/shard_map/ppermute | solution.py:210
  8.8 3.2 %copy-start.4 = (bf16[1280,3,1024]{2,0,1:T(8,128)(2,1)S(1)}, bf16[1280,3,1024]{2,0,1:T(8,128)(2,1)}, u32[]{:S(2)}) copy-start(bf16[1280,3,1024]{2,0,1:T(8,128)(2,1)} %param.16) | copy-start | bytes 23592964
  13.9 1.9 copy-start.2
  17.6 1.9 copy-start
  19.4 1.7 copy-start.5
  21.2 2.4 %copy-start.11 = (s32[512]{0:T(512)S(1)}, s32[512]{0:T(512)}, u32[]{:S(2)}) copy-start(s32[512]{0:T(512)} %param.18) | copy-start | bytes 6148
  22.0 1.6 copy-start.6
  23.6 9.0 %collective-permute-start.3 = (f32[16,1024]{1,0:T(8,128)S(1)}, f32[16,1024]{1,0:T(8,128)S(1)}, u32[]{:S(2)}, u32[]{:S(2)}) collective-permute-start(f32[16,1024]{1,0:T(8,128)S(1)} %collective-permute-done.refs_0_), channel_id=1, source_target_pairs={{4,8},{8,4},{5,9},{9,5},{6,10},{10,6},{7,11},{11,7},{20,24},{24,20... | collective-permute-start | bytes 196616 | tf_op jit(solution)/shard_map/ppermute | solution.py:188
  25.6 8.3 %collective-permute-start.6 = (f32[16,1024]{1,0:T(8,128)S(1)}, f32[16,1024]{1,0:T(8,128)S(1)}, u32[]{:S(2)}, u32[]{:S(2)}) collective-permute-start(f32[16,1024]{1,0:T(8,128)S(1)} %collective-permute-done.5), channel_id=1, source_target_pairs={{4,0},{8,12},{5,1},{9,13},{6,2},{10,14},{7,3},{11,15},{20,16},{24,... | collective-permute-start | bytes 196616 | tf_op jit(solution)/shard_map/ppermute | solution.py:189
  32.6 3.6 %collective-permute-start.4 = (f32[16,1024]{1,0:T(8,128)S(1)}, f32[16,1024]{1,0:T(8,128)S(1)}, u32[]{:S(2)}, u32[]{:S(2)}) collective-permute-start(f32[16,1024]{1,0:T(8,128)S(1)} %collective-permute-done.3), channel_id=1, source_target_pairs={{4,0},{8,12},{5,1},{9,13},{6,2},{10,14},{7,3},{11,15},{20,16},{24,... | collective-permute-start | bytes 196616 | tf_op jit(solution)/shard_map/ppermute | solution.py:190
  42.1 19.4 %collective-permute-start.2 = (bf16[2,2,384,256]{3,2,1,0:T(8,128)(2,1)S(1)}, bf16[2,2,384,256]{3,2,1,0:T(8,128)(2,1)S(1)}, u32[]{:S(2)}, u32[]{:S(2)}) collective-permute-start(bf16[2,2,384,256]{3,2,1,0:T(8,128)(2,1)S(1)} %pad_maximum_fusion.1), channel_id=1, source_target_pairs={{0,2},{1,3},{2,0},{3,1},{4,6},{5,7},{6,4},{7,5},{8,10},{9,11},{10,... | collective-permute-start | bytes 2359304 | tf_op jit(solution)/shard_map/ppermute | solution.py:210
  53.6 17.8 %collective-permute-start.7 = (f16[128,1280]{1,0:T(8,128)(2,1)S(1)}, f16[128,1280]{1,0:T(8,128)(2,1)S(1)}, u32[]{:S(2)}, u32[]{:S(2)}) collective-permute-start(f16[128,1280]{1,0:T(8,128)(2,1)S(1)} %multiply_convert_fusion.4), channel_id=1, source_target_pairs={{0,4},{12,8},{1,5},{13,9},{2,6},{14,10},{3,7},{15,11},{16,20},{28,... | collective-permute-start | bytes 983048 | tf_op jit(solution)/shard_map/ppermute | solution.py:281
  71.4 18.7 %copy-start.10 = (bf16[1280]{0:T(1024)(128)(2,1)S(1)}, bf16[1280]{0:T(1024)(128)(2,1)}, u32[]{:S(2)}) copy-start(bf16[1280]{0:T(1024)(128)(2,1)} %param.13) | copy-start | bytes 7684
  71.4 29.2 %copy-start.8 = (f32[1280]{0:T(1024)S(1)}, f32[1280]{0:T(1024)}, u32[]{:S(2)}) copy-start(f32[1280]{0:T(1024)} %param.15) | copy-start | bytes 15364
  71.4 29.2 %copy-start.9 = (f32[1280]{0:T(1024)S(1)}, f32[1280]{0:T(1024)}, u32[]{:S(2)}) copy-start(f32[1280]{0:T(1024)} %param.14) | copy-start | bytes 15364
  71.6 10.6 %collective-permute-start.10 = (f16[128,1280]{1,0:T(8,128)(2,1)S(1)}, f16[128,1280]{1,0:T(8,128)(2,1)S(1)}, u32[]{:S(2)}, u32[]{:S(2)}) collective-permute-start(f16[128,1280]{1,0:T(8,128)(2,1)S(1)} %get-tuple-element.28), channel_id=1, source_target_pairs={{4,8},{8,4},{5,9},{9,5},{6,10},{10,6},{7,11},{11,7},{20,24},{24,20... | collective-permute-start | bytes 983048 | tf_op jit(solution)/shard_map/ppermute | solution.py:203
  74.9 11.4 %collective-permute-start.8 = (f16[128,1280]{1,0:T(8,128)(2,1)S(1)}, f16[128,1280]{1,0:T(8,128)(2,1)S(1)}, u32[]{:S(2)}, u32[]{:S(2)}) collective-permute-start(f16[128,1280]{1,0:T(8,128)(2,1)S(1)} %get-tuple-element.50), channel_id=1, source_target_pairs={{0,4},{12,8},{1,5},{13,9},{2,6},{14,10},{3,7},{15,11},{16,20},{28,... | collective-permute-start | bytes 983048 | tf_op jit(solution)/shard_map/ppermute | solution.py:282
  82.3 9.4 %collective-permute-start.11 = (f16[128,1280]{1,0:T(8,128)(2,1)S(1)}, f16[128,1280]{1,0:T(8,128)(2,1)S(1)}, u32[]{:S(2)}, u32[]{:S(2)}) collective-permute-start(f16[128,1280]{1,0:T(8,128)(2,1)S(1)} %multiply_convert_fusion), channel_id=1, source_target_pairs={{0,4},{4,0},{8,12},{12,8},{1,5},{5,1},{9,13},{13,9},{2,6},{6,2},{1... | collective-permute-start | bytes 983048 | tf_op jit(solution)/shard_map/ppermute | solution.py:205
  86.4 9.0 %collective-permute-start.9 = (f16[128,1280]{1,0:T(8,128)(2,1)S(1)}, f16[128,1280]{1,0:T(8,128)(2,1)S(1)}, u32[]{:S(2)}, u32[]{:S(2)}) collective-permute-start(f16[128,1280]{1,0:T(8,128)(2,1)S(1)} %multiply_convert_fusion.1), channel_id=1, source_target_pairs={{4,8},{8,4},{5,9},{9,5},{6,10},{10,6},{7,11},{11,7},{20,24},{24,20... | collective-permute-start | bytes 983048 | tf_op jit(solution)/shard_map/ppermute | solution.py:204
  95.7 1.2 collective-permute-start.12
  96.9 3.6 %collective-permute-start.13 = (f32[2,128]{1,0:T(2,128)S(1)}, f32[2,128]{1,0:T(2,128)S(1)}, u32[]{:S(2)}, u32[]{:S(2)}) collective-permute-start(f32[2,128]{1,0:T(2,128)S(1)} %fusion.23), channel_id=1, source_target_pairs={{0,2},{1,3},{2,0},{3,1},{4,6},{5,7},{6,4},{7,5},{8,10},{9,11},{10,... | collective-permute-start | bytes 3080 | tf_op jit(solution)/shard_map/ppermute | solution.py:210
  100.8 8.7 %collective-permute-start.14 = (bf16[128,1280]{1,0:T(8,128)(2,1)S(1)}, bf16[128,1280]{1,0:T(8,128)(2,1)S(1)}, u32[]{:S(2)}, u32[]{:S(2)}) collective-permute-start(bf16[128,1280]{1,0:T(8,128)(2,1)S(1)} %add_convert_fusion.2), channel_id=1, source_target_pairs={{0,4},{4,0},{8,12},{12,8},{1,5},{5,1},{9,13},{13,9},{2,6},{6,2},{1... | collective-permute-start | bytes 983048 | tf_op jit(solution)/shard_map/ppermute | solution.py:186
  100.9 10.6 %collective-permute-start.17 = (bf16[128,1280]{1,0:T(8,128)(2,1)S(1)}, bf16[128,1280]{1,0:T(8,128)(2,1)}, u32[]{:S(2)}, u32[]{:S(2)}) collective-permute-start(bf16[128,1280]{1,0:T(8,128)(2,1)S(1)} %add_convert_fusion.2), channel_id=1, source_target_pairs={{4,8},{8,4},{5,9},{9,5},{6,10},{10,6},{7,11},{11,7},{20,24},{24,20... | collective-permute-start | bytes 983048 | tf_op jit(solution)/shard_map/ppermute | solution.py:187
  109.5 20.1 %copy-start.3 = (bf16[1280,1536]{1,0:T(8,128)(2,1)S(1)}, bf16[1280,1536]{1,0:T(8,128)(2,1)}, u32[]{:S(2)}) copy-start(bf16[1280,1536]{1,0:T(8,128)(2,1)} %copy-done.2) | copy-start | bytes 11796484
  111.5 8.3 %collective-permute-start.18 = (bf16[128,1280]{1,0:T(8,128)(2,1)}, bf16[128,1280]{1,0:T(8,128)(2,1)S(1)}, u32[]{:S(2)}, u32[]{:S(2)}) collective-permute-start(bf16[128,1280]{1,0:T(8,128)(2,1)} %collective-permute-done.17), channel_id=1, source_target_pairs={{4,0},{8,12},{5,1},{9,13},{6,2},{10,14},{7,3},{11,15},{20,16},{24,... | collective-permute-start | bytes 983048 | tf_op jit(solution)/shard_map/ppermute | solution.py:189
  116.1 23.6 %collective-permute-start.15 = (f16[256,1536]{1,0:T(8,128)(2,1)S(1)}, f16[256,1536]{1,0:T(8,128)(2,1)S(1)}, u32[]{:S(2)}, u32[]{:S(2)}) collective-permute-start(f16[256,1536]{1,0:T(8,128)(2,1)S(1)} %convolution_convert_fusion), channel_id=1, source_target_pairs={{0,1},{1,0},{2,3},{3,2},{4,5},{5,4},{6,7},{7,6},{8,9},{9,8},{10,11... | collective-permute-start | bytes 2359304 | tf_op jit(solution)/shard_map/ppermute | solution.py:210
  116.2 12.0 %collective-permute-start.21 = (bf16[128,1280]{1,0:T(8,128)(2,1)S(1)}, bf16[128,1280]{1,0:T(8,128)(2,1)S(1)}, u32[]{:S(2)}, u32[]{:S(2)}) collective-permute-start(bf16[128,1280]{1,0:T(8,128)(2,1)S(1)} %collective-permute-done.14), channel_id=1, source_target_pairs={{4,8},{8,4},{5,9},{9,5},{6,10},{10,6},{7,11},{11,7},{20,24},{24,20... | collective-permute-start | bytes 983048 | tf_op jit(solution)/shard_map/ppermute | solution.py:188
  128.2 8.4 %collective-permute-start.22 = (bf16[128,1280]{1,0:T(8,128)(2,1)S(1)}, bf16[128,1280]{1,0:T(8,128)(2,1)S(1)}, u32[]{:S(2)}, u32[]{:S(2)}) collective-permute-start(bf16[128,1280]{1,0:T(8,128)(2,1)S(1)} %collective-permute-done.21), channel_id=1, source_target_pairs={{4,0},{8,12},{5,1},{9,13},{6,2},{10,14},{7,3},{11,15},{20,16},{24,... | collective-permute-start | bytes 983048 | tf_op jit(solution)/shard_map/ppermute | solution.py:190
  130.4 7.0 %copy-start.1 = (bf16[1280,1536]{1,0:T(8,128)(2,1)S(1)}, bf16[1280,1536]{1,0:T(8,128)(2,1)}, u32[]{:S(2)}) copy-start(bf16[1280,1536]{1,0:T(8,128)(2,1)} %copy-done) | copy-start | bytes 11796484
  130.4 7.0 %collective-permute-start.19 = (f16[128,1536]{1,0:T(8,128)(2,1)S(1)}, f16[128,1536]{1,0:T(8,128)(2,1)S(1)}, u32[]{:S(2)}, u32[]{:S(2)}) collective-permute-start(f16[128,1536]{1,0:T(8,128)(2,1)S(1)} %convolution_convert_fusion.2), channel_id=1, source_target_pairs={{0,1},{1,0},{2,3},{3,2},{4,5},{5,4},{6,7},{7,6},{8,9},{9,8},{10,11... | collective-permute-start | bytes 1179656 | tf_op jit(solution)/shard_map/ppermute | solution.py:210
  137.3 8.6 %collective-permute-start.23 = (f16[128,1536]{1,0:T(8,128)(2,1)S(1)}, f16[128,1536]{1,0:T(8,128)(2,1)S(1)}, u32[]{:S(2)}, u32[]{:S(2)}) collective-permute-start(f16[128,1536]{1,0:T(8,128)(2,1)S(1)} %convolution_convert_fusion.1), channel_id=1, source_target_pairs={{0,1},{1,0},{2,3},{3,2},{4,5},{5,4},{6,7},{7,6},{8,9},{9,8},{10,11... | collective-permute-start | bytes 1179656 | tf_op jit(solution)/shard_map/ppermute | solution.py:210
  138.1 7.8 %collective-permute-start.20 = (f16[128,768]{1,0:T(8,128)(2,1)S(1)}, f16[128,768]{1,0:T(8,128)(2,1)S(1)}, u32[]{:S(2)}, u32[]{:S(2)}) collective-permute-start(f16[128,768]{1,0:T(8,128)(2,1)S(1)} %slice_convert_fusion.3), channel_id=1, source_target_pairs={{0,2},{1,3},{2,0},{3,1},{4,6},{5,7},{6,4},{7,5},{8,10},{9,11},{10,... | collective-permute-start | bytes 589832 | tf_op jit(solution)/shard_map/ppermute | solution.py:210
  140.9 13.4 %collective-permute-start.16 = (f16[256,768]{1,0:T(8,128)(2,1)S(1)}, f16[256,768]{1,0:T(8,128)(2,1)S(1)}, u32[]{:S(2)}, u32[]{:S(2)}) collective-permute-start(f16[256,768]{1,0:T(8,128)(2,1)S(1)} %slice_convert_fusion), channel_id=1, source_target_pairs={{0,2},{1,3},{2,0},{3,1},{4,6},{5,7},{6,4},{7,5},{8,10},{9,11},{10,... | collective-permute-start | bytes 1179656 | tf_op jit(solution)/shard_map/ppermute | solution.py:210
  146.7 11.4 %collective-permute-start.24 = (f16[128,768]{1,0:T(8,128)(2,1)S(1)}, f16[128,768]{1,0:T(8,128)(2,1)S(1)}, u32[]{:S(2)}, u32[]{:S(2)}) collective-permute-start(f16[128,768]{1,0:T(8,128)(2,1)S(1)} %slice_convert_fusion.2), channel_id=1, source_target_pairs={{0,2},{1,3},{2,0},{3,1},{4,6},{5,7},{6,4},{7,5},{8,10},{9,11},{10,... | collective-permute-start | bytes 589832 | tf_op jit(solution)/shard_map/ppermute | solution.py:210
  160.6 5.2 %collective-permute-start.27 = (bf16[256,256]{1,0:T(8,128)(2,1)S(1)}, bf16[256,256]{1,0:T(8,128)(2,1)S(1)}, u32[]{:S(2)}, u32[]{:S(2)}) collective-permute-start(bf16[256,256]{1,0:T(8,128)(2,1)S(1)} %attend.3), channel_id=1, source_target_pairs={{0,2},{1,3},{2,0},{3,1},{4,6},{5,7},{6,4},{7,5},{8,10},{9,11},{10,... | collective-permute-start | bytes 393224 | tf_op jit(solution)/shard_map/ppermute | solution.py:210
  165.8 8.6 %collective-permute-start.28 = (bf16[256,512]{1,0:T(8,128)(2,1)S(1)}, bf16[256,512]{1,0:T(8,128)(2,1)S(1)}, u32[]{:S(2)}, u32[]{:S(2)}) collective-permute-start(bf16[256,512]{1,0:T(8,128)(2,1)S(1)} %pad_maximum_fusion.4), channel_id=1, source_target_pairs={{0,1},{1,0},{2,3},{3,2},{4,5},{5,4},{6,7},{7,6},{8,9},{9,8},{10,11... | collective-permute-start | bytes 786440 | tf_op jit(solution)/shard_map/ppermute | solution.py:210
  168.3 11.4 %copy-start.7 = (bf16[1024,1280]{1,0:T(8,128)(2,1)S(1)}, bf16[1024,1280]{1,0:T(8,128)(2,1)}, u32[]{:S(2)}) copy-start(bf16[1024,1280]{1,0:T(8,128)(2,1)} %copy-done.6) | copy-start | bytes 7864324
  168.3 6.0 %collective-permute-start.25 = (bf16[256,256]{1,0:T(8,128)(2,1)S(1)}, bf16[256,256]{1,0:T(8,128)(2,1)S(1)}, u32[]{:S(2)}, u32[]{:S(2)}) collective-permute-start(bf16[256,256]{1,0:T(8,128)(2,1)S(1)} %attend.2), channel_id=1, source_target_pairs={{0,2},{1,3},{2,0},{3,1},{4,6},{5,7},{6,4},{7,5},{8,10},{9,11},{10,... | collective-permute-start | bytes 393224 | tf_op jit(solution)/shard_map/ppermute | solution.py:210
  174.3 5.4 %collective-permute-start.26 = (bf16[256,512]{1,0:T(8,128)(2,1)S(1)}, bf16[256,512]{1,0:T(8,128)(2,1)S(1)}, u32[]{:S(2)}, u32[]{:S(2)}) collective-permute-start(bf16[256,512]{1,0:T(8,128)(2,1)S(1)} %pad_maximum_fusion.3), channel_id=1, source_target_pairs={{0,1},{1,0},{2,3},{3,2},{4,5},{5,4},{6,7},{7,6},{8,9},{9,8},{10,11... | collective-permute-start | bytes 786440 | tf_op jit(solution)/shard_map/ppermute | solution.py:210
  177.0 12.4 %collective-permute-start.29 = (bf16[128,1280]{1,0:T(8,128)(2,1)S(1)}, bf16[128,1280]{1,0:T(8,128)(2,1)S(1)}, u32[]{:S(2)}, u32[]{:S(2)}) collective-permute-start(bf16[128,1280]{1,0:T(8,128)(2,1)S(1)} %get-tuple-element.47), channel_id=1, source_target_pairs={{0,4},{12,8},{1,5},{13,9},{2,6},{14,10},{3,7},{15,11},{16,20},{28,... | collective-permute-start | bytes 983048 | tf_op jit(solution)/shard_map/ppermute | solution.py:195
  178.3 17.8 %collective-permute-start.30 = (bf16[128,1280]{1,0:T(8,128)(2,1)S(1)}, bf16[128,1280]{1,0:T(8,128)(2,1)S(1)}, u32[]{:S(2)}, u32[]{:S(2)}) collective-permute-start(bf16[128,1280]{1,0:T(8,128)(2,1)S(1)} %get-tuple-element.46), channel_id=1, source_target_pairs={{0,4},{12,8},{1,5},{13,9},{2,6},{14,10},{3,7},{15,11},{16,20},{28,... | collective-permute-start | bytes 983048 | tf_op jit(solution)/shard_map/ppermute | solution.py:196
  189.5 11.1 %collective-permute-start.32 = (bf16[128,1280]{1,0:T(8,128)(2,1)S(1)}, bf16[128,1280]{1,0:T(8,128)(2,1)S(1)}, u32[]{:S(2)}, u32[]{:S(2)}) collective-permute-start(bf16[128,1280]{1,0:T(8,128)(2,1)S(1)} %get-tuple-element.38), channel_id=1, source_target_pairs={{4,8},{8,4},{5,9},{9,5},{6,10},{10,6},{7,11},{11,7},{20,24},{24,20... | collective-permute-start | bytes 983048 | tf_op jit(solution)/shard_map/ppermute | solution.py:203
  196.2 11.4 %collective-permute-start.31 = (bf16[128,1280]{1,0:T(8,128)(2,1)S(1)}, bf16[128,1280]{1,0:T(8,128)(2,1)S(1)}, u32[]{:S(2)}, u32[]{:S(2)}) collective-permute-start(bf16[128,1280]{1,0:T(8,128)(2,1)S(1)} %add_convert_fusion), channel_id=1, source_target_pairs={{4,8},{8,4},{5,9},{9,5},{6,10},{10,6},{7,11},{11,7},{20,24},{24,20... | collective-permute-start | bytes 983048 | tf_op jit(solution)/shard_map/ppermute | solution.py:204
  200.6 8.5 %collective-permute-start.33 = (bf16[128,1280]{1,0:T(8,128)(2,1)S(1)}, bf16[128,1280]{1,0:T(8,128)(2,1)S(1)}, u32[]{:S(2)}, u32[]{:S(2)}) collective-permute-start(bf16[128,1280]{1,0:T(8,128)(2,1)S(1)} %fusion.1), channel_id=1, source_target_pairs={{0,4},{4,0},{8,12},{12,8},{1,5},{5,1},{9,13},{13,9},{2,6},{6,2},{1... | collective-permute-start | bytes 983048 | tf_op jit(solution)/shard_map/ppermute | solution.py:205

commit v3 on v2

--- a/solution.py
+++ b/solution.py
@@ -12,6 +12,7 @@
 HEAD = 128
 GROUP = 8
 VMEM_BYTES = 20 * 1024 * 1024
+STREAM_BYTES = 56 * 1024 * 1024
 
 
 def densify_kernel(base_ref, *refs, topk, latents, lanes):
@@ -89,7 +90,7 @@
             in_specs=[pl.BlockSpec((1, depth, width), lambda j, t, order: (t, 0, order[j]))],
             out_specs=pl.BlockSpec((depth, width), lambda j, t, order: (0, j * kinds + t)),
         ),
-        compiler_params=pltpu.CompilerParams(vmem_limit_bytes=VMEM_BYTES),
+        compiler_params=pltpu.CompilerParams(vmem_limit_bytes=STREAM_BYTES),
         cost_estimate=pl.CostEstimate(
             flops=0, bytes_accessed=4 * depth * count * kinds * width, transcendentals=0
         ),
@@ -108,7 +109,7 @@
             in_specs=[pl.BlockSpec((height, columns), lambda j, order: (order[j], 0))],
             out_specs=pl.BlockSpec((height, columns), lambda j, order: (j, 0)),
         ),
-        compiler_params=pltpu.CompilerParams(vmem_limit_bytes=VMEM_BYTES),
+        compiler_params=pltpu.CompilerParams(vmem_limit_bytes=STREAM_BYTES),
         cost_estimate=pl.CostEstimate(
             flops=0, bytes_accessed=4 * count * height * columns, transcendentals=0
         ),
@@ -182,19 +183,11 @@
     return [index, index ^ 1, jnp.where(low, 2, 1), jnp.where(low, 3, 0)]
 
 
-def line_gather(own, outer):
-    near = lax.ppermute(own, "lat", PAIRS)
-    across = lax.ppermute(own, "lat", MIDDLE)
-    far = lax.ppermute(near, "lat", MIDDLE)
-    across_out = lax.ppermute(across, "lat", OUTWARD)
-    far_out = lax.ppermute(far, "lat", OUTWARD)
-    return [own, near, jnp.where(outer, across_out, across), jnp.where(outer, far_out, far)]
-
-
-def line_sum(parts, encode, decode_sent):
-    in_far = lax.ppermute(encode(parts[3]), "lat", INWARD)
-    in_across = lax.ppermute(encode(parts[2]), "lat", INWARD)
-    return line_end(parts, in_far, in_across, encode, decode_sent)
+def line_gather_direct(own, outer):
+    near = lax.ppermute(own, "lat", [(i, i ^ 1) for i in range(4)])
+    two = lax.ppermute(own, "lat", [(i, i ^ 2) for i in range(4)])
+    three = lax.ppermute(own, "lat", [(i, i ^ 3) for i in range(4)])
+    return [own, near, jnp.where(outer, two, three), jnp.where(outer, three, two)]
 
 
 def line_end(parts, in_far, in_across, encode, decode_sent):
@@ -251,15 +244,14 @@
     hold = lax.optimization_barrier
 
     packed = pack(code_ids, code_vals)
-    packed = line_gather(packed, outer)
+    packed = line_gather_direct(packed, outer)
     base = (lat * latents).reshape(1)
 
     def cache_of(j):
         start = (col ^ j) * own_width
         return lax.dynamic_slice_in_dim(cache_kv, start, own_width, 2)
 
-    sent = swap(jnp.stack([cache_of(1), cache_of(3)]), 1, cols)
-    other = swap(jnp.stack([cache_of(2), sent[1]]), 2, cols)
+    across = swap(jnp.stack([cache_of(2), cache_of(3)]), 2, cols)
 
     weights = w_qkv.transpose(1, 0, 2)
     away_weights = select_columns(weights, jnp.stack([col ^ 1, col ^ 3]), own_width)
@@ -276,8 +268,9 @@
     codes_far = densify([packed[3], packed[2]], base, topk, latents)
     codes_near = densify([near_packed[1], near_packed[0]], base, topk, latents)
     far = jnp.dot(codes_far, decoder, preferred_element_type=jnp.float32)
-    codes_near, other, query_pos = hold((codes_near, other, query_pos))
-    cached = [cache_of(0), sent[0], other[0], other[1]]
+    codes_near, across, query_pos = hold((codes_near, across, query_pos))
+    beside = swap(jnp.stack([cache_of(1), across[1]]), 1, cols)
+    cached = [cache_of(0), across[0], beside[0], beside[1]]
     in_far = lax.ppermute(to_half(far[:rows]), "lat", INWARD)
     in_across = lax.ppermute(to_half(far[rows:]), "lat", INWARD)
     near = jnp.dot(codes_near, decoder, preferred_element_type=jnp.float32)
@@ -289,33 +282,60 @@
     sums = jnp.stack([jnp.sum(residual, axis=1), jnp.sum(residual * residual, axis=1)])
     sums = sums + swap(sums, 1, cols)
     sums = sums + swap(sums, 2, cols)
-    normed = line_gather(normalize(residual, sums, ln_gain, ln_bias), outer)
+    own = normalize(residual, sums, ln_gain, ln_bias)
+    near = lax.ppermute(own, "lat", PAIRS)
+    across = lax.ppermute(own, "lat", MIDDLE)
+    far = lax.ppermute(near, "lat", MIDDLE)
+    across_out = lax.ppermute(across, "lat", OUTWARD)
+    far_out = lax.ppermute(far, "lat", OUTWARD)
 
     quarter = keep_weights.shape[1] // 2
 
-    def project(block, after):
-        block, _ = hold((block, after))
+    def project(block):
         away = jnp.dot(block, away_weights, preferred_element_type=jnp.float32).astype(jnp.float16)
         keep = jnp.dot(block, keep_weights, preferred_element_type=jnp.float32)
         keep = keep + swap(away, 1, cols).astype(jnp.float32)
-        came = swap(keep[:, quarter:].astype(jnp.float16), 2, cols).astype(jnp.float32)
-        return (keep[:, :quarter] + came).astype(jnp.bfloat16), away
-
-    pair, sent = project(jnp.concatenate(normed[:2], axis=0), normed[0])
-    third, sent = project(normed[2], sent)
-    fourth, sent = project(normed[3], sent)
-    qkv = [pair[:rows], pair[rows:], third, fourth]
-
-    branch = [None] * 4
-    for group in ((3, 2), (1, 0)):
-        pos = jnp.concatenate([query_pos[g * rows : (g + 1) * rows] for g in group], axis=0)
-        mixed = attend(pos, key_pos.reshape(1, -1), qkv, cached, group, heads)
-        mixed = jnp.concatenate([mixed, swap(mixed, 2, cols)], axis=1)
-        mixed = jnp.concatenate([mixed, swap(mixed, 1, cols)], axis=1)
-        product = jnp.dot(mixed, out_weights, preferred_element_type=jnp.float32)
-        branch[group[0]], branch[group[1]] = product[:rows], product[rows:]
-    added = line_sum(
-        branch, lambda v: v.astype(jnp.bfloat16), lambda v: v.astype(jnp.float32)
+        return keep[:, :quarter], keep[:, quarter:].astype(jnp.float16)
+
+    def finish(keep, payload):
+        return (keep + swap(payload, 2, cols).astype(jnp.float32)).astype(jnp.bfloat16)
+
+    pair, across = hold((jnp.concatenate([own, near], axis=0), across))
+    keep0, payload0 = project(pair)
+    third, far, payload0 = hold((jnp.where(outer, across_out, across), far, payload0))
+    keep2, payload2 = project(third)
+    fourth, payload2 = hold((jnp.where(outer, far_out, far), payload2))
+    keep3, payload3 = project(fourth)
+    first = finish(keep0, payload0)
+    qkv = [first[:rows], first[rows:], finish(keep2, payload2), finish(keep3, payload3)]
+
+    key_row = key_pos.reshape(1, -1)
+
+    def pos_of(a, b):
+        return jnp.concatenate(
+            [query_pos[a * rows : (a + 1) * rows], query_pos[b * rows : (b + 1) * rows]], axis=0
+        )
+
+    mixed_far = attend(pos_of(3, 2), key_row, qkv, cached, (3, 2), heads)
+    near_pos, mixed_far = hold((pos_of(1, 0), mixed_far))
+    mixed_near = attend(near_pos, key_row, qkv, cached, (1, 0), heads)
+    mixed_far = jnp.concatenate([mixed_far, swap(mixed_far, 2, cols)], axis=1)
+    mixed_far = jnp.concatenate([mixed_far, swap(mixed_far, 1, cols)], axis=1)
+    product_far = jnp.dot(mixed_far, out_weights, preferred_element_type=jnp.float32)
+    sent_far = product_far.astype(jnp.bfloat16)
+    in_far = lax.ppermute(sent_far[:rows], "lat", INWARD)
+    in_across = lax.ppermute(sent_far[rows:], "lat", INWARD)
+    mixed_near = jnp.concatenate([mixed_near, swap(mixed_near, 2, cols)], axis=1)
+    mixed_near, sent_far = hold((mixed_near, sent_far))
+    mixed_near = jnp.concatenate([mixed_near, swap(mixed_near, 1, cols)], axis=1)
+    product_near = jnp.dot(mixed_near, out_weights, preferred_element_type=jnp.float32)
+    branch = [product_near[rows:], product_near[:rows], product_far[rows:], product_far[:rows]]
+    added = line_end(
+        branch,
+        in_far,
+        in_across,
+        lambda v: v.astype(jnp.bfloat16),
+        lambda v: v.astype(jnp.float32),
     )
     return (residual + added).astype(jnp.bfloat16)
 

time: 212 us -> 196 us (0.925)
  Pallas kernels: 20.6 us -> 34.1 us
  waiting for transfers between devices: 90.2 us -> 77.4 us
  starting transfers between devices: 49.9 us -> 37.7 us
  local copies, waits for them, and re-layouts: 12.7 us -> 2.4 us
  other arithmetic: 5.38 us -> 9.4 us
    unnamed x25 -> x19, local copies, waits for them, and re-layouts: 10.3 us -> 0.05 us
    pallas_call x2, Pallas kernels: 3.56 us -> 13 us  [select_columns(): pl.pallas_call(copy_kernel, out_shape=jax.ShapeDtypeStruct((depth, count...]
    ppermute x14, waiting for transfers between devices: 31.6 us -> 24.8 us  [swap(): return lax.ppermute(value, 'col', [(i, i ^ distance) for i in range(size)])]
    ppermute x12 -> x10, starting transfers between devices: 22.3 us -> 15.5 us  [the longest x1 3.14 us: line_gather_direct(): three = lax.ppermute(own, 'lat', [(i, i ^ 3) for i in range(4)])]
    ppermute x2, waiting for transfers between devices: 6.69 us -> 1.87 us  [line_end(): far = lax.ppermute(far, 'lat', MIDDLE)]
    pallas_call x1, Pallas kernels: 0.79 us -> 4.87 us  [select_rows(): pl.pallas_call(copy_kernel, out_shape=jax.ShapeDtypeStruct((count * heigh...]
    ppermute x12 -> x10, waiting for transfers between devices: 34.2 us -> 30.2 us  [the longest x1 9.72 us: line_body(): far = lax.ppermute(near, 'lat', MIDDLE)]
    ppermute x14, starting transfers between devices: 10.6 us -> 7.82 us  [swap(): return lax.ppermute(value, 'col', [(i, i ^ distance) for i in range(size)])]
  transfers between devices with their start and end apart: 34 -> 32, of which waited for: 22 -> 19; matrix products, arithmetic and copies ran while one was open for 16% -> 19% of each run, Pallas kernels for 9% -> 16%
where the time goes in v3:
time: 196 us; the launch traced here: 194 us
  waiting for transfers between devices  77.4 us (39%)
  starting transfers between devices  37.7 us (19%)
  Pallas kernels  34.1 us (17%)
  matrix products  31.9 us (16%)
  other arithmetic  9.4 us (5%)
  local copies, waits for them, and re-layouts  2.4 us (1%)
    ppermute x14, waiting for transfers between devices, swap(): return lax.ppermute(value, 'col', [(i, i ^ distance) for i in range(size)])  24.8 us
    pallas_call x2, Pallas kernels, select_columns(): pl.pallas_call(copy_kernel, out_shape=jax.ShapeDtypeStruct((depth, count...  13 us
    ppermute x2, waiting for transfers between devices, line_end(): lax.ppermute(encode(second + decode_sent(in_across)), 'lat', MIDDLE)  12.4 us
    pallas_call x2, Pallas kernels, densify(): pl.pallas_call(functools.partial(densify_kernel, topk=topk, latents=laten...  11.4 us
    dot_general x1, matrix products, line_body(): near = jnp.dot(codes_near, decoder, preferred_element_type=jnp.float32)  9.9 us
    dot_general x1, matrix products, line_body(): far = jnp.dot(codes_far, decoder, preferred_element_type=jnp.float32)  9.9 us
    ppermute x1, waiting for transfers between devices, line_body(): far = lax.ppermute(near, 'lat', MIDDLE)  9.72 us
    ppermute x1, waiting for transfers between devices, line_body(): in_far = lax.ppermute(sent_far[:rows], 'lat', INWARD)  8.93 us
  transfers between devices with their start and end apart: 32, of which 19 were waited for; matrix products, arithmetic and copies ran while one was open for 19% of the time, Pallas kernels for 16%

profile of v3, /device:TPU:8, one launch (start us, length us, event | category | flops | bytes accessed | tf_op | source)
XLA Modules:
  0.0 193.6 jit_solution(489686887749672137)
XLA Ops:
  1.9 3.1 %collective-permute-start.2 = (f32[16,1024]{1,0:T(8,128)S(1)}, f32[16,1024]{1,0:T(8,128)S(1)}, u32[]{:S(2)}, u32[]{:S(2)}) collective-permute-start(f32[16,1024]{1,0:T(8,128)S(1)} %constant_dynamic-update-slice_fusion.refs_1_), channel_id=1, source_target_pairs={{0,12},{4,8},{8,4},{12,0},{1,13},{5,9},{9,5},{13,1},{2,14},{6,10},... | collective-permute-start | bytes 196616 | tf_op jit(solution)/shard_map/ppermute | solution.py:189
  5.1 1.2 collective-permute-start.3
  6.3 1.5 dynamic-slice_bitcast_fusion
  7.9 1.6 collective-permute-start.1
  10.7 6.5 %select_columns.2 = bf16[1280,1536]{1,0:T(8,128)(2,1)} custom-call(s32[2]{0:T(128)} %get-tuple-element.85.order_ref, bf16[3,1280,1024]{2,1,0:T(8,128)(2,1)} %bitcast.53), custom_call_target="tpu_custom_call" | custom-call | bytes 7864320 | tf_op jit(solution)/shard_map/select_columns/pallas_call | solution.py:84
  17.2 6.5 %select_columns.3 = bf16[1280,1536]{1,0:T(8,128)(2,1)} custom-call(s32[2]{0:T(128)} %get-tuple-element.86.order_ref, bf16[3,1280,1024]{2,1,0:T(8,128)(2,1)} %bitcast.54), custom_call_target="tpu_custom_call" | custom-call | bytes 7864320 | tf_op jit(solution)/shard_map/select_columns/pallas_call | solution.py:84
  23.7 4.9 %select_rows.1 = bf16[1024,1280]{1,0:T(8,128)(2,1)} custom-call(s32[4]{0:T(128)} %pad_add_fusion.5.order_ref, bf16[1024,1280]{1,0:T(8,128)(2,1)} %from_ref.1), custom_call_target="tpu_custom_call" | custom-call | bytes 5242880 | tf_op jit(solution)/shard_map/select_rows/pallas_call | solution.py:103
  28.7 5.7 %densify.3 = bf16[256,8192]{1,0:T(8,128)(2,1)S(1)} custom-call(s32[1]{0:T(128)} %bitcast.base_ref, f32[16,1024]{1,0:T(8,128)S(1)} %get-tuple-element.74.refs_0_, f32[16,1024]{1,0:T(8,128)S(1)} %get-tuple-element.73.refs_1_), custom_call_target="tpu_custom_call" | custom-call | flops 2147483648 | bytes 4194304 | tf_op jit(solution)/shard_map/densify/pallas_call | solution.py:63
  34.4 9.9 %fusion.31 = f32[256,1280]{1,0:T(8,128)S(1)} fusion(bf16[256,8192]{1,0:T(8,128)(2,1)S(1)} %densify.3, bf16[8192,1280]{1,0:T(8,128)(2,1)} %param.12), kind=kOutput, calls=%fused_computation.83 | convolution fusion | flops 5368709120 | bytes 26476544 | tf_op jit(solution)/shard_map/dot_general | solution.py:270
  44.4 1.3 collective-permute-start.4
  45.7 5.7 %densify.2 = bf16[256,8192]{1,0:T(8,128)(2,1)S(1)} custom-call(s32[1]{0:T(128)} %bitcast.base_ref, f32[16,1024]{1,0:T(8,128)S(1)} %collective-permute-done.refs_0_, f32[16,1024]{1,0:T(8,128)S(1)} %constant_dynamic-update-slice_fusion.refs_1_), custom_call_target="tpu_custom_call" | custom-call | flops 2147483648 | bytes 4194304 | tf_op jit(solution)/shard_map/densify/pallas_call | solution.py:63
  51.4 9.9 %fusion.30 = f32[256,1280]{1,0:T(8,128)S(1)} fusion(bf16[256,8192]{1,0:T(8,128)(2,1)S(1)} %densify.2, bf16[8192,1280]{1,0:T(8,128)(2,1)} %param.12), kind=kOutput, calls=%fused_computation.82 | convolution fusion | flops 5368709120 | bytes 26476544 | tf_op jit(solution)/shard_map/dot_general | solution.py:276
  61.5 1.3 collective-permute-start.5
  62.8 3.5 %collective-permute-start.7 = (f16[128,1280]{1,0:T(8,128)(2,1)S(1)}, f16[128,1280]{1,0:T(8,128)(2,1)S(1)}, u32[]{:S(2)}, u32[]{:S(2)}) collective-permute-start(f16[128,1280]{1,0:T(8,128)(2,1)S(1)} %get-tuple-element.35), channel_id=1, source_target_pairs={{4,8},{8,4},{5,9},{9,5},{6,10},{10,6},{7,11},{11,7},{20,24},{24,20... | collective-permute-start | bytes 983048 | tf_op jit(solution)/shard_map/ppermute | solution.py:196
  66.3 5.5 %collective-permute-done.5 = f16[128,1280]{1,0:T(8,128)(2,1)S(1)} collective-permute-done((f16[128,1280]{1,0:T(8,128)(2,1)S(1)}, f16[128,1280]{1,0:T(8,128)(2,1)S(1)}, u32[]{:S(2)}, u32[]{:S(2)}) %collective-permute-start.5) | collective-permute-done | bytes 327712 | tf_op jit(solution)/shard_map/ppermute | solution.py:275
  71.9 3.5 %collective-permute-start.6 = (f16[128,1280]{1,0:T(8,128)(2,1)S(1)}, f16[128,1280]{1,0:T(8,128)(2,1)S(1)}, u32[]{:S(2)}, u32[]{:S(2)}) collective-permute-start(f16[128,1280]{1,0:T(8,128)(2,1)S(1)} %multiply_convert_fusion.1), channel_id=1, source_target_pairs={{4,8},{8,4},{5,9},{9,5},{6,10},{10,6},{7,11},{11,7},{20,24},{24,20... | collective-permute-start | bytes 983048 | tf_op jit(solution)/shard_map/ppermute | solution.py:197
  75.7 5.6 %collective-permute-done.6 = f16[128,1280]{1,0:T(8,128)(2,1)S(1)} collective-permute-done((f16[128,1280]{1,0:T(8,128)(2,1)S(1)}, f16[128,1280]{1,0:T(8,128)(2,1)S(1)}, u32[]{:S(2)}, u32[]{:S(2)}) %collective-permute-start.6) | collective-permute-done | bytes 327712 | tf_op jit(solution)/shard_map/ppermute | solution.py:197
  81.2 1.6 collective-permute-done.8
  83.2 1.1 collective-permute-done.9
  85.9 2.0 %collective-permute-done.10 = f32[2,128]{1,0:T(2,128)S(1)} collective-permute-done((f32[2,128]{1,0:T(2,128)S(1)}, f32[2,128]{1,0:T(2,128)S(1)}, u32[]{:S(2)}, u32[]{:S(2)}) %collective-permute-start.10) | collective-permute-done | bytes 1056 | tf_op jit(solution)/shard_map/ppermute | solution.py:203
  88.5 2.3 %collective-permute-start.12 = (bf16[128,1280]{1,0:T(8,128)(2,1)S(1)}, bf16[128,1280]{1,0:T(8,128)(2,1)}, u32[]{:S(2)}, u32[]{:S(2)}) collective-permute-start(bf16[128,1280]{1,0:T(8,128)(2,1)S(1)} %add_convert_fusion.1), channel_id=1, source_target_pairs={{4,8},{8,4},{5,9},{9,5},{6,10},{10,6},{7,11},{11,7},{20,24},{24,20... | collective-permute-start | bytes 983048 | tf_op jit(solution)/shard_map/ppermute | solution.py:287
  90.9 6.1 %collective-permute-done.11 = bf16[128,1280]{1,0:T(8,128)(2,1)} collective-permute-done((bf16[128,1280]{1,0:T(8,128)(2,1)S(1)}, bf16[128,1280]{1,0:T(8,128)(2,1)}, u32[]{:S(2)}, u32[]{:S(2)}) %collective-permute-start.11) | collective-permute-done | bytes 327712 | tf_op jit(solution)/shard_map/ppermute | solution.py:286
  98.9 2.1 %convolution_convert_fusion = f16[256,1536]{1,0:T(8,128)(2,1)} fusion(bf16[256,1280]{1,0:T(8,128)(2,1)S(1)} %pad_maximum_fusion.2, bf16[1280,1536]{1,0:T(8,128)(2,1)S(1)} %copy-done.1), kind=kOutput, calls=%fused_computation.1 | convolution fusion | flops 1007026176 | bytes 5373952 | tf_op jit(solution)/shard_map/dot_general | solution.py:295
  101.0 2.0 %collective-permute-start.14 = (bf16[128,1280]{1,0:T(8,128)(2,1)}, bf16[128,1280]{1,0:T(8,128)(2,1)}, u32[]{:S(2)}, u32[]{:S(2)}) collective-permute-start(bf16[128,1280]{1,0:T(8,128)(2,1)} %collective-permute-done.12), channel_id=1, source_target_pairs={{4,0},{8,12},{5,1},{9,13},{6,2},{10,14},{7,3},{11,15},{20,16},{24,... | collective-permute-start | bytes 983048 | tf_op jit(solution)/shard_map/ppermute | solution.py:289
  103.0 2.3 %collective-permute-start.15 = (bf16[128,1280]{1,0:T(8,128)(2,1)}, bf16[128,1280]{1,0:T(8,128)(2,1)}, u32[]{:S(2)}, u32[]{:S(2)}) collective-permute-start(bf16[128,1280]{1,0:T(8,128)(2,1)} %collective-permute-done.11), channel_id=1, source_target_pairs={{4,8},{8,4},{5,9},{9,5},{6,10},{10,6},{7,11},{11,7},{20,24},{24,20... | collective-permute-start | bytes 983048 | tf_op jit(solution)/shard_map/ppermute | solution.py:288
  105.6 9.7 %collective-permute-done.15 = bf16[128,1280]{1,0:T(8,128)(2,1)} collective-permute-done((bf16[128,1280]{1,0:T(8,128)(2,1)}, bf16[128,1280]{1,0:T(8,128)(2,1)}, u32[]{:S(2)}, u32[]{:S(2)}) %collective-permute-start.15) | collective-permute-done | bytes 327712 | tf_op jit(solution)/shard_map/ppermute | solution.py:288
  115.3 1.5 collective-permute-start.18
  117.9 3.8 %convolution_add_fusion = f32[256,1536]{1,0:T(8,128)S(1)} fusion(bf16[256,1280]{1,0:T(8,128)(2,1)} %copy-done.4, bf16[1280,1536]{1,0:T(8,128)(2,1)} %select_columns.3, f16[256,1536]{1,0:T(8,128)(2,1)} %collective-permute-done.13), kind=kOutput, calls=%fused_computation | convolution fusion | flops 1007419392 | bytes 6946816 | tf_op jit(solution)/shard_map/dot_general | solution.py:296
  122.6 1.1 collective-permute-start.16
  126.5 1.1 collective-permute-start.19
  127.6 6.9 %collective-permute-done.16 = f16[256,768]{1,0:T(8,128)(2,1)S(1)} collective-permute-done((f16[256,768]{1,0:T(8,128)(2,1)S(1)}, f16[256,768]{1,0:T(8,128)(2,1)S(1)}, u32[]{:S(2)}, u32[]{:S(2)}) %collective-permute-start.16) | collective-permute-done | bytes 393248 | tf_op jit(solution)/shard_map/ppermute | solution.py:203
  135.4 1.1 collective-permute-start.21
  136.5 2.3 %collective-permute-done.19 = f16[128,768]{1,0:T(8,128)(2,1)S(1)} collective-permute-done((f16[128,768]{1,0:T(8,128)(2,1)S(1)}, f16[128,768]{1,0:T(8,128)(2,1)S(1)}, u32[]{:S(2)}, u32[]{:S(2)}) %collective-permute-start.19) | collective-permute-done | bytes 196640 | tf_op jit(solution)/shard_map/ppermute | solution.py:203
  138.8 3.7 %collective-permute-done.21 = f16[128,768]{1,0:T(8,128)(2,1)S(1)} collective-permute-done((f16[128,768]{1,0:T(8,128)(2,1)S(1)}, f16[128,768]{1,0:T(8,128)(2,1)S(1)}, u32[]{:S(2)}, u32[]{:S(2)}) %collective-permute-start.21) | collective-permute-done | bytes 196640 | tf_op jit(solution)/shard_map/ppermute | solution.py:203
  142.6 2.4 %attend.2 = bf16[256,256]{1,0:T(8,128)(2,1)S(1)} custom-call(s32[256,1]{1,0:T(8,128)S(1)} %copy.21.refs_0_, s32[1,512]{1,0:T(1,128)S(1)} %bitcast.51, bf16[128,768]{1,0:T(8,128)(2,1)S(1)} %get-tuple-element.72.refs_2_, bf16[128,768]{1,0:T(8,128)(2,1)S(1)} %get-tuple-element.71.refs_3_, bf16[128,768]{1,0:T(8,128)(2,1)S(1)} %fusion.17.refs_4_, ...), custom_call_target="tpu_custom_call" | custom-call | flops 536870912 | bytes 2097152 | tf_op jit(solution)/shard_map/attend/pallas_call | solution.py:160
  146.2 3.8 %collective-permute-done.24 = bf16[256,256]{1,0:T(8,128)(2,1)S(1)} collective-permute-done((bf16[256,256]{1,0:T(8,128)(2,1)S(1)}, bf16[256,256]{1,0:T(8,128)(2,1)S(1)}, u32[]{:S(2)}, u32[]{:S(2)}) %collective-permute-start.24) | collective-permute-done | bytes 131104 | tf_op jit(solution)/shard_map/ppermute | solution.py:203
  150.1 2.4 %attend.3 = bf16[256,256]{1,0:T(8,128)(2,1)S(1)} custom-call(s32[256,1]{1,0:T(8,128)S(1)} %copy.22.refs_0_, s32[1,512]{1,0:T(1,128)S(1)} %bitcast.52, bf16[128,768]{1,0:T(8,128)(2,1)S(1)} %get-tuple-element.72.refs_2_, bf16[128,768]{1,0:T(8,128)(2,1)S(1)} %get-tuple-element.71.refs_3_, bf16[128,768]{1,0:T(8,128)(2,1)S(1)} %fusion.17.refs_4_, ...), custom_call_target="tpu_custom_call" | custom-call | flops 536870912 | bytes 2097152 | tf_op jit(solution)/shard_map/attend/pallas_call | solution.py:160
  153.6 4.9 %collective-permute-done.23 = bf16[256,256]{1,0:T(8,128)(2,1)S(1)} collective-permute-done((bf16[256,256]{1,0:T(8,128)(2,1)S(1)}, bf16[256,256]{1,0:T(8,128)(2,1)S(1)}, u32[]{:S(2)}, u32[]{:S(2)}) %collective-permute-start.23) | collective-permute-done | bytes 131104 | tf_op jit(solution)/shard_map/ppermute | solution.py:203
  158.6 2.6 %fusion.29 = (bf16[256,1280]{1,0:T(8,128)(2,1)S(1)}, f32[256,1280]{1,0:T(8,128)S(1)}) fusion(bf16[1024,1280]{1,0:T(8,128)(2,1)} %select_rows.1, bf16[256,512]{1,0:T(8,128)(2,1)S(1)} %collective-permute-done.25, bf16[256,256]{1,0:T(8,128)(2,1)S(1)} %collective-permute-done.24, bf16[256,256]{1,0:T(8,128)(2,1)S(1)} %attend.2), kind=kOutput, calls=%fused_computation.81 | convolution fusion | flops 672989184 | bytes 5111808 | tf_op jit(solution)/shard_map/dot_general | solution.py:324
  161.3 1.3 collective-permute-start.27
  162.6 1.3 collective-permute-start.28
  164.8 8.9 %collective-permute-done.27 = bf16[128,1280]{1,0:T(8,128)(2,1)S(1)} collective-permute-done((bf16[128,1280]{1,0:T(8,128)(2,1)S(1)}, bf16[128,1280]{1,0:T(8,128)(2,1)S(1)}, u32[]{:S(2)}, u32[]{:S(2)}) %collective-permute-start.27) | collective-permute-done | bytes 327712 | tf_op jit(solution)/shard_map/ppermute | solution.py:326
  173.8 2.3 %collective-permute-start.30 = (bf16[128,1280]{1,0:T(8,128)(2,1)S(1)}, bf16[128,1280]{1,0:T(8,128)(2,1)S(1)}, u32[]{:S(2)}, u32[]{:S(2)}) collective-permute-start(bf16[128,1280]{1,0:T(8,128)(2,1)S(1)} %get-tuple-element.52), channel_id=1, source_target_pairs={{4,8},{8,4},{5,9},{9,5},{6,10},{10,6},{7,11},{11,7},{20,24},{24,20... | collective-permute-start | bytes 983048 | tf_op jit(solution)/shard_map/ppermute | solution.py:196
  176.1 4.2 %collective-permute-done.28 = bf16[128,1280]{1,0:T(8,128)(2,1)S(1)} collective-permute-done((bf16[128,1280]{1,0:T(8,128)(2,1)S(1)}, bf16[128,1280]{1,0:T(8,128)(2,1)S(1)}, u32[]{:S(2)}, u32[]{:S(2)}) %collective-permute-start.28) | collective-permute-done | bytes 327712 | tf_op jit(solution)/shard_map/ppermute | solution.py:327
  180.4 2.3 %collective-permute-start.29 = (bf16[128,1280]{1,0:T(8,128)(2,1)S(1)}, bf16[128,1280]{1,0:T(8,128)(2,1)S(1)}, u32[]{:S(2)}, u32[]{:S(2)}) collective-permute-start(bf16[128,1280]{1,0:T(8,128)(2,1)S(1)} %add_convert_fusion), channel_id=1, source_target_pairs={{4,8},{8,4},{5,9},{9,5},{6,10},{10,6},{7,11},{11,7},{20,24},{24,20... | collective-permute-start | bytes 983048 | tf_op jit(solution)/shard_map/ppermute | solution.py:197
  182.7 1.9 collective-permute-done.30
  184.8 6.9 %collective-permute-done.29 = bf16[128,1280]{1,0:T(8,128)(2,1)S(1)} collective-permute-done((bf16[128,1280]{1,0:T(8,128)(2,1)S(1)}, bf16[128,1280]{1,0:T(8,128)(2,1)S(1)}, u32[]{:S(2)}, u32[]{:S(2)}) %collective-permute-start.29) | collective-permute-done | bytes 327712 | tf_op jit(solution)/shard_map/ppermute | solution.py:197
  191.6 1.1 collective-permute-done.31
  (103 shorter events, 18.8 us)
Async XLA Ops:
  1.9 42.4 %collective-permute-start = (f32[16,1024]{1,0:T(8,128)S(1)}, f32[16,1024]{1,0:T(8,128)S(1)}, u32[]{:S(2)}, u32[]{:S(2)}) collective-permute-start(f32[16,1024]{1,0:T(8,128)S(1)} %constant_dynamic-update-slice_fusion.refs_1_), channel_id=1, source_target_pairs={{0,4},{4,0},{8,12},{12,8},{1,5},{5,1},{9,13},{13,9},{2,6},{6,2},{1... | collective-permute-start | bytes 196616 | tf_op jit(solution)/shard_map/ppermute | solution.py:187
  1.9 26.7 %collective-permute-start.2 = (f32[16,1024]{1,0:T(8,128)S(1)}, f32[16,1024]{1,0:T(8,128)S(1)}, u32[]{:S(2)}, u32[]{:S(2)}) collective-permute-start(f32[16,1024]{1,0:T(8,128)S(1)} %constant_dynamic-update-slice_fusion.refs_1_), channel_id=1, source_target_pairs={{0,12},{4,8},{8,4},{12,0},{1,13},{5,9},{9,5},{13,1},{2,14},{6,10},... | collective-permute-start | bytes 196616 | tf_op jit(solution)/shard_map/ppermute | solution.py:189
  5.1 23.6 %collective-permute-start.3 = (f32[16,1024]{1,0:T(8,128)S(1)}, f32[16,1024]{1,0:T(8,128)S(1)}, u32[]{:S(2)}, u32[]{:S(2)}) collective-permute-start(f32[16,1024]{1,0:T(8,128)S(1)} %constant_dynamic-update-slice_fusion.refs_1_), channel_id=1, source_target_pairs={{0,8},{4,12},{8,0},{12,4},{1,9},{5,13},{9,1},{13,5},{2,10},{6,14},... | collective-permute-start | bytes 196616 | tf_op jit(solution)/shard_map/ppermute | solution.py:188
  7.9 43.5 %collective-permute-start.1 = (bf16[2,2,384,256]{3,2,1,0:T(8,128)(2,1)S(1)}, bf16[2,2,384,256]{3,2,1,0:T(8,128)(2,1)S(1)}, u32[]{:S(2)}, u32[]{:S(2)}) collective-permute-start(bf16[2,2,384,256]{3,2,1,0:T(8,128)(2,1)S(1)} %pad_maximum_fusion), channel_id=1, source_target_pairs={{0,2},{1,3},{2,0},{3,1},{4,6},{5,7},{6,4},{7,5},{8,10},{9,11},{10,... | collective-permute-start | bytes 2359304 | tf_op jit(solution)/shard_map/ppermute | solution.py:203
  23.7 4.9 %copy-start.8 = (s32[512]{0:T(512)S(1)}, s32[512]{0:T(512)}, u32[]{:S(2)}) copy-start(s32[512]{0:T(512)} %param.18) | copy-start | bytes 6148
  44.4 16.9 %collective-permute-start.4 = (f16[128,1280]{1,0:T(8,128)(2,1)S(1)}, f16[128,1280]{1,0:T(8,128)(2,1)S(1)}, u32[]{:S(2)}, u32[]{:S(2)}) collective-permute-start(f16[128,1280]{1,0:T(8,128)(2,1)S(1)} %multiply_convert_fusion.4), channel_id=1, source_target_pairs={{0,4},{12,8},{1,5},{13,9},{2,6},{14,10},{3,7},{15,11},{16,20},{28,... | collective-permute-start | bytes 983048 | tf_op jit(solution)/shard_map/ppermute | solution.py:274
  61.3 14.3 %copy-start.7 = (bf16[1280]{0:T(1024)(128)(2,1)S(1)}, bf16[1280]{0:T(1024)(128)(2,1)}, u32[]{:S(2)}) copy-start(bf16[1280]{0:T(1024)(128)(2,1)} %param.13) | copy-start | bytes 7684
  61.5 26.5 %copy-start.5 = (f32[1280]{0:T(1024)S(1)}, f32[1280]{0:T(1024)}, u32[]{:S(2)}) copy-start(f32[1280]{0:T(1024)} %param.15) | copy-start | bytes 15364
  61.5 26.5 %copy-start.6 = (f32[1280]{0:T(1024)S(1)}, f32[1280]{0:T(1024)}, u32[]{:S(2)}) copy-start(f32[1280]{0:T(1024)} %param.14) | copy-start | bytes 15364
  61.5 10.3 %collective-permute-start.5 = (f16[128,1280]{1,0:T(8,128)(2,1)S(1)}, f16[128,1280]{1,0:T(8,128)(2,1)S(1)}, u32[]{:S(2)}, u32[]{:S(2)}) collective-permute-start(f16[128,1280]{1,0:T(8,128)(2,1)S(1)} %get-tuple-element.62), channel_id=1, source_target_pairs={{0,4},{12,8},{1,5},{13,9},{2,6},{14,10},{3,7},{15,11},{16,20},{28,... | collective-permute-start | bytes 983048 | tf_op jit(solution)/shard_map/ppermute | solution.py:275
  62.8 12.6 %collective-permute-start.7 = (f16[128,1280]{1,0:T(8,128)(2,1)S(1)}, f16[128,1280]{1,0:T(8,128)(2,1)S(1)}, u32[]{:S(2)}, u32[]{:S(2)}) collective-permute-start(f16[128,1280]{1,0:T(8,128)(2,1)S(1)} %get-tuple-element.35), channel_id=1, source_target_pairs={{4,8},{8,4},{5,9},{9,5},{6,10},{10,6},{7,11},{11,7},{20,24},{24,20... | collective-permute-start | bytes 983048 | tf_op jit(solution)/shard_map/ppermute | solution.py:196
  71.9 9.3 %collective-permute-start.6 = (f16[128,1280]{1,0:T(8,128)(2,1)S(1)}, f16[128,1280]{1,0:T(8,128)(2,1)S(1)}, u32[]{:S(2)}, u32[]{:S(2)}) collective-permute-start(f16[128,1280]{1,0:T(8,128)(2,1)S(1)} %multiply_convert_fusion.1), channel_id=1, source_target_pairs={{4,8},{8,4},{5,9},{9,5},{6,10},{10,6},{7,11},{11,7},{20,24},{24,20... | collective-permute-start | bytes 983048 | tf_op jit(solution)/shard_map/ppermute | solution.py:197
  75.5 23.3 %copy-start.1 = (bf16[1280,1536]{1,0:T(8,128)(2,1)S(1)}, bf16[1280,1536]{1,0:T(8,128)(2,1)}, u32[]{:S(2)}) copy-start(bf16[1280,1536]{1,0:T(8,128)(2,1)} %select_columns.2) | copy-start | bytes 11796484
  75.6 7.2 %collective-permute-start.8 = (f16[128,1280]{1,0:T(8,128)(2,1)S(1)}, f16[128,1280]{1,0:T(8,128)(2,1)S(1)}, u32[]{:S(2)}, u32[]{:S(2)}) collective-permute-start(f16[128,1280]{1,0:T(8,128)(2,1)S(1)} %multiply_convert_fusion), channel_id=1, source_target_pairs={{0,4},{4,0},{8,12},{12,8},{1,5},{5,1},{9,13},{13,9},{2,6},{6,2},{1... | collective-permute-start | bytes 983048 | tf_op jit(solution)/shard_map/ppermute | solution.py:198
  83.1 1.2 collective-permute-start.9
  84.3 3.6 %collective-permute-start.10 = (f32[2,128]{1,0:T(2,128)S(1)}, f32[2,128]{1,0:T(2,128)S(1)}, u32[]{:S(2)}, u32[]{:S(2)}) collective-permute-start(f32[2,128]{1,0:T(2,128)S(1)} %fusion.22), channel_id=1, source_target_pairs={{0,2},{1,3},{2,0},{3,1},{4,6},{5,7},{6,4},{7,5},{8,10},{9,11},{10,... | collective-permute-start | bytes 3080 | tf_op jit(solution)/shard_map/ppermute | solution.py:203
  85.9 19.6 %collective-permute-start.22 = (bf16[2,2,384,256]{3,2,1,0:T(8,128)(2,1)}, bf16[2,2,384,256]{3,2,1,0:T(8,128)(2,1)S(1)}, u32[]{:S(2)}, u32[]{:S(2)}) collective-permute-start(bf16[2,2,384,256]{3,2,1,0:T(8,128)(2,1)} %pad_maximum_fusion.1), channel_id=1, source_target_pairs={{0,1},{1,0},{2,3},{3,2},{4,5},{5,4},{6,7},{7,6},{8,9},{9,8},{10,11... | collective-permute-start | bytes 2359304 | tf_op jit(solution)/shard_map/ppermute | solution.py:203
  88.2 8.8 %collective-permute-start.11 = (bf16[128,1280]{1,0:T(8,128)(2,1)S(1)}, bf16[128,1280]{1,0:T(8,128)(2,1)}, u32[]{:S(2)}, u32[]{:S(2)}) collective-permute-start(bf16[128,1280]{1,0:T(8,128)(2,1)S(1)} %add_convert_fusion.1), channel_id=1, source_target_pairs={{0,4},{4,0},{8,12},{12,8},{1,5},{5,1},{9,13},{13,9},{2,6},{6,2},{1... | collective-permute-start | bytes 983048 | tf_op jit(solution)/shard_map/ppermute | solution.py:286
  88.5 10.3 %collective-permute-start.12 = (bf16[128,1280]{1,0:T(8,128)(2,1)S(1)}, bf16[128,1280]{1,0:T(8,128)(2,1)}, u32[]{:S(2)}, u32[]{:S(2)}) collective-permute-start(bf16[128,1280]{1,0:T(8,128)(2,1)S(1)} %add_convert_fusion.1), channel_id=1, source_target_pairs={{4,8},{8,4},{5,9},{9,5},{6,10},{10,6},{7,11},{11,7},{20,24},{24,20... | collective-permute-start | bytes 983048 | tf_op jit(solution)/shard_map/ppermute | solution.py:287
  98.0 7.4 %copy-start.4 = (bf16[256,1280]{1,0:T(8,128)(2,1)}, bf16[256,1280]{1,0:T(8,128)(2,1)S(1)}, u32[]{:S(2)}) copy-start(bf16[256,1280]{1,0:T(8,128)(2,1)S(1)} %pad_maximum_fusion.2) | copy-start | bytes 1966084
  101.0 16.9 %collective-permute-start.13 = (f16[256,1536]{1,0:T(8,128)(2,1)}, f16[256,1536]{1,0:T(8,128)(2,1)}, u32[]{:S(2)}, u32[]{:S(2)}) collective-permute-start(f16[256,1536]{1,0:T(8,128)(2,1)} %convolution_convert_fusion), channel_id=1, source_target_pairs={{0,1},{1,0},{2,3},{3,2},{4,5},{5,4},{6,7},{7,6},{8,9},{9,8},{10,11... | collective-permute-start | bytes 2359304 | tf_op jit(solution)/shard_map/ppermute | solution.py:203
  101.0 15.8 %collective-permute-start.14 = (bf16[128,1280]{1,0:T(8,128)(2,1)}, bf16[128,1280]{1,0:T(8,128)(2,1)}, u32[]{:S(2)}, u32[]{:S(2)}) collective-permute-start(bf16[128,1280]{1,0:T(8,128)(2,1)} %collective-permute-done.12), channel_id=1, source_target_pairs={{4,0},{8,12},{5,1},{9,13},{6,2},{10,14},{7,3},{11,15},{20,16},{24,... | collective-permute-start | bytes 983048 | tf_op jit(solution)/shard_map/ppermute | solution.py:289
  103.0 12.3 %collective-permute-start.15 = (bf16[128,1280]{1,0:T(8,128)(2,1)}, bf16[128,1280]{1,0:T(8,128)(2,1)}, u32[]{:S(2)}, u32[]{:S(2)}) collective-permute-start(bf16[128,1280]{1,0:T(8,128)(2,1)} %collective-permute-done.11), channel_id=1, source_target_pairs={{4,8},{8,4},{5,9},{9,5},{6,10},{10,6},{7,11},{11,7},{20,24},{24,20... | collective-permute-start | bytes 983048 | tf_op jit(solution)/shard_map/ppermute | solution.py:288
  115.3 8.7 %collective-permute-start.18 = (bf16[128,1280]{1,0:T(8,128)(2,1)}, bf16[128,1280]{1,0:T(8,128)(2,1)S(1)}, u32[]{:S(2)}, u32[]{:S(2)}) collective-permute-start(bf16[128,1280]{1,0:T(8,128)(2,1)} %collective-permute-done.15), channel_id=1, source_target_pairs={{4,0},{8,12},{5,1},{9,13},{6,2},{10,14},{7,3},{11,15},{20,16},{24,... | collective-permute-start | bytes 983048 | tf_op jit(solution)/shard_map/ppermute | solution.py:290
  117.8 3.9 %copy-start.2 = (bf16[1280,1536]{1,0:T(8,128)(2,1)S(1)}, bf16[1280,1536]{1,0:T(8,128)(2,1)}, u32[]{:S(2)}) copy-start(bf16[1280,1536]{1,0:T(8,128)(2,1)} %select_columns.2) | copy-start | bytes 11796484
  121.7 3.3 %copy-start = (bf16[1280,1536]{1,0:T(8,128)(2,1)S(1)}, bf16[1280,1536]{1,0:T(8,128)(2,1)}, u32[]{:S(2)}) copy-start(bf16[1280,1536]{1,0:T(8,128)(2,1)} %select_columns.3) | copy-start | bytes 11796484
  122.5 2.6 %collective-permute-start.17 = (f16[128,1536]{1,0:T(8,128)(2,1)S(1)}, f16[128,1536]{1,0:T(8,128)(2,1)S(1)}, u32[]{:S(2)}, u32[]{:S(2)}) collective-permute-start(f16[128,1536]{1,0:T(8,128)(2,1)S(1)} %convolution_convert_fusion.2), channel_id=1, source_target_pairs={{0,1},{1,0},{2,3},{3,2},{4,5},{5,4},{6,7},{7,6},{8,9},{9,8},{10,11... | collective-permute-start | bytes 1179656 | tf_op jit(solution)/shard_map/ppermute | solution.py:203
  122.6 12.0 %collective-permute-start.16 = (f16[256,768]{1,0:T(8,128)(2,1)S(1)}, f16[256,768]{1,0:T(8,128)(2,1)S(1)}, u32[]{:S(2)}, u32[]{:S(2)}) collective-permute-start(f16[256,768]{1,0:T(8,128)(2,1)S(1)} %slice_convert_fusion), channel_id=1, source_target_pairs={{0,2},{1,3},{2,0},{3,1},{4,6},{5,7},{6,4},{7,5},{8,10},{9,11},{10,... | collective-permute-start | bytes 1179656 | tf_op jit(solution)/shard_map/ppermute | solution.py:203
  126.5 8.2 %collective-permute-start.20 = (f16[128,1536]{1,0:T(8,128)(2,1)S(1)}, f16[128,1536]{1,0:T(8,128)(2,1)S(1)}, u32[]{:S(2)}, u32[]{:S(2)}) collective-permute-start(f16[128,1536]{1,0:T(8,128)(2,1)S(1)} %convolution_convert_fusion.1), channel_id=1, source_target_pairs={{0,1},{1,0},{2,3},{3,2},{4,5},{5,4},{6,7},{7,6},{8,9},{9,8},{10,11... | collective-permute-start | bytes 1179656 | tf_op jit(solution)/shard_map/ppermute | solution.py:203
  126.5 12.2 %collective-permute-start.19 = (f16[128,768]{1,0:T(8,128)(2,1)S(1)}, f16[128,768]{1,0:T(8,128)(2,1)S(1)}, u32[]{:S(2)}, u32[]{:S(2)}) collective-permute-start(f16[128,768]{1,0:T(8,128)(2,1)S(1)} %slice_convert_fusion.2), channel_id=1, source_target_pairs={{0,2},{1,3},{2,0},{3,1},{4,6},{5,7},{6,4},{7,5},{8,10},{9,11},{10,... | collective-permute-start | bytes 589832 | tf_op jit(solution)/shard_map/ppermute | solution.py:203
  135.4 7.1 %collective-permute-start.21 = (f16[128,768]{1,0:T(8,128)(2,1)S(1)}, f16[128,768]{1,0:T(8,128)(2,1)S(1)}, u32[]{:S(2)}, u32[]{:S(2)}) collective-permute-start(f16[128,768]{1,0:T(8,128)(2,1)S(1)} %slice_convert_fusion.1), channel_id=1, source_target_pairs={{0,2},{1,3},{2,0},{3,1},{4,6},{5,7},{6,4},{7,5},{8,10},{9,11},{10,... | collective-permute-start | bytes 589832 | tf_op jit(solution)/shard_map/ppermute | solution.py:203
  145.0 5.0 %collective-permute-start.24 = (bf16[256,256]{1,0:T(8,128)(2,1)S(1)}, bf16[256,256]{1,0:T(8,128)(2,1)S(1)}, u32[]{:S(2)}, u32[]{:S(2)}) collective-permute-start(bf16[256,256]{1,0:T(8,128)(2,1)S(1)} %attend.2), channel_id=1, source_target_pairs={{0,2},{1,3},{2,0},{3,1},{4,6},{5,7},{6,4},{7,5},{8,10},{9,11},{10,... | collective-permute-start | bytes 393224 | tf_op jit(solution)/shard_map/ppermute | solution.py:203
  150.0 8.5 %collective-permute-start.25 = (bf16[256,512]{1,0:T(8,128)(2,1)S(1)}, bf16[256,512]{1,0:T(8,128)(2,1)S(1)}, u32[]{:S(2)}, u32[]{:S(2)}) collective-permute-start(bf16[256,512]{1,0:T(8,128)(2,1)S(1)} %pad_maximum_fusion.4), channel_id=1, source_target_pairs={{0,1},{1,0},{2,3},{3,2},{4,5},{5,4},{6,7},{7,6},{8,9},{9,8},{10,11... | collective-permute-start | bytes 786440 | tf_op jit(solution)/shard_map/ppermute | solution.py:203
  152.5 11.4 %copy-start.3 = (bf16[1024,1280]{1,0:T(8,128)(2,1)S(1)}, bf16[1024,1280]{1,0:T(8,128)(2,1)}, u32[]{:S(2)}) copy-start(bf16[1024,1280]{1,0:T(8,128)(2,1)} %select_rows.1) | copy-start | bytes 7864324
  152.6 6.0 %collective-permute-start.23 = (bf16[256,256]{1,0:T(8,128)(2,1)S(1)}, bf16[256,256]{1,0:T(8,128)(2,1)S(1)}, u32[]{:S(2)}, u32[]{:S(2)}) collective-permute-start(bf16[256,256]{1,0:T(8,128)(2,1)S(1)} %attend.3), channel_id=1, source_target_pairs={{0,2},{1,3},{2,0},{3,1},{4,6},{5,7},{6,4},{7,5},{8,10},{9,11},{10,... | collective-permute-start | bytes 393224 | tf_op jit(solution)/shard_map/ppermute | solution.py:203
  161.2 2.7 %collective-permute-start.26 = (bf16[256,512]{1,0:T(8,128)(2,1)S(1)}, bf16[256,512]{1,0:T(8,128)(2,1)S(1)}, u32[]{:S(2)}, u32[]{:S(2)}) collective-permute-start(bf16[256,512]{1,0:T(8,128)(2,1)S(1)} %pad_maximum_fusion.3), channel_id=1, source_target_pairs={{0,1},{1,0},{2,3},{3,2},{4,5},{5,4},{6,7},{7,6},{8,9},{9,8},{10,11... | collective-permute-start | bytes 786440 | tf_op jit(solution)/shard_map/ppermute | solution.py:203
  161.3 12.4 %collective-permute-start.27 = (bf16[128,1280]{1,0:T(8,128)(2,1)S(1)}, bf16[128,1280]{1,0:T(8,128)(2,1)S(1)}, u32[]{:S(2)}, u32[]{:S(2)}) collective-permute-start(bf16[128,1280]{1,0:T(8,128)(2,1)S(1)} %get-tuple-element.70), channel_id=1, source_target_pairs={{0,4},{12,8},{1,5},{13,9},{2,6},{14,10},{3,7},{15,11},{16,20},{28,... | collective-permute-start | bytes 983048 | tf_op jit(solution)/shard_map/ppermute | solution.py:326
  162.6 17.7 %collective-permute-start.28 = (bf16[128,1280]{1,0:T(8,128)(2,1)S(1)}, bf16[128,1280]{1,0:T(8,128)(2,1)S(1)}, u32[]{:S(2)}, u32[]{:S(2)}) collective-permute-start(bf16[128,1280]{1,0:T(8,128)(2,1)S(1)} %get-tuple-element.69), channel_id=1, source_target_pairs={{0,4},{12,8},{1,5},{13,9},{2,6},{14,10},{3,7},{15,11},{16,20},{28,... | collective-permute-start | bytes 983048 | tf_op jit(solution)/shard_map/ppermute | solution.py:327
  173.8 10.8 %collective-permute-start.30 = (bf16[128,1280]{1,0:T(8,128)(2,1)S(1)}, bf16[128,1280]{1,0:T(8,128)(2,1)S(1)}, u32[]{:S(2)}, u32[]{:S(2)}) collective-permute-start(bf16[128,1280]{1,0:T(8,128)(2,1)S(1)} %get-tuple-element.52), channel_id=1, source_target_pairs={{4,8},{8,4},{5,9},{9,5},{6,10},{10,6},{7,11},{11,7},{20,24},{24,20... | collective-permute-start | bytes 983048 | tf_op jit(solution)/shard_map/ppermute | solution.py:196
  180.4 11.2 %collective-permute-start.29 = (bf16[128,1280]{1,0:T(8,128)(2,1)S(1)}, bf16[128,1280]{1,0:T(8,128)(2,1)S(1)}, u32[]{:S(2)}, u32[]{:S(2)}) collective-permute-start(bf16[128,1280]{1,0:T(8,128)(2,1)S(1)} %add_convert_fusion), channel_id=1, source_target_pairs={{4,8},{8,4},{5,9},{9,5},{6,10},{10,6},{7,11},{11,7},{20,24},{24,20... | collective-permute-start | bytes 983048 | tf_op jit(solution)/shard_map/ppermute | solution.py:197
  184.7 8.1 %collective-permute-start.31 = (bf16[128,1280]{1,0:T(8,128)(2,1)S(1)}, bf16[128,1280]{1,0:T(8,128)(2,1)S(1)}, u32[]{:S(2)}, u32[]{:S(2)}) collective-permute-start(bf16[128,1280]{1,0:T(8,128)(2,1)S(1)} %fusion.1), channel_id=1, source_target_pairs={{0,4},{4,0},{8,12},{12,8},{1,5},{5,1},{9,13},{13,9},{2,6},{6,2},{1... | collective-permute-start | bytes 983048 | tf_op jit(solution)/shard_map/ppermute | solution.py:198

commit v4 on v3

--- a/solution.py
+++ b/solution.py
@@ -12,7 +12,6 @@
 HEAD = 128
 GROUP = 8
 VMEM_BYTES = 20 * 1024 * 1024
-STREAM_BYTES = 56 * 1024 * 1024
 
 
 def densify_kernel(base_ref, *refs, topk, latents, lanes):
@@ -90,7 +89,7 @@
             in_specs=[pl.BlockSpec((1, depth, width), lambda j, t, order: (t, 0, order[j]))],
             out_specs=pl.BlockSpec((depth, width), lambda j, t, order: (0, j * kinds + t)),
         ),
-        compiler_params=pltpu.CompilerParams(vmem_limit_bytes=STREAM_BYTES),
+        compiler_params=pltpu.CompilerParams(vmem_limit_bytes=VMEM_BYTES),
         cost_estimate=pl.CostEstimate(
             flops=0, bytes_accessed=4 * depth * count * kinds * width, transcendentals=0
         ),
@@ -109,7 +108,7 @@
             in_specs=[pl.BlockSpec((height, columns), lambda j, order: (order[j], 0))],
             out_specs=pl.BlockSpec((height, columns), lambda j, order: (j, 0)),
         ),
-        compiler_params=pltpu.CompilerParams(vmem_limit_bytes=STREAM_BYTES),
+        compiler_params=pltpu.CompilerParams(vmem_limit_bytes=VMEM_BYTES),
         cost_estimate=pl.CostEstimate(
             flops=0, bytes_accessed=4 * count * height * columns, transcendentals=0
         ),
@@ -190,15 +189,6 @@
     return [own, near, jnp.where(outer, two, three), jnp.where(outer, three, two)]
 
 
-def line_end(parts, in_far, in_across, encode, decode_sent):
-    far = encode(parts[3] + decode_sent(in_far))
-    second, far = lax.optimization_barrier((parts[2], far))
-    far = lax.ppermute(far, "lat", MIDDLE)
-    across = lax.ppermute(encode(second + decode_sent(in_across)), "lat", MIDDLE)
-    near = lax.ppermute(encode(parts[1] + decode_sent(far)), "lat", PAIRS)
-    return parts[0] + decode_sent(across) + decode_sent(near)
-
-
 def swap(value, distance, size):
     return lax.ppermute(value, "col", [(i, i ^ distance) for i in range(size)])
 
@@ -253,30 +243,36 @@
 
     across = swap(jnp.stack([cache_of(2), cache_of(3)]), 2, cols)
 
-    weights = w_qkv.transpose(1, 0, 2)
-    away_weights = select_columns(weights, jnp.stack([col ^ 1, col ^ 3]), own_width)
-    keep_weights = select_columns(weights, jnp.stack([col, col ^ 2]), own_width)
-    out_weights = select_rows(w_out, jnp.stack([col, col ^ 2, col ^ 1, col ^ 3]), own_width)
     key_pos = jnp.concatenate(
         [lax.dynamic_slice_in_dim(positions, s * rows, rows, 0) for s in slots]
     )
     query_pos = key_pos.reshape(-1, 1)
 
-    near_packed, away_weights, keep_weights, out_weights = hold(
-        (packed[:2], away_weights, keep_weights, out_weights)
+    codes_far = densify([packed[3], packed[2]], base, topk, latents)
+    far = jnp.dot(codes_far, decoder, preferred_element_type=jnp.float32)
+    in_far = lax.ppermute(to_half(far[:rows]), "lat", INWARD)
+    near_packed, far = hold(((packed[1], packed[0]), far))
+    codes_near = densify(near_packed, base, topk, latents)
+    codes_near, in_far = hold((codes_near, in_far))
+    mid_far = to_half(far[:rows] + from_half(in_far))
+    second, codes_near, across, query_pos, mid_far = hold(
+        (far[rows:], codes_near, across, query_pos, mid_far)
     )
-    codes_far = densify([packed[3], packed[2]], base, topk, latents)
-    codes_near = densify([near_packed[1], near_packed[0]], base, topk, latents)
-    far = jnp.dot(codes_far, decoder, preferred_element_type=jnp.float32)
-    codes_near, across, query_pos = hold((codes_near, across, query_pos))
+    mid_far = lax.ppermute(mid_far, "lat", MIDDLE)
+    in_across = lax.ppermute(to_half(second), "lat", INWARD)
+    near = jnp.dot(codes_near, decoder, preferred_element_type=jnp.float32)
+    near, mid_far = hold((near, mid_far))
+    last = to_half(near[:rows] + from_half(mid_far))
+    across, last, second, weights = hold((across, last, second, w_qkv.transpose(1, 0, 2)))
+    last = lax.ppermute(last, "lat", PAIRS)
+    mid_across = lax.ppermute(to_half(second + from_half(in_across)), "lat", MIDDLE)
+
+    away_weights = select_columns(weights, jnp.stack([col ^ 1, col ^ 3]), own_width)
+    keep_weights = select_columns(weights, jnp.stack([col, col ^ 2]), own_width)
     beside = swap(jnp.stack([cache_of(1), across[1]]), 1, cols)
+    last, away_weights, keep_weights, beside = hold((last, away_weights, keep_weights, beside))
     cached = [cache_of(0), across[0], beside[0], beside[1]]
-    in_far = lax.ppermute(to_half(far[:rows]), "lat", INWARD)
-    in_across = lax.ppermute(to_half(far[rows:]), "lat", INWARD)
-    near = jnp.dot(codes_near, decoder, preferred_element_type=jnp.float32)
-    near, in_far = hold((near, in_far))
-    parts = [near[rows:], near[:rows], far[rows:], far[:rows]]
-    residual = line_end(parts, in_far, in_across, to_half, from_half)
+    residual = near[rows:] + from_half(mid_across) + from_half(last)
     residual = residual + dec_bias.astype(jnp.float32)
 
     sums = jnp.stack([jnp.sum(residual, axis=1), jnp.sum(residual * residual, axis=1)])
@@ -300,14 +296,24 @@
     def finish(keep, payload):
         return (keep + swap(payload, 2, cols).astype(jnp.float32)).astype(jnp.bfloat16)
 
-    pair, across = hold((jnp.concatenate([own, near], axis=0), across))
-    keep0, payload0 = project(pair)
-    third, far, payload0 = hold((jnp.where(outer, across_out, across), far, payload0))
+    keep0, payload0 = project(own)
+    near_block, across, payload0 = hold((near, across, payload0))
+    keep1, payload1 = project(near_block)
+    third, far, payload1, out_source = hold(
+        (jnp.where(outer, across_out, across), far, payload1, w_out)
+    )
+    out_weights = select_rows(
+        out_source, jnp.stack([col, col ^ 2, col ^ 1, col ^ 3]), own_width
+    )
     keep2, payload2 = project(third)
-    fourth, payload2 = hold((jnp.where(outer, far_out, far), payload2))
+    fourth, payload2, out_weights = hold((jnp.where(outer, far_out, far), payload2, out_weights))
     keep3, payload3 = project(fourth)
-    first = finish(keep0, payload0)
-    qkv = [first[:rows], first[rows:], finish(keep2, payload2), finish(keep3, payload3)]
+    qkv = [
+        finish(keep0, payload0),
+        finish(keep1, payload1),
+        finish(keep2, payload2),
+        finish(keep3, payload3),
+    ]
 
     key_row = key_pos.reshape(1, -1)
 
@@ -319,25 +325,26 @@
     mixed_far = attend(pos_of(3, 2), key_row, qkv, cached, (3, 2), heads)
     near_pos, mixed_far = hold((pos_of(1, 0), mixed_far))
     mixed_near = attend(near_pos, key_row, qkv, cached, (1, 0), heads)
-    mixed_far = jnp.concatenate([mixed_far, swap(mixed_far, 2, cols)], axis=1)
+    swapped_far, mixed_near = hold((swap(mixed_far, 2, cols), mixed_near))
+    mixed_far = jnp.concatenate([mixed_far, swapped_far], axis=1)
     mixed_far = jnp.concatenate([mixed_far, swap(mixed_far, 1, cols)], axis=1)
     product_far = jnp.dot(mixed_far, out_weights, preferred_element_type=jnp.float32)
-    sent_far = product_far.astype(jnp.bfloat16)
-    in_far = lax.ppermute(sent_far[:rows], "lat", INWARD)
-    in_across = lax.ppermute(sent_far[rows:], "lat", INWARD)
+    sent_far, mixed_near = hold((product_far[:rows].astype(jnp.bfloat16), mixed_near))
+    in_far = lax.ppermute(sent_far, "lat", INWARD)
     mixed_near = jnp.concatenate([mixed_near, swap(mixed_near, 2, cols)], axis=1)
-    mixed_near, sent_far = hold((mixed_near, sent_far))
     mixed_near = jnp.concatenate([mixed_near, swap(mixed_near, 1, cols)], axis=1)
     product_near = jnp.dot(mixed_near, out_weights, preferred_element_type=jnp.float32)
-    branch = [product_near[rows:], product_near[:rows], product_far[rows:], product_far[:rows]]
-    added = line_end(
-        branch,
-        in_far,
-        in_across,
-        lambda v: v.astype(jnp.bfloat16),
-        lambda v: v.astype(jnp.float32),
-    )
-    return (residual + added).astype(jnp.bfloat16)
+    mid_far = (product_far[:rows] + in_far.astype(jnp.float32)).astype(jnp.bfloat16)
+    second, mid_far = hold((product_far[rows:], mid_far))
+    mid_far = lax.ppermute(mid_far, "lat", MIDDLE)
+    in_across = lax.ppermute(second.astype(jnp.bfloat16), "lat", INWARD)
+    last = (product_near[:rows] + mid_far.astype(jnp.float32)).astype(jnp.bfloat16)
+    second, last = hold((second, last))
+    last = lax.ppermute(last, "lat", PAIRS)
+    mid_across = (second + in_across.astype(jnp.float32)).astype(jnp.bfloat16)
+    mid_across = lax.ppermute(mid_across, "lat", MIDDLE)
+    branch = product_near[rows:] + mid_across.astype(jnp.float32) + last.astype(jnp.float32)
+    return (residual + branch).astype(jnp.bfloat16)
 
 
 def attend_block(queries, keys, values, query_pos, key_pos):

time: 196 us -> 177 us (0.903)
  Pallas kernels: 34.1 us -> 20.6 us
  waiting for transfers between devices: 77.4 us -> 69.3 us
  starting transfers between devices: 37.7 us -> 42.7 us
  other arithmetic: 9.4 us -> 5.34 us
    pallas_call x2, Pallas kernels: 13 us -> 3.56 us  [select_columns(): pl.pallas_call(copy_kernel, out_shape=jax.ShapeDtypeStruct((depth, count...]
    ppermute x1, waiting for transfers between devices: 0.89 us -> 9.36 us  [line_body(): across = lax.ppermute(own, 'lat', MIDDLE)]
    ppermute x14 -> x16, waiting for transfers between devices: 24.8 us -> 17.6 us  [swap(): return lax.ppermute(value, 'col', [(i, i ^ distance) for i in range(size)])]
    ppermute x1, waiting for transfers between devices: 9.72 us -> 3.5 us  [line_body(): far = lax.ppermute(near, 'lat', MIDDLE)]
    ppermute x1, waiting for transfers between devices: 6.07 us -> 0.01 us  [line_body(): near = lax.ppermute(own, 'lat', PAIRS)]
    ppermute x14 -> x16, starting transfers between devices: 7.82 us -> 12.7 us  [swap(): return lax.ppermute(value, 'col', [(i, i ^ distance) for i in range(size)])]
    pallas_call x1, Pallas kernels: 4.87 us -> 0.79 us  [select_rows(): pl.pallas_call(copy_kernel, out_shape=jax.ShapeDtypeStruct((count * heigh...]
    ppermute x1, waiting for transfers between devices: 0.01 us -> 3.84 us  [line_body(): in_far = lax.ppermute(to_half(far[:rows]), 'lat', INWARD)]
  transfers between devices with their start and end apart: 32 -> 34, of which waited for: 19 -> 20; matrix products, arithmetic and copies ran while one was open for 19% -> 13% of each run, Pallas kernels for 16% -> 10%
where the time goes in v4:
time: 177 us; the launch traced here: 175 us
  waiting for transfers between devices  69.3 us (39%)
  starting transfers between devices  42.7 us (24%)
  matrix products  31.8 us (18%)
  Pallas kernels  20.6 us (12%)
  other arithmetic  5.34 us (3%)
  local copies, waits for them, and re-layouts  4.26 us (2%)
    ppermute x16, waiting for transfers between devices, swap(): return lax.ppermute(value, 'col', [(i, i ^ distance) for i in range(size)])  17.6 us
    ppermute x16, starting transfers between devices, swap(): return lax.ppermute(value, 'col', [(i, i ^ distance) for i in range(size)])  12.7 us
    ppermute x2, waiting for transfers between devices, line_body(): mid_far = lax.ppermute(mid_far, 'lat', MIDDLE)  11.6 us
    pallas_call x2, Pallas kernels, densify(): pl.pallas_call(functools.partial(densify_kernel, topk=topk, latents=laten...  11.4 us
    dot_general x1, matrix products, line_body(): near = jnp.dot(codes_near, decoder, preferred_element_type=jnp.float32)  10 us
    dot_general x1, matrix products, line_body(): far = jnp.dot(codes_far, decoder, preferred_element_type=jnp.float32)  9.9 us
    ppermute x1, waiting for transfers between devices, line_body(): across = lax.ppermute(own, 'lat', MIDDLE)  9.36 us
    ppermute x2, starting transfers between devices, line_body(): mid_far = lax.ppermute(mid_far, 'lat', MIDDLE)  6.89 us
  transfers between devices with their start and end apart: 34, of which 20 were waited for; matrix products, arithmetic and copies ran while one was open for 13% of the time, Pallas kernels for 10%

profile of v4, /device:TPU:8, one launch (start us, length us, event | category | flops | bytes accessed | tf_op | source)
XLA Modules:
  0.0 174.8 jit_solution(13643745926942315559)
XLA Ops:
  1.9 2.6 %collective-permute-start.2 = (f32[16,1024]{1,0:T(8,128)S(1)}, f32[16,1024]{1,0:T(8,128)S(1)}, u32[]{:S(2)}, u32[]{:S(2)}) collective-permute-start(f32[16,1024]{1,0:T(8,128)S(1)} %constant_dynamic-update-slice_fusion.refs_1_), channel_id=1, source_target_pairs={{0,8},{4,12},{8,0},{12,4},{1,9},{5,13},{9,1},{13,5},{2,10},{6,14},... | collective-permute-start | bytes 196616 | tf_op jit(solution)/shard_map/ppermute | solution.py:187
  4.5 1.8 %collective-permute-start = (f32[16,1024]{1,0:T(8,128)S(1)}, f32[16,1024]{1,0:T(8,128)S(1)}, u32[]{:S(2)}, u32[]{:S(2)}) collective-permute-start(f32[16,1024]{1,0:T(8,128)S(1)} %constant_dynamic-update-slice_fusion.refs_1_), channel_id=1, source_target_pairs={{0,4},{4,0},{8,12},{12,8},{1,5},{5,1},{9,13},{13,9},{2,6},{6,2},{1... | collective-permute-start | bytes 196616 | tf_op jit(solution)/shard_map/ppermute | solution.py:186
  6.3 1.5 constant_dynamic-slice_fusion
  8.8 1.5 collective-permute-start.4
  10.3 5.7 %densify.2 = bf16[256,8192]{1,0:T(8,128)(2,1)S(1)} custom-call(s32[1]{0:T(128)} %bitcast.base_ref, f32[16,1024]{1,0:T(8,128)S(1)} %get-tuple-element.101.refs_0_, f32[16,1024]{1,0:T(8,128)S(1)} %get-tuple-element.100.refs_1_), custom_call_target="tpu_custom_call" | custom-call | flops 2147483648 | bytes 4194304 | tf_op jit(solution)/shard_map/densify/pallas_call | solution.py:62
  16.0 9.9 %fusion.29 = f32[256,1280]{1,0:T(8,128)S(1)} fusion(bf16[256,8192]{1,0:T(8,128)(2,1)S(1)} %densify.2, bf16[8192,1280]{1,0:T(8,128)(2,1)} %param.12), kind=kOutput, calls=%fused_computation.85 | convolution fusion | flops 5368709120 | bytes 26476544 | tf_op jit(solution)/shard_map/dot_general | solution.py:252
  26.0 1.3 collective-permute-start.3
  27.4 5.7 %densify.3 = bf16[256,8192]{1,0:T(8,128)(2,1)S(1)} custom-call(s32[1]{0:T(128)} %bitcast.base_ref, f32[16,1024]{1,0:T(8,128)S(1)} %collective-permute-done.refs_0_, f32[16,1024]{1,0:T(8,128)S(1)} %constant_dynamic-update-slice_fusion.refs_1_), custom_call_target="tpu_custom_call" | custom-call | flops 2147483648 | bytes 4194304 | tf_op jit(solution)/shard_map/densify/pallas_call | solution.py:62
  33.1 3.8 %collective-permute-done.3 = f16[128,1280]{1,0:T(8,128)(2,1)S(1)} collective-permute-done((f16[128,1280]{1,0:T(8,128)(2,1)S(1)}, f16[128,1280]{1,0:T(8,128)(2,1)S(1)}, u32[]{:S(2)}, u32[]{:S(2)}) %collective-permute-start.3) | collective-permute-done | bytes 327712 | tf_op jit(solution)/shard_map/ppermute | solution.py:253
  37.2 10.0 %fusion.30 = f32[256,1280]{1,0:T(8,128)S(1)} fusion(bf16[256,8192]{1,0:T(8,128)(2,1)S(1)} %densify.3, bf16[8192,1280]{1,0:T(8,128)(2,1)} %param.12), kind=kOutput, calls=%fused_computation.86 | convolution fusion | flops 5368709120 | bytes 26476544 | tf_op jit(solution)/shard_map/dot_general | solution.py:263
  47.2 4.4 %collective-permute-start.5 = (f16[128,1280]{1,0:T(8,128)(2,1)S(1)}, f16[128,1280]{1,0:T(8,128)(2,1)S(1)}, u32[]{:S(2)}, u32[]{:S(2)}) collective-permute-start(f16[128,1280]{1,0:T(8,128)(2,1)S(1)} %get-tuple-element.51), channel_id=1, source_target_pairs={{4,8},{8,4},{5,9},{9,5},{6,10},{10,6},{7,11},{11,7},{20,24},{24,20... | collective-permute-start | bytes 983048 | tf_op jit(solution)/shard_map/ppermute | solution.py:261
  53.0 5.3 %collective-permute-done.5 = f16[128,1280]{1,0:T(8,128)(2,1)S(1)} collective-permute-done((f16[128,1280]{1,0:T(8,128)(2,1)S(1)}, f16[128,1280]{1,0:T(8,128)(2,1)S(1)}, u32[]{:S(2)}, u32[]{:S(2)}) %collective-permute-start.5) | collective-permute-done | bytes 327712 | tf_op jit(solution)/shard_map/ppermute | solution.py:261
  58.8 5.4 %collective-permute-done.6 = f16[128,1280]{1,0:T(8,128)(2,1)S(1)} collective-permute-done((f16[128,1280]{1,0:T(8,128)(2,1)S(1)}, f16[128,1280]{1,0:T(8,128)(2,1)S(1)}, u32[]{:S(2)}, u32[]{:S(2)}) %collective-permute-start.6) | collective-permute-done | bytes 327712 | tf_op jit(solution)/shard_map/ppermute | solution.py:262
  64.3 1.9 %collective-permute-start.7 = (f16[128,1280]{1,0:T(8,128)(2,1)S(1)}, f16[128,1280]{1,0:T(8,128)(2,1)S(1)}, u32[]{:S(2)}, u32[]{:S(2)}) collective-permute-start(f16[128,1280]{1,0:T(8,128)(2,1)S(1)} %multiply_convert_fusion), channel_id=1, source_target_pairs={{4,8},{8,4},{5,9},{9,5},{6,10},{10,6},{7,11},{11,7},{20,24},{24,20... | collective-permute-start | bytes 983048 | tf_op jit(solution)/shard_map/ppermute | solution.py:268
  66.3 1.8 %select_columns.3 = bf16[1280,1536]{1,0:T(8,128)(2,1)S(1)} custom-call(s32[2]{0:T(128)S(1)} %get-tuple-element.111.order_ref, bf16[3,1280,1024]{2,1,0:T(8,128)(2,1)S(1)} %bitcast.56), custom_call_target="tpu_custom_call" | custom-call | bytes 7864320 | tf_op jit(solution)/shard_map/select_columns/pallas_call | solution.py:83
  68.1 1.9 %copy-done = bf16[1280,1536]{1,0:T(8,128)(2,1)} copy-done((bf16[1280,1536]{1,0:T(8,128)(2,1)}, bf16[1280,1536]{1,0:T(8,128)(2,1)S(1)}, u32[]{:S(2)}) %copy-start) | copy-done | bytes 3932184
  70.0 1.8 %select_columns.2 = bf16[1280,1536]{1,0:T(8,128)(2,1)S(1)} custom-call(s32[2]{0:T(128)S(1)} %get-tuple-element.110.order_ref, bf16[3,1280,1024]{2,1,0:T(8,128)(2,1)S(1)} %bitcast.57), custom_call_target="tpu_custom_call" | custom-call | bytes 7864320 | tf_op jit(solution)/shard_map/select_columns/pallas_call | solution.py:83
  71.8 1.4 collective-permute-done.7
  74.8 1.5 collective-permute-start.11
  76.3 2.1 %collective-permute-done.11 = f32[2,128]{1,0:T(2,128)S(1)} collective-permute-done((f32[2,128]{1,0:T(2,128)S(1)}, f32[2,128]{1,0:T(2,128)S(1)}, u32[]{:S(2)}, u32[]{:S(2)}) %collective-permute-start.11) | collective-permute-done | bytes 1056 | tf_op jit(solution)/shard_map/ppermute | solution.py:193
  78.7 1.5 convolution_convert_fusion.3
  80.3 2.8 %collective-permute-start.14 = (bf16[128,1280]{1,0:T(8,128)(2,1)S(1)}, bf16[128,1280]{1,0:T(8,128)(2,1)S(1)}, u32[]{:S(2)}, u32[]{:S(2)}) collective-permute-start(bf16[128,1280]{1,0:T(8,128)(2,1)S(1)} %add_convert_fusion.2), channel_id=1, source_target_pairs={{4,8},{8,4},{5,9},{9,5},{6,10},{10,6},{7,11},{11,7},{20,24},{24,20... | collective-permute-start | bytes 983048 | tf_op jit(solution)/shard_map/ppermute | solution.py:283
  83.2 9.4 %collective-permute-done.14 = bf16[128,1280]{1,0:T(8,128)(2,1)S(1)} collective-permute-done((bf16[128,1280]{1,0:T(8,128)(2,1)S(1)}, bf16[128,1280]{1,0:T(8,128)(2,1)S(1)}, u32[]{:S(2)}, u32[]{:S(2)}) %collective-permute-start.14) | collective-permute-done | bytes 327712 | tf_op jit(solution)/shard_map/ppermute | solution.py:283
  92.6 1.3 collective-permute-start.17
  93.9 2.5 %collective-permute-start.18 = (bf16[128,1280]{1,0:T(8,128)(2,1)S(1)}, bf16[128,1280]{1,0:T(8,128)(2,1)S(1)}, u32[]{:S(2)}, u32[]{:S(2)}) collective-permute-start(bf16[128,1280]{1,0:T(8,128)(2,1)S(1)} %collective-permute-done.13), channel_id=1, source_target_pairs={{4,8},{8,4},{5,9},{9,5},{6,10},{10,6},{7,11},{11,7},{20,24},{24,20... | collective-permute-start | bytes 983048 | tf_op jit(solution)/shard_map/ppermute | solution.py:284
  96.4 2.9 %convolution_add_fusion.3 = f32[128,1536]{1,0:T(8,128)S(1)} fusion(bf16[128,1280]{1,0:T(8,128)(2,1)S(1)} %add_convert_fusion.2, bf16[1280,1536]{1,0:T(8,128)(2,1)} %copy-done, f16[128,1536]{1,0:T(8,128)(2,1)} %collective-permute-done.12), kind=kOutput, calls=%fused_computation.3 | convolution fusion | flops 503709696 | bytes 5439488 | tf_op jit(solution)/shard_map/dot_general | solution.py:292
  99.3 1.5 collective-permute-start.15
  101.6 3.5 %collective-permute-done.18 = bf16[128,1280]{1,0:T(8,128)(2,1)S(1)} collective-permute-done((bf16[128,1280]{1,0:T(8,128)(2,1)S(1)}, bf16[128,1280]{1,0:T(8,128)(2,1)S(1)}, u32[]{:S(2)}, u32[]{:S(2)}) %collective-permute-start.18) | collective-permute-done | bytes 327712 | tf_op jit(solution)/shard_map/ppermute | solution.py:284
  105.1 1.5 collective-permute-start.21
  107.4 1.5 collective-permute-start.19
  110.5 2.1 %collective-permute-done.21 = bf16[128,1280]{1,0:T(8,128)(2,1)S(1)} collective-permute-done((bf16[128,1280]{1,0:T(8,128)(2,1)S(1)}, bf16[128,1280]{1,0:T(8,128)(2,1)S(1)}, u32[]{:S(2)}, u32[]{:S(2)}) %collective-permute-start.21) | collective-permute-done | bytes 327712 | tf_op jit(solution)/shard_map/ppermute | solution.py:286
  114.3 1.5 collective-permute-start.22
  116.6 1.5 collective-permute-start.24
  118.2 3.9 %collective-permute-done.22 = f16[128,768]{1,0:T(8,128)(2,1)S(1)} collective-permute-done((f16[128,768]{1,0:T(8,128)(2,1)S(1)}, f16[128,768]{1,0:T(8,128)(2,1)S(1)}, u32[]{:S(2)}, u32[]{:S(2)}) %collective-permute-start.22) | collective-permute-done | bytes 196640 | tf_op jit(solution)/shard_map/ppermute | solution.py:193
  122.1 3.7 %collective-permute-done.24 = f16[128,768]{1,0:T(8,128)(2,1)S(1)} collective-permute-done((f16[128,768]{1,0:T(8,128)(2,1)S(1)}, f16[128,768]{1,0:T(8,128)(2,1)S(1)}, u32[]{:S(2)}, u32[]{:S(2)}) %collective-permute-start.24) | collective-permute-done | bytes 196640 | tf_op jit(solution)/shard_map/ppermute | solution.py:193
  125.9 2.4 %attend.2 = bf16[256,256]{1,0:T(8,128)(2,1)S(1)} custom-call(s32[256,1]{1,0:T(8,128)S(1)} %copy.21.refs_0_, s32[1,512]{1,0:T(1,128)S(1)} %bitcast.59, bf16[128,768]{1,0:T(8,128)(2,1)S(1)} %fusion.20.refs_2_, bf16[128,768]{1,0:T(8,128)(2,1)S(1)} %fusion.19.refs_3_, bf16[128,768]{1,0:T(8,128)(2,1)S(1)} %fusion.18.refs_4_, ...), custom_call_target="tpu_custom_call" | custom-call | flops 536870912 | bytes 2097152 | tf_op jit(solution)/shard_map/attend/pallas_call | solution.py:159
  128.3 1.5 collective-permute-start.25
  130.0 2.4 %attend.3 = bf16[256,256]{1,0:T(8,128)(2,1)S(1)} custom-call(s32[256,1]{1,0:T(8,128)S(1)} %copy.22.refs_0_, s32[1,512]{1,0:T(1,128)S(1)} %bitcast.60, bf16[128,768]{1,0:T(8,128)(2,1)S(1)} %fusion.20.refs_2_, bf16[128,768]{1,0:T(8,128)(2,1)S(1)} %fusion.19.refs_3_, bf16[128,768]{1,0:T(8,128)(2,1)S(1)} %fusion.18.refs_4_, ...), custom_call_target="tpu_custom_call" | custom-call | flops 536870912 | bytes 2097152 | tf_op jit(solution)/shard_map/attend/pallas_call | solution.py:159
  133.6 1.5 collective-permute-done.26
  135.2 2.6 %fusion.5 = f32[256,1280]{1,0:T(8,128)S(1)} fusion(bf16[1024,1280]{1,0:T(8,128)(2,1)} %copy-done.5, bf16[256,512]{1,0:T(8,128)(2,1)S(1)} %collective-permute-done.26, bf16[256,256]{1,0:T(8,128)(2,1)S(1)} %collective-permute-done.25, bf16[256,256]{1,0:T(8,128)(2,1)S(1)} %attend.2), kind=kOutput, calls=%fused_computation.28 | convolution fusion | flops 672661504 | bytes 4456448 | tf_op jit(solution)/shard_map/dot_general | solution.py:331
  139.1 1.5 collective-permute-start.27
  140.6 4.1 %collective-permute-done.27 = bf16[256,256]{1,0:T(8,128)(2,1)S(1)} collective-permute-done((bf16[256,256]{1,0:T(8,128)(2,1)S(1)}, bf16[256,256]{1,0:T(8,128)(2,1)S(1)}, u32[]{:S(2)}, u32[]{:S(2)}) %collective-permute-start.27) | collective-permute-done | bytes 131104 | tf_op jit(solution)/shard_map/ppermute | solution.py:193
  144.8 4.8 %collective-permute-done.29 = bf16[128,1280]{1,0:T(8,128)(2,1)S(1)} collective-permute-done((bf16[128,1280]{1,0:T(8,128)(2,1)S(1)}, bf16[128,1280]{1,0:T(8,128)(2,1)S(1)}, u32[]{:S(2)}, u32[]{:S(2)}) %collective-permute-start.29) | collective-permute-done | bytes 327712 | tf_op jit(solution)/shard_map/ppermute | solution.py:333
  149.7 2.5 %collective-permute-start.30 = (bf16[128,1280]{1,0:T(8,128)(2,1)S(1)}, bf16[128,1280]{1,0:T(8,128)(2,1)S(1)}, u32[]{:S(2)}, u32[]{:S(2)}) collective-permute-start(bf16[128,1280]{1,0:T(8,128)(2,1)S(1)} %get-tuple-element.82), channel_id=1, source_target_pairs={{4,8},{8,4},{5,9},{9,5},{6,10},{10,6},{7,11},{11,7},{20,24},{24,20... | collective-permute-start | bytes 983048 | tf_op jit(solution)/shard_map/ppermute | solution.py:339
  154.4 6.2 %collective-permute-done.30 = bf16[128,1280]{1,0:T(8,128)(2,1)S(1)} collective-permute-done((bf16[128,1280]{1,0:T(8,128)(2,1)S(1)}, bf16[128,1280]{1,0:T(8,128)(2,1)S(1)}, u32[]{:S(2)}, u32[]{:S(2)}) %collective-permute-start.30) | collective-permute-done | bytes 327712 | tf_op jit(solution)/shard_map/ppermute | solution.py:339
  160.7 2.2 %collective-permute-done.31 = bf16[128,1280]{1,0:T(8,128)(2,1)S(1)} collective-permute-done((bf16[128,1280]{1,0:T(8,128)(2,1)S(1)}, bf16[128,1280]{1,0:T(8,128)(2,1)S(1)}, u32[]{:S(2)}, u32[]{:S(2)}) %collective-permute-start.31) | collective-permute-done | bytes 327712 | tf_op jit(solution)/shard_map/ppermute | solution.py:340
  163.0 3.4 %collective-permute-start.32 = (bf16[128,1280]{1,0:T(8,128)(2,1)S(1)}, bf16[128,1280]{1,0:T(8,128)(2,1)S(1)}, u32[]{:S(2)}, u32[]{:S(2)}) collective-permute-start(bf16[128,1280]{1,0:T(8,128)(2,1)S(1)} %add_convert_fusion), channel_id=1, source_target_pairs={{4,8},{8,4},{5,9},{9,5},{6,10},{10,6},{7,11},{11,7},{20,24},{24,20... | collective-permute-start | bytes 983048 | tf_op jit(solution)/shard_map/ppermute | solution.py:345
  166.4 6.3 %collective-permute-done.32 = bf16[128,1280]{1,0:T(8,128)(2,1)S(1)} collective-permute-done((bf16[128,1280]{1,0:T(8,128)(2,1)S(1)}, bf16[128,1280]{1,0:T(8,128)(2,1)S(1)}, u32[]{:S(2)}, u32[]{:S(2)}) %collective-permute-start.32) | collective-permute-done | bytes 327712 | tf_op jit(solution)/shard_map/ppermute | solution.py:345
  (120 shorter events, 20.1 us)
Async XLA Ops:
  1.9 8.4 %collective-permute-start.2 = (f32[16,1024]{1,0:T(8,128)S(1)}, f32[16,1024]{1,0:T(8,128)S(1)}, u32[]{:S(2)}, u32[]{:S(2)}) collective-permute-start(f32[16,1024]{1,0:T(8,128)S(1)} %constant_dynamic-update-slice_fusion.refs_1_), channel_id=1, source_target_pairs={{0,8},{4,12},{8,0},{12,4},{1,9},{5,13},{9,1},{13,5},{2,10},{6,14},... | collective-permute-start | bytes 196616 | tf_op jit(solution)/shard_map/ppermute | solution.py:187
  4.5 5.7 %collective-permute-start.1 = (f32[16,1024]{1,0:T(8,128)S(1)}, f32[16,1024]{1,0:T(8,128)S(1)}, u32[]{:S(2)}, u32[]{:S(2)}) collective-permute-start(f32[16,1024]{1,0:T(8,128)S(1)} %constant_dynamic-update-slice_fusion.refs_1_), channel_id=1, source_target_pairs={{0,12},{4,8},{8,4},{12,0},{1,13},{5,9},{9,5},{13,1},{2,14},{6,10},... | collective-permute-start | bytes 196616 | tf_op jit(solution)/shard_map/ppermute | solution.py:188
  4.5 22.9 %collective-permute-start = (f32[16,1024]{1,0:T(8,128)S(1)}, f32[16,1024]{1,0:T(8,128)S(1)}, u32[]{:S(2)}, u32[]{:S(2)}) collective-permute-start(f32[16,1024]{1,0:T(8,128)S(1)} %constant_dynamic-update-slice_fusion.refs_1_), channel_id=1, source_target_pairs={{0,4},{4,0},{8,12},{12,8},{1,5},{5,1},{9,13},{13,9},{2,6},{6,2},{1... | collective-permute-start | bytes 196616 | tf_op jit(solution)/shard_map/ppermute | solution.py:186
  8.8 28.4 %collective-permute-start.4 = (bf16[2,2,384,256]{3,2,1,0:T(8,128)(2,1)}, bf16[2,2,384,256]{3,2,1,0:T(8,128)(2,1)S(1)}, u32[]{:S(2)}, u32[]{:S(2)}) collective-permute-start(bf16[2,2,384,256]{3,2,1,0:T(8,128)(2,1)} %pad_maximum_fusion), channel_id=1, source_target_pairs={{0,2},{1,3},{2,0},{3,1},{4,6},{5,7},{6,4},{7,5},{8,10},{9,11},{10,... | collective-permute-start | bytes 2359304 | tf_op jit(solution)/shard_map/ppermute | solution.py:193
  16.0 11.3 %copy-start.10 = (s32[512]{0:T(512)S(1)}, s32[512]{0:T(512)}, u32[]{:S(2)}) copy-start(s32[512]{0:T(512)} %param.18) | copy-start | bytes 6148
  26.0 11.0 %collective-permute-start.3 = (f16[128,1280]{1,0:T(8,128)(2,1)S(1)}, f16[128,1280]{1,0:T(8,128)(2,1)S(1)}, u32[]{:S(2)}, u32[]{:S(2)}) collective-permute-start(f16[128,1280]{1,0:T(8,128)(2,1)S(1)} %fusion.4), channel_id=1, source_target_pairs={{0,4},{12,8},{1,5},{13,9},{2,6},{14,10},{3,7},{15,11},{16,20},{28,... | collective-permute-start | bytes 983048 | tf_op jit(solution)/shard_map/ppermute | solution.py:253
  37.1 29.2 %slice-start = ((s8[7864320]{0:T(1024)(128)(4,1)}), s8[4194304]{0:T(1024)(128)(4,1)S(1)}, s32[]{:S(2)}) async-start(s8[7864320]{0:T(1024)(128)(4,1)} %bitcast.54), calls=%async_computation | async-start | bytes 8388608
  37.1 29.2 %slice-start.1 = ((s8[7864320]{0:T(1024)(128)(4,1)}), s8[3670016]{0:T(1024)(128)(4,1)S(1)}, s32[]{:S(2)}) async-start(s8[7864320]{0:T(1024)(128)(4,1)} %bitcast.54), calls=%async_computation.1 | async-start | bytes 7340032
  47.2 19.0 %copy-start.9 = (bf16[1280]{0:T(1024)(128)(2,1)S(1)}, bf16[1280]{0:T(1024)(128)(2,1)}, u32[]{:S(2)}) copy-start(bf16[1280]{0:T(1024)(128)(2,1)} %param.13) | copy-start | bytes 7684
  47.2 11.1 %collective-permute-start.5 = (f16[128,1280]{1,0:T(8,128)(2,1)S(1)}, f16[128,1280]{1,0:T(8,128)(2,1)S(1)}, u32[]{:S(2)}, u32[]{:S(2)}) collective-permute-start(f16[128,1280]{1,0:T(8,128)(2,1)S(1)} %get-tuple-element.51), channel_id=1, source_target_pairs={{4,8},{8,4},{5,9},{9,5},{6,10},{10,6},{7,11},{11,7},{20,24},{24,20... | collective-permute-start | bytes 983048 | tf_op jit(solution)/shard_map/ppermute | solution.py:261
  51.7 12.5 %collective-permute-start.6 = (f16[128,1280]{1,0:T(8,128)(2,1)S(1)}, f16[128,1280]{1,0:T(8,128)(2,1)S(1)}, u32[]{:S(2)}, u32[]{:S(2)}) collective-permute-start(f16[128,1280]{1,0:T(8,128)(2,1)S(1)} %multiply_convert_fusion.1), channel_id=1, source_target_pairs={{0,4},{12,8},{1,5},{13,9},{2,6},{14,10},{3,7},{15,11},{16,20},{28,... | collective-permute-start | bytes 983048 | tf_op jit(solution)/shard_map/ppermute | solution.py:262
  58.5 13.3 %collective-permute-start.8 = (f16[128,1280]{1,0:T(8,128)(2,1)S(1)}, f16[128,1280]{1,0:T(8,128)(2,1)S(1)}, u32[]{:S(2)}, u32[]{:S(2)}) collective-permute-start(f16[128,1280]{1,0:T(8,128)(2,1)S(1)} %multiply_convert_fusion.2), channel_id=1, source_target_pairs={{0,4},{4,0},{8,12},{12,8},{1,5},{5,1},{9,13},{13,9},{2,6},{6,2},{1... | collective-permute-start | bytes 983048 | tf_op jit(solution)/shard_map/ppermute | solution.py:267
  58.7 13.1 %collective-permute-start.9 = (bf16[2,2,384,256]{3,2,1,0:T(8,128)(2,1)S(1)}, bf16[2,2,384,256]{3,2,1,0:T(8,128)(2,1)S(1)}, u32[]{:S(2)}, u32[]{:S(2)}) collective-permute-start(bf16[2,2,384,256]{3,2,1,0:T(8,128)(2,1)S(1)} %pad_maximum_fusion.1), channel_id=1, source_target_pairs={{0,1},{1,0},{2,3},{3,2},{4,5},{5,4},{6,7},{7,6},{8,9},{9,8},{10,11... | collective-permute-start | bytes 2359304 | tf_op jit(solution)/shard_map/ppermute | solution.py:193
  64.3 9.0 %collective-permute-start.7 = (f16[128,1280]{1,0:T(8,128)(2,1)S(1)}, f16[128,1280]{1,0:T(8,128)(2,1)S(1)}, u32[]{:S(2)}, u32[]{:S(2)}) collective-permute-start(f16[128,1280]{1,0:T(8,128)(2,1)S(1)} %multiply_convert_fusion), channel_id=1, source_target_pairs={{4,8},{8,4},{5,9},{9,5},{6,10},{10,6},{7,11},{11,7},{20,24},{24,20... | collective-permute-start | bytes 983048 | tf_op jit(solution)/shard_map/ppermute | solution.py:268
  68.1 1.9 %copy-start = (bf16[1280,1536]{1,0:T(8,128)(2,1)}, bf16[1280,1536]{1,0:T(8,128)(2,1)S(1)}, u32[]{:S(2)}) copy-start(bf16[1280,1536]{1,0:T(8,128)(2,1)S(1)} %select_columns.3) | copy-start | bytes 11796484
  70.0 8.5 %copy-start.7 = (f32[1280]{0:T(1024)S(1)}, f32[1280]{0:T(1024)}, u32[]{:S(2)}) copy-start(f32[1280]{0:T(1024)} %param.15) | copy-start | bytes 15364
  70.0 8.5 %copy-start.8 = (f32[1280]{0:T(1024)S(1)}, f32[1280]{0:T(1024)}, u32[]{:S(2)}) copy-start(f32[1280]{0:T(1024)} %param.14) | copy-start | bytes 15364
  71.8 6.9 %copy-start.2 = (bf16[1280,1536]{1,0:T(8,128)(2,1)}, bf16[1280,1536]{1,0:T(8,128)(2,1)S(1)}, u32[]{:S(2)}) copy-start(bf16[1280,1536]{1,0:T(8,128)(2,1)S(1)} %select_columns.2) | copy-start | bytes 11796484
  73.6 1.2 collective-permute-start.10
  74.8 3.6 %collective-permute-start.11 = (f32[2,128]{1,0:T(2,128)S(1)}, f32[2,128]{1,0:T(2,128)S(1)}, u32[]{:S(2)}, u32[]{:S(2)}) collective-permute-start(f32[2,128]{1,0:T(2,128)S(1)} %fusion.25), channel_id=1, source_target_pairs={{0,2},{1,3},{2,0},{3,1},{4,6},{5,7},{6,4},{7,5},{8,10},{9,11},{10,... | collective-permute-start | bytes 3080 | tf_op jit(solution)/shard_map/ppermute | solution.py:193
  80.1 16.3 %collective-permute-start.12 = (f16[128,1536]{1,0:T(8,128)(2,1)}, f16[128,1536]{1,0:T(8,128)(2,1)}, u32[]{:S(2)}, u32[]{:S(2)}) collective-permute-start(f16[128,1536]{1,0:T(8,128)(2,1)} %convolution_convert_fusion.3), channel_id=1, source_target_pairs={{0,1},{1,0},{2,3},{3,2},{4,5},{5,4},{6,7},{7,6},{8,9},{9,8},{10,11... | collective-permute-start | bytes 1179656 | tf_op jit(solution)/shard_map/ppermute | solution.py:193
  80.3 20.6 %copy-start.3 = (bf16[1280,1536]{1,0:T(8,128)(2,1)S(1)}, bf16[1280,1536]{1,0:T(8,128)(2,1)}, u32[]{:S(2)}) copy-start(bf16[1280,1536]{1,0:T(8,128)(2,1)} %copy-done.2) | copy-start | bytes 11796484
  80.3 12.3 %collective-permute-start.14 = (bf16[128,1280]{1,0:T(8,128)(2,1)S(1)}, bf16[128,1280]{1,0:T(8,128)(2,1)S(1)}, u32[]{:S(2)}, u32[]{:S(2)}) collective-permute-start(bf16[128,1280]{1,0:T(8,128)(2,1)S(1)} %add_convert_fusion.2), channel_id=1, source_target_pairs={{4,8},{8,4},{5,9},{9,5},{6,10},{10,6},{7,11},{11,7},{20,24},{24,20... | collective-permute-start | bytes 983048 | tf_op jit(solution)/shard_map/ppermute | solution.py:283
  83.1 10.8 %collective-permute-start.13 = (bf16[128,1280]{1,0:T(8,128)(2,1)S(1)}, bf16[128,1280]{1,0:T(8,128)(2,1)S(1)}, u32[]{:S(2)}, u32[]{:S(2)}) collective-permute-start(bf16[128,1280]{1,0:T(8,128)(2,1)S(1)} %add_convert_fusion.2), channel_id=1, source_target_pairs={{0,4},{4,0},{8,12},{12,8},{1,5},{5,1},{9,13},{13,9},{2,6},{6,2},{1... | collective-permute-start | bytes 983048 | tf_op jit(solution)/shard_map/ppermute | solution.py:282
  92.6 14.0 %collective-permute-start.17 = (bf16[128,1280]{1,0:T(8,128)(2,1)S(1)}, bf16[128,1280]{1,0:T(8,128)(2,1)S(1)}, u32[]{:S(2)}, u32[]{:S(2)}) collective-permute-start(bf16[128,1280]{1,0:T(8,128)(2,1)S(1)} %collective-permute-done.14), channel_id=1, source_target_pairs={{4,0},{8,12},{5,1},{9,13},{6,2},{10,14},{7,3},{11,15},{20,16},{24,... | collective-permute-start | bytes 983048 | tf_op jit(solution)/shard_map/ppermute | solution.py:285
  93.9 11.2 %collective-permute-start.18 = (bf16[128,1280]{1,0:T(8,128)(2,1)S(1)}, bf16[128,1280]{1,0:T(8,128)(2,1)S(1)}, u32[]{:S(2)}, u32[]{:S(2)}) collective-permute-start(bf16[128,1280]{1,0:T(8,128)(2,1)S(1)} %collective-permute-done.13), channel_id=1, source_target_pairs={{4,8},{8,4},{5,9},{9,5},{6,10},{10,6},{7,11},{11,7},{20,24},{24,20... | collective-permute-start | bytes 983048 | tf_op jit(solution)/shard_map/ppermute | solution.py:284
  99.3 7.4 %copy-start.1 = (bf16[1280,1536]{1,0:T(8,128)(2,1)S(1)}, bf16[1280,1536]{1,0:T(8,128)(2,1)}, u32[]{:S(2)}) copy-start(bf16[1280,1536]{1,0:T(8,128)(2,1)} %copy-done) | copy-start | bytes 11796484
  99.3 14.9 %collective-permute-start.15 = (f16[128,768]{1,0:T(8,128)(2,1)S(1)}, f16[128,768]{1,0:T(8,128)(2,1)S(1)}, u32[]{:S(2)}, u32[]{:S(2)}) collective-permute-start(f16[128,768]{1,0:T(8,128)(2,1)S(1)} %slice_convert_fusion.4), channel_id=1, source_target_pairs={{0,2},{1,3},{2,0},{3,1},{4,6},{5,7},{6,4},{7,5},{8,10},{9,11},{10,... | collective-permute-start | bytes 589832 | tf_op jit(solution)/shard_map/ppermute | solution.py:193
  101.5 5.1 %collective-permute-start.16 = (f16[128,1536]{1,0:T(8,128)(2,1)S(1)}, f16[128,1536]{1,0:T(8,128)(2,1)S(1)}, u32[]{:S(2)}, u32[]{:S(2)}) collective-permute-start(f16[128,1536]{1,0:T(8,128)(2,1)S(1)} %convolution_convert_fusion.2), channel_id=1, source_target_pairs={{0,1},{1,0},{2,3},{3,2},{4,5},{5,4},{6,7},{7,6},{8,9},{9,8},{10,11... | collective-permute-start | bytes 1179656 | tf_op jit(solution)/shard_map/ppermute | solution.py:193
  105.1 7.5 %collective-permute-start.21 = (bf16[128,1280]{1,0:T(8,128)(2,1)S(1)}, bf16[128,1280]{1,0:T(8,128)(2,1)S(1)}, u32[]{:S(2)}, u32[]{:S(2)}) collective-permute-start(bf16[128,1280]{1,0:T(8,128)(2,1)S(1)} %collective-permute-done.18), channel_id=1, source_target_pairs={{4,0},{8,12},{5,1},{9,13},{6,2},{10,14},{7,3},{11,15},{20,16},{24,... | collective-permute-start | bytes 983048 | tf_op jit(solution)/shard_map/ppermute | solution.py:286
  107.4 2.3 %copy-start.4 = (bf16[1024,1280]{1,0:T(8,128)(2,1)S(1)}, bf16[1024,1280]{1,0:T(8,128)(2,1)}, u32[]{:S(2)}) copy-start(bf16[1024,1280]{1,0:T(8,128)(2,1)} %from_ref) | copy-start | bytes 7864324
  107.4 6.8 %collective-permute-start.19 = (f16[128,768]{1,0:T(8,128)(2,1)S(1)}, f16[128,768]{1,0:T(8,128)(2,1)S(1)}, u32[]{:S(2)}, u32[]{:S(2)}) collective-permute-start(f16[128,768]{1,0:T(8,128)(2,1)S(1)} %slice_convert_fusion.3), channel_id=1, source_target_pairs={{0,2},{1,3},{2,0},{3,1},{4,6},{5,7},{6,4},{7,5},{8,10},{9,11},{10,... | collective-permute-start | bytes 589832 | tf_op jit(solution)/shard_map/ppermute | solution.py:193
  109.6 3.0 %collective-permute-start.20 = (f16[128,1536]{1,0:T(8,128)(2,1)S(1)}, f16[128,1536]{1,0:T(8,128)(2,1)S(1)}, u32[]{:S(2)}, u32[]{:S(2)}) collective-permute-start(f16[128,1536]{1,0:T(8,128)(2,1)S(1)} %convolution_convert_fusion.1), channel_id=1, source_target_pairs={{0,1},{1,0},{2,3},{3,2},{4,5},{5,4},{6,7},{7,6},{8,9},{9,8},{10,11... | collective-permute-start | bytes 1179656 | tf_op jit(solution)/shard_map/ppermute | solution.py:193
  110.5 3.6 %copy-start.5 = (bf16[1024,1280]{1,0:T(8,128)(2,1)}, bf16[1024,1280]{1,0:T(8,128)(2,1)S(1)}, u32[]{:S(2)}) copy-start(bf16[1024,1280]{1,0:T(8,128)(2,1)S(1)} %select_rows.1) | copy-start | bytes 7864324
  114.1 1.8 %collective-permute-start.23 = (f16[128,1536]{1,0:T(8,128)(2,1)S(1)}, f16[128,1536]{1,0:T(8,128)(2,1)S(1)}, u32[]{:S(2)}, u32[]{:S(2)}) collective-permute-start(f16[128,1536]{1,0:T(8,128)(2,1)S(1)} %convolution_convert_fusion), channel_id=1, source_target_pairs={{0,1},{1,0},{2,3},{3,2},{4,5},{5,4},{6,7},{7,6},{8,9},{9,8},{10,11... | collective-permute-start | bytes 1179656 | tf_op jit(solution)/shard_map/ppermute | solution.py:193
  114.3 7.8 %collective-permute-start.22 = (f16[128,768]{1,0:T(8,128)(2,1)S(1)}, f16[128,768]{1,0:T(8,128)(2,1)S(1)}, u32[]{:S(2)}, u32[]{:S(2)}) collective-permute-start(f16[128,768]{1,0:T(8,128)(2,1)S(1)} %slice_convert_fusion.2), channel_id=1, source_target_pairs={{0,2},{1,3},{2,0},{3,1},{4,6},{5,7},{6,4},{7,5},{8,10},{9,11},{10,... | collective-permute-start | bytes 589832 | tf_op jit(solution)/shard_map/ppermute | solution.py:193
  116.6 9.2 %collective-permute-start.24 = (f16[128,768]{1,0:T(8,128)(2,1)S(1)}, f16[128,768]{1,0:T(8,128)(2,1)S(1)}, u32[]{:S(2)}, u32[]{:S(2)}) collective-permute-start(f16[128,768]{1,0:T(8,128)(2,1)S(1)} %slice_convert_fusion.1), channel_id=1, source_target_pairs={{0,2},{1,3},{2,0},{3,1},{4,6},{5,7},{6,4},{7,5},{8,10},{9,11},{10,... | collective-permute-start | bytes 589832 | tf_op jit(solution)/shard_map/ppermute | solution.py:193
  128.3 5.2 %collective-permute-start.25 = (bf16[256,256]{1,0:T(8,128)(2,1)S(1)}, bf16[256,256]{1,0:T(8,128)(2,1)S(1)}, u32[]{:S(2)}, u32[]{:S(2)}) collective-permute-start(bf16[256,256]{1,0:T(8,128)(2,1)S(1)} %attend.2), channel_id=1, source_target_pairs={{0,2},{1,3},{2,0},{3,1},{4,6},{5,7},{6,4},{7,5},{8,10},{9,11},{10,... | collective-permute-start | bytes 393224 | tf_op jit(solution)/shard_map/ppermute | solution.py:193
  133.6 20.0 %copy-start.6 = (bf16[1024,1280]{1,0:T(8,128)(2,1)S(1)}, bf16[1024,1280]{1,0:T(8,128)(2,1)}, u32[]{:S(2)}) copy-start(bf16[1024,1280]{1,0:T(8,128)(2,1)} %copy-done.5) | copy-start | bytes 7864324
  133.6 1.6 collective-permute-start.26
  137.8 11.8 %collective-permute-start.29 = (bf16[128,1280]{1,0:T(8,128)(2,1)S(1)}, bf16[128,1280]{1,0:T(8,128)(2,1)S(1)}, u32[]{:S(2)}, u32[]{:S(2)}) collective-permute-start(bf16[128,1280]{1,0:T(8,128)(2,1)S(1)} %slice.167), channel_id=1, source_target_pairs={{0,4},{12,8},{1,5},{13,9},{2,6},{14,10},{3,7},{15,11},{16,20},{28,... | collective-permute-start | bytes 983048 | tf_op jit(solution)/shard_map/ppermute | solution.py:333
  139.1 5.6 %collective-permute-start.27 = (bf16[256,256]{1,0:T(8,128)(2,1)S(1)}, bf16[256,256]{1,0:T(8,128)(2,1)S(1)}, u32[]{:S(2)}, u32[]{:S(2)}) collective-permute-start(bf16[256,256]{1,0:T(8,128)(2,1)S(1)} %attend.3), channel_id=1, source_target_pairs={{0,2},{1,3},{2,0},{3,1},{4,6},{5,7},{6,4},{7,5},{8,10},{9,11},{10,... | collective-permute-start | bytes 393224 | tf_op jit(solution)/shard_map/ppermute | solution.py:193
  144.7 8.8 %collective-permute-start.28 = (bf16[256,512]{1,0:T(8,128)(2,1)S(1)}, bf16[256,512]{1,0:T(8,128)(2,1)S(1)}, u32[]{:S(2)}, u32[]{:S(2)}) collective-permute-start(bf16[256,512]{1,0:T(8,128)(2,1)S(1)} %pad_maximum_fusion.3), channel_id=1, source_target_pairs={{0,1},{1,0},{2,3},{3,2},{4,5},{5,4},{6,7},{7,6},{8,9},{9,8},{10,11... | collective-permute-start | bytes 786440 | tf_op jit(solution)/shard_map/ppermute | solution.py:193
  149.7 10.9 %collective-permute-start.30 = (bf16[128,1280]{1,0:T(8,128)(2,1)S(1)}, bf16[128,1280]{1,0:T(8,128)(2,1)S(1)}, u32[]{:S(2)}, u32[]{:S(2)}) collective-permute-start(bf16[128,1280]{1,0:T(8,128)(2,1)S(1)} %get-tuple-element.82), channel_id=1, source_target_pairs={{4,8},{8,4},{5,9},{9,5},{6,10},{10,6},{7,11},{11,7},{20,24},{24,20... | collective-permute-start | bytes 983048 | tf_op jit(solution)/shard_map/ppermute | solution.py:339
  152.2 10.7 %collective-permute-start.31 = (bf16[128,1280]{1,0:T(8,128)(2,1)S(1)}, bf16[128,1280]{1,0:T(8,128)(2,1)S(1)}, u32[]{:S(2)}, u32[]{:S(2)}) collective-permute-start(bf16[128,1280]{1,0:T(8,128)(2,1)S(1)} %convert_element_type.163), channel_id=1, source_target_pairs={{0,4},{12,8},{1,5},{13,9},{2,6},{14,10},{3,7},{15,11},{16,20},{28,... | collective-permute-start | bytes 983048 | tf_op jit(solution)/shard_map/ppermute | solution.py:340
  163.0 9.7 %collective-permute-start.32 = (bf16[128,1280]{1,0:T(8,128)(2,1)S(1)}, bf16[128,1280]{1,0:T(8,128)(2,1)S(1)}, u32[]{:S(2)}, u32[]{:S(2)}) collective-permute-start(bf16[128,1280]{1,0:T(8,128)(2,1)S(1)} %add_convert_fusion), channel_id=1, source_target_pairs={{4,8},{8,4},{5,9},{9,5},{6,10},{10,6},{7,11},{11,7},{20,24},{24,20... | collective-permute-start | bytes 983048 | tf_op jit(solution)/shard_map/ppermute | solution.py:345
  166.3 7.6 %collective-permute-start.33 = (bf16[128,1280]{1,0:T(8,128)(2,1)S(1)}, bf16[128,1280]{1,0:T(8,128)(2,1)S(1)}, u32[]{:S(2)}, u32[]{:S(2)}) collective-permute-start(bf16[128,1280]{1,0:T(8,128)(2,1)S(1)} %fusion), channel_id=1, source_target_pairs={{0,4},{4,0},{8,12},{12,8},{1,5},{5,1},{9,13},{13,9},{2,6},{6,2},{1... | collective-permute-start | bytes 983048 | tf_op jit(solution)/shard_map/ppermute | solution.py:343

commit v5 on v4

--- a/solution.py
+++ b/solution.py
@@ -12,6 +12,7 @@
 HEAD = 128
 GROUP = 8
 VMEM_BYTES = 20 * 1024 * 1024
+DECODE_BYTES = 44 * 1024 * 1024
 
 
 def densify_kernel(base_ref, *refs, topk, latents, lanes):
@@ -71,6 +72,33 @@
         ),
         name="densify",
     )(base, *packed)
+
+
+def decode_kernel(codes_ref, weights_ref, out_ref):
+    out_ref[...] = jnp.dot(codes_ref[...], weights_ref[...], preferred_element_type=jnp.float32)
+
+
+def decode(codes, decoder):
+    rows, latents = codes.shape
+    columns = decoder.shape[1]
+    width = math.gcd(columns, 256)
+    return pl.pallas_call(
+        decode_kernel,
+        out_shape=jax.ShapeDtypeStruct((rows, columns), jnp.float32),
+        grid=(columns // width,),
+        in_specs=[
+            pl.BlockSpec((rows, latents), lambda n: (0, 0)),
+            pl.BlockSpec((latents, width), lambda n: (0, n)),
+        ],
+        out_specs=pl.BlockSpec((rows, width), lambda n: (0, n)),
+        compiler_params=pltpu.CompilerParams(vmem_limit_bytes=DECODE_BYTES),
+        cost_estimate=pl.CostEstimate(
+            flops=2 * rows * latents * columns,
+            bytes_accessed=latents * (rows + columns) * 2 + rows * columns * 4,
+            transcendentals=0,
+        ),
+        name="decode",
+    )(codes, decoder)
 
 
 def copy_kernel(order_ref, from_ref, to_ref):
@@ -260,7 +288,7 @@
     )
     mid_far = lax.ppermute(mid_far, "lat", MIDDLE)
     in_across = lax.ppermute(to_half(second), "lat", INWARD)
-    near = jnp.dot(codes_near, decoder, preferred_element_type=jnp.float32)
+    near = decode(codes_near, decoder)
     near, mid_far = hold((near, mid_far))
     last = to_half(near[:rows] + from_half(mid_far))
     across, last, second, weights = hold((across, last, second, w_qkv.transpose(1, 0, 2)))
@@ -269,8 +297,11 @@
 
     away_weights = select_columns(weights, jnp.stack([col ^ 1, col ^ 3]), own_width)
     keep_weights = select_columns(weights, jnp.stack([col, col ^ 2]), own_width)
+    out_weights = select_rows(w_out, jnp.stack([col, col ^ 2, col ^ 1, col ^ 3]), own_width)
     beside = swap(jnp.stack([cache_of(1), across[1]]), 1, cols)
-    last, away_weights, keep_weights, beside = hold((last, away_weights, keep_weights, beside))
+    last, away_weights, keep_weights, out_weights, beside = hold(
+        (last, away_weights, keep_weights, out_weights, beside)
+    )
     cached = [cache_of(0), across[0], beside[0], beside[1]]
     residual = near[rows:] + from_half(mid_across) + from_half(last)
     residual = residual + dec_bias.astype(jnp.float32)
@@ -299,21 +330,10 @@
     keep0, payload0 = project(own)
     near_block, across, payload0 = hold((near, across, payload0))
     keep1, payload1 = project(near_block)
-    third, far, payload1, out_source = hold(
-        (jnp.where(outer, across_out, across), far, payload1, w_out)
-    )
-    out_weights = select_rows(
-        out_source, jnp.stack([col, col ^ 2, col ^ 1, col ^ 3]), own_width
-    )
-    keep2, payload2 = project(third)
-    fourth, payload2, out_weights = hold((jnp.where(outer, far_out, far), payload2, out_weights))
-    keep3, payload3 = project(fourth)
-    qkv = [
-        finish(keep0, payload0),
-        finish(keep1, payload1),
-        finish(keep2, payload2),
-        finish(keep3, payload3),
-    ]
+    third, far, payload1 = hold((jnp.where(outer, across_out, across), far, payload1))
+    third = finish(*project(third))
+    fourth, third = hold((jnp.where(outer, far_out, far), third))
+    qkv = [finish(keep0, payload0), finish(keep1, payload1), third, finish(*project(fourth))]
 
     key_row = key_pos.reshape(1, -1)
 
@@ -343,8 +363,9 @@
     last = lax.ppermute(last, "lat", PAIRS)
     mid_across = (second + in_across.astype(jnp.float32)).astype(jnp.bfloat16)
     mid_across = lax.ppermute(mid_across, "lat", MIDDLE)
-    branch = product_near[rows:] + mid_across.astype(jnp.float32) + last.astype(jnp.float32)
-    return (residual + branch).astype(jnp.bfloat16)
+    branch = product_near[rows:] + last.astype(jnp.float32)
+    branch, mid_across = hold((residual + branch, mid_across))
+    return (branch + mid_across.astype(jnp.float32)).astype(jnp.bfloat16)
 
 
 def attend_block(queries, keys, values, query_pos, key_pos):

time: 177 us -> 174 us (0.983)
  Pallas kernels: 20.6 us -> 31.7 us
  matrix products: 31.8 us -> 21 us
  waiting for transfers between devices: 69.3 us -> 72 us
  starting transfers between devices: 42.7 us -> 40.8 us
  local copies, waits for them, and re-layouts: 4.26 us -> 2.42 us
    pallas_call x0 -> x1, Pallas kernels: none -> 11.1 us  [decode(): pl.pallas_call(decode_kernel, out_shape=jax.ShapeDtypeStruct((rows, colum...]
    dot_general x1 -> x0, matrix products: 10 us -> none  [line_body(): near = jnp.dot(codes_near, decoder, preferred_element_type=jnp.float32)]
    ppermute x1, waiting for transfers between devices: 5.38 us -> 0.01 us  [line_body(): in_across = lax.ppermute(to_half(second), 'lat', INWARD)]
    ppermute x16, waiting for transfers between devices: 17.6 us -> 22.9 us  [swap(): return lax.ppermute(value, 'col', [(i, i ^ distance) for i in range(size)])]
    ppermute x2, waiting for transfers between devices: 11.6 us -> 6.38 us  [line_body(): mid_far = lax.ppermute(mid_far, 'lat', MIDDLE)]
    ppermute x1, waiting for transfers between devices: 1.44 us -> 5.3 us  [line_body(): lax.ppermute(to_half(second + from_half(in_across)), 'lat', MIDDLE)]
    ppermute x16, starting transfers between devices: 12.7 us -> 9.39 us  [swap(): return lax.ppermute(value, 'col', [(i, i ^ distance) for i in range(size)])]
    ppermute x1, waiting for transfers between devices: 0.01 us -> 3.12 us  [line_body(): across_out = lax.ppermute(across, 'lat', OUTWARD)]
  transfers between devices with their start and end apart: 34 -> 34, of which waited for: 20 -> 22; matrix products, arithmetic and copies ran while one was open for 13% -> 12% of each run, Pallas kernels for 10% -> 17%
where the time goes in v5:
time: 174 us; the launch traced here: 173 us
  waiting for transfers between devices  72 us (41%)
  starting transfers between devices  40.8 us (23%)
  Pallas kernels  31.7 us (18%)
  matrix products  21 us (12%)
  other arithmetic  4.48 us (3%)
  local copies, waits for them, and re-layouts  2.42 us (1%)
    ppermute x16, waiting for transfers between devices, swap(): return lax.ppermute(value, 'col', [(i, i ^ distance) for i in range(size)])  22.9 us
    pallas_call x2, Pallas kernels, densify(): pl.pallas_call(functools.partial(densify_kernel, topk=topk, latents=laten...  11.4 us
    pallas_call x1, Pallas kernels, decode(): pl.pallas_call(decode_kernel, out_shape=jax.ShapeDtypeStruct((rows, colum...  11.1 us
    dot_general x1, matrix products, line_body(): far = jnp.dot(codes_far, decoder, preferred_element_type=jnp.float32)  9.85 us
    ppermute x1, waiting for transfers between devices, line_body(): across = lax.ppermute(own, 'lat', MIDDLE)  9.71 us
    ppermute x16, starting transfers between devices, swap(): return lax.ppermute(value, 'col', [(i, i ^ distance) for i in range(size)])  9.39 us
    ppermute x2, waiting for transfers between devices, line_body(): mid_far = lax.ppermute(mid_far, 'lat', MIDDLE)  6.38 us
    ppermute x2, starting transfers between devices, line_body(): mid_far = lax.ppermute(mid_far, 'lat', MIDDLE)  6.03 us
  transfers between devices with their start and end apart: 34, of which 22 were waited for; matrix products, arithmetic and copies ran while one was open for 12% of the time, Pallas kernels for 17%

profile of v5, /device:TPU:8, one launch (start us, length us, event | category | flops | bytes accessed | tf_op | source)
XLA Modules:
  0.0 173.3 jit_solution(15429641984340510474)
XLA Ops:
  1.9 3.0 %collective-permute-start.2 = (f32[16,1024]{1,0:T(8,128)S(1)}, f32[16,1024]{1,0:T(8,128)S(1)}, u32[]{:S(2)}, u32[]{:S(2)}) collective-permute-start(f32[16,1024]{1,0:T(8,128)S(1)} %constant_dynamic-update-slice_fusion.refs_1_), channel_id=1, source_target_pairs={{0,8},{4,12},{8,0},{12,4},{1,9},{5,13},{9,1},{13,5},{2,10},{6,14},... | collective-permute-start | bytes 196616 | tf_op jit(solution)/shard_map/ppermute | solution.py:215
  5.4 1.5 constant_dynamic-slice_fusion
  7.0 1.6 collective-permute-start.4
  8.5 1.0 collective-permute-done.2
  10.5 5.7 %densify.2 = bf16[256,8192]{1,0:T(8,128)(2,1)S(1)} custom-call(s32[1]{0:T(128)} %bitcast.base_ref, f32[16,1024]{1,0:T(8,128)S(1)} %get-tuple-element.103.refs_0_, f32[16,1024]{1,0:T(8,128)S(1)} %get-tuple-element.102.refs_1_), custom_call_target="tpu_custom_call" | custom-call | flops 2147483648 | bytes 4194304 | tf_op jit(solution)/shard_map/densify/pallas_call | solution.py:63
  16.2 9.9 %fusion.27 = f32[256,1280]{1,0:T(8,128)S(1)} fusion(bf16[256,8192]{1,0:T(8,128)(2,1)S(1)} %densify.2, bf16[8192,1280]{1,0:T(8,128)(2,1)} %weights_ref.1), kind=kOutput, calls=%fused_computation.84 | convolution fusion | flops 5368709120 | bytes 26476544 | tf_op jit(solution)/shard_map/dot_general | solution.py:280
  26.1 1.3 collective-permute-start.3
  27.6 5.7 %densify.3.codes_ref = bf16[256,8192]{1,0:T(8,128)(2,1)S(1)} custom-call(s32[1]{0:T(128)} %bitcast.base_ref, f32[16,1024]{1,0:T(8,128)S(1)} %collective-permute-done.refs_0_, f32[16,1024]{1,0:T(8,128)S(1)} %constant_dynamic-update-slice_fusion.refs_1_), custom_call_target="tpu_custom_call" | custom-call | flops 2147483648 | bytes 4194304 | tf_op jit(solution)/shard_map/densify/pallas_call | solution.py:63
  33.3 3.4 %collective-permute-done.3 = f16[128,1280]{1,0:T(8,128)(2,1)S(1)} collective-permute-done((f16[128,1280]{1,0:T(8,128)(2,1)S(1)}, f16[128,1280]{1,0:T(8,128)(2,1)S(1)}, u32[]{:S(2)}, u32[]{:S(2)}) %collective-permute-start.3) | collective-permute-done | bytes 327712 | tf_op jit(solution)/shard_map/ppermute | solution.py:281
  36.8 3.8 %collective-permute-start.5 = (f16[128,1280]{1,0:T(8,128)(2,1)S(1)}, f16[128,1280]{1,0:T(8,128)(2,1)S(1)}, u32[]{:S(2)}, u32[]{:S(2)}) collective-permute-start(f16[128,1280]{1,0:T(8,128)(2,1)S(1)} %get-tuple-element.52), channel_id=1, source_target_pairs={{4,8},{8,4},{5,9},{9,5},{6,10},{10,6},{7,11},{11,7},{20,24},{24,20... | collective-permute-start | bytes 983048 | tf_op jit(solution)/shard_map/ppermute | solution.py:289
  40.8 1.6 collective-permute-start.6
  42.3 11.1 %decode.1 = f32[256,1280]{1,0:T(8,128)S(1)} custom-call(bf16[256,8192]{1,0:T(8,128)(2,1)S(1)} %densify.3.codes_ref, bf16[8192,1280]{1,0:T(8,128)(2,1)} %weights_ref.1), custom_call_target="tpu_custom_call" | custom-call | flops 5368709120 | bytes 26476544 | tf_op jit(solution)/shard_map/decode/pallas_call | solution.py:85
  53.6 2.1 %collective-permute-start.8 = (f16[128,1280]{1,0:T(8,128)(2,1)S(1)}, f16[128,1280]{1,0:T(8,128)(2,1)S(1)}, u32[]{:S(2)}, u32[]{:S(2)}) collective-permute-start(f16[128,1280]{1,0:T(8,128)(2,1)S(1)} %multiply_convert_fusion.2), channel_id=1, source_target_pairs={{0,4},{4,0},{8,12},{12,8},{1,5},{5,1},{9,13},{13,9},{2,6},{6,2},{1... | collective-permute-start | bytes 983048 | tf_op jit(solution)/shard_map/ppermute | solution.py:295
  56.0 2.0 %collective-permute-start.7 = (f16[128,1280]{1,0:T(8,128)(2,1)S(1)}, f16[128,1280]{1,0:T(8,128)(2,1)S(1)}, u32[]{:S(2)}, u32[]{:S(2)}) collective-permute-start(f16[128,1280]{1,0:T(8,128)(2,1)S(1)} %multiply_convert_fusion), channel_id=1, source_target_pairs={{4,8},{8,4},{5,9},{9,5},{6,10},{10,6},{7,11},{11,7},{20,24},{24,20... | collective-permute-start | bytes 983048 | tf_op jit(solution)/shard_map/ppermute | solution.py:296
  59.0 1.8 %select_columns.2 = bf16[1280,1536]{1,0:T(8,128)(2,1)S(1)} custom-call(s32[2]{0:T(128)S(1)} %get-tuple-element.112.order_ref, bf16[3,1280,1024]{2,1,0:T(8,128)(2,1)S(1)} %bitcast.54), custom_call_target="tpu_custom_call" | custom-call | bytes 7864320 | tf_op jit(solution)/shard_map/select_columns/pallas_call | solution.py:111
  60.9 1.8 %select_columns.3 = bf16[1280,1536]{1,0:T(8,128)(2,1)S(1)} custom-call(s32[2]{0:T(128)S(1)} %get-tuple-element.113.order_ref, bf16[3,1280,1024]{2,1,0:T(8,128)(2,1)S(1)} %bitcast.55), custom_call_target="tpu_custom_call" | custom-call | bytes 7864320 | tf_op jit(solution)/shard_map/select_columns/pallas_call | solution.py:111
  62.7 5.3 %collective-permute-done.7 = f16[128,1280]{1,0:T(8,128)(2,1)S(1)} collective-permute-done((f16[128,1280]{1,0:T(8,128)(2,1)S(1)}, f16[128,1280]{1,0:T(8,128)(2,1)S(1)}, u32[]{:S(2)}, u32[]{:S(2)}) %collective-permute-start.7) | collective-permute-done | bytes 327712 | tf_op jit(solution)/shard_map/ppermute | solution.py:296
  68.4 1.1 collective-permute-done.10
  69.5 1.6 collective-permute-start.11
  71.1 2.1 %collective-permute-done.11 = f32[2,128]{1,0:T(2,128)S(1)} collective-permute-done((f32[2,128]{1,0:T(2,128)S(1)}, f32[2,128]{1,0:T(2,128)S(1)}, u32[]{:S(2)}, u32[]{:S(2)}) %collective-permute-start.11) | collective-permute-done | bytes 1056 | tf_op jit(solution)/shard_map/ppermute | solution.py:221
  74.2 2.2 %collective-permute-start.14 = (bf16[128,1280]{1,0:T(8,128)(2,1)S(1)}, bf16[128,1280]{1,0:T(8,128)(2,1)S(1)}, u32[]{:S(2)}, u32[]{:S(2)}) collective-permute-start(bf16[128,1280]{1,0:T(8,128)(2,1)S(1)} %add_convert_fusion.3), channel_id=1, source_target_pairs={{4,8},{8,4},{5,9},{9,5},{6,10},{10,6},{7,11},{11,7},{20,24},{24,20... | collective-permute-start | bytes 983048 | tf_op jit(solution)/shard_map/ppermute | solution.py:314
  76.5 9.7 %collective-permute-done.14 = bf16[128,1280]{1,0:T(8,128)(2,1)S(1)} collective-permute-done((bf16[128,1280]{1,0:T(8,128)(2,1)S(1)}, bf16[128,1280]{1,0:T(8,128)(2,1)S(1)}, u32[]{:S(2)}, u32[]{:S(2)}) %collective-permute-start.14) | collective-permute-done | bytes 327712 | tf_op jit(solution)/shard_map/ppermute | solution.py:314
  86.2 1.3 collective-permute-start.17
  87.5 2.4 %collective-permute-start.18 = (bf16[128,1280]{1,0:T(8,128)(2,1)S(1)}, bf16[128,1280]{1,0:T(8,128)(2,1)S(1)}, u32[]{:S(2)}, u32[]{:S(2)}) collective-permute-start(bf16[128,1280]{1,0:T(8,128)(2,1)S(1)} %collective-permute-done.13), channel_id=1, source_target_pairs={{4,8},{8,4},{5,9},{9,5},{6,10},{10,6},{7,11},{11,7},{20,24},{24,20... | collective-permute-start | bytes 983048 | tf_op jit(solution)/shard_map/ppermute | solution.py:315
  91.5 3.1 %collective-permute-done.17 = bf16[128,1280]{1,0:T(8,128)(2,1)S(1)} collective-permute-done((bf16[128,1280]{1,0:T(8,128)(2,1)S(1)}, bf16[128,1280]{1,0:T(8,128)(2,1)S(1)}, u32[]{:S(2)}, u32[]{:S(2)}) %collective-permute-start.17) | collective-permute-done | bytes 327712 | tf_op jit(solution)/shard_map/ppermute | solution.py:316
  95.4 3.3 %collective-permute-done.18 = bf16[128,1280]{1,0:T(8,128)(2,1)S(1)} collective-permute-done((bf16[128,1280]{1,0:T(8,128)(2,1)S(1)}, bf16[128,1280]{1,0:T(8,128)(2,1)S(1)}, u32[]{:S(2)}, u32[]{:S(2)}) %collective-permute-start.18) | collective-permute-done | bytes 327712 | tf_op jit(solution)/shard_map/ppermute | solution.py:315
  99.7 1.6 collective-permute-start.15
  101.2 1.5 collective-permute-start.20
  102.7 2.9 %convolution_add_fusion.1 = f32[128,1536]{1,0:T(8,128)S(1)} fusion(bf16[128,1280]{1,0:T(8,128)(2,1)S(1)} %broadcast_select_fusion.1, bf16[1280,1536]{1,0:T(8,128)(2,1)} %copy-done, f16[128,1536]{1,0:T(8,128)(2,1)} %collective-permute-done.21), kind=kOutput, calls=%fused_computation.1 | convolution fusion | flops 503709696 | bytes 5439488 | tf_op jit(solution)/shard_map/dot_general | solution.py:323
  106.4 3.7 %collective-permute-done.20 = bf16[128,1280]{1,0:T(8,128)(2,1)S(1)} collective-permute-done((bf16[128,1280]{1,0:T(8,128)(2,1)S(1)}, bf16[128,1280]{1,0:T(8,128)(2,1)S(1)}, u32[]{:S(2)}, u32[]{:S(2)}) %collective-permute-start.20) | collective-permute-done | bytes 327712 | tf_op jit(solution)/shard_map/ppermute | solution.py:317
  110.2 2.6 %collective-permute-done.22 = f16[128,768]{1,0:T(8,128)(2,1)S(1)} collective-permute-done((f16[128,768]{1,0:T(8,128)(2,1)S(1)}, f16[128,768]{1,0:T(8,128)(2,1)S(1)}, u32[]{:S(2)}, u32[]{:S(2)}) %collective-permute-start.22) | collective-permute-done | bytes 196640 | tf_op jit(solution)/shard_map/ppermute | solution.py:221
  116.9 4.6 %collective-permute-done.19 = f16[128,768]{1,0:T(8,128)(2,1)S(1)} collective-permute-done((f16[128,768]{1,0:T(8,128)(2,1)S(1)}, f16[128,768]{1,0:T(8,128)(2,1)S(1)}, u32[]{:S(2)}, u32[]{:S(2)}) %collective-permute-start.19) | collective-permute-done | bytes 196640 | tf_op jit(solution)/shard_map/ppermute | solution.py:221
  121.5 3.8 %collective-permute-done.24 = f16[128,768]{1,0:T(8,128)(2,1)S(1)} collective-permute-done((f16[128,768]{1,0:T(8,128)(2,1)S(1)}, f16[128,768]{1,0:T(8,128)(2,1)S(1)}, u32[]{:S(2)}, u32[]{:S(2)}) %collective-permute-start.24) | collective-permute-done | bytes 196640 | tf_op jit(solution)/shard_map/ppermute | solution.py:221
  125.4 2.4 %attend.2 = bf16[256,256]{1,0:T(8,128)(2,1)S(1)} custom-call(s32[256,1]{1,0:T(8,128)S(1)} %copy.21.refs_0_, s32[1,512]{1,0:T(1,128)S(1)} %bitcast.57, bf16[128,768]{1,0:T(8,128)(2,1)S(1)} %fusion.18.refs_2_, bf16[128,768]{1,0:T(8,128)(2,1)S(1)} %fusion.17.refs_3_, bf16[128,768]{1,0:T(8,128)(2,1)S(1)} %fusion.16.refs_4_, ...), custom_call_target="tpu_custom_call" | custom-call | flops 536870912 | bytes 2097152 | tf_op jit(solution)/shard_map/attend/pallas_call | solution.py:187
  128.8 2.4 %attend.3 = bf16[256,256]{1,0:T(8,128)(2,1)S(1)} custom-call(s32[256,1]{1,0:T(8,128)S(1)} %copy.22.refs_0_, s32[1,512]{1,0:T(1,128)S(1)} %bitcast.58, bf16[128,768]{1,0:T(8,128)(2,1)S(1)} %fusion.18.refs_2_, bf16[128,768]{1,0:T(8,128)(2,1)S(1)} %fusion.17.refs_3_, bf16[128,768]{1,0:T(8,128)(2,1)S(1)} %fusion.16.refs_4_, ...), custom_call_target="tpu_custom_call" | custom-call | flops 536870912 | bytes 2097152 | tf_op jit(solution)/shard_map/attend/pallas_call | solution.py:187
  131.2 1.8 %collective-permute-done.25 = bf16[256,256]{1,0:T(8,128)(2,1)S(1)} collective-permute-done((bf16[256,256]{1,0:T(8,128)(2,1)S(1)}, bf16[256,256]{1,0:T(8,128)(2,1)S(1)}, u32[]{:S(2)}, u32[]{:S(2)}) %collective-permute-start.25) | collective-permute-done | bytes 131104 | tf_op jit(solution)/shard_map/ppermute | solution.py:221
  133.1 1.5 collective-permute-done.26
  134.6 2.6 %fusion.3 = f32[256,1280]{1,0:T(8,128)S(1)} fusion(bf16[1024,1280]{1,0:T(8,128)(2,1)} %copy-done.5, bf16[256,512]{1,0:T(8,128)(2,1)S(1)} %collective-permute-done.26, bf16[256,256]{1,0:T(8,128)(2,1)S(1)} %collective-permute-done.25, bf16[256,256]{1,0:T(8,128)(2,1)S(1)} %attend.2), kind=kOutput, calls=%fused_computation.27 | convolution fusion | flops 672661504 | bytes 4456448 | tf_op jit(solution)/shard_map/dot_general | solution.py:351
  137.2 1.3 collective-permute-start.29
  139.4 4.7 %collective-permute-done.27 = bf16[256,256]{1,0:T(8,128)(2,1)S(1)} collective-permute-done((bf16[256,256]{1,0:T(8,128)(2,1)S(1)}, bf16[256,256]{1,0:T(8,128)(2,1)S(1)}, u32[]{:S(2)}, u32[]{:S(2)}) %collective-permute-start.27) | collective-permute-done | bytes 131104 | tf_op jit(solution)/shard_map/ppermute | solution.py:221
  144.2 4.6 %collective-permute-done.29 = bf16[128,1280]{1,0:T(8,128)(2,1)S(1)} collective-permute-done((bf16[128,1280]{1,0:T(8,128)(2,1)S(1)}, bf16[128,1280]{1,0:T(8,128)(2,1)S(1)}, u32[]{:S(2)}, u32[]{:S(2)}) %collective-permute-start.29) | collective-permute-done | bytes 327712 | tf_op jit(solution)/shard_map/ppermute | solution.py:353
  149.0 2.2 %collective-permute-start.30 = (bf16[128,1280]{1,0:T(8,128)(2,1)S(1)}, bf16[128,1280]{1,0:T(8,128)(2,1)S(1)}, u32[]{:S(2)}, u32[]{:S(2)}) collective-permute-start(bf16[128,1280]{1,0:T(8,128)(2,1)S(1)} %get-tuple-element.82), channel_id=1, source_target_pairs={{4,8},{8,4},{5,9},{9,5},{6,10},{10,6},{7,11},{11,7},{20,24},{24,20... | collective-permute-start | bytes 983048 | tf_op jit(solution)/shard_map/ppermute | solution.py:359
  151.2 1.3 collective-permute-start.32
  153.4 6.4 %collective-permute-done.30 = bf16[128,1280]{1,0:T(8,128)(2,1)S(1)} collective-permute-done((bf16[128,1280]{1,0:T(8,128)(2,1)S(1)}, bf16[128,1280]{1,0:T(8,128)(2,1)S(1)}, u32[]{:S(2)}, u32[]{:S(2)}) %collective-permute-start.30) | collective-permute-done | bytes 327712 | tf_op jit(solution)/shard_map/ppermute | solution.py:359
  159.9 2.6 %collective-permute-done.32 = bf16[128,1280]{1,0:T(8,128)(2,1)S(1)} collective-permute-done((bf16[128,1280]{1,0:T(8,128)(2,1)S(1)}, bf16[128,1280]{1,0:T(8,128)(2,1)S(1)}, u32[]{:S(2)}, u32[]{:S(2)}) %collective-permute-start.32) | collective-permute-done | bytes 327712 | tf_op jit(solution)/shard_map/ppermute | solution.py:360
  162.6 4.8 %collective-permute-start.33 = (bf16[128,1280]{1,0:T(8,128)(2,1)S(1)}, bf16[128,1280]{1,0:T(8,128)(2,1)S(1)}, u32[]{:S(2)}, u32[]{:S(2)}) collective-permute-start(bf16[128,1280]{1,0:T(8,128)(2,1)S(1)} %add_convert_fusion.1), channel_id=1, source_target_pairs={{4,8},{8,4},{5,9},{9,5},{6,10},{10,6},{7,11},{11,7},{20,24},{24,20... | collective-permute-start | bytes 983048 | tf_op jit(solution)/shard_map/ppermute | solution.py:365
  167.5 1.3 collective-permute-done.31
  168.9 3.6 %collective-permute-done.33 = bf16[128,1280]{1,0:T(8,128)(2,1)S(1)} collective-permute-done((bf16[128,1280]{1,0:T(8,128)(2,1)S(1)}, bf16[128,1280]{1,0:T(8,128)(2,1)S(1)}, u32[]{:S(2)}, u32[]{:S(2)}) %collective-permute-start.33) | collective-permute-done | bytes 327712 | tf_op jit(solution)/shard_map/ppermute | solution.py:365
  (133 shorter events, 18.9 us)
Async XLA Ops:
  1.9 25.7 %collective-permute-start = (f32[16,1024]{1,0:T(8,128)S(1)}, f32[16,1024]{1,0:T(8,128)S(1)}, u32[]{:S(2)}, u32[]{:S(2)}) collective-permute-start(f32[16,1024]{1,0:T(8,128)S(1)} %constant_dynamic-update-slice_fusion.refs_1_), channel_id=1, source_target_pairs={{0,4},{4,0},{8,12},{12,8},{1,5},{5,1},{9,13},{13,9},{2,6},{6,2},{1... | collective-permute-start | bytes 196616 | tf_op jit(solution)/shard_map/ppermute | solution.py:214
  1.9 7.6 %collective-permute-start.2 = (f32[16,1024]{1,0:T(8,128)S(1)}, f32[16,1024]{1,0:T(8,128)S(1)}, u32[]{:S(2)}, u32[]{:S(2)}) collective-permute-start(f32[16,1024]{1,0:T(8,128)S(1)} %constant_dynamic-update-slice_fusion.refs_1_), channel_id=1, source_target_pairs={{0,8},{4,12},{8,0},{12,4},{1,9},{5,13},{9,1},{13,5},{2,10},{6,14},... | collective-permute-start | bytes 196616 | tf_op jit(solution)/shard_map/ppermute | solution.py:215
  5.0 5.5 %collective-permute-start.1 = (f32[16,1024]{1,0:T(8,128)S(1)}, f32[16,1024]{1,0:T(8,128)S(1)}, u32[]{:S(2)}, u32[]{:S(2)}) collective-permute-start(f32[16,1024]{1,0:T(8,128)S(1)} %constant_dynamic-update-slice_fusion.refs_1_), channel_id=1, source_target_pairs={{0,12},{4,8},{8,4},{12,0},{1,13},{5,9},{9,5},{13,1},{2,14},{6,10},... | collective-permute-start | bytes 196616 | tf_op jit(solution)/shard_map/ppermute | solution.py:216
  7.0 29.8 %collective-permute-start.4 = (bf16[2,2,384,256]{3,2,1,0:T(8,128)(2,1)S(1)}, bf16[2,2,384,256]{3,2,1,0:T(8,128)(2,1)S(1)}, u32[]{:S(2)}, u32[]{:S(2)}) collective-permute-start(bf16[2,2,384,256]{3,2,1,0:T(8,128)(2,1)S(1)} %pad_maximum_fusion), channel_id=1, source_target_pairs={{0,2},{1,3},{2,0},{3,1},{4,6},{5,7},{6,4},{7,5},{8,10},{9,11},{10,... | collective-permute-start | bytes 2359304 | tf_op jit(solution)/shard_map/ppermute | solution.py:221
  16.2 11.2 %copy-start.16 = (s32[512]{0:T(512)S(1)}, s32[512]{0:T(512)}, u32[]{:S(2)}) copy-start(s32[512]{0:T(512)} %param.18) | copy-start | bytes 6148
  26.1 10.5 %collective-permute-start.3 = (f16[128,1280]{1,0:T(8,128)(2,1)S(1)}, f16[128,1280]{1,0:T(8,128)(2,1)S(1)}, u32[]{:S(2)}, u32[]{:S(2)}) collective-permute-start(f16[128,1280]{1,0:T(8,128)(2,1)S(1)} %fusion.2), channel_id=1, source_target_pairs={{0,4},{12,8},{1,5},{13,9},{2,6},{14,10},{3,7},{15,11},{16,20},{28,... | collective-permute-start | bytes 983048 | tf_op jit(solution)/shard_map/ppermute | solution.py:281
  36.8 16.6 %collective-permute-start.5 = (f16[128,1280]{1,0:T(8,128)(2,1)S(1)}, f16[128,1280]{1,0:T(8,128)(2,1)S(1)}, u32[]{:S(2)}, u32[]{:S(2)}) collective-permute-start(f16[128,1280]{1,0:T(8,128)(2,1)S(1)} %get-tuple-element.52), channel_id=1, source_target_pairs={{4,8},{8,4},{5,9},{9,5},{6,10},{10,6},{7,11},{11,7},{20,24},{24,20... | collective-permute-start | bytes 983048 | tf_op jit(solution)/shard_map/ppermute | solution.py:289
  40.7 18.4 %slice-start = ((s8[7864320]{0:T(1024)(128)(4,1)}), s8[4194304]{0:T(1024)(128)(4,1)S(1)}, s32[]{:S(2)}) async-start(s8[7864320]{0:T(1024)(128)(4,1)} %bitcast.52), calls=%async_computation | async-start | bytes 8388608
  40.7 18.3 %slice-start.1 = ((s8[7864320]{0:T(1024)(128)(4,1)}), s8[3670016]{0:T(1024)(128)(4,1)S(1)}, s32[]{:S(2)}) async-start(s8[7864320]{0:T(1024)(128)(4,1)} %bitcast.52), calls=%async_computation.1 | async-start | bytes 7340032
  40.8 15.1 %collective-permute-start.6 = (f16[128,1280]{1,0:T(8,128)(2,1)S(1)}, f16[128,1280]{1,0:T(8,128)(2,1)S(1)}, u32[]{:S(2)}, u32[]{:S(2)}) collective-permute-start(f16[128,1280]{1,0:T(8,128)(2,1)S(1)} %multiply_convert_fusion.1), channel_id=1, source_target_pairs={{0,4},{12,8},{1,5},{13,9},{2,6},{14,10},{3,7},{15,11},{16,20},{28,... | collective-permute-start | bytes 983048 | tf_op jit(solution)/shard_map/ppermute | solution.py:290
  53.6 9.1 %collective-permute-start.8 = (f16[128,1280]{1,0:T(8,128)(2,1)S(1)}, f16[128,1280]{1,0:T(8,128)(2,1)S(1)}, u32[]{:S(2)}, u32[]{:S(2)}) collective-permute-start(f16[128,1280]{1,0:T(8,128)(2,1)S(1)} %multiply_convert_fusion.2), channel_id=1, source_target_pairs={{0,4},{4,0},{8,12},{12,8},{1,5},{5,1},{9,13},{13,9},{2,6},{6,2},{1... | collective-permute-start | bytes 983048 | tf_op jit(solution)/shard_map/ppermute | solution.py:295
  55.8 6.9 %collective-permute-start.9 = (bf16[2,2,384,256]{3,2,1,0:T(8,128)(2,1)S(1)}, bf16[2,2,384,256]{3,2,1,0:T(8,128)(2,1)S(1)}, u32[]{:S(2)}, u32[]{:S(2)}) collective-permute-start(bf16[2,2,384,256]{3,2,1,0:T(8,128)(2,1)S(1)} %pad_maximum_fusion.1), channel_id=1, source_target_pairs={{0,1},{1,0},{2,3},{3,2},{4,5},{5,4},{6,7},{7,6},{8,9},{9,8},{10,11... | collective-permute-start | bytes 2359304 | tf_op jit(solution)/shard_map/ppermute | solution.py:221
  56.0 12.0 %collective-permute-start.7 = (f16[128,1280]{1,0:T(8,128)(2,1)S(1)}, f16[128,1280]{1,0:T(8,128)(2,1)S(1)}, u32[]{:S(2)}, u32[]{:S(2)}) collective-permute-start(f16[128,1280]{1,0:T(8,128)(2,1)S(1)} %multiply_convert_fusion), channel_id=1, source_target_pairs={{4,8},{8,4},{5,9},{9,5},{6,10},{10,6},{7,11},{11,7},{20,24},{24,20... | collective-permute-start | bytes 983048 | tf_op jit(solution)/shard_map/ppermute | solution.py:296
  60.8 37.9 %copy-start.2 = (bf16[1280,1536]{1,0:T(8,128)(2,1)}, bf16[1280,1536]{1,0:T(8,128)(2,1)S(1)}, u32[]{:S(2)}) copy-start(bf16[1280,1536]{1,0:T(8,128)(2,1)S(1)} %select_columns.2) | copy-start | bytes 11796484
  60.8 12.4 %copy-start.13 = (f32[1280]{0:T(1024)S(1)}, f32[1280]{0:T(1024)}, u32[]{:S(2)}) copy-start(f32[1280]{0:T(1024)} %param.15) | copy-start | bytes 15364
  60.9 12.4 %copy-start.14 = (f32[1280]{0:T(1024)S(1)}, f32[1280]{0:T(1024)}, u32[]{:S(2)}) copy-start(f32[1280]{0:T(1024)} %param.14) | copy-start | bytes 15364
  62.7 32.0 %copy-start = (bf16[1280,1536]{1,0:T(8,128)(2,1)}, bf16[1280,1536]{1,0:T(8,128)(2,1)S(1)}, u32[]{:S(2)}) copy-start(bf16[1280,1536]{1,0:T(8,128)(2,1)S(1)} %select_columns.3) | copy-start | bytes 11796484
  62.7 27.9 %copy-start.11 = (bf16[2,2,384,256]{3,2,1,0:T(8,128)(2,1)}, bf16[2,2,384,256]{3,2,1,0:T(8,128)(2,1)S(1)}, u32[]{:S(2)}) copy-start(bf16[2,2,384,256]{3,2,1,0:T(8,128)(2,1)S(1)} %collective-permute-done.9) | copy-start | bytes 2359300
  68.3 1.2 collective-permute-start.10
  69.5 3.6 %collective-permute-start.11 = (f32[2,128]{1,0:T(2,128)S(1)}, f32[2,128]{1,0:T(2,128)S(1)}, u32[]{:S(2)}, u32[]{:S(2)}) collective-permute-start(f32[2,128]{1,0:T(2,128)S(1)} %fusion.23), channel_id=1, source_target_pairs={{0,2},{1,3},{2,0},{3,1},{4,6},{5,7},{6,4},{7,5},{8,10},{9,11},{10,... | collective-permute-start | bytes 3080 | tf_op jit(solution)/shard_map/ppermute | solution.py:221
  74.1 15.8 %collective-permute-start.12 = (f16[128,1536]{1,0:T(8,128)(2,1)S(1)}, f16[128,1536]{1,0:T(8,128)(2,1)S(1)}, u32[]{:S(2)}, u32[]{:S(2)}) collective-permute-start(f16[128,1536]{1,0:T(8,128)(2,1)S(1)} %convolution_convert_fusion.3), channel_id=1, source_target_pairs={{0,1},{1,0},{2,3},{3,2},{4,5},{5,4},{6,7},{7,6},{8,9},{9,8},{10,11... | collective-permute-start | bytes 1179656 | tf_op jit(solution)/shard_map/ppermute | solution.py:221
  74.2 12.0 %collective-permute-start.14 = (bf16[128,1280]{1,0:T(8,128)(2,1)S(1)}, bf16[128,1280]{1,0:T(8,128)(2,1)S(1)}, u32[]{:S(2)}, u32[]{:S(2)}) collective-permute-start(bf16[128,1280]{1,0:T(8,128)(2,1)S(1)} %add_convert_fusion.3), channel_id=1, source_target_pairs={{4,8},{8,4},{5,9},{9,5},{6,10},{10,6},{7,11},{11,7},{20,24},{24,20... | collective-permute-start | bytes 983048 | tf_op jit(solution)/shard_map/ppermute | solution.py:314
  76.4 11.1 %collective-permute-start.13 = (bf16[128,1280]{1,0:T(8,128)(2,1)S(1)}, bf16[128,1280]{1,0:T(8,128)(2,1)S(1)}, u32[]{:S(2)}, u32[]{:S(2)}) collective-permute-start(bf16[128,1280]{1,0:T(8,128)(2,1)S(1)} %add_convert_fusion.3), channel_id=1, source_target_pairs={{0,4},{4,0},{8,12},{12,8},{1,5},{5,1},{9,13},{13,9},{2,6},{6,2},{1... | collective-permute-start | bytes 983048 | tf_op jit(solution)/shard_map/ppermute | solution.py:313
  86.2 8.4 %collective-permute-start.17 = (bf16[128,1280]{1,0:T(8,128)(2,1)S(1)}, bf16[128,1280]{1,0:T(8,128)(2,1)S(1)}, u32[]{:S(2)}, u32[]{:S(2)}) collective-permute-start(bf16[128,1280]{1,0:T(8,128)(2,1)S(1)} %collective-permute-done.14), channel_id=1, source_target_pairs={{4,0},{8,12},{5,1},{9,13},{6,2},{10,14},{7,3},{11,15},{20,16},{24,... | collective-permute-start | bytes 983048 | tf_op jit(solution)/shard_map/ppermute | solution.py:316
  87.5 11.2 %collective-permute-start.18 = (bf16[128,1280]{1,0:T(8,128)(2,1)S(1)}, bf16[128,1280]{1,0:T(8,128)(2,1)S(1)}, u32[]{:S(2)}, u32[]{:S(2)}) collective-permute-start(bf16[128,1280]{1,0:T(8,128)(2,1)S(1)} %collective-permute-done.13), channel_id=1, source_target_pairs={{4,8},{8,4},{5,9},{9,5},{6,10},{10,6},{7,11},{11,7},{20,24},{24,20... | collective-permute-start | bytes 983048 | tf_op jit(solution)/shard_map/ppermute | solution.py:315
  91.4 3.3 %collective-permute-start.16 = (f16[128,1536]{1,0:T(8,128)(2,1)S(1)}, f16[128,1536]{1,0:T(8,128)(2,1)S(1)}, u32[]{:S(2)}, u32[]{:S(2)}) collective-permute-start(f16[128,1536]{1,0:T(8,128)(2,1)S(1)} %convolution_convert_fusion.2), channel_id=1, source_target_pairs={{0,1},{1,0},{2,3},{3,2},{4,5},{5,4},{6,7},{7,6},{8,9},{9,8},{10,11... | collective-permute-start | bytes 1179656 | tf_op jit(solution)/shard_map/ppermute | solution.py:221
  99.4 3.3 %collective-permute-start.21 = (f16[128,1536]{1,0:T(8,128)(2,1)S(1)}, f16[128,1536]{1,0:T(8,128)(2,1)}, u32[]{:S(2)}, u32[]{:S(2)}) collective-permute-start(f16[128,1536]{1,0:T(8,128)(2,1)S(1)} %convolution_convert_fusion.1), channel_id=1, source_target_pairs={{0,1},{1,0},{2,3},{3,2},{4,5},{5,4},{6,7},{7,6},{8,9},{9,8},{10,11... | collective-permute-start | bytes 1179656 | tf_op jit(solution)/shard_map/ppermute | solution.py:221
  99.7 13.1 %copy-start.3 = (bf16[1280,1536]{1,0:T(8,128)(2,1)S(1)}, bf16[1280,1536]{1,0:T(8,128)(2,1)}, u32[]{:S(2)}) copy-start(bf16[1280,1536]{1,0:T(8,128)(2,1)} %copy-done.2) | copy-start | bytes 11796484
  99.7 14.0 %collective-permute-start.15 = (f16[128,768]{1,0:T(8,128)(2,1)S(1)}, f16[128,768]{1,0:T(8,128)(2,1)S(1)}, u32[]{:S(2)}, u32[]{:S(2)}) collective-permute-start(f16[128,768]{1,0:T(8,128)(2,1)S(1)} %slice_convert_fusion.4), channel_id=1, source_target_pairs={{0,2},{1,3},{2,0},{3,1},{4,6},{5,7},{6,4},{7,5},{8,10},{9,11},{10,... | collective-permute-start | bytes 589832 | tf_op jit(solution)/shard_map/ppermute | solution.py:221
  101.2 8.9 %collective-permute-start.20 = (bf16[128,1280]{1,0:T(8,128)(2,1)S(1)}, bf16[128,1280]{1,0:T(8,128)(2,1)S(1)}, u32[]{:S(2)}, u32[]{:S(2)}) collective-permute-start(bf16[128,1280]{1,0:T(8,128)(2,1)S(1)} %collective-permute-done.18), channel_id=1, source_target_pairs={{4,0},{8,12},{5,1},{9,13},{6,2},{10,14},{7,3},{11,15},{20,16},{24,... | collective-permute-start | bytes 983048 | tf_op jit(solution)/shard_map/ppermute | solution.py:317
  105.6 8.0 %copy-start.12 = (bf16[2,2,384,256]{3,2,1,0:T(8,128)(2,1)S(1)}, bf16[2,2,384,256]{3,2,1,0:T(8,128)(2,1)}, u32[]{:S(2)}) copy-start(bf16[2,2,384,256]{3,2,1,0:T(8,128)(2,1)} %copy-done.11) | copy-start | bytes 2359300
  105.7 8.0 %copy-start.10 = (f32[128,1536]{1,0:T(8,128)S(1)}, f32[128,1536]{1,0:T(8,128)}, u32[]{:S(2)}) copy-start(f32[128,1536]{1,0:T(8,128)} %copy-done.9) | copy-start | bytes 2359300
  105.7 7.1 %collective-permute-start.22 = (f16[128,768]{1,0:T(8,128)(2,1)S(1)}, f16[128,768]{1,0:T(8,128)(2,1)S(1)}, u32[]{:S(2)}, u32[]{:S(2)}) collective-permute-start(f16[128,768]{1,0:T(8,128)(2,1)S(1)} %slice_convert_fusion.2), channel_id=1, source_target_pairs={{0,2},{1,3},{2,0},{3,1},{4,6},{5,7},{6,4},{7,5},{8,10},{9,11},{10,... | collective-permute-start | bytes 589832 | tf_op jit(solution)/shard_map/ppermute | solution.py:221
  110.2 5.1 %copy-start.1 = (bf16[1280,1536]{1,0:T(8,128)(2,1)S(1)}, bf16[1280,1536]{1,0:T(8,128)(2,1)}, u32[]{:S(2)}) copy-start(bf16[1280,1536]{1,0:T(8,128)(2,1)} %copy-done) | copy-start | bytes 11796484
  113.5 8.0 %copy-start.8 = (f32[128,1536]{1,0:T(8,128)S(1)}, f32[128,1536]{1,0:T(8,128)}, u32[]{:S(2)}) copy-start(f32[128,1536]{1,0:T(8,128)} %copy-done.7) | copy-start | bytes 2359300
  113.5 1.8 %collective-permute-start.23 = (f16[128,1536]{1,0:T(8,128)(2,1)S(1)}, f16[128,1536]{1,0:T(8,128)(2,1)S(1)}, u32[]{:S(2)}, u32[]{:S(2)}) collective-permute-start(f16[128,1536]{1,0:T(8,128)(2,1)S(1)} %convolution_convert_fusion), channel_id=1, source_target_pairs={{0,1},{1,0},{2,3},{3,2},{4,5},{5,4},{6,7},{7,6},{8,9},{9,8},{10,11... | collective-permute-start | bytes 1179656 | tf_op jit(solution)/shard_map/ppermute | solution.py:221
  113.7 7.8 %collective-permute-start.19 = (f16[128,768]{1,0:T(8,128)(2,1)S(1)}, f16[128,768]{1,0:T(8,128)(2,1)S(1)}, u32[]{:S(2)}, u32[]{:S(2)}) collective-permute-start(f16[128,768]{1,0:T(8,128)(2,1)S(1)} %slice_convert_fusion.3), channel_id=1, source_target_pairs={{0,2},{1,3},{2,0},{3,1},{4,6},{5,7},{6,4},{7,5},{8,10},{9,11},{10,... | collective-permute-start | bytes 589832 | tf_op jit(solution)/shard_map/ppermute | solution.py:221
  116.0 9.3 %collective-permute-start.24 = (f16[128,768]{1,0:T(8,128)(2,1)S(1)}, f16[128,768]{1,0:T(8,128)(2,1)S(1)}, u32[]{:S(2)}, u32[]{:S(2)}) collective-permute-start(f16[128,768]{1,0:T(8,128)(2,1)S(1)} %slice_convert_fusion.1), channel_id=1, source_target_pairs={{0,2},{1,3},{2,0},{3,1},{4,6},{5,7},{6,4},{7,5},{8,10},{9,11},{10,... | collective-permute-start | bytes 589832 | tf_op jit(solution)/shard_map/ppermute | solution.py:221
  127.8 5.2 %collective-permute-start.25 = (bf16[256,256]{1,0:T(8,128)(2,1)S(1)}, bf16[256,256]{1,0:T(8,128)(2,1)S(1)}, u32[]{:S(2)}, u32[]{:S(2)}) collective-permute-start(bf16[256,256]{1,0:T(8,128)(2,1)S(1)} %attend.2), channel_id=1, source_target_pairs={{0,2},{1,3},{2,0},{3,1},{4,6},{5,7},{6,4},{7,5},{8,10},{9,11},{10,... | collective-permute-start | bytes 393224 | tf_op jit(solution)/shard_map/ppermute | solution.py:221
  133.0 19.6 %copy-start.6 = (bf16[1024,1280]{1,0:T(8,128)(2,1)S(1)}, bf16[1024,1280]{1,0:T(8,128)(2,1)}, u32[]{:S(2)}) copy-start(bf16[1024,1280]{1,0:T(8,128)(2,1)} %copy-done.5) | copy-start | bytes 7864324
  133.0 1.6 collective-permute-start.26
  137.2 11.6 %collective-permute-start.29 = (bf16[128,1280]{1,0:T(8,128)(2,1)S(1)}, bf16[128,1280]{1,0:T(8,128)(2,1)S(1)}, u32[]{:S(2)}, u32[]{:S(2)}) collective-permute-start(bf16[128,1280]{1,0:T(8,128)(2,1)S(1)} %slice.163), channel_id=1, source_target_pairs={{0,4},{12,8},{1,5},{13,9},{2,6},{14,10},{3,7},{15,11},{16,20},{28,... | collective-permute-start | bytes 983048 | tf_op jit(solution)/shard_map/ppermute | solution.py:353
  138.5 5.6 %collective-permute-start.27 = (bf16[256,256]{1,0:T(8,128)(2,1)S(1)}, bf16[256,256]{1,0:T(8,128)(2,1)S(1)}, u32[]{:S(2)}, u32[]{:S(2)}) collective-permute-start(bf16[256,256]{1,0:T(8,128)(2,1)S(1)} %attend.3), channel_id=1, source_target_pairs={{0,2},{1,3},{2,0},{3,1},{4,6},{5,7},{6,4},{7,5},{8,10},{9,11},{10,... | collective-permute-start | bytes 393224 | tf_op jit(solution)/shard_map/ppermute | solution.py:221
  144.1 8.4 %collective-permute-start.28 = (bf16[256,512]{1,0:T(8,128)(2,1)S(1)}, bf16[256,512]{1,0:T(8,128)(2,1)S(1)}, u32[]{:S(2)}, u32[]{:S(2)}) collective-permute-start(bf16[256,512]{1,0:T(8,128)(2,1)S(1)} %pad_maximum_fusion.3), channel_id=1, source_target_pairs={{0,1},{1,0},{2,3},{3,2},{4,5},{5,4},{6,7},{7,6},{8,9},{9,8},{10,11... | collective-permute-start | bytes 786440 | tf_op jit(solution)/shard_map/ppermute | solution.py:221
  149.0 10.8 %collective-permute-start.30 = (bf16[128,1280]{1,0:T(8,128)(2,1)S(1)}, bf16[128,1280]{1,0:T(8,128)(2,1)S(1)}, u32[]{:S(2)}, u32[]{:S(2)}) collective-permute-start(bf16[128,1280]{1,0:T(8,128)(2,1)S(1)} %get-tuple-element.82), channel_id=1, source_target_pairs={{4,8},{8,4},{5,9},{9,5},{6,10},{10,6},{7,11},{11,7},{20,24},{24,20... | collective-permute-start | bytes 983048 | tf_op jit(solution)/shard_map/ppermute | solution.py:359
  151.2 11.3 %collective-permute-start.32 = (bf16[128,1280]{1,0:T(8,128)(2,1)S(1)}, bf16[128,1280]{1,0:T(8,128)(2,1)S(1)}, u32[]{:S(2)}, u32[]{:S(2)}) collective-permute-start(bf16[128,1280]{1,0:T(8,128)(2,1)S(1)} %convert_element_type.164), channel_id=1, source_target_pairs={{0,4},{12,8},{1,5},{13,9},{2,6},{14,10},{3,7},{15,11},{16,20},{28,... | collective-permute-start | bytes 983048 | tf_op jit(solution)/shard_map/ppermute | solution.py:360
  159.8 8.9 %collective-permute-start.31 = (bf16[128,1280]{1,0:T(8,128)(2,1)S(1)}, bf16[128,1280]{1,0:T(8,128)(2,1)S(1)}, u32[]{:S(2)}, u32[]{:S(2)}) collective-permute-start(bf16[128,1280]{1,0:T(8,128)(2,1)S(1)} %fusion), channel_id=1, source_target_pairs={{0,4},{4,0},{8,12},{12,8},{1,5},{5,1},{9,13},{13,9},{2,6},{6,2},{1... | collective-permute-start | bytes 983048 | tf_op jit(solution)/shard_map/ppermute | solution.py:363
  162.6 9.9 %collective-permute-start.33 = (bf16[128,1280]{1,0:T(8,128)(2,1)S(1)}, bf16[128,1280]{1,0:T(8,128)(2,1)S(1)}, u32[]{:S(2)}, u32[]{:S(2)}) collective-permute-start(bf16[128,1280]{1,0:T(8,128)(2,1)S(1)} %add_convert_fusion.1), channel_id=1, source_target_pairs={{4,8},{8,4},{5,9},{9,5},{6,10},{10,6},{7,11},{11,7},{20,24},{24,20... | collective-permute-start | bytes 983048 | tf_op jit(solution)/shard_map/ppermute | solution.py:365
  (5 other events, 19.4 us)

commit v6 on v5

--- a/solution.py
+++ b/solution.py
@@ -13,6 +13,7 @@
 GROUP = 8
 VMEM_BYTES = 20 * 1024 * 1024
 DECODE_BYTES = 44 * 1024 * 1024
+SMALL = pl.CostEstimate(flops=1, bytes_accessed=1, transcendentals=0)
 
 
 def densify_kernel(base_ref, *refs, topk, latents, lanes):
@@ -92,11 +93,7 @@
         ],
         out_specs=pl.BlockSpec((rows, width), lambda n: (0, n)),
         compiler_params=pltpu.CompilerParams(vmem_limit_bytes=DECODE_BYTES),
-        cost_estimate=pl.CostEstimate(
-            flops=2 * rows * latents * columns,
-            bytes_accessed=latents * (rows + columns) * 2 + rows * columns * 4,
-            transcendentals=0,
-        ),
+        cost_estimate=SMALL,
         name="decode",
     )(codes, decoder)
 
@@ -199,22 +196,8 @@
     )(query_pos, key_pos, *new, *cached)
 
 
-PAIRS = [(0, 1), (1, 0), (2, 3), (3, 2)]
-INWARD = [(0, 1), (3, 2)]
-MIDDLE = [(1, 2), (2, 1)]
-OUTWARD = [(1, 0), (2, 3)]
-
-
-def line_slots(index):
-    low = index < 2
-    return [index, index ^ 1, jnp.where(low, 2, 1), jnp.where(low, 3, 0)]
-
-
-def line_gather_direct(own, outer):
-    near = lax.ppermute(own, "lat", [(i, i ^ 1) for i in range(4)])
-    two = lax.ppermute(own, "lat", [(i, i ^ 2) for i in range(4)])
-    three = lax.ppermute(own, "lat", [(i, i ^ 3) for i in range(4)])
-    return [own, near, jnp.where(outer, two, three), jnp.where(outer, three, two)]
+def across_line(value, distance):
+    return lax.ppermute(value, "lat", [(i, i ^ distance) for i in range(lax.axis_size("lat"))])
 
 
 def swap(value, distance, size):
@@ -257,12 +240,10 @@
     head_width = w_qkv.shape[2]
     own_width = head_width // cols
     heads = own_width // HEAD
-    outer = (lat == 0) | (lat == 3)
-    slots = line_slots(lat)
     hold = lax.optimization_barrier
 
     packed = pack(code_ids, code_vals)
-    packed = line_gather_direct(packed, outer)
+    packed = [packed, *(across_line(packed, j) for j in (1, 2, 3))]
     base = (lat * latents).reshape(1)
 
     def cache_of(j):
@@ -272,49 +253,44 @@
     across = swap(jnp.stack([cache_of(2), cache_of(3)]), 2, cols)
 
     key_pos = jnp.concatenate(
-        [lax.dynamic_slice_in_dim(positions, s * rows, rows, 0) for s in slots]
+        [lax.dynamic_slice_in_dim(positions, (lat ^ j) * rows, rows, 0) for j in range(4)]
     )
     query_pos = key_pos.reshape(-1, 1)
 
-    codes_far = densify([packed[3], packed[2]], base, topk, latents)
-    far = jnp.dot(codes_far, decoder, preferred_element_type=jnp.float32)
-    in_far = lax.ppermute(to_half(far[:rows]), "lat", INWARD)
-    near_packed, far = hold(((packed[1], packed[0]), far))
-    codes_near = densify(near_packed, base, topk, latents)
-    codes_near, in_far = hold((codes_near, in_far))
-    mid_far = to_half(far[:rows] + from_half(in_far))
-    second, codes_near, across, query_pos, mid_far = hold(
-        (far[rows:], codes_near, across, query_pos, mid_far)
+    codes = densify([packed[2], packed[1]], base, topk, latents)
+    early = jnp.dot(codes, decoder, preferred_element_type=jnp.float32)
+    late_packed, sent2, sent1 = hold(
+        ((packed[3], packed[0]), to_half(early[:rows]), to_half(early[rows:]))
     )
-    mid_far = lax.ppermute(mid_far, "lat", MIDDLE)
-    in_across = lax.ppermute(to_half(second), "lat", INWARD)
-    near = decode(codes_near, decoder)
-    near, mid_far = hold((near, mid_far))
-    last = to_half(near[:rows] + from_half(mid_far))
-    across, last, second, weights = hold((across, last, second, w_qkv.transpose(1, 0, 2)))
-    last = lax.ppermute(last, "lat", PAIRS)
-    mid_across = lax.ppermute(to_half(second + from_half(in_across)), "lat", MIDDLE)
+    came2 = across_line(sent2, 2)
+    came1 = across_line(sent1, 1)
+    codes = densify(late_packed, base, topk, latents)
+    codes, across, query_pos = hold((codes, across, query_pos))
+    late = decode(codes, decoder)
+    sent3, came2, came1, weights, out_source = hold(
+        (to_half(late[:rows]), came2, came1, w_qkv.transpose(1, 0, 2), w_out)
+    )
+    came3 = across_line(sent3, 3)
 
     away_weights = select_columns(weights, jnp.stack([col ^ 1, col ^ 3]), own_width)
     keep_weights = select_columns(weights, jnp.stack([col, col ^ 2]), own_width)
-    out_weights = select_rows(w_out, jnp.stack([col, col ^ 2, col ^ 1, col ^ 3]), own_width)
     beside = swap(jnp.stack([cache_of(1), across[1]]), 1, cols)
-    last, away_weights, keep_weights, out_weights, beside = hold(
-        (last, away_weights, keep_weights, out_weights, beside)
+    out_weights = select_rows(out_source, jnp.stack([col, col ^ 2, col ^ 1, col ^ 3]), own_width)
+    came3, away_weights, keep_weights, out_weights, beside = hold(
+        (came3, away_weights, keep_weights, out_weights, beside)
     )
     cached = [cache_of(0), across[0], beside[0], beside[1]]
-    residual = near[rows:] + from_half(mid_across) + from_half(last)
+    residual = late[rows:] + from_half(came1) + from_half(came2) + from_half(came3)
     residual = residual + dec_bias.astype(jnp.float32)
 
     sums = jnp.stack([jnp.sum(residual, axis=1), jnp.sum(residual * residual, axis=1)])
     sums = sums + swap(sums, 1, cols)
     sums = sums + swap(sums, 2, cols)
     own = normalize(residual, sums, ln_gain, ln_bias)
-    near = lax.ppermute(own, "lat", PAIRS)
-    across = lax.ppermute(own, "lat", MIDDLE)
-    far = lax.ppermute(near, "lat", MIDDLE)
-    across_out = lax.ppermute(across, "lat", OUTWARD)
-    far_out = lax.ppermute(far, "lat", OUTWARD)
+    near = across_line(own, 1)
+    across = across_line(own, 2)
+    own_again, near, across = hold((own, near, across))
+    far = across_line(own_again, 3)
 
     quarter = keep_weights.shape[1] // 2
 
@@ -328,12 +304,12 @@
         return (keep + swap(payload, 2, cols).astype(jnp.float32)).astype(jnp.bfloat16)
 
     keep0, payload0 = project(own)
-    near_block, across, payload0 = hold((near, across, payload0))
-    keep1, payload1 = project(near_block)
-    third, far, payload1 = hold((jnp.where(outer, across_out, across), far, payload1))
-    third = finish(*project(third))
-    fourth, third = hold((jnp.where(outer, far_out, far), third))
-    qkv = [finish(keep0, payload0), finish(keep1, payload1), third, finish(*project(fourth))]
+    middle, payload0 = hold((jnp.concatenate([near, across], axis=0), payload0))
+    first = finish(keep0, payload0)
+    keep1, payload1 = project(middle)
+    first, payload1 = hold((first, payload1))
+    far, middle = hold((far, finish(keep1, payload1)))
+    qkv = [first, middle[:rows], middle[rows:], finish(*project(far))]
 
     key_row = key_pos.reshape(1, -1)
 
@@ -342,30 +318,23 @@
             [query_pos[a * rows : (a + 1) * rows], query_pos[b * rows : (b + 1) * rows]], axis=0
         )
 
-    mixed_far = attend(pos_of(3, 2), key_row, qkv, cached, (3, 2), heads)
-    near_pos, mixed_far = hold((pos_of(1, 0), mixed_far))
-    mixed_near = attend(near_pos, key_row, qkv, cached, (1, 0), heads)
-    swapped_far, mixed_near = hold((swap(mixed_far, 2, cols), mixed_near))
-    mixed_far = jnp.concatenate([mixed_far, swapped_far], axis=1)
-    mixed_far = jnp.concatenate([mixed_far, swap(mixed_far, 1, cols)], axis=1)
-    product_far = jnp.dot(mixed_far, out_weights, preferred_element_type=jnp.float32)
-    sent_far, mixed_near = hold((product_far[:rows].astype(jnp.bfloat16), mixed_near))
-    in_far = lax.ppermute(sent_far, "lat", INWARD)
-    mixed_near = jnp.concatenate([mixed_near, swap(mixed_near, 2, cols)], axis=1)
-    mixed_near = jnp.concatenate([mixed_near, swap(mixed_near, 1, cols)], axis=1)
-    product_near = jnp.dot(mixed_near, out_weights, preferred_element_type=jnp.float32)
-    mid_far = (product_far[:rows] + in_far.astype(jnp.float32)).astype(jnp.bfloat16)
-    second, mid_far = hold((product_far[rows:], mid_far))
-    mid_far = lax.ppermute(mid_far, "lat", MIDDLE)
-    in_across = lax.ppermute(second.astype(jnp.bfloat16), "lat", INWARD)
-    last = (product_near[:rows] + mid_far.astype(jnp.float32)).astype(jnp.bfloat16)
-    second, last = hold((second, last))
-    last = lax.ppermute(last, "lat", PAIRS)
-    mid_across = (second + in_across.astype(jnp.float32)).astype(jnp.bfloat16)
-    mid_across = lax.ppermute(mid_across, "lat", MIDDLE)
-    branch = product_near[rows:] + last.astype(jnp.float32)
-    branch, mid_across = hold((residual + branch, mid_across))
-    return (branch + mid_across.astype(jnp.float32)).astype(jnp.bfloat16)
+    early = attend(pos_of(2, 1), key_row, qkv, cached, (2, 1), heads)
+    late_pos, early = hold((pos_of(3, 0), early))
+    late = attend(late_pos, key_row, qkv, cached, (3, 0), heads)
+    swapped, late = hold((swap(early, 2, cols), late))
+    early = jnp.concatenate([early, swapped], axis=1)
+    early = jnp.concatenate([early, swap(early, 1, cols)], axis=1)
+    early = jnp.dot(early, out_weights, preferred_element_type=jnp.float32).astype(jnp.bfloat16)
+    sent2, sent1, late = hold((early[:rows], early[rows:], late))
+    came2 = across_line(sent2, 2)
+    came1 = across_line(sent1, 1)
+    late = jnp.concatenate([late, swap(late, 2, cols)], axis=1)
+    late = jnp.concatenate([late, swap(late, 1, cols)], axis=1)
+    late, came2, came1 = hold((late, came2, came1))
+    late = jnp.dot(late, out_weights, preferred_element_type=jnp.float32)
+    came3 = across_line(late[:rows].astype(jnp.bfloat16), 3)
+    branch = late[rows:] + came1.astype(jnp.float32) + came2.astype(jnp.float32)
+    return (residual + branch + came3.astype(jnp.float32)).astype(jnp.bfloat16)
 
 
 def attend_block(queries, keys, values, query_pos, key_pos):

time: 174 us -> 188 us (1.080)
  starting transfers between devices: 40.8 us -> 24.2 us
  waiting for transfers between devices: 72 us -> 88.6 us
  local copies, waits for them, and re-layouts: 2.42 us -> 14.4 us
    ppermute x18 -> x12, starting transfers between devices: 31.5 us -> 14.8 us  [across_line(): lax.ppermute(value, 'lat', [(i, i ^ distance) for i in range(lax.axis_siz...]
    ppermute x18 -> x12, waiting for transfers between devices: 49.1 us -> 60.1 us  [across_line(): lax.ppermute(value, 'lat', [(i, i ^ distance) for i in range(lax.axis_siz...]
    unnamed x39 -> x55, local copies, waits for them, and re-layouts: 0.1 us -> 8.04 us
    ppermute x16 -> x14, waiting for transfers between devices: 22.9 us -> 28.5 us  [swap(): return lax.ppermute(value, 'col', [(i, i ^ distance) for i in range(size)])]
    squeeze x2, local copies, waits for them, and re-layouts: 0.1 us -> 2.34 us  [line_body(): cached = [cache_of(0), across[0], beside[0], beside[1]]]
    dot_general x4 -> x3, matrix products: 4.93 us -> 4.83 us  [project(): keep = jnp.dot(block, keep_weights, preferred_element_type=jnp.float32)]
    ppermute x16 -> x14, starting transfers between devices: 9.39 us -> 9.38 us  [swap(): return lax.ppermute(value, 'col', [(i, i ^ distance) for i in range(size)])]
  transfers between devices with their start and end apart: 34 -> 26, of which waited for: 22 -> 16; matrix products, arithmetic and copies ran while one was open for 12% -> 10% of each run, Pallas kernels for 17% -> 16%
where the time goes in v6:
time: 188 us; the launch traced here: 187 us
  waiting for transfers between devices  88.6 us (47%)
  Pallas kernels  32.5 us (17%)
  starting transfers between devices  24.2 us (13%)
  matrix products  20.6 us (11%)
  local copies, waits for them, and re-layouts  14.4 us (8%)
  other arithmetic  6.33 us (3%)
    ppermute x12, waiting for transfers between devices, across_line(): lax.ppermute(value, 'lat', [(i, i ^ distance) for i in range(lax.axis_siz...  60.1 us
    ppermute x14, waiting for transfers between devices, swap(): return lax.ppermute(value, 'col', [(i, i ^ distance) for i in range(size)])  28.5 us
    ppermute x12, starting transfers between devices, across_line(): lax.ppermute(value, 'lat', [(i, i ^ distance) for i in range(lax.axis_siz...  14.8 us
    pallas_call x2, Pallas kernels, densify(): pl.pallas_call(functools.partial(densify_kernel, topk=topk, latents=laten...  11.4 us
    pallas_call x1, Pallas kernels, decode(): pl.pallas_call(decode_kernel, out_shape=jax.ShapeDtypeStruct((rows, colum...  11.1 us
    dot_general x1, matrix products, line_body(): early = jnp.dot(codes, decoder, preferred_element_type=jnp.float32)  9.87 us
    ppermute x14, starting transfers between devices, swap(): return lax.ppermute(value, 'col', [(i, i ^ distance) for i in range(size)])  9.38 us
    unnamed x55, local copies, waits for them, and re-layouts  8.04 us
  transfers between devices with their start and end apart: 26, of which 16 were waited for; matrix products, arithmetic and copies ran while one was open for 10% of the time, Pallas kernels for 16%

profile of v6, /device:TPU:8, one launch (start us, length us, event | category | flops | bytes accessed | tf_op | source)
XLA Modules:
  0.0 187.3 jit_solution(9349220192039747089)
XLA Ops:
  2.0 3.0 %collective-permute-start.1 = (f32[16,1024]{1,0:T(8,128)S(1)}, f32[16,1024]{1,0:T(8,128)S(1)}, u32[]{:S(2)}, u32[]{:S(2)}) collective-permute-start(f32[16,1024]{1,0:T(8,128)S(1)} %constant_dynamic-update-slice_fusion.refs_1_), channel_id=1, source_target_pairs={{0,8},{4,12},{8,0},{12,4},{1,9},{5,13},{9,1},{13,5},{2,10},{6,14},... | collective-permute-start | bytes 196616 | tf_op jit(solution)/shard_map/ppermute | solution.py:200
  5.4 2.2 %constant_dynamic-slice_fusion = (bf16[2,384,256]{2,1,0:T(8,128)(2,1)}, bf16[1,2,384,256]{3,2,1,0:T(8,128)(2,1)S(1)}, bf16[1,2,384,256]{3,2,1,0:T(8,128)(2,1)S(1)}, bf16[1,2,384,256]{3,2,1,0:T(8,128)(2,1)S(1)}) fusion(bf16[2,384,1024]{2,1,0:T(8,128)(2,1)} %param.17, s32[]{:T(128)S(6)} %select_n.31, s32[]{:T(128)S(6)} %select_n.25, s32[]{:T(128)S(6)} %select_n.24, ...), kind=kLoop, calls=%fused_computation.58 | loop fusion | bytes 3145744 | tf_op jit(solution)/shard_map/dynamic_slice | solution.py:251
  7.7 1.6 collective-permute-start.3
  9.6 5.7 %densify.2 = bf16[256,8192]{1,0:T(8,128)(2,1)S(1)} custom-call(s32[1]{0:T(128)} %bitcast.base_ref, f32[16,1024]{1,0:T(8,128)S(1)} %collective-permute-done.1.refs_0_, f32[16,1024]{1,0:T(8,128)S(1)} %collective-permute-done.2.refs_1_), custom_call_target="tpu_custom_call" | custom-call | flops 2147483648 | bytes 4194304 | tf_op jit(solution)/shard_map/densify/pallas_call | solution.py:64
  15.3 9.9 %fusion.28 = f32[256,1280]{1,0:T(8,128)S(1)} fusion(bf16[256,8192]{1,0:T(8,128)(2,1)S(1)} %densify.2, bf16[8192,1280]{1,0:T(8,128)(2,1)} %weights_ref.1), kind=kOutput, calls=%fused_computation.73 | convolution fusion | flops 5368709120 | bytes 26476544 | tf_op jit(solution)/shard_map/dot_general | solution.py:261
  25.3 3.5 %collective-permute-start.4 = (f16[128,1280]{1,0:T(8,128)(2,1)S(1)}, f16[128,1280]{1,0:T(8,128)(2,1)S(1)}, u32[]{:S(2)}, u32[]{:S(2)}) collective-permute-start(f16[128,1280]{1,0:T(8,128)(2,1)S(1)} %get-tuple-element.44), channel_id=1, source_target_pairs={{0,8},{4,12},{8,0},{12,4},{1,9},{5,13},{9,1},{13,5},{2,10},{6,14},... | collective-permute-start | bytes 983048 | tf_op jit(solution)/shard_map/ppermute | solution.py:200
  28.7 5.7 %densify.3.codes_ref = bf16[256,8192]{1,0:T(8,128)(2,1)S(1)} custom-call(s32[1]{0:T(128)} %bitcast.base_ref, f32[16,1024]{1,0:T(8,128)S(1)} %collective-permute-done.refs_0_, f32[16,1024]{1,0:T(8,128)S(1)} %constant_dynamic-update-slice_fusion.refs_1_), custom_call_target="tpu_custom_call" | custom-call | flops 2147483648 | bytes 4194304 | tf_op jit(solution)/shard_map/densify/pallas_call | solution.py:64
  35.4 11.1 %decode.1 = f32[256,1280]{1,0:T(8,128)S(1)} custom-call(bf16[256,8192]{1,0:T(8,128)(2,1)S(1)} %densify.3.codes_ref, bf16[8192,1280]{1,0:T(8,128)(2,1)} %weights_ref.1), custom_call_target="tpu_custom_call" | custom-call | flops 1 | bytes 1 | tf_op jit(solution)/shard_map/decode/pallas_call | solution.py:86
  46.5 1.2 slice_bitcast_fusion.2
  48.8 1.8 select_columns.3
  50.7 1.8 select_columns.2
  52.5 1.4 copy-done.5
  53.8 1.0 select_rows.1
  54.8 10.4 %collective-permute-done.6 = f16[128,1280]{1,0:T(8,128)(2,1)S(1)} collective-permute-done((f16[128,1280]{1,0:T(8,128)(2,1)S(1)}, f16[128,1280]{1,0:T(8,128)(2,1)S(1)}, u32[]{:S(2)}, u32[]{:S(2)}) %collective-permute-start.6) | collective-permute-done | bytes 327712 | tf_op jit(solution)/shard_map/ppermute | solution.py:200
  65.6 1.1 collective-permute-done.8
  66.8 1.5 collective-permute-start.9
  68.3 2.1 %collective-permute-done.9 = f32[2,128]{1,0:T(2,128)S(1)} collective-permute-done((f32[2,128]{1,0:T(2,128)S(1)}, f32[2,128]{1,0:T(2,128)S(1)}, u32[]{:S(2)}, u32[]{:S(2)}) %collective-permute-start.9) | collective-permute-done | bytes 1056 | tf_op jit(solution)/shard_map/ppermute | solution.py:204
  70.7 2.1 %collective-permute-start.11 = (bf16[128,1280]{1,0:T(8,128)(2,1)S(1)}, bf16[128,1280]{1,0:T(8,128)(2,1)S(1)}, u32[]{:S(2)}, u32[]{:S(2)}) collective-permute-start(bf16[128,1280]{1,0:T(8,128)(2,1)S(1)} %add_convert_fusion), channel_id=1, source_target_pairs={{0,4},{4,0},{8,12},{12,8},{1,5},{5,1},{9,13},{13,9},{2,6},{6,2},{1... | collective-permute-start | bytes 983048 | tf_op jit(solution)/shard_map/ppermute | solution.py:200
  73.6 10.6 %collective-permute-done.12 = bf16[128,1280]{1,0:T(8,128)(2,1)S(1)} collective-permute-done((bf16[128,1280]{1,0:T(8,128)(2,1)S(1)}, bf16[128,1280]{1,0:T(8,128)(2,1)S(1)}, u32[]{:S(2)}, u32[]{:S(2)}) %collective-permute-start.12) | collective-permute-done | bytes 327712 | tf_op jit(solution)/shard_map/ppermute | solution.py:200
  84.2 2.3 %collective-permute-done.11 = bf16[128,1280]{1,0:T(8,128)(2,1)S(1)} collective-permute-done((bf16[128,1280]{1,0:T(8,128)(2,1)S(1)}, bf16[128,1280]{1,0:T(8,128)(2,1)S(1)}, u32[]{:S(2)}, u32[]{:S(2)}) %collective-permute-start.11) | collective-permute-done | bytes 327712 | tf_op jit(solution)/shard_map/ppermute | solution.py:200
  87.3 1.2 convolution_convert_fusion.1
  88.5 1.5 collective-permute-start.13
  90.1 5.8 %collective-permute-done.13 = f16[128,768]{1,0:T(8,128)(2,1)S(1)} collective-permute-done((f16[128,768]{1,0:T(8,128)(2,1)S(1)}, f16[128,768]{1,0:T(8,128)(2,1)S(1)}, u32[]{:S(2)}, u32[]{:S(2)}) %collective-permute-start.13) | collective-permute-done | bytes 196640 | tf_op jit(solution)/shard_map/ppermute | solution.py:204
  96.6 1.2 convolution_add_fusion
  97.8 1.5 collective-permute-start.16
  99.3 1.4 collective-permute-start.15
  100.7 7.8 %collective-permute-done.16 = f16[256,768]{1,0:T(8,128)(2,1)S(1)} collective-permute-done((f16[256,768]{1,0:T(8,128)(2,1)S(1)}, f16[256,768]{1,0:T(8,128)(2,1)S(1)}, u32[]{:S(2)}, u32[]{:S(2)}) %collective-permute-start.16) | collective-permute-done | bytes 393248 | tf_op jit(solution)/shard_map/ppermute | solution.py:204
  109.4 6.0 %collective-permute-done.15 = bf16[128,1280]{1,0:T(8,128)(2,1)S(1)} collective-permute-done((bf16[128,1280]{1,0:T(8,128)(2,1)S(1)}, bf16[128,1280]{1,0:T(8,128)(2,1)S(1)}, u32[]{:S(2)}, u32[]{:S(2)}) %collective-permute-start.15) | collective-permute-done | bytes 327712 | tf_op jit(solution)/shard_map/ppermute | solution.py:200
  115.4 1.4 convolution_convert_fusion.2
  117.0 1.2 slice_bitcast_fusion
  118.9 3.0 %convolution_add_fusion.1 = f32[128,1536]{1,0:T(8,128)S(1)} fusion(bf16[128,1280]{1,0:T(8,128)(2,1)} %copy-done.16, bf16[1280,1536]{1,0:T(8,128)(2,1)} %copy-done, f16[128,1536]{1,0:T(8,128)(2,1)} %collective-permute-done.17), kind=kOutput, calls=%fused_computation.3 | convolution fusion | flops 503709696 | bytes 5439488 | tf_op jit(solution)/shard_map/dot_general | solution.py:299
  122.5 1.0 fusion.25
  123.5 5.3 %collective-permute-done.18 = f16[128,768]{1,0:T(8,128)(2,1)S(1)} collective-permute-done((f16[128,768]{1,0:T(8,128)(2,1)S(1)}, f16[128,768]{1,0:T(8,128)(2,1)S(1)}, u32[]{:S(2)}, u32[]{:S(2)}) %collective-permute-start.18) | collective-permute-done | bytes 196640 | tf_op jit(solution)/shard_map/ppermute | solution.py:204
  129.0 3.1 %attend.2 = bf16[256,256]{1,0:T(8,128)(2,1)} custom-call(s32[256,1]{1,0:T(8,128)S(1)} %copy.21.refs_0_, s32[1,512]{1,0:T(1,128)S(1)} %bitcast.54, bf16[128,768]{1,0:T(8,128)(2,1)S(1)} %copy-done.6, bf16[128,768]{1,0:T(8,128)(2,1)S(1)} %get-tuple-element.93.refs_3_, bf16[128,768]{1,0:T(8,128)(2,1)S(1)} %get-tuple-element.92.refs_4_, ...), custom_call_target="tpu_custom_call" | custom-call | flops 536870912 | bytes 2097152 | tf_op jit(solution)/shard_map/attend/pallas_call | solution.py:184
  132.8 1.0 copy-done.2
  133.8 1.0 copy-done.4
  134.8 0.9 copy-done.7
  136.7 0.9 copy-done.11
  138.5 2.4 %attend.3 = bf16[256,256]{1,0:T(8,128)(2,1)S(1)} custom-call(s32[256,1]{1,0:T(8,128)S(1)} %copy.22.refs_0_, s32[1,512]{1,0:T(1,128)S(1)} %bitcast.55, bf16[128,768]{1,0:T(8,128)(2,1)S(1)} %copy-done.7, bf16[128,768]{1,0:T(8,128)(2,1)S(1)} %copy-done.11, bf16[128,768]{1,0:T(8,128)(2,1)S(1)} %copy-done.9, bf16[128,768]{1,0:T(8,128)(2,1)S(1)} %copy-done.13, ...), custom_call_target="tpu_custom_call" | custom-call | flops 536870912 | bytes 2097152 | tf_op jit(solution)/shard_map/attend/pallas_call | solution.py:184
  140.9 1.0 pad_maximum_fusion.4
  142.0 1.5 collective-permute-done.20
  143.5 1.8 convolution_convert_fusion
  145.4 1.5 collective-permute-start.21
  147.0 4.1 %collective-permute-done.21 = bf16[256,256]{1,0:T(8,128)(2,1)S(1)} collective-permute-done((bf16[256,256]{1,0:T(8,128)(2,1)S(1)}, bf16[256,256]{1,0:T(8,128)(2,1)S(1)}, u32[]{:S(2)}, u32[]{:S(2)}) %collective-permute-start.21) | collective-permute-done | bytes 131104 | tf_op jit(solution)/shard_map/ppermute | solution.py:204
  151.2 2.8 %collective-permute-start.24 = (bf16[128,1280]{1,0:T(8,128)(2,1)S(1)}, bf16[128,1280]{1,0:T(8,128)(2,1)S(1)}, u32[]{:S(2)}, u32[]{:S(2)}) collective-permute-start(bf16[128,1280]{1,0:T(8,128)(2,1)S(1)} %get-tuple-element.73), channel_id=1, source_target_pairs={{0,4},{4,0},{8,12},{12,8},{1,5},{5,1},{9,13},{13,9},{2,6},{6,2},{1... | collective-permute-start | bytes 983048 | tf_op jit(solution)/shard_map/ppermute | solution.py:200
  154.1 12.0 %collective-permute-done.23 = bf16[128,1280]{1,0:T(8,128)(2,1)S(1)} collective-permute-done((bf16[128,1280]{1,0:T(8,128)(2,1)S(1)}, bf16[128,1280]{1,0:T(8,128)(2,1)S(1)}, u32[]{:S(2)}, u32[]{:S(2)}) %collective-permute-start.23) | collective-permute-done | bytes 327712 | tf_op jit(solution)/shard_map/ppermute | solution.py:200
  166.1 3.1 %collective-permute-done.24 = bf16[128,1280]{1,0:T(8,128)(2,1)S(1)} collective-permute-done((bf16[128,1280]{1,0:T(8,128)(2,1)S(1)}, bf16[128,1280]{1,0:T(8,128)(2,1)S(1)}, u32[]{:S(2)}, u32[]{:S(2)}) %collective-permute-start.24) | collective-permute-done | bytes 327712 | tf_op jit(solution)/shard_map/ppermute | solution.py:200
  170.7 15.7 %collective-permute-done.25 = bf16[128,1280]{1,0:T(8,128)(2,1)S(1)} collective-permute-done((bf16[128,1280]{1,0:T(8,128)(2,1)S(1)}, bf16[128,1280]{1,0:T(8,128)(2,1)S(1)}, u32[]{:S(2)}, u32[]{:S(2)}) %collective-permute-start.25) | collective-permute-done | bytes 327712 | tf_op jit(solution)/shard_map/ppermute | solution.py:200
  (122 shorter events, 15.8 us)
Async XLA Ops:
  0.0 9.3 %copy-start.24 = (s32[512]{0:T(512)S(1)}, s32[512]{0:T(512)}, u32[]{:S(2)}) copy-start(s32[512]{0:T(512)} %param.18) | copy-start | bytes 6148
  1.9 7.5 %collective-permute-start.2 = (f32[16,1024]{1,0:T(8,128)S(1)}, f32[16,1024]{1,0:T(8,128)S(1)}, u32[]{:S(2)}, u32[]{:S(2)}) collective-permute-start(f32[16,1024]{1,0:T(8,128)S(1)} %constant_dynamic-update-slice_fusion.refs_1_), channel_id=1, source_target_pairs={{0,4},{4,0},{8,12},{12,8},{1,5},{5,1},{9,13},{13,9},{2,6},{6,2},{1... | collective-permute-start | bytes 196616 | tf_op jit(solution)/shard_map/ppermute | solution.py:200
  2.0 7.6 %collective-permute-start.1 = (f32[16,1024]{1,0:T(8,128)S(1)}, f32[16,1024]{1,0:T(8,128)S(1)}, u32[]{:S(2)}, u32[]{:S(2)}) collective-permute-start(f32[16,1024]{1,0:T(8,128)S(1)} %constant_dynamic-update-slice_fusion.refs_1_), channel_id=1, source_target_pairs={{0,8},{4,12},{8,0},{12,4},{1,9},{5,13},{9,1},{13,5},{2,10},{6,14},... | collective-permute-start | bytes 196616 | tf_op jit(solution)/shard_map/ppermute | solution.py:200
  5.0 20.3 %collective-permute-start = (f32[16,1024]{1,0:T(8,128)S(1)}, f32[16,1024]{1,0:T(8,128)S(1)}, u32[]{:S(2)}, u32[]{:S(2)}) collective-permute-start(f32[16,1024]{1,0:T(8,128)S(1)} %constant_dynamic-update-slice_fusion.refs_1_), channel_id=1, source_target_pairs={{0,12},{4,8},{8,4},{12,0},{1,13},{5,9},{9,5},{13,1},{2,14},{6,10},... | collective-permute-start | bytes 196616 | tf_op jit(solution)/shard_map/ppermute | solution.py:200
  7.7 26.7 %collective-permute-start.3 = (bf16[2,2,384,256]{3,2,1,0:T(8,128)(2,1)S(1)}, bf16[2,2,384,256]{3,2,1,0:T(8,128)(2,1)S(1)}, u32[]{:S(2)}, u32[]{:S(2)}) collective-permute-start(bf16[2,2,384,256]{3,2,1,0:T(8,128)(2,1)S(1)} %pad_maximum_fusion), channel_id=1, source_target_pairs={{0,2},{1,3},{2,0},{3,1},{4,6},{5,7},{6,4},{7,5},{8,10},{9,11},{10,... | collective-permute-start | bytes 2359304 | tf_op jit(solution)/shard_map/ppermute | solution.py:204
  25.3 22.7 %collective-permute-start.4 = (f16[128,1280]{1,0:T(8,128)(2,1)S(1)}, f16[128,1280]{1,0:T(8,128)(2,1)S(1)}, u32[]{:S(2)}, u32[]{:S(2)}) collective-permute-start(f16[128,1280]{1,0:T(8,128)(2,1)S(1)} %get-tuple-element.44), channel_id=1, source_target_pairs={{0,8},{4,12},{8,0},{12,4},{1,9},{5,13},{9,1},{13,5},{2,10},{6,14},... | collective-permute-start | bytes 983048 | tf_op jit(solution)/shard_map/ppermute | solution.py:200
  28.7 19.2 %collective-permute-start.5 = (f16[128,1280]{1,0:T(8,128)(2,1)S(1)}, f16[128,1280]{1,0:T(8,128)(2,1)S(1)}, u32[]{:S(2)}, u32[]{:S(2)}) collective-permute-start(f16[128,1280]{1,0:T(8,128)(2,1)S(1)} %get-tuple-element.45), channel_id=1, source_target_pairs={{0,4},{4,0},{8,12},{12,8},{1,5},{5,1},{9,13},{13,9},{2,6},{6,2},{1... | collective-permute-start | bytes 983048 | tf_op jit(solution)/shard_map/ppermute | solution.py:200
  34.5 14.3 %slice-start = ((s8[7864320]{0:T(1024)(128)(4,1)}), s8[4194304]{0:T(1024)(128)(4,1)S(1)}, s32[]{:S(2)}) async-start(s8[7864320]{0:T(1024)(128)(4,1)} %bitcast.49), calls=%async_computation | async-start | bytes 8388608
  35.4 13.4 %slice-start.1 = ((s8[7864320]{0:T(1024)(128)(4,1)}), s8[3670016]{0:T(1024)(128)(4,1)S(1)}, s32[]{:S(2)}) async-start(s8[7864320]{0:T(1024)(128)(4,1)} %bitcast.49), calls=%async_computation.1 | async-start | bytes 7340032
  46.5 2.1 %copy-start.23 = (bf16[1280]{0:T(1024)(128)(2,1)S(1)}, bf16[1280]{0:T(1024)(128)(2,1)}, u32[]{:S(2)}) copy-start(bf16[1280]{0:T(1024)(128)(2,1)} %param.13) | copy-start | bytes 7684
  47.8 17.4 %collective-permute-start.7 = (bf16[2,2,384,256]{3,2,1,0:T(8,128)(2,1)S(1)}, bf16[2,2,384,256]{3,2,1,0:T(8,128)(2,1)S(1)}, u32[]{:S(2)}, u32[]{:S(2)}) collective-permute-start(bf16[2,2,384,256]{3,2,1,0:T(8,128)(2,1)S(1)} %pad_maximum_fusion.1), channel_id=1, source_target_pairs={{0,1},{1,0},{2,3},{3,2},{4,5},{5,4},{6,7},{7,6},{8,9},{9,8},{10,11... | collective-permute-start | bytes 2359304 | tf_op jit(solution)/shard_map/ppermute | solution.py:204
  48.0 2.7 %copy-start.19 = (f16[128,1280]{1,0:T(8,128)(2,1)}, f16[128,1280]{1,0:T(8,128)(2,1)S(1)}, u32[]{:S(2)}) copy-start(f16[128,1280]{1,0:T(8,128)(2,1)S(1)} %collective-permute-done.5) | copy-start | bytes 983044
  48.0 17.2 %collective-permute-start.6 = (f16[128,1280]{1,0:T(8,128)(2,1)S(1)}, f16[128,1280]{1,0:T(8,128)(2,1)S(1)}, u32[]{:S(2)}, u32[]{:S(2)}) collective-permute-start(f16[128,1280]{1,0:T(8,128)(2,1)S(1)} %fusion.5), channel_id=1, source_target_pairs={{0,12},{4,8},{8,4},{12,0},{1,13},{5,9},{9,5},{13,1},{2,14},{6,10},... | collective-permute-start | bytes 983048 | tf_op jit(solution)/shard_map/ppermute | solution.py:200
  50.6 45.9 %copy-start = (bf16[1280,1536]{1,0:T(8,128)(2,1)}, bf16[1280,1536]{1,0:T(8,128)(2,1)S(1)}, u32[]{:S(2)}) copy-start(bf16[1280,1536]{1,0:T(8,128)(2,1)S(1)} %select_columns.3) | copy-start | bytes 11796484
  50.6 3.2 %copy-start.5 = (bf16[1024,1280]{1,0:T(8,128)(2,1)S(1)}, bf16[1024,1280]{1,0:T(8,128)(2,1)}, u32[]{:S(2)}) copy-start(bf16[1024,1280]{1,0:T(8,128)(2,1)} %from_ref) | copy-start | bytes 7864324
  53.8 11.4 %copy-start.20 = (f16[128,1280]{1,0:T(8,128)(2,1)S(1)}, f16[128,1280]{1,0:T(8,128)(2,1)}, u32[]{:S(2)}) copy-start(f16[128,1280]{1,0:T(8,128)(2,1)} %copy-done.19) | copy-start | bytes 983044
  53.8 16.6 %copy-start.21 = (f32[1280]{0:T(1024)S(1)}, f32[1280]{0:T(1024)}, u32[]{:S(2)}) copy-start(f32[1280]{0:T(1024)} %param.15) | copy-start | bytes 15364
  53.8 16.7 %copy-start.22 = (f32[1280]{0:T(1024)S(1)}, f32[1280]{0:T(1024)}, u32[]{:S(2)}) copy-start(f32[1280]{0:T(1024)} %param.14) | copy-start | bytes 15364
  65.2 8.3 %copy-start.17 = (bf16[2,2,384,256]{3,2,1,0:T(8,128)(2,1)}, bf16[2,2,384,256]{3,2,1,0:T(8,128)(2,1)S(1)}, u32[]{:S(2)}) copy-start(bf16[2,2,384,256]{3,2,1,0:T(8,128)(2,1)S(1)} %collective-permute-done.7) | copy-start | bytes 2359300
  65.5 21.7 %copy-start.14 = (f32[128,1280]{1,0:T(8,128)}, f32[128,1280]{1,0:T(8,128)S(1)}, u32[]{:S(2)}) copy-start(f32[128,1280]{1,0:T(8,128)S(1)} %get-tuple-element.79) | copy-start | bytes 1966084
  65.6 1.2 collective-permute-start.8
  66.8 3.6 %collective-permute-start.9 = (f32[2,128]{1,0:T(2,128)S(1)}, f32[2,128]{1,0:T(2,128)S(1)}, u32[]{:S(2)}, u32[]{:S(2)}) collective-permute-start(f32[2,128]{1,0:T(2,128)S(1)} %fusion.21), channel_id=1, source_target_pairs={{0,2},{1,3},{2,0},{3,1},{4,6},{5,7},{6,4},{7,5},{8,10},{9,11},{10,... | collective-permute-start | bytes 3080 | tf_op jit(solution)/shard_map/ppermute | solution.py:204
  70.7 13.5 %collective-permute-start.12 = (bf16[128,1280]{1,0:T(8,128)(2,1)S(1)}, bf16[128,1280]{1,0:T(8,128)(2,1)S(1)}, u32[]{:S(2)}, u32[]{:S(2)}) collective-permute-start(bf16[128,1280]{1,0:T(8,128)(2,1)S(1)} %add_convert_fusion), channel_id=1, source_target_pairs={{0,8},{4,12},{8,0},{12,4},{1,9},{5,13},{9,1},{13,5},{2,10},{6,14},... | collective-permute-start | bytes 983048 | tf_op jit(solution)/shard_map/ppermute | solution.py:200
  70.7 15.7 %collective-permute-start.11 = (bf16[128,1280]{1,0:T(8,128)(2,1)S(1)}, bf16[128,1280]{1,0:T(8,128)(2,1)S(1)}, u32[]{:S(2)}, u32[]{:S(2)}) collective-permute-start(bf16[128,1280]{1,0:T(8,128)(2,1)S(1)} %add_convert_fusion), channel_id=1, source_target_pairs={{0,4},{4,0},{8,12},{12,8},{1,5},{5,1},{9,13},{13,9},{2,6},{6,2},{1... | collective-permute-start | bytes 983048 | tf_op jit(solution)/shard_map/ppermute | solution.py:200
  73.5 13.0 %collective-permute-start.10 = (f16[128,1536]{1,0:T(8,128)(2,1)S(1)}, f16[128,1536]{1,0:T(8,128)(2,1)S(1)}, u32[]{:S(2)}, u32[]{:S(2)}) collective-permute-start(f16[128,1536]{1,0:T(8,128)(2,1)S(1)} %convolution_convert_fusion.3), channel_id=1, source_target_pairs={{0,1},{1,0},{2,3},{3,2},{4,5},{5,4},{6,7},{7,6},{8,9},{9,8},{10,11... | collective-permute-start | bytes 1179656 | tf_op jit(solution)/shard_map/ppermute | solution.py:204
  88.4 8.1 %collective-permute-start.14 = (f16[256,1536]{1,0:T(8,128)(2,1)S(1)}, f16[256,1536]{1,0:T(8,128)(2,1)S(1)}, u32[]{:S(2)}, u32[]{:S(2)}) collective-permute-start(f16[256,1536]{1,0:T(8,128)(2,1)S(1)} %convolution_convert_fusion.1), channel_id=1, source_target_pairs={{0,1},{1,0},{2,3},{3,2},{4,5},{5,4},{6,7},{7,6},{8,9},{9,8},{10,11... | collective-permute-start | bytes 2359304 | tf_op jit(solution)/shard_map/ppermute | solution.py:204
  88.5 7.3 %collective-permute-start.13 = (f16[128,768]{1,0:T(8,128)(2,1)S(1)}, f16[128,768]{1,0:T(8,128)(2,1)S(1)}, u32[]{:S(2)}, u32[]{:S(2)}) collective-permute-start(f16[128,768]{1,0:T(8,128)(2,1)S(1)} %slice_convert_fusion.3), channel_id=1, source_target_pairs={{0,2},{1,3},{2,0},{3,1},{4,6},{5,7},{6,4},{7,5},{8,10},{9,11},{10,... | collective-permute-start | bytes 589832 | tf_op jit(solution)/shard_map/ppermute | solution.py:204
  97.8 10.7 %collective-permute-start.16 = (f16[256,768]{1,0:T(8,128)(2,1)S(1)}, f16[256,768]{1,0:T(8,128)(2,1)S(1)}, u32[]{:S(2)}, u32[]{:S(2)}) collective-permute-start(f16[256,768]{1,0:T(8,128)(2,1)S(1)} %slice_convert_fusion), channel_id=1, source_target_pairs={{0,2},{1,3},{2,0},{3,1},{4,6},{5,7},{6,4},{7,5},{8,10},{9,11},{10,... | collective-permute-start | bytes 1179656 | tf_op jit(solution)/shard_map/ppermute | solution.py:204
  99.3 16.0 %collective-permute-start.15 = (bf16[128,1280]{1,0:T(8,128)(2,1)S(1)}, bf16[128,1280]{1,0:T(8,128)(2,1)S(1)}, u32[]{:S(2)}, u32[]{:S(2)}) collective-permute-start(bf16[128,1280]{1,0:T(8,128)(2,1)S(1)} %add_convert_fusion), channel_id=1, source_target_pairs={{0,12},{4,8},{8,4},{12,0},{1,13},{5,9},{9,5},{13,1},{2,14},{6,10},... | collective-permute-start | bytes 983048 | tf_op jit(solution)/shard_map/ppermute | solution.py:200
  115.4 1.4 copy-start.16
  116.8 2.1 %collective-permute-start.17 = (f16[128,1536]{1,0:T(8,128)(2,1)}, f16[128,1536]{1,0:T(8,128)(2,1)}, u32[]{:S(2)}, u32[]{:S(2)}) collective-permute-start(f16[128,1536]{1,0:T(8,128)(2,1)} %convolution_convert_fusion.2), channel_id=1, source_target_pairs={{0,1},{1,0},{2,3},{3,2},{4,5},{5,4},{6,7},{7,6},{8,9},{9,8},{10,11... | collective-permute-start | bytes 1179656 | tf_op jit(solution)/shard_map/ppermute | solution.py:204
  118.1 13.9 %copy-start.1 = (bf16[2,384,256]{2,1,0:T(8,128)(2,1)}, bf16[2,384,256]{2,1,0:T(8,128)(2,1)S(1)}, u32[]{:S(2)}) copy-start(bf16[2,384,256]{2,1,0:T(8,128)(2,1)S(1)} %get-tuple-element.87.refs_8_) | copy-start | bytes 1179652
  118.1 10.8 %copy-start.3 = (bf16[2,384,256]{2,1,0:T(8,128)(2,1)S(1)}, bf16[2,384,256]{2,1,0:T(8,128)(2,1)}, u32[]{:S(2)}) copy-start(bf16[2,384,256]{2,1,0:T(8,128)(2,1)} %get-tuple-element.80.refs_6_) | copy-start | bytes 1179652
  118.1 10.8 %copy-start.6 = (bf16[128,768]{1,0:T(8,128)(2,1)S(1)}, bf16[128,768]{1,0:T(8,128)(2,1)}, u32[]{:S(2)}) copy-start(bf16[128,768]{1,0:T(8,128)(2,1)} %fusion.17.refs_2_) | copy-start | bytes 589828
  121.9 7.0 %collective-permute-start.18 = (f16[128,768]{1,0:T(8,128)(2,1)S(1)}, f16[128,768]{1,0:T(8,128)(2,1)S(1)}, u32[]{:S(2)}, u32[]{:S(2)}) collective-permute-start(f16[128,768]{1,0:T(8,128)(2,1)S(1)} %slice_convert_fusion.2), channel_id=1, source_target_pairs={{0,2},{1,3},{2,0},{3,1},{4,6},{5,7},{6,4},{7,5},{8,10},{9,11},{10,... | collective-permute-start | bytes 589832 | tf_op jit(solution)/shard_map/ppermute | solution.py:204
  123.5 8.5 %copy-start.8 = (bf16[128,768]{1,0:T(8,128)(2,1)}, bf16[128,768]{1,0:T(8,128)(2,1)S(1)}, u32[]{:S(2)}) copy-start(bf16[128,768]{1,0:T(8,128)(2,1)S(1)} %get-tuple-element.92.refs_4_) | copy-start | bytes 589828
  123.5 8.5 %copy-start.10 = (bf16[128,768]{1,0:T(8,128)(2,1)}, bf16[128,768]{1,0:T(8,128)(2,1)S(1)}, u32[]{:S(2)}) copy-start(bf16[128,768]{1,0:T(8,128)(2,1)S(1)} %get-tuple-element.93.refs_3_) | copy-start | bytes 589828
  129.0 3.1 %copy-start.12 = (bf16[128,768]{1,0:T(8,128)(2,1)}, bf16[128,768]{1,0:T(8,128)(2,1)S(1)}, u32[]{:S(2)}) copy-start(bf16[128,768]{1,0:T(8,128)(2,1)S(1)} %fusion.16.refs_5_) | copy-start | bytes 589828
  132.1 8.9 %collective-permute-start.19 = (bf16[256,256]{1,0:T(8,128)(2,1)}, bf16[256,256]{1,0:T(8,128)(2,1)}, u32[]{:S(2)}, u32[]{:S(2)}) collective-permute-start(bf16[256,256]{1,0:T(8,128)(2,1)} %attend.2), channel_id=1, source_target_pairs={{0,2},{1,3},{2,0},{3,1},{4,6},{5,7},{6,4},{7,5},{8,10},{9,11},{10,... | collective-permute-start | bytes 393224 | tf_op jit(solution)/shard_map/ppermute | solution.py:204
  132.8 1.0 copy-start.2
  133.8 1.0 copy-start.4
  141.9 1.6 collective-permute-start.20
  145.3 41.0 %copy-start.15 = (f32[128,1280]{1,0:T(8,128)S(1)}, f32[128,1280]{1,0:T(8,128)}, u32[]{:S(2)}) copy-start(f32[128,1280]{1,0:T(8,128)} %copy-done.14) | copy-start | bytes 1966084
  145.4 5.6 %collective-permute-start.21 = (bf16[256,256]{1,0:T(8,128)(2,1)S(1)}, bf16[256,256]{1,0:T(8,128)(2,1)S(1)}, u32[]{:S(2)}, u32[]{:S(2)}) collective-permute-start(bf16[256,256]{1,0:T(8,128)(2,1)S(1)} %attend.3), channel_id=1, source_target_pairs={{0,2},{1,3},{2,0},{3,1},{4,6},{5,7},{6,4},{7,5},{8,10},{9,11},{10,... | collective-permute-start | bytes 393224 | tf_op jit(solution)/shard_map/ppermute | solution.py:204
  151.0 3.0 %collective-permute-start.22 = (bf16[256,512]{1,0:T(8,128)(2,1)S(1)}, bf16[256,512]{1,0:T(8,128)(2,1)S(1)}, u32[]{:S(2)}, u32[]{:S(2)}) collective-permute-start(bf16[256,512]{1,0:T(8,128)(2,1)S(1)} %pad_maximum_fusion.5), channel_id=1, source_target_pairs={{0,1},{1,0},{2,3},{3,2},{4,5},{5,4},{6,7},{7,6},{8,9},{9,8},{10,11... | collective-permute-start | bytes 786440 | tf_op jit(solution)/shard_map/ppermute | solution.py:204
  151.1 14.9 %collective-permute-start.23 = (bf16[128,1280]{1,0:T(8,128)(2,1)S(1)}, bf16[128,1280]{1,0:T(8,128)(2,1)S(1)}, u32[]{:S(2)}, u32[]{:S(2)}) collective-permute-start(bf16[128,1280]{1,0:T(8,128)(2,1)S(1)} %get-tuple-element.72), channel_id=1, source_target_pairs={{0,8},{4,12},{8,0},{12,4},{1,9},{5,13},{9,1},{13,5},{2,10},{6,14},... | collective-permute-start | bytes 983048 | tf_op jit(solution)/shard_map/ppermute | solution.py:200
  151.2 17.9 %collective-permute-start.24 = (bf16[128,1280]{1,0:T(8,128)(2,1)S(1)}, bf16[128,1280]{1,0:T(8,128)(2,1)S(1)}, u32[]{:S(2)}, u32[]{:S(2)}) collective-permute-start(bf16[128,1280]{1,0:T(8,128)(2,1)S(1)} %get-tuple-element.73), channel_id=1, source_target_pairs={{0,4},{4,0},{8,12},{12,8},{1,5},{5,1},{9,13},{13,9},{2,6},{6,2},{1... | collective-permute-start | bytes 983048 | tf_op jit(solution)/shard_map/ppermute | solution.py:200
  170.0 16.4 %collective-permute-start.25 = (bf16[128,1280]{1,0:T(8,128)(2,1)S(1)}, bf16[128,1280]{1,0:T(8,128)(2,1)S(1)}, u32[]{:S(2)}, u32[]{:S(2)}) collective-permute-start(bf16[128,1280]{1,0:T(8,128)(2,1)S(1)} %slice.167), channel_id=1, source_target_pairs={{0,12},{4,8},{8,4},{12,0},{1,13},{5,9},{9,5},{13,1},{2,14},{6,10},... | collective-permute-start | bytes 983048 | tf_op jit(solution)/shard_map/ppermute | solution.py:200
  (5 other events, 4.6 us)

commit v7 on v5

--- a/solution.py
+++ b/solution.py
@@ -13,6 +13,7 @@
 GROUP = 8
 VMEM_BYTES = 20 * 1024 * 1024
 DECODE_BYTES = 44 * 1024 * 1024
+SMALL = pl.CostEstimate(flops=1, bytes_accessed=1, transcendentals=0)
 
 
 def densify_kernel(base_ref, *refs, topk, latents, lanes):
@@ -92,11 +93,7 @@
         ],
         out_specs=pl.BlockSpec((rows, width), lambda n: (0, n)),
         compiler_params=pltpu.CompilerParams(vmem_limit_bytes=DECODE_BYTES),
-        cost_estimate=pl.CostEstimate(
-            flops=2 * rows * latents * columns,
-            bytes_accessed=latents * (rows + columns) * 2 + rows * columns * 4,
-            transcendentals=0,
-        ),
+        cost_estimate=SMALL,
         name="decode",
     )(codes, decoder)
 
@@ -276,20 +273,22 @@
     )
     query_pos = key_pos.reshape(-1, 1)
 
-    codes_far = densify([packed[3], packed[2]], base, topk, latents)
-    far = jnp.dot(codes_far, decoder, preferred_element_type=jnp.float32)
-    in_far = lax.ppermute(to_half(far[:rows]), "lat", INWARD)
-    near_packed, far = hold(((packed[1], packed[0]), far))
+    far = jnp.dot(
+        densify([packed[3]], base, topk, latents), decoder, preferred_element_type=jnp.float32
+    )
+    packed2, sent = hold((packed[2], to_half(far)))
+    in_far = lax.ppermute(sent, "lat", INWARD)
+    second = decode(densify([packed2], base, topk, latents), decoder)
+    second, in_far = hold((second, in_far))
+    near_packed, sent_far, sent_across = hold(
+        ((packed[1], packed[0]), to_half(far + from_half(in_far)), to_half(second))
+    )
+    mid_far = lax.ppermute(sent_far, "lat", MIDDLE)
+    in_across = lax.ppermute(sent_across, "lat", INWARD)
     codes_near = densify(near_packed, base, topk, latents)
-    codes_near, in_far = hold((codes_near, in_far))
-    mid_far = to_half(far[:rows] + from_half(in_far))
-    second, codes_near, across, query_pos, mid_far = hold(
-        (far[rows:], codes_near, across, query_pos, mid_far)
-    )
-    mid_far = lax.ppermute(mid_far, "lat", MIDDLE)
-    in_across = lax.ppermute(to_half(second), "lat", INWARD)
+    codes_near, across, query_pos = hold((codes_near, across, query_pos))
     near = decode(codes_near, decoder)
-    near, mid_far = hold((near, mid_far))
+    near, mid_far, in_across = hold((near, mid_far, in_across))
     last = to_half(near[:rows] + from_half(mid_far))
     across, last, second, weights = hold((across, last, second, w_qkv.transpose(1, 0, 2)))
     last = lax.ppermute(last, "lat", PAIRS)
@@ -330,10 +329,14 @@
     keep0, payload0 = project(own)
     near_block, across, payload0 = hold((near, across, payload0))
     keep1, payload1 = project(near_block)
-    third, far, payload1 = hold((jnp.where(outer, across_out, across), far, payload1))
-    third = finish(*project(third))
+    third, far, payload1, first = hold(
+        (jnp.where(outer, across_out, across), far, payload1, finish(keep0, payload0))
+    )
+    keep2, payload2 = project(third)
+    second, payload2 = hold((finish(keep1, payload1), payload2))
+    third = finish(keep2, payload2)
     fourth, third = hold((jnp.where(outer, far_out, far), third))
-    qkv = [finish(keep0, payload0), finish(keep1, payload1), third, finish(*project(fourth))]
+    qkv = [first, second, third, finish(*project(fourth))]
 
     key_row = key_pos.reshape(1, -1)
 

time: 174 us -> 184 us (1.057)
  Pallas kernels: 31.7 us -> 41.6 us
  starting transfers between devices: 40.8 us -> 38 us
    pallas_call x1 -> x2, Pallas kernels: 11.1 us -> 21 us  [decode(): pl.pallas_call(decode_kernel, out_shape=jax.ShapeDtypeStruct((rows, colum...]
    ppermute x16, waiting for transfers between devices: 22.9 us -> 28.5 us  [swap(): return lax.ppermute(value, 'col', [(i, i ^ distance) for i in range(size)])]
    ppermute x2 -> x3, starting transfers between devices: 2.85 us -> 6.36 us  [the longest x1 3.79 us: line_body(): mid_far = lax.ppermute(sent_far, 'lat', MIDDLE)]
    ppermute x2 -> x3, waiting for transfers between devices: 3.37 us -> 0.01 us  [the longest x1 0.01 us: line_body(): in_far = lax.ppermute(sent, 'lat', INWARD)]
    ppermute x2 -> x1, starting transfers between devices: 6.03 us -> 2.79 us  [line_body(): mid_far = lax.ppermute(mid_far, 'lat', MIDDLE)]
    ppermute x1, waiting for transfers between devices: 3.12 us -> 0.01 us  [line_body(): across_out = lax.ppermute(across, 'lat', OUTWARD)]
    ppermute x16, starting transfers between devices: 9.39 us -> 6.54 us  [swap(): return lax.ppermute(value, 'col', [(i, i ^ distance) for i in range(size)])]
    ppermute x2, waiting for transfers between devices: 1.32 us -> 3.73 us  [line_body(): last = lax.ppermute(last, 'lat', PAIRS)]
  transfers between devices with their start and end apart: 34 -> 34, of which waited for: 22 -> 22; matrix products, arithmetic and copies ran while one was open for 12% -> 11% of each run, Pallas kernels for 17% -> 21%
where the time goes in v7:
time: 184 us; the launch traced here: 183 us
  waiting for transfers between devices  70.8 us (38%)
  Pallas kernels  41.6 us (23%)
  starting transfers between devices  38 us (21%)
  matrix products  21.7 us (12%)
  other arithmetic  6.23 us (3%)
  local copies, waits for them, and re-layouts  4.26 us (2%)
    ppermute x16, waiting for transfers between devices, swap(): return lax.ppermute(value, 'col', [(i, i ^ distance) for i in range(size)])  28.5 us
    pallas_call x2, Pallas kernels, decode(): pl.pallas_call(decode_kernel, out_shape=jax.ShapeDtypeStruct((rows, colum...  21 us
    pallas_call x3, Pallas kernels, densify(): pl.pallas_call(functools.partial(densify_kernel, topk=topk, latents=laten...  11.4 us
    dot_general x1, matrix products, line_body(): jnp.dot(densify([packed[3]], base, topk, latents), decoder, preferred_ele...  10.7 us
    ppermute x1, waiting for transfers between devices, line_body(): across = lax.ppermute(own, 'lat', MIDDLE)  9.71 us
    ppermute x16, starting transfers between devices, swap(): return lax.ppermute(value, 'col', [(i, i ^ distance) for i in range(size)])  6.54 us
    ppermute x1, waiting for transfers between devices, line_body(): mid_far = lax.ppermute(mid_far, 'lat', MIDDLE)  5.81 us
    dot_general x4, matrix products, project(): keep = jnp.dot(block, keep_weights, preferred_element_type=jnp.float32)  4.87 us
  transfers between devices with their start and end apart: 34, of which 22 were waited for; matrix products, arithmetic and copies ran while one was open for 11% of the time, Pallas kernels for 21%

profile of v7, /device:TPU:8, one launch (start us, length us, event | category | flops | bytes accessed | tf_op | source)
XLA Modules:
  0.0 183.4 jit_solution(17415001236679417230)
XLA Ops:
  1.9 1.6 collective-permute-start.1
  4.6 1.4 collective-permute-start
  6.0 3.2 %collective-permute-done.1 = f32[16,1024]{1,0:T(8,128)S(1)} collective-permute-done((f32[16,1024]{1,0:T(8,128)S(1)}, f32[16,1024]{1,0:T(8,128)S(1)}, u32[]{:S(2)}, u32[]{:S(2)}) %collective-permute-start.1) | collective-permute-done | bytes 65568 | tf_op jit(solution)/shard_map/ppermute | solution.py:213
  9.5 2.8 %densify.3 = bf16[128,8192]{1,0:T(8,128)(2,1)S(1)} custom-call(s32[1]{0:T(128)} %bitcast.base_ref, f32[16,1024]{1,0:T(8,128)S(1)} %get-tuple-element.111.refs_0_), custom_call_target="tpu_custom_call" | custom-call | flops 1073741824 | bytes 2097152 | tf_op jit(solution)/shard_map/densify/pallas_call | solution.py:64
  12.4 10.7 %multiply_convert_fusion.4 = (f16[128,1280]{1,0:T(8,128)(2,1)}, f32[128,1280]{1,0:T(8,128)S(1)}) fusion(bf16[128,8192]{1,0:T(8,128)(2,1)S(1)} %densify.3, bf16[8192,1280]{1,0:T(8,128)(2,1)} %weights_ref.3), kind=kOutput, calls=%fused_computation.24 | convolution fusion | flops 2684682240 | bytes 24051712 | tf_op jit(solution)/shard_map/dot_general | solution.py:276
  23.1 1.3 collective-permute-start.3
  26.3 1.5 collective-permute-start.4
  27.8 2.9 %densify.4.codes_ref = bf16[128,8192]{1,0:T(8,128)(2,1)S(1)} custom-call(s32[1]{0:T(128)} %bitcast.base_ref, f32[16,1024]{1,0:T(8,128)S(1)} %get-tuple-element.51.refs_0_), custom_call_target="tpu_custom_call" | custom-call | flops 1073741824 | bytes 2097152 | tf_op jit(solution)/shard_map/densify/pallas_call | solution.py:64
  30.7 9.2 %decode.2 = f32[128,1280]{1,0:T(8,128)S(1)} custom-call(bf16[128,8192]{1,0:T(8,128)(2,1)S(1)} %densify.4.codes_ref, bf16[8192,1280]{1,0:T(8,128)(2,1)} %weights_ref.3), custom_call_target="tpu_custom_call" | custom-call | flops 1 | bytes 1 | tf_op jit(solution)/shard_map/decode/pallas_call | solution.py:86
  41.1 3.8 %collective-permute-start.5 = (f16[128,1280]{1,0:T(8,128)(2,1)S(1)}, f16[128,1280]{1,0:T(8,128)(2,1)S(1)}, u32[]{:S(2)}, u32[]{:S(2)}) collective-permute-start(f16[128,1280]{1,0:T(8,128)(2,1)S(1)} %get-tuple-element.58), channel_id=1, source_target_pairs={{4,8},{8,4},{5,9},{9,5},{6,10},{10,6},{7,11},{11,7},{20,24},{24,20... | collective-permute-start | bytes 983048 | tf_op jit(solution)/shard_map/ppermute | solution.py:286
  44.9 1.3 collective-permute-start.6
  46.3 5.7 %densify.5.codes_ref = bf16[256,8192]{1,0:T(8,128)(2,1)S(1)} custom-call(s32[1]{0:T(128)} %bitcast.base_ref, f32[16,1024]{1,0:T(8,128)S(1)} %collective-permute-done.refs_0_, f32[16,1024]{1,0:T(8,128)S(1)} %constant_dynamic-update-slice_fusion.refs_1_), custom_call_target="tpu_custom_call" | custom-call | flops 2147483648 | bytes 4194304 | tf_op jit(solution)/shard_map/densify/pallas_call | solution.py:64
  52.1 11.8 %decode.3 = f32[256,1280]{1,0:T(8,128)S(1)} custom-call(bf16[256,8192]{1,0:T(8,128)(2,1)S(1)} %densify.5.codes_ref, bf16[8192,1280]{1,0:T(8,128)(2,1)} %weights_ref.3), custom_call_target="tpu_custom_call" | custom-call | flops 1 | bytes 1 | tf_op jit(solution)/shard_map/decode/pallas_call | solution.py:86
  64.1 1.3 slice_bitcast_fusion.2
  65.5 2.7 %collective-permute-start.8 = (f16[128,1280]{1,0:T(8,128)(2,1)S(1)}, f16[128,1280]{1,0:T(8,128)(2,1)S(1)}, u32[]{:S(2)}, u32[]{:S(2)}) collective-permute-start(f16[128,1280]{1,0:T(8,128)(2,1)S(1)} %multiply_convert_fusion.1), channel_id=1, source_target_pairs={{0,4},{4,0},{8,12},{12,8},{1,5},{5,1},{9,13},{13,9},{2,6},{6,2},{1... | collective-permute-start | bytes 983048 | tf_op jit(solution)/shard_map/ppermute | solution.py:294
  68.4 2.1 %collective-permute-start.7 = (f16[128,1280]{1,0:T(8,128)(2,1)S(1)}, f16[128,1280]{1,0:T(8,128)(2,1)S(1)}, u32[]{:S(2)}, u32[]{:S(2)}) collective-permute-start(f16[128,1280]{1,0:T(8,128)(2,1)S(1)} %multiply_convert_fusion), channel_id=1, source_target_pairs={{4,8},{8,4},{5,9},{9,5},{6,10},{10,6},{7,11},{11,7},{20,24},{24,20... | collective-permute-start | bytes 983048 | tf_op jit(solution)/shard_map/ppermute | solution.py:295
  71.5 1.8 select_columns.2
  73.3 1.8 select_columns.3
  75.1 1.5 collective-permute-done.8
  76.6 3.5 %collective-permute-done.7 = f16[128,1280]{1,0:T(8,128)(2,1)S(1)} collective-permute-done((f16[128,1280]{1,0:T(8,128)(2,1)S(1)}, f16[128,1280]{1,0:T(8,128)(2,1)S(1)}, u32[]{:S(2)}, u32[]{:S(2)}) %collective-permute-start.7) | collective-permute-done | bytes 327712 | tf_op jit(solution)/shard_map/ppermute | solution.py:295
  82.2 3.0 %collective-permute-done.11 = f32[2,128]{1,0:T(2,128)S(1)} collective-permute-done((f32[2,128]{1,0:T(2,128)S(1)}, f32[2,128]{1,0:T(2,128)S(1)}, u32[]{:S(2)}, u32[]{:S(2)}) %collective-permute-start.11) | collective-permute-done | bytes 1056 | tf_op jit(solution)/shard_map/ppermute | solution.py:218
  86.2 2.2 %collective-permute-start.12 = (bf16[128,1280]{1,0:T(8,128)(2,1)S(1)}, bf16[128,1280]{1,0:T(8,128)(2,1)S(1)}, u32[]{:S(2)}, u32[]{:S(2)}) collective-permute-start(bf16[128,1280]{1,0:T(8,128)(2,1)S(1)} %add_convert_fusion.3), channel_id=1, source_target_pairs={{4,8},{8,4},{5,9},{9,5},{6,10},{10,6},{7,11},{11,7},{20,24},{24,20... | collective-permute-start | bytes 983048 | tf_op jit(solution)/shard_map/ppermute | solution.py:313
  88.5 9.7 %collective-permute-done.12 = bf16[128,1280]{1,0:T(8,128)(2,1)S(1)} collective-permute-done((bf16[128,1280]{1,0:T(8,128)(2,1)S(1)}, bf16[128,1280]{1,0:T(8,128)(2,1)S(1)}, u32[]{:S(2)}, u32[]{:S(2)}) %collective-permute-start.12) | collective-permute-done | bytes 327712 | tf_op jit(solution)/shard_map/ppermute | solution.py:313
  98.2 1.3 collective-permute-start.13
  99.5 2.6 %collective-permute-start.16 = (bf16[128,1280]{1,0:T(8,128)(2,1)S(1)}, bf16[128,1280]{1,0:T(8,128)(2,1)S(1)}, u32[]{:S(2)}, u32[]{:S(2)}) collective-permute-start(bf16[128,1280]{1,0:T(8,128)(2,1)S(1)} %collective-permute-done.14), channel_id=1, source_target_pairs={{4,8},{8,4},{5,9},{9,5},{6,10},{10,6},{7,11},{11,7},{20,24},{24,20... | collective-permute-start | bytes 983048 | tf_op jit(solution)/shard_map/ppermute | solution.py:314
  104.3 4.7 %collective-permute-done.18 = f16[128,768]{1,0:T(8,128)(2,1)S(1)} collective-permute-done((f16[128,768]{1,0:T(8,128)(2,1)S(1)}, f16[128,768]{1,0:T(8,128)(2,1)S(1)}, u32[]{:S(2)}, u32[]{:S(2)}) %collective-permute-start.18) | collective-permute-done | bytes 196640 | tf_op jit(solution)/shard_map/ppermute | solution.py:218
  112.1 1.3 collective-permute-start.21
  113.4 3.0 %collective-permute-done.19 = f16[128,768]{1,0:T(8,128)(2,1)S(1)} collective-permute-done((f16[128,768]{1,0:T(8,128)(2,1)S(1)}, f16[128,768]{1,0:T(8,128)(2,1)S(1)}, u32[]{:S(2)}, u32[]{:S(2)}) %collective-permute-start.19) | collective-permute-done | bytes 196640 | tf_op jit(solution)/shard_map/ppermute | solution.py:218
  117.9 3.4 %collective-permute-done.21 = bf16[128,1280]{1,0:T(8,128)(2,1)S(1)} collective-permute-done((bf16[128,1280]{1,0:T(8,128)(2,1)S(1)}, bf16[128,1280]{1,0:T(8,128)(2,1)S(1)}, u32[]{:S(2)}, u32[]{:S(2)}) %collective-permute-start.21) | collective-permute-done | bytes 327712 | tf_op jit(solution)/shard_map/ppermute | solution.py:316
  121.3 1.6 collective-permute-done.22
  123.9 1.5 collective-permute-done.23
  125.5 2.8 %convolution_add_fusion = f32[128,1536]{1,0:T(8,128)S(1)} fusion(bf16[128,1280]{1,0:T(8,128)(2,1)S(1)} %broadcast_select_fusion, bf16[1280,1536]{1,0:T(8,128)(2,1)} %copy-done, f16[128,1536]{1,0:T(8,128)(2,1)S(1)} %collective-permute-done.23), kind=kOutput, calls=%fused_computation | convolution fusion | flops 503709696 | bytes 5439488 | tf_op jit(solution)/shard_map/dot_general | solution.py:322
  130.1 5.2 %collective-permute-done.24 = f16[128,768]{1,0:T(8,128)(2,1)S(1)} collective-permute-done((f16[128,768]{1,0:T(8,128)(2,1)S(1)}, f16[128,768]{1,0:T(8,128)(2,1)S(1)}, u32[]{:S(2)}, u32[]{:S(2)}) %collective-permute-start.24) | collective-permute-done | bytes 196640 | tf_op jit(solution)/shard_map/ppermute | solution.py:218
  135.4 2.4 %attend.2 = bf16[256,256]{1,0:T(8,128)(2,1)S(1)} custom-call(s32[256,1]{1,0:T(8,128)S(1)} %copy.21.refs_0_, s32[1,512]{1,0:T(1,128)S(1)} %bitcast.57, bf16[128,768]{1,0:T(8,128)(2,1)S(1)} %fusion.17.refs_2_, bf16[128,768]{1,0:T(8,128)(2,1)S(1)} %fusion.16.refs_3_, bf16[128,768]{1,0:T(8,128)(2,1)S(1)} %fusion.15.refs_4_, ...), custom_call_target="tpu_custom_call" | custom-call | flops 536870912 | bytes 2097152 | tf_op jit(solution)/shard_map/attend/pallas_call | solution.py:184
  138.6 2.4 %attend.3 = bf16[256,256]{1,0:T(8,128)(2,1)S(1)} custom-call(s32[256,1]{1,0:T(8,128)S(1)} %copy.22.refs_0_, s32[1,512]{1,0:T(1,128)S(1)} %bitcast.58, bf16[128,768]{1,0:T(8,128)(2,1)S(1)} %fusion.17.refs_2_, bf16[128,768]{1,0:T(8,128)(2,1)S(1)} %fusion.16.refs_3_, bf16[128,768]{1,0:T(8,128)(2,1)S(1)} %fusion.15.refs_4_, ...), custom_call_target="tpu_custom_call" | custom-call | flops 536870912 | bytes 2097152 | tf_op jit(solution)/shard_map/attend/pallas_call | solution.py:184
  141.0 1.8 collective-permute-done.25
  143.0 1.5 collective-permute-done.26
  144.5 2.6 %fusion.2 = f32[256,1280]{1,0:T(8,128)S(1)} fusion(bf16[1024,1280]{1,0:T(8,128)(2,1)} %copy-done.2, bf16[256,512]{1,0:T(8,128)(2,1)S(1)} %collective-permute-done.26, bf16[256,256]{1,0:T(8,128)(2,1)S(1)} %collective-permute-done.25, bf16[256,256]{1,0:T(8,128)(2,1)S(1)} %attend.2), kind=kOutput, calls=%fused_computation.26 | convolution fusion | flops 672661504 | bytes 4456448 | tf_op jit(solution)/shard_map/dot_general | solution.py:354
  147.1 1.3 collective-permute-start.29
  149.1 5.0 %collective-permute-done.27 = bf16[256,256]{1,0:T(8,128)(2,1)S(1)} collective-permute-done((bf16[256,256]{1,0:T(8,128)(2,1)S(1)}, bf16[256,256]{1,0:T(8,128)(2,1)S(1)}, u32[]{:S(2)}, u32[]{:S(2)}) %collective-permute-start.27) | collective-permute-done | bytes 131104 | tf_op jit(solution)/shard_map/ppermute | solution.py:218
  154.1 4.6 %collective-permute-done.29 = bf16[128,1280]{1,0:T(8,128)(2,1)S(1)} collective-permute-done((bf16[128,1280]{1,0:T(8,128)(2,1)S(1)}, bf16[128,1280]{1,0:T(8,128)(2,1)S(1)}, u32[]{:S(2)}, u32[]{:S(2)}) %collective-permute-start.29) | collective-permute-done | bytes 327712 | tf_op jit(solution)/shard_map/ppermute | solution.py:356
  158.9 2.8 %collective-permute-start.30 = (bf16[128,1280]{1,0:T(8,128)(2,1)S(1)}, bf16[128,1280]{1,0:T(8,128)(2,1)S(1)}, u32[]{:S(2)}, u32[]{:S(2)}) collective-permute-start(bf16[128,1280]{1,0:T(8,128)(2,1)S(1)} %get-tuple-element.92), channel_id=1, source_target_pairs={{4,8},{8,4},{5,9},{9,5},{6,10},{10,6},{7,11},{11,7},{20,24},{24,20... | collective-permute-start | bytes 983048 | tf_op jit(solution)/shard_map/ppermute | solution.py:362
  161.7 1.3 collective-permute-start.32
  163.9 5.8 %collective-permute-done.30 = bf16[128,1280]{1,0:T(8,128)(2,1)S(1)} collective-permute-done((bf16[128,1280]{1,0:T(8,128)(2,1)S(1)}, bf16[128,1280]{1,0:T(8,128)(2,1)S(1)}, u32[]{:S(2)}, u32[]{:S(2)}) %collective-permute-start.30) | collective-permute-done | bytes 327712 | tf_op jit(solution)/shard_map/ppermute | solution.py:362
  169.8 3.8 %collective-permute-done.32 = bf16[128,1280]{1,0:T(8,128)(2,1)S(1)} collective-permute-done((bf16[128,1280]{1,0:T(8,128)(2,1)S(1)}, bf16[128,1280]{1,0:T(8,128)(2,1)S(1)}, u32[]{:S(2)}, u32[]{:S(2)}) %collective-permute-start.32) | collective-permute-done | bytes 327712 | tf_op jit(solution)/shard_map/ppermute | solution.py:363
  173.7 3.3 %collective-permute-start.33 = (bf16[128,1280]{1,0:T(8,128)(2,1)S(1)}, bf16[128,1280]{1,0:T(8,128)(2,1)S(1)}, u32[]{:S(2)}, u32[]{:S(2)}) collective-permute-start(bf16[128,1280]{1,0:T(8,128)(2,1)S(1)} %add_convert_fusion.1), channel_id=1, source_target_pairs={{4,8},{8,4},{5,9},{9,5},{6,10},{10,6},{7,11},{11,7},{20,24},{24,20... | collective-permute-start | bytes 983048 | tf_op jit(solution)/shard_map/ppermute | solution.py:368
  177.0 2.2 %collective-permute-done.31 = bf16[128,1280]{1,0:T(8,128)(2,1)S(1)} collective-permute-done((bf16[128,1280]{1,0:T(8,128)(2,1)S(1)}, bf16[128,1280]{1,0:T(8,128)(2,1)S(1)}, u32[]{:S(2)}, u32[]{:S(2)}) %collective-permute-start.31) | collective-permute-done | bytes 327712 | tf_op jit(solution)/shard_map/ppermute | solution.py:366
  179.4 3.3 %collective-permute-done.33 = bf16[128,1280]{1,0:T(8,128)(2,1)S(1)} collective-permute-done((bf16[128,1280]{1,0:T(8,128)(2,1)S(1)}, bf16[128,1280]{1,0:T(8,128)(2,1)S(1)}, u32[]{:S(2)}, u32[]{:S(2)}) %collective-permute-start.33) | collective-permute-done | bytes 327712 | tf_op jit(solution)/shard_map/ppermute | solution.py:368
  (121 shorter events, 24.3 us)
Async XLA Ops:
  1.9 7.3 %collective-permute-start.1 = (f32[16,1024]{1,0:T(8,128)S(1)}, f32[16,1024]{1,0:T(8,128)S(1)}, u32[]{:S(2)}, u32[]{:S(2)}) collective-permute-start(f32[16,1024]{1,0:T(8,128)S(1)} %constant_dynamic-update-slice_fusion.refs_1_), channel_id=1, source_target_pairs={{0,12},{4,8},{8,4},{12,0},{1,13},{5,9},{9,5},{13,1},{2,14},{6,10},... | collective-permute-start | bytes 196616 | tf_op jit(solution)/shard_map/ppermute | solution.py:213
  3.5 6.0 %collective-permute-start.2 = (f32[16,1024]{1,0:T(8,128)S(1)}, f32[16,1024]{1,0:T(8,128)S(1)}, u32[]{:S(2)}, u32[]{:S(2)}) collective-permute-start(f32[16,1024]{1,0:T(8,128)S(1)} %constant_dynamic-update-slice_fusion.refs_1_), channel_id=1, source_target_pairs={{0,8},{4,12},{8,0},{12,4},{1,9},{5,13},{9,1},{13,5},{2,10},{6,14},... | collective-permute-start | bytes 196616 | tf_op jit(solution)/shard_map/ppermute | solution.py:212
  4.6 36.5 %collective-permute-start = (f32[16,1024]{1,0:T(8,128)S(1)}, f32[16,1024]{1,0:T(8,128)S(1)}, u32[]{:S(2)}, u32[]{:S(2)}) collective-permute-start(f32[16,1024]{1,0:T(8,128)S(1)} %constant_dynamic-update-slice_fusion.refs_1_), channel_id=1, source_target_pairs={{0,4},{4,0},{8,12},{12,8},{1,5},{5,1},{9,13},{13,9},{2,6},{6,2},{1... | collective-permute-start | bytes 196616 | tf_op jit(solution)/shard_map/ppermute | solution.py:211
  12.4 12.0 %copy-start.4 = (bf16[2,384,1024]{2,1,0:T(8,128)(2,1)S(1)}, bf16[2,384,1024]{2,1,0:T(8,128)(2,1)}, u32[]{:S(2)}) copy-start(bf16[2,384,1024]{2,1,0:T(8,128)(2,1)} %param.17) | copy-start | bytes 4718596
  23.1 16.8 %collective-permute-start.3 = (f16[128,1280]{1,0:T(8,128)(2,1)}, f16[128,1280]{1,0:T(8,128)(2,1)}, u32[]{:S(2)}, u32[]{:S(2)}) collective-permute-start(f16[128,1280]{1,0:T(8,128)(2,1)} %get-tuple-element.52), channel_id=1, source_target_pairs={{0,4},{12,8},{1,5},{13,9},{2,6},{14,10},{3,7},{15,11},{16,20},{28,... | collective-permute-start | bytes 983048 | tf_op jit(solution)/shard_map/ppermute | solution.py:280
  26.3 25.7 %collective-permute-start.4 = (bf16[2,2,384,256]{3,2,1,0:T(8,128)(2,1)}, bf16[2,2,384,256]{3,2,1,0:T(8,128)(2,1)}, u32[]{:S(2)}, u32[]{:S(2)}) collective-permute-start(bf16[2,2,384,256]{3,2,1,0:T(8,128)(2,1)} %pad_maximum_fusion), channel_id=1, source_target_pairs={{0,2},{1,3},{2,0},{3,1},{4,6},{5,7},{6,4},{7,5},{8,10},{9,11},{10,... | collective-permute-start | bytes 2359304 | tf_op jit(solution)/shard_map/ppermute | solution.py:218
  30.7 15.5 %copy-start.10 = (s32[512]{0:T(512)S(1)}, s32[512]{0:T(512)}, u32[]{:S(2)}) copy-start(s32[512]{0:T(512)} %param.18) | copy-start | bytes 6148
  41.1 22.8 %collective-permute-start.5 = (f16[128,1280]{1,0:T(8,128)(2,1)S(1)}, f16[128,1280]{1,0:T(8,128)(2,1)S(1)}, u32[]{:S(2)}, u32[]{:S(2)}) collective-permute-start(f16[128,1280]{1,0:T(8,128)(2,1)S(1)} %get-tuple-element.58), channel_id=1, source_target_pairs={{4,8},{8,4},{5,9},{9,5},{6,10},{10,6},{7,11},{11,7},{20,24},{24,20... | collective-permute-start | bytes 983048 | tf_op jit(solution)/shard_map/ppermute | solution.py:286
  44.9 19.0 %collective-permute-start.6 = (f16[128,1280]{1,0:T(8,128)(2,1)S(1)}, f16[128,1280]{1,0:T(8,128)(2,1)S(1)}, u32[]{:S(2)}, u32[]{:S(2)}) collective-permute-start(f16[128,1280]{1,0:T(8,128)(2,1)S(1)} %get-tuple-element.59), channel_id=1, source_target_pairs={{0,4},{12,8},{1,5},{13,9},{2,6},{14,10},{3,7},{15,11},{16,20},{28,... | collective-permute-start | bytes 983048 | tf_op jit(solution)/shard_map/ppermute | solution.py:287
  52.0 19.4 %slice-start = ((s8[7864320]{0:T(1024)(128)(4,1)}), s8[4194304]{0:T(1024)(128)(4,1)S(1)}, s32[]{:S(2)}) async-start(s8[7864320]{0:T(1024)(128)(4,1)} %bitcast.52), calls=%async_computation | async-start | bytes 8388608
  52.0 13.3 %copy-start.5 = (bf16[1,2,384,256]{3,2,1,0:T(8,128)(2,1)S(1)}, bf16[1,2,384,256]{3,2,1,0:T(8,128)(2,1)}, u32[]{:S(2)}) copy-start(bf16[1,2,384,256]{3,2,1,0:T(8,128)(2,1)} %get-tuple-element.103) | copy-start | bytes 1179652
  52.1 19.4 %slice-start.1 = ((s8[7864320]{0:T(1024)(128)(4,1)}), s8[3670016]{0:T(1024)(128)(4,1)S(1)}, s32[]{:S(2)}) async-start(s8[7864320]{0:T(1024)(128)(4,1)} %bitcast.52), calls=%async_computation.1 | async-start | bytes 7340032
  63.9 6.6 %copy-start.9 = (bf16[1280]{0:T(1024)(128)(2,1)S(1)}, bf16[1280]{0:T(1024)(128)(2,1)}, u32[]{:S(2)}) copy-start(bf16[1280]{0:T(1024)(128)(2,1)} %param.13) | copy-start | bytes 7684
  63.9 6.7 %copy-start.1 = (bf16[1024,1280]{1,0:T(8,128)(2,1)S(1)}, bf16[1024,1280]{1,0:T(8,128)(2,1)}, u32[]{:S(2)}) copy-start(bf16[1024,1280]{1,0:T(8,128)(2,1)} %from_ref.1) | copy-start | bytes 7864324
  65.5 11.1 %collective-permute-start.9 = (bf16[2,2,384,256]{3,2,1,0:T(8,128)(2,1)S(1)}, bf16[2,2,384,256]{3,2,1,0:T(8,128)(2,1)S(1)}, u32[]{:S(2)}, u32[]{:S(2)}) collective-permute-start(bf16[2,2,384,256]{3,2,1,0:T(8,128)(2,1)S(1)} %pad_maximum_fusion.1), channel_id=1, source_target_pairs={{0,1},{1,0},{2,3},{3,2},{4,5},{5,4},{6,7},{7,6},{8,9},{9,8},{10,11... | collective-permute-start | bytes 2359304 | tf_op jit(solution)/shard_map/ppermute | solution.py:218
  65.5 11.0 %collective-permute-start.8 = (f16[128,1280]{1,0:T(8,128)(2,1)S(1)}, f16[128,1280]{1,0:T(8,128)(2,1)S(1)}, u32[]{:S(2)}, u32[]{:S(2)}) collective-permute-start(f16[128,1280]{1,0:T(8,128)(2,1)S(1)} %multiply_convert_fusion.1), channel_id=1, source_target_pairs={{0,4},{4,0},{8,12},{12,8},{1,5},{5,1},{9,13},{13,9},{2,6},{6,2},{1... | collective-permute-start | bytes 983048 | tf_op jit(solution)/shard_map/ppermute | solution.py:294
  68.4 11.7 %collective-permute-start.7 = (f16[128,1280]{1,0:T(8,128)(2,1)S(1)}, f16[128,1280]{1,0:T(8,128)(2,1)S(1)}, u32[]{:S(2)}, u32[]{:S(2)}) collective-permute-start(f16[128,1280]{1,0:T(8,128)(2,1)S(1)} %multiply_convert_fusion), channel_id=1, source_target_pairs={{4,8},{8,4},{5,9},{9,5},{6,10},{10,6},{7,11},{11,7},{20,24},{24,20... | collective-permute-start | bytes 983048 | tf_op jit(solution)/shard_map/ppermute | solution.py:295
  71.4 1.9 %copy-start.2 = (bf16[1024,1280]{1,0:T(8,128)(2,1)}, bf16[1024,1280]{1,0:T(8,128)(2,1)S(1)}, u32[]{:S(2)}) copy-start(bf16[1024,1280]{1,0:T(8,128)(2,1)S(1)} %select_rows.1) | copy-start | bytes 7864324
  73.3 12.0 %copy-start.7 = (f32[1280]{0:T(1024)S(1)}, f32[1280]{0:T(1024)}, u32[]{:S(2)}) copy-start(f32[1280]{0:T(1024)} %param.15) | copy-start | bytes 15364
  73.3 12.0 %copy-start.8 = (f32[1280]{0:T(1024)S(1)}, f32[1280]{0:T(1024)}, u32[]{:S(2)}) copy-start(f32[1280]{0:T(1024)} %param.14) | copy-start | bytes 15364
  75.1 41.4 %copy-start = (bf16[1280,1536]{1,0:T(8,128)(2,1)}, bf16[1280,1536]{1,0:T(8,128)(2,1)S(1)}, u32[]{:S(2)}) copy-start(bf16[1280,1536]{1,0:T(8,128)(2,1)S(1)} %select_columns.3) | copy-start | bytes 11796484
  76.6 26.3 %copy-start.6 = (bf16[2,2,384,256]{3,2,1,0:T(8,128)(2,1)}, bf16[2,2,384,256]{3,2,1,0:T(8,128)(2,1)S(1)}, u32[]{:S(2)}) copy-start(bf16[2,2,384,256]{3,2,1,0:T(8,128)(2,1)S(1)} %collective-permute-done.9) | copy-start | bytes 2359300
  80.4 1.2 collective-permute-start.10
  81.6 3.6 %collective-permute-start.11 = (f32[2,128]{1,0:T(2,128)S(1)}, f32[2,128]{1,0:T(2,128)S(1)}, u32[]{:S(2)}, u32[]{:S(2)}) collective-permute-start(f32[2,128]{1,0:T(2,128)S(1)} %fusion.22), channel_id=1, source_target_pairs={{0,2},{1,3},{2,0},{3,1},{4,6},{5,7},{6,4},{7,5},{8,10},{9,11},{10,... | collective-permute-start | bytes 3080 | tf_op jit(solution)/shard_map/ppermute | solution.py:218
  86.2 16.0 %collective-permute-start.15 = (f16[128,1536]{1,0:T(8,128)(2,1)S(1)}, f16[128,1536]{1,0:T(8,128)(2,1)S(1)}, u32[]{:S(2)}, u32[]{:S(2)}) collective-permute-start(f16[128,1536]{1,0:T(8,128)(2,1)S(1)} %convolution_convert_fusion.3), channel_id=1, source_target_pairs={{0,1},{1,0},{2,3},{3,2},{4,5},{5,4},{6,7},{7,6},{8,9},{9,8},{10,11... | collective-permute-start | bytes 1179656 | tf_op jit(solution)/shard_map/ppermute | solution.py:218
  86.2 12.0 %collective-permute-start.12 = (bf16[128,1280]{1,0:T(8,128)(2,1)S(1)}, bf16[128,1280]{1,0:T(8,128)(2,1)S(1)}, u32[]{:S(2)}, u32[]{:S(2)}) collective-permute-start(bf16[128,1280]{1,0:T(8,128)(2,1)S(1)} %add_convert_fusion.3), channel_id=1, source_target_pairs={{4,8},{8,4},{5,9},{9,5},{6,10},{10,6},{7,11},{11,7},{20,24},{24,20... | collective-permute-start | bytes 983048 | tf_op jit(solution)/shard_map/ppermute | solution.py:313
  88.4 11.1 %collective-permute-start.14 = (bf16[128,1280]{1,0:T(8,128)(2,1)S(1)}, bf16[128,1280]{1,0:T(8,128)(2,1)S(1)}, u32[]{:S(2)}, u32[]{:S(2)}) collective-permute-start(bf16[128,1280]{1,0:T(8,128)(2,1)S(1)} %add_convert_fusion.3), channel_id=1, source_target_pairs={{0,4},{4,0},{8,12},{12,8},{1,5},{5,1},{9,13},{13,9},{2,6},{6,2},{1... | collective-permute-start | bytes 983048 | tf_op jit(solution)/shard_map/ppermute | solution.py:312
  98.2 10.8 %collective-permute-start.13 = (bf16[128,1280]{1,0:T(8,128)(2,1)S(1)}, bf16[128,1280]{1,0:T(8,128)(2,1)S(1)}, u32[]{:S(2)}, u32[]{:S(2)}) collective-permute-start(bf16[128,1280]{1,0:T(8,128)(2,1)S(1)} %collective-permute-done.12), channel_id=1, source_target_pairs={{4,0},{8,12},{5,1},{9,13},{6,2},{10,14},{7,3},{11,15},{20,16},{24,... | collective-permute-start | bytes 983048 | tf_op jit(solution)/shard_map/ppermute | solution.py:315
  99.5 11.2 %collective-permute-start.16 = (bf16[128,1280]{1,0:T(8,128)(2,1)S(1)}, bf16[128,1280]{1,0:T(8,128)(2,1)S(1)}, u32[]{:S(2)}, u32[]{:S(2)}) collective-permute-start(bf16[128,1280]{1,0:T(8,128)(2,1)S(1)} %collective-permute-done.14), channel_id=1, source_target_pairs={{4,8},{8,4},{5,9},{9,5},{6,10},{10,6},{7,11},{11,7},{20,24},{24,20... | collective-permute-start | bytes 983048 | tf_op jit(solution)/shard_map/ppermute | solution.py:314
  102.9 6.1 %collective-permute-start.18 = (f16[128,768]{1,0:T(8,128)(2,1)S(1)}, f16[128,768]{1,0:T(8,128)(2,1)S(1)}, u32[]{:S(2)}, u32[]{:S(2)}) collective-permute-start(f16[128,768]{1,0:T(8,128)(2,1)S(1)} %slice_convert_fusion.4), channel_id=1, source_target_pairs={{0,2},{1,3},{2,0},{3,1},{4,6},{5,7},{6,4},{7,5},{8,10},{9,11},{10,... | collective-permute-start | bytes 589832 | tf_op jit(solution)/shard_map/ppermute | solution.py:218
  104.2 4.9 %collective-permute-start.17 = (f16[128,1536]{1,0:T(8,128)(2,1)S(1)}, f16[128,1536]{1,0:T(8,128)(2,1)S(1)}, u32[]{:S(2)}, u32[]{:S(2)}) collective-permute-start(f16[128,1536]{1,0:T(8,128)(2,1)S(1)} %convolution_convert_fusion.2), channel_id=1, source_target_pairs={{0,1},{1,0},{2,3},{3,2},{4,5},{5,4},{6,7},{7,6},{8,9},{9,8},{10,11... | collective-permute-start | bytes 1179656 | tf_op jit(solution)/shard_map/ppermute | solution.py:218
  110.8 5.7 %collective-permute-start.19 = (f16[128,768]{1,0:T(8,128)(2,1)S(1)}, f16[128,768]{1,0:T(8,128)(2,1)S(1)}, u32[]{:S(2)}, u32[]{:S(2)}) collective-permute-start(f16[128,768]{1,0:T(8,128)(2,1)S(1)} %slice_convert_fusion.3), channel_id=1, source_target_pairs={{0,2},{1,3},{2,0},{3,1},{4,6},{5,7},{6,4},{7,5},{8,10},{9,11},{10,... | collective-permute-start | bytes 589832 | tf_op jit(solution)/shard_map/ppermute | solution.py:218
  112.0 4.5 %collective-permute-start.20 = (f16[128,1536]{1,0:T(8,128)(2,1)S(1)}, f16[128,1536]{1,0:T(8,128)(2,1)S(1)}, u32[]{:S(2)}, u32[]{:S(2)}) collective-permute-start(f16[128,1536]{1,0:T(8,128)(2,1)S(1)} %convolution_convert_fusion.1), channel_id=1, source_target_pairs={{0,1},{1,0},{2,3},{3,2},{4,5},{5,4},{6,7},{7,6},{8,9},{9,8},{10,11... | collective-permute-start | bytes 1179656 | tf_op jit(solution)/shard_map/ppermute | solution.py:218
  112.1 9.2 %collective-permute-start.21 = (bf16[128,1280]{1,0:T(8,128)(2,1)S(1)}, bf16[128,1280]{1,0:T(8,128)(2,1)S(1)}, u32[]{:S(2)}, u32[]{:S(2)}) collective-permute-start(bf16[128,1280]{1,0:T(8,128)(2,1)S(1)} %collective-permute-done.16), channel_id=1, source_target_pairs={{4,0},{8,12},{5,1},{9,13},{6,2},{10,14},{7,3},{11,15},{20,16},{24,... | collective-permute-start | bytes 983048 | tf_op jit(solution)/shard_map/ppermute | solution.py:316
  117.2 5.7 %collective-permute-start.22 = (f16[128,768]{1,0:T(8,128)(2,1)S(1)}, f16[128,768]{1,0:T(8,128)(2,1)S(1)}, u32[]{:S(2)}, u32[]{:S(2)}) collective-permute-start(f16[128,768]{1,0:T(8,128)(2,1)S(1)} %slice_convert_fusion.2), channel_id=1, source_target_pairs={{0,2},{1,3},{2,0},{3,1},{4,6},{5,7},{6,4},{7,5},{8,10},{9,11},{10,... | collective-permute-start | bytes 589832 | tf_op jit(solution)/shard_map/ppermute | solution.py:218
  123.7 1.8 collective-permute-start.23
  128.3 7.0 %collective-permute-start.24 = (f16[128,768]{1,0:T(8,128)(2,1)S(1)}, f16[128,768]{1,0:T(8,128)(2,1)S(1)}, u32[]{:S(2)}, u32[]{:S(2)}) collective-permute-start(f16[128,768]{1,0:T(8,128)(2,1)S(1)} %slice_convert_fusion.1), channel_id=1, source_target_pairs={{0,2},{1,3},{2,0},{3,1},{4,6},{5,7},{6,4},{7,5},{8,10},{9,11},{10,... | collective-permute-start | bytes 589832 | tf_op jit(solution)/shard_map/ppermute | solution.py:218
  137.8 5.0 %collective-permute-start.25 = (bf16[256,256]{1,0:T(8,128)(2,1)S(1)}, bf16[256,256]{1,0:T(8,128)(2,1)S(1)}, u32[]{:S(2)}, u32[]{:S(2)}) collective-permute-start(bf16[256,256]{1,0:T(8,128)(2,1)S(1)} %attend.2), channel_id=1, source_target_pairs={{0,2},{1,3},{2,0},{3,1},{4,6},{5,7},{6,4},{7,5},{8,10},{9,11},{10,... | collective-permute-start | bytes 393224 | tf_op jit(solution)/shard_map/ppermute | solution.py:218
  142.9 20.1 %copy-start.3 = (bf16[1024,1280]{1,0:T(8,128)(2,1)S(1)}, bf16[1024,1280]{1,0:T(8,128)(2,1)}, u32[]{:S(2)}) copy-start(bf16[1024,1280]{1,0:T(8,128)(2,1)} %copy-done.2) | copy-start | bytes 7864324
  142.9 1.6 collective-permute-start.26
  147.1 11.6 %collective-permute-start.29 = (bf16[128,1280]{1,0:T(8,128)(2,1)S(1)}, bf16[128,1280]{1,0:T(8,128)(2,1)S(1)}, u32[]{:S(2)}, u32[]{:S(2)}) collective-permute-start(bf16[128,1280]{1,0:T(8,128)(2,1)S(1)} %slice.146), channel_id=1, source_target_pairs={{0,4},{12,8},{1,5},{13,9},{2,6},{14,10},{3,7},{15,11},{16,20},{28,... | collective-permute-start | bytes 983048 | tf_op jit(solution)/shard_map/ppermute | solution.py:356
  148.4 5.6 %collective-permute-start.27 = (bf16[256,256]{1,0:T(8,128)(2,1)S(1)}, bf16[256,256]{1,0:T(8,128)(2,1)S(1)}, u32[]{:S(2)}, u32[]{:S(2)}) collective-permute-start(bf16[256,256]{1,0:T(8,128)(2,1)S(1)} %attend.3), channel_id=1, source_target_pairs={{0,2},{1,3},{2,0},{3,1},{4,6},{5,7},{6,4},{7,5},{8,10},{9,11},{10,... | collective-permute-start | bytes 393224 | tf_op jit(solution)/shard_map/ppermute | solution.py:218
  154.1 9.0 %collective-permute-start.28 = (bf16[256,512]{1,0:T(8,128)(2,1)S(1)}, bf16[256,512]{1,0:T(8,128)(2,1)S(1)}, u32[]{:S(2)}, u32[]{:S(2)}) collective-permute-start(bf16[256,512]{1,0:T(8,128)(2,1)S(1)} %pad_maximum_fusion.3), channel_id=1, source_target_pairs={{0,1},{1,0},{2,3},{3,2},{4,5},{5,4},{6,7},{7,6},{8,9},{9,8},{10,11... | collective-permute-start | bytes 786440 | tf_op jit(solution)/shard_map/ppermute | solution.py:218
  158.9 10.8 %collective-permute-start.30 = (bf16[128,1280]{1,0:T(8,128)(2,1)S(1)}, bf16[128,1280]{1,0:T(8,128)(2,1)S(1)}, u32[]{:S(2)}, u32[]{:S(2)}) collective-permute-start(bf16[128,1280]{1,0:T(8,128)(2,1)S(1)} %get-tuple-element.92), channel_id=1, source_target_pairs={{4,8},{8,4},{5,9},{9,5},{6,10},{10,6},{7,11},{11,7},{20,24},{24,20... | collective-permute-start | bytes 983048 | tf_op jit(solution)/shard_map/ppermute | solution.py:362
  161.7 11.9 %collective-permute-start.32 = (bf16[128,1280]{1,0:T(8,128)(2,1)S(1)}, bf16[128,1280]{1,0:T(8,128)(2,1)S(1)}, u32[]{:S(2)}, u32[]{:S(2)}) collective-permute-start(bf16[128,1280]{1,0:T(8,128)(2,1)S(1)} %convert_element_type.164), channel_id=1, source_target_pairs={{0,4},{12,8},{1,5},{13,9},{2,6},{14,10},{3,7},{15,11},{16,20},{28,... | collective-permute-start | bytes 983048 | tf_op jit(solution)/shard_map/ppermute | solution.py:363
  169.7 9.5 %collective-permute-start.31 = (bf16[128,1280]{1,0:T(8,128)(2,1)S(1)}, bf16[128,1280]{1,0:T(8,128)(2,1)S(1)}, u32[]{:S(2)}, u32[]{:S(2)}) collective-permute-start(bf16[128,1280]{1,0:T(8,128)(2,1)S(1)} %fusion), channel_id=1, source_target_pairs={{0,4},{4,0},{8,12},{12,8},{1,5},{5,1},{9,13},{13,9},{2,6},{6,2},{1... | collective-permute-start | bytes 983048 | tf_op jit(solution)/shard_map/ppermute | solution.py:366
  173.7 9.0 %collective-permute-start.33 = (bf16[128,1280]{1,0:T(8,128)(2,1)S(1)}, bf16[128,1280]{1,0:T(8,128)(2,1)S(1)}, u32[]{:S(2)}, u32[]{:S(2)}) collective-permute-start(bf16[128,1280]{1,0:T(8,128)(2,1)S(1)} %add_convert_fusion.1), channel_id=1, source_target_pairs={{4,8},{8,4},{5,9},{9,5},{6,10},{10,6},{7,11},{11,7},{20,24},{24,20... | collective-permute-start | bytes 983048 | tf_op jit(solution)/shard_map/ppermute | solution.py:368

commit v8 on v7

--- a/solution.py
+++ b/solution.py
@@ -75,27 +75,32 @@
     )(base, *packed)
 
 
-def decode_kernel(codes_ref, weights_ref, out_ref):
+def decode_kernel(codes_ref, weights_ref, *rest):
+    out_ref = rest[-1]
     out_ref[...] = jnp.dot(codes_ref[...], weights_ref[...], preferred_element_type=jnp.float32)
 
 
-def decode(codes, decoder):
+def decode(codes, decoder, first, count, into=None):
     rows, latents = codes.shape
     columns = decoder.shape[1]
     width = math.gcd(columns, 256)
+    here = pl.BlockSpec((rows, width), lambda n: (0, first + n))
+    operands = [codes, decoder] + ([] if into is None else [into])
     return pl.pallas_call(
         decode_kernel,
         out_shape=jax.ShapeDtypeStruct((rows, columns), jnp.float32),
-        grid=(columns // width,),
+        grid=(count,),
         in_specs=[
             pl.BlockSpec((rows, latents), lambda n: (0, 0)),
-            pl.BlockSpec((latents, width), lambda n: (0, n)),
-        ],
-        out_specs=pl.BlockSpec((rows, width), lambda n: (0, n)),
+            pl.BlockSpec((latents, width), lambda n: (0, first + n)),
+        ]
+        + ([] if into is None else [pl.BlockSpec(memory_space=pl.ANY)]),
+        out_specs=here,
+        input_output_aliases={} if into is None else {2: 0},
         compiler_params=pltpu.CompilerParams(vmem_limit_bytes=DECODE_BYTES),
         cost_estimate=SMALL,
         name="decode",
-    )(codes, decoder)
+    )(*operands)
 
 
 def copy_kernel(order_ref, from_ref, to_ref):
@@ -273,21 +278,22 @@
     )
     query_pos = key_pos.reshape(-1, 1)
 
-    far = jnp.dot(
-        densify([packed[3]], base, topk, latents), decoder, preferred_element_type=jnp.float32
+    codes_far = densify([packed[3], packed[2]], base, topk, latents)
+    far = jnp.dot(codes_far, decoder, preferred_element_type=jnp.float32)
+    near_packed, sent = hold(((packed[1], packed[0]), to_half(far[:rows])))
+    in_far = lax.ppermute(sent, "lat", INWARD)
+    codes_near = densify(near_packed, base, topk, latents)
+    blocks = columns // math.gcd(columns, 256)
+    ahead = blocks * 2 // 5
+    near = decode(codes_near, decoder, 0, ahead)
+    near, in_far = hold((near, in_far))
+    mid_far = to_half(far[:rows] + from_half(in_far))
+    second, near, codes_near, across, query_pos, mid_far = hold(
+        (far[rows:], near, codes_near, across, query_pos, mid_far)
     )
-    packed2, sent = hold((packed[2], to_half(far)))
-    in_far = lax.ppermute(sent, "lat", INWARD)
-    second = decode(densify([packed2], base, topk, latents), decoder)
-    second, in_far = hold((second, in_far))
-    near_packed, sent_far, sent_across = hold(
-        ((packed[1], packed[0]), to_half(far + from_half(in_far)), to_half(second))
-    )
-    mid_far = lax.ppermute(sent_far, "lat", MIDDLE)
-    in_across = lax.ppermute(sent_across, "lat", INWARD)
-    codes_near = densify(near_packed, base, topk, latents)
-    codes_near, across, query_pos = hold((codes_near, across, query_pos))
-    near = decode(codes_near, decoder)
+    mid_far = lax.ppermute(mid_far, "lat", MIDDLE)
+    in_across = lax.ppermute(to_half(second), "lat", INWARD)
+    near = decode(codes_near, decoder, ahead, blocks - ahead, into=near)
     near, mid_far, in_across = hold((near, mid_far, in_across))
     last = to_half(near[:rows] + from_half(mid_far))
     across, last, second, weights = hold((across, last, second, w_qkv.transpose(1, 0, 2)))

time: 184 us -> 167 us (0.908)
  waiting for transfers between devices: 70.8 us -> 59.6 us
  Pallas kernels: 41.6 us -> 32.3 us
  starting transfers between devices: 38 us -> 44.9 us
    pallas_call x2, Pallas kernels: 21 us -> 11.7 us  [decode(): pl.pallas_call(decode_kernel, out_shape=jax.ShapeDtypeStruct((rows, colum...]
    ppermute x16, starting transfers between devices: 6.54 us -> 13 us  [swap(): return lax.ppermute(value, 'col', [(i, i ^ distance) for i in range(size)])]
    ppermute x16, waiting for transfers between devices: 28.5 us -> 22.3 us  [swap(): return lax.ppermute(value, 'col', [(i, i ^ distance) for i in range(size)])]
    ppermute x1 -> x2, starting transfers between devices: 2.79 us -> 7.02 us  [line_body(): mid_far = lax.ppermute(mid_far, 'lat', MIDDLE)]
    ppermute x2 -> x1, starting transfers between devices: 5.08 us -> 1.56 us  [line_body(): in_across = lax.ppermute(to_half(second), 'lat', INWARD)]
    ppermute x1, waiting for transfers between devices: 3.18 us -> 0.06 us  [line_gather_direct(): three = lax.ppermute(own, 'lat', [(i, i ^ 3) for i in range(4)])]
    ppermute x2, starting transfers between devices: 2.78 us -> 0.14 us  [line_body(): last = lax.ppermute(last, 'lat', PAIRS)]
    ppermute x1 -> x2, waiting for transfers between devices: 5.81 us -> 5.53 us  [line_body(): mid_far = lax.ppermute(mid_far, 'lat', MIDDLE)]
  transfers between devices with their start and end apart: 34 -> 34, of which waited for: 22 -> 21; matrix products, arithmetic and copies ran while one was open for 11% -> 11% of each run, Pallas kernels for 21% -> 18%
where the time goes in v8:
time: 167 us; the launch traced here: 166 us
  waiting for transfers between devices  59.6 us (36%)
  starting transfers between devices  44.9 us (27%)
  Pallas kernels  32.3 us (19%)
  matrix products  20.9 us (13%)
  other arithmetic  4.43 us (3%)
  local copies, waits for them, and re-layouts  3.5 us (2%)
    ppermute x16, waiting for transfers between devices, swap(): return lax.ppermute(value, 'col', [(i, i ^ distance) for i in range(size)])  22.3 us
    ppermute x16, starting transfers between devices, swap(): return lax.ppermute(value, 'col', [(i, i ^ distance) for i in range(size)])  13 us
    pallas_call x2, Pallas kernels, decode(): pl.pallas_call(decode_kernel, out_shape=jax.ShapeDtypeStruct((rows, colum...  11.7 us
    pallas_call x2, Pallas kernels, densify(): pl.pallas_call(functools.partial(densify_kernel, topk=topk, latents=laten...  11.4 us
    dot_general x1, matrix products, line_body(): far = jnp.dot(codes_far, decoder, preferred_element_type=jnp.float32)  9.88 us
    ppermute x1, waiting for transfers between devices, line_body(): across = lax.ppermute(own, 'lat', MIDDLE)  8.7 us
    ppermute x2, starting transfers between devices, line_body(): mid_far = lax.ppermute(mid_far, 'lat', MIDDLE)  7.02 us
    ppermute x2, waiting for transfers between devices, line_body(): mid_far = lax.ppermute(mid_far, 'lat', MIDDLE)  5.53 us
  transfers between devices with their start and end apart: 34, of which 21 were waited for; matrix products, arithmetic and copies ran while one was open for 11% of the time, Pallas kernels for 18%

profile of v8, /device:TPU:8, one launch (start us, length us, event | category | flops | bytes accessed | tf_op | source)
XLA Modules:
  0.0 166.5 jit_solution(1138115256500503307)
XLA Ops:
  1.9 1.6 collective-permute-start
  4.6 1.4 collective-permute-start.2
  6.0 1.5 constant_dynamic-slice_fusion
  7.5 1.6 collective-permute-start.4
  9.5 5.7 %densify.2 = bf16[256,8192]{1,0:T(8,128)(2,1)S(1)} custom-call(s32[1]{0:T(128)} %bitcast.base_ref, f32[16,1024]{1,0:T(8,128)S(1)} %get-tuple-element.113.refs_0_, f32[16,1024]{1,0:T(8,128)S(1)} %get-tuple-element.112.refs_1_), custom_call_target="tpu_custom_call" | custom-call | flops 2147483648 | bytes 4194304 | tf_op jit(solution)/shard_map/densify/pallas_call | solution.py:64
  15.2 9.9 %fusion.26 = f32[256,1280]{1,0:T(8,128)S(1)} fusion(bf16[256,8192]{1,0:T(8,128)(2,1)S(1)} %densify.2, bf16[8192,1280]{1,0:T(8,128)(2,1)} %weights_ref.3), kind=kOutput, calls=%fused_computation.83 | convolution fusion | flops 5368709120 | bytes 26476544 | tf_op jit(solution)/shard_map/dot_general | solution.py:282
  25.2 1.3 collective-permute-start.3
  26.6 5.7 %densify.3.codes_ref = bf16[256,8192]{1,0:T(8,128)(2,1)S(1)} custom-call(s32[1]{0:T(128)} %bitcast.base_ref, f32[16,1024]{1,0:T(8,128)S(1)} %collective-permute-done.2.refs_0_, f32[16,1024]{1,0:T(8,128)S(1)} %constant_dynamic-update-slice_fusion.refs_1_), custom_call_target="tpu_custom_call" | custom-call | flops 2147483648 | bytes 4194304 | tf_op jit(solution)/shard_map/densify/pallas_call | solution.py:64
  32.3 4.8 %decode.2.rest_0_ = f32[256,1280]{1,0:T(8,128)S(1)} custom-call(bf16[256,8192]{1,0:T(8,128)(2,1)S(1)} %densify.3.codes_ref, bf16[8192,1280]{1,0:T(8,128)(2,1)} %weights_ref.3), custom_call_target="tpu_custom_call" | custom-call | flops 1 | bytes 1 | tf_op jit(solution)/shard_map/decode/pallas_call | solution.py:89
  37.4 1.6 collective-permute-start.6
  38.9 4.0 %collective-permute-start.5 = (f16[128,1280]{1,0:T(8,128)(2,1)S(1)}, f16[128,1280]{1,0:T(8,128)(2,1)S(1)}, u32[]{:S(2)}, u32[]{:S(2)}) collective-permute-start(f16[128,1280]{1,0:T(8,128)(2,1)S(1)} %get-tuple-element.58), channel_id=1, source_target_pairs={{4,8},{8,4},{5,9},{9,5},{6,10},{10,6},{7,11},{11,7},{20,24},{24,20... | collective-permute-start | bytes 983048 | tf_op jit(solution)/shard_map/ppermute | solution.py:294
  42.9 6.9 %decode.3 = f32[256,1280]{1,0:T(8,128)S(1)} custom-call(bf16[256,8192]{1,0:T(8,128)(2,1)S(1)} %densify.3.codes_ref, bf16[8192,1280]{1,0:T(8,128)(2,1)} %weights_ref.3, f32[256,1280]{1,0:T(8,128)S(1)} %decode.2.rest_0_), custom_call_target="tpu_custom_call", output_to_operand_aliasing={{}: (2, {})} | custom-call | flops 1 | bytes 1 | tf_op jit(solution)/shard_map/decode/pallas_call | solution.py:89
  50.4 3.5 %collective-permute-start.7 = (f16[128,1280]{1,0:T(8,128)(2,1)S(1)}, f16[128,1280]{1,0:T(8,128)(2,1)S(1)}, u32[]{:S(2)}, u32[]{:S(2)}) collective-permute-start(f16[128,1280]{1,0:T(8,128)(2,1)S(1)} %multiply_convert_fusion), channel_id=1, source_target_pairs={{4,8},{8,4},{5,9},{9,5},{6,10},{10,6},{7,11},{11,7},{20,24},{24,20... | collective-permute-start | bytes 983048 | tf_op jit(solution)/shard_map/ppermute | solution.py:301
  54.9 1.8 %select_columns.2 = bf16[1280,1536]{1,0:T(8,128)(2,1)S(1)} custom-call(s32[2]{0:T(128)S(1)} %get-tuple-element.122.order_ref, bf16[3,1280,1024]{2,1,0:T(8,128)(2,1)S(1)} %bitcast.54), custom_call_target="tpu_custom_call" | custom-call | bytes 7864320 | tf_op jit(solution)/shard_map/select_columns/pallas_call | solution.py:113
  56.7 1.8 %select_columns.3 = bf16[1280,1536]{1,0:T(8,128)(2,1)S(1)} custom-call(s32[2]{0:T(128)S(1)} %get-tuple-element.123.order_ref, bf16[3,1280,1024]{2,1,0:T(8,128)(2,1)S(1)} %bitcast.55), custom_call_target="tpu_custom_call" | custom-call | bytes 7864320 | tf_op jit(solution)/shard_map/select_columns/pallas_call | solution.py:113
  58.5 1.8 %collective-permute-done.8 = f16[128,1280]{1,0:T(8,128)(2,1)S(1)} collective-permute-done((f16[128,1280]{1,0:T(8,128)(2,1)S(1)}, f16[128,1280]{1,0:T(8,128)(2,1)S(1)}, u32[]{:S(2)}, u32[]{:S(2)}) %collective-permute-start.8) | collective-permute-done | bytes 327712 | tf_op jit(solution)/shard_map/ppermute | solution.py:300
  60.3 2.0 %collective-permute-done.7 = f16[128,1280]{1,0:T(8,128)(2,1)S(1)} collective-permute-done((f16[128,1280]{1,0:T(8,128)(2,1)S(1)}, f16[128,1280]{1,0:T(8,128)(2,1)S(1)}, u32[]{:S(2)}, u32[]{:S(2)}) %collective-permute-start.7) | collective-permute-done | bytes 327712 | tf_op jit(solution)/shard_map/ppermute | solution.py:301
  63.9 1.6 collective-permute-start.11
  65.4 2.1 %collective-permute-done.11 = f32[2,128]{1,0:T(2,128)S(1)} collective-permute-done((f32[2,128]{1,0:T(2,128)S(1)}, f32[2,128]{1,0:T(2,128)S(1)}, u32[]{:S(2)}, u32[]{:S(2)}) %collective-permute-start.11) | collective-permute-done | bytes 1056 | tf_op jit(solution)/shard_map/ppermute | solution.py:223
  68.5 3.2 %collective-permute-start.12 = (bf16[128,1280]{1,0:T(8,128)(2,1)S(1)}, bf16[128,1280]{1,0:T(8,128)(2,1)S(1)}, u32[]{:S(2)}, u32[]{:S(2)}) collective-permute-start(bf16[128,1280]{1,0:T(8,128)(2,1)S(1)} %add_convert_fusion.3), channel_id=1, source_target_pairs={{4,8},{8,4},{5,9},{9,5},{6,10},{10,6},{7,11},{11,7},{20,24},{24,20... | collective-permute-start | bytes 983048 | tf_op jit(solution)/shard_map/ppermute | solution.py:319
  71.8 8.7 %collective-permute-done.12 = bf16[128,1280]{1,0:T(8,128)(2,1)S(1)} collective-permute-done((bf16[128,1280]{1,0:T(8,128)(2,1)S(1)}, bf16[128,1280]{1,0:T(8,128)(2,1)S(1)}, u32[]{:S(2)}, u32[]{:S(2)}) %collective-permute-start.12) | collective-permute-done | bytes 327712 | tf_op jit(solution)/shard_map/ppermute | solution.py:319
  80.5 1.3 collective-permute-start.13
  81.8 3.4 %collective-permute-start.16 = (bf16[128,1280]{1,0:T(8,128)(2,1)S(1)}, bf16[128,1280]{1,0:T(8,128)(2,1)S(1)}, u32[]{:S(2)}, u32[]{:S(2)}) collective-permute-start(bf16[128,1280]{1,0:T(8,128)(2,1)S(1)} %collective-permute-done.14), channel_id=1, source_target_pairs={{4,8},{8,4},{5,9},{9,5},{6,10},{10,6},{7,11},{11,7},{20,24},{24,20... | collective-permute-start | bytes 983048 | tf_op jit(solution)/shard_map/ppermute | solution.py:320
  86.0 1.6 collective-permute-start.18
  88.3 4.0 %collective-permute-done.18 = f16[128,768]{1,0:T(8,128)(2,1)S(1)} collective-permute-done((f16[128,768]{1,0:T(8,128)(2,1)S(1)}, f16[128,768]{1,0:T(8,128)(2,1)S(1)}, u32[]{:S(2)}, u32[]{:S(2)}) %collective-permute-start.18) | collective-permute-done | bytes 196640 | tf_op jit(solution)/shard_map/ppermute | solution.py:223
  93.2 1.6 collective-permute-start.19
  95.5 1.3 collective-permute-start.21
  96.8 2.1 %collective-permute-done.19 = f16[128,768]{1,0:T(8,128)(2,1)S(1)} collective-permute-done((f16[128,768]{1,0:T(8,128)(2,1)S(1)}, f16[128,768]{1,0:T(8,128)(2,1)S(1)}, u32[]{:S(2)}, u32[]{:S(2)}) %collective-permute-start.19) | collective-permute-done | bytes 196640 | tf_op jit(solution)/shard_map/ppermute | solution.py:223
  99.7 1.6 collective-permute-start.22
  101.2 3.4 %collective-permute-done.21 = bf16[128,1280]{1,0:T(8,128)(2,1)S(1)} collective-permute-done((bf16[128,1280]{1,0:T(8,128)(2,1)S(1)}, bf16[128,1280]{1,0:T(8,128)(2,1)S(1)}, u32[]{:S(2)}, u32[]{:S(2)}) %collective-permute-start.21) | collective-permute-done | bytes 327712 | tf_op jit(solution)/shard_map/ppermute | solution.py:322
  106.4 1.5 collective-permute-done.23
  107.9 2.8 %convolution_add_fusion = f32[128,1536]{1,0:T(8,128)S(1)} fusion(bf16[128,1280]{1,0:T(8,128)(2,1)S(1)} %broadcast_select_fusion, bf16[1280,1536]{1,0:T(8,128)(2,1)} %copy-done, f16[128,1536]{1,0:T(8,128)(2,1)S(1)} %collective-permute-done.23), kind=kOutput, calls=%fused_computation | convolution fusion | flops 503709696 | bytes 5439488 | tf_op jit(solution)/shard_map/dot_general | solution.py:328
  110.8 1.6 collective-permute-start.24
  113.5 4.3 %collective-permute-done.24 = f16[128,768]{1,0:T(8,128)(2,1)S(1)} collective-permute-done((f16[128,768]{1,0:T(8,128)(2,1)S(1)}, f16[128,768]{1,0:T(8,128)(2,1)S(1)}, u32[]{:S(2)}, u32[]{:S(2)}) %collective-permute-start.24) | collective-permute-done | bytes 196640 | tf_op jit(solution)/shard_map/ppermute | solution.py:223
  117.9 2.4 %attend.2 = bf16[256,256]{1,0:T(8,128)(2,1)S(1)} custom-call(s32[256,1]{1,0:T(8,128)S(1)} %copy.22.refs_0_, s32[1,512]{1,0:T(1,128)S(1)} %bitcast.57, bf16[128,768]{1,0:T(8,128)(2,1)S(1)} %fusion.17.refs_2_, bf16[128,768]{1,0:T(8,128)(2,1)S(1)} %fusion.16.refs_3_, bf16[128,768]{1,0:T(8,128)(2,1)S(1)} %fusion.15.refs_4_, ...), custom_call_target="tpu_custom_call" | custom-call | flops 536870912 | bytes 2097152 | tf_op jit(solution)/shard_map/attend/pallas_call | solution.py:189
  120.3 1.6 collective-permute-start.25
  122.0 2.4 %attend.3 = bf16[256,256]{1,0:T(8,128)(2,1)S(1)} custom-call(s32[256,1]{1,0:T(8,128)S(1)} %copy.23.refs_0_, s32[1,512]{1,0:T(1,128)S(1)} %bitcast.58, bf16[128,768]{1,0:T(8,128)(2,1)S(1)} %fusion.17.refs_2_, bf16[128,768]{1,0:T(8,128)(2,1)S(1)} %fusion.16.refs_3_, bf16[128,768]{1,0:T(8,128)(2,1)S(1)} %fusion.15.refs_4_, ...), custom_call_target="tpu_custom_call" | custom-call | flops 536870912 | bytes 2097152 | tf_op jit(solution)/shard_map/attend/pallas_call | solution.py:189
  125.4 1.5 collective-permute-done.26
  126.9 2.6 %fusion.2 = f32[256,1280]{1,0:T(8,128)S(1)} fusion(bf16[1024,1280]{1,0:T(8,128)(2,1)} %copy-done.2, bf16[256,512]{1,0:T(8,128)(2,1)S(1)} %collective-permute-done.26, bf16[256,256]{1,0:T(8,128)(2,1)S(1)} %collective-permute-done.25, bf16[256,256]{1,0:T(8,128)(2,1)S(1)} %attend.2), kind=kOutput, calls=%fused_computation.26 | convolution fusion | flops 672661504 | bytes 4456448 | tf_op jit(solution)/shard_map/dot_general | solution.py:360
  130.9 1.5 collective-permute-start.27
  132.4 4.1 %collective-permute-done.27 = bf16[256,256]{1,0:T(8,128)(2,1)S(1)} collective-permute-done((bf16[256,256]{1,0:T(8,128)(2,1)S(1)}, bf16[256,256]{1,0:T(8,128)(2,1)S(1)}, u32[]{:S(2)}, u32[]{:S(2)}) %collective-permute-start.27) | collective-permute-done | bytes 131104 | tf_op jit(solution)/shard_map/ppermute | solution.py:223
  136.6 4.6 %collective-permute-done.29 = bf16[128,1280]{1,0:T(8,128)(2,1)S(1)} collective-permute-done((bf16[128,1280]{1,0:T(8,128)(2,1)S(1)}, bf16[128,1280]{1,0:T(8,128)(2,1)S(1)}, u32[]{:S(2)}, u32[]{:S(2)}) %collective-permute-start.29) | collective-permute-done | bytes 327712 | tf_op jit(solution)/shard_map/ppermute | solution.py:362
  141.3 3.1 %collective-permute-start.30 = (bf16[128,1280]{1,0:T(8,128)(2,1)S(1)}, bf16[128,1280]{1,0:T(8,128)(2,1)S(1)}, u32[]{:S(2)}, u32[]{:S(2)}) collective-permute-start(bf16[128,1280]{1,0:T(8,128)(2,1)S(1)} %get-tuple-element.92), channel_id=1, source_target_pairs={{4,8},{8,4},{5,9},{9,5},{6,10},{10,6},{7,11},{11,7},{20,24},{24,20... | collective-permute-start | bytes 983048 | tf_op jit(solution)/shard_map/ppermute | solution.py:368
  146.6 5.5 %collective-permute-done.30 = bf16[128,1280]{1,0:T(8,128)(2,1)S(1)} collective-permute-done((bf16[128,1280]{1,0:T(8,128)(2,1)S(1)}, bf16[128,1280]{1,0:T(8,128)(2,1)S(1)}, u32[]{:S(2)}, u32[]{:S(2)}) %collective-permute-start.30) | collective-permute-done | bytes 327712 | tf_op jit(solution)/shard_map/ppermute | solution.py:368
  152.3 4.4 %collective-permute-done.32 = bf16[128,1280]{1,0:T(8,128)(2,1)S(1)} collective-permute-done((bf16[128,1280]{1,0:T(8,128)(2,1)S(1)}, bf16[128,1280]{1,0:T(8,128)(2,1)S(1)}, u32[]{:S(2)}, u32[]{:S(2)}) %collective-permute-start.32) | collective-permute-done | bytes 327712 | tf_op jit(solution)/shard_map/ppermute | solution.py:369
  156.7 2.5 %collective-permute-start.33 = (bf16[128,1280]{1,0:T(8,128)(2,1)S(1)}, bf16[128,1280]{1,0:T(8,128)(2,1)S(1)}, u32[]{:S(2)}, u32[]{:S(2)}) collective-permute-start(bf16[128,1280]{1,0:T(8,128)(2,1)S(1)} %add_convert_fusion.1), channel_id=1, source_target_pairs={{4,8},{8,4},{5,9},{9,5},{6,10},{10,6},{7,11},{11,7},{20,24},{24,20... | collective-permute-start | bytes 983048 | tf_op jit(solution)/shard_map/ppermute | solution.py:374
  159.2 2.8 %collective-permute-done.31 = bf16[128,1280]{1,0:T(8,128)(2,1)S(1)} collective-permute-done((bf16[128,1280]{1,0:T(8,128)(2,1)S(1)}, bf16[128,1280]{1,0:T(8,128)(2,1)S(1)}, u32[]{:S(2)}, u32[]{:S(2)}) %collective-permute-start.31) | collective-permute-done | bytes 327712 | tf_op jit(solution)/shard_map/ppermute | solution.py:372
  162.1 3.6 %collective-permute-done.33 = bf16[128,1280]{1,0:T(8,128)(2,1)S(1)} collective-permute-done((bf16[128,1280]{1,0:T(8,128)(2,1)S(1)}, bf16[128,1280]{1,0:T(8,128)(2,1)S(1)}, u32[]{:S(2)}, u32[]{:S(2)}) %collective-permute-start.33) | collective-permute-done | bytes 327712 | tf_op jit(solution)/shard_map/ppermute | solution.py:374
  (118 shorter events, 20.5 us)
Async XLA Ops:
  1.9 7.3 %collective-permute-start = (f32[16,1024]{1,0:T(8,128)S(1)}, f32[16,1024]{1,0:T(8,128)S(1)}, u32[]{:S(2)}, u32[]{:S(2)}) collective-permute-start(f32[16,1024]{1,0:T(8,128)S(1)} %constant_dynamic-update-slice_fusion.refs_1_), channel_id=1, source_target_pairs={{0,12},{4,8},{8,4},{12,0},{1,13},{5,9},{9,5},{13,1},{2,14},{6,10},... | collective-permute-start | bytes 196616 | tf_op jit(solution)/shard_map/ppermute | solution.py:218
  3.5 6.0 %collective-permute-start.1 = (f32[16,1024]{1,0:T(8,128)S(1)}, f32[16,1024]{1,0:T(8,128)S(1)}, u32[]{:S(2)}, u32[]{:S(2)}) collective-permute-start(f32[16,1024]{1,0:T(8,128)S(1)} %constant_dynamic-update-slice_fusion.refs_1_), channel_id=1, source_target_pairs={{0,8},{4,12},{8,0},{12,4},{1,9},{5,13},{9,1},{13,5},{2,10},{6,14},... | collective-permute-start | bytes 196616 | tf_op jit(solution)/shard_map/ppermute | solution.py:217
  4.6 20.6 %collective-permute-start.2 = (f32[16,1024]{1,0:T(8,128)S(1)}, f32[16,1024]{1,0:T(8,128)S(1)}, u32[]{:S(2)}, u32[]{:S(2)}) collective-permute-start(f32[16,1024]{1,0:T(8,128)S(1)} %constant_dynamic-update-slice_fusion.refs_1_), channel_id=1, source_target_pairs={{0,4},{4,0},{8,12},{12,8},{1,5},{5,1},{9,13},{13,9},{2,6},{6,2},{1... | collective-permute-start | bytes 196616 | tf_op jit(solution)/shard_map/ppermute | solution.py:216
  7.5 29.7 %collective-permute-start.4 = (bf16[2,2,384,256]{3,2,1,0:T(8,128)(2,1)S(1)}, bf16[2,2,384,256]{3,2,1,0:T(8,128)(2,1)S(1)}, u32[]{:S(2)}, u32[]{:S(2)}) collective-permute-start(bf16[2,2,384,256]{3,2,1,0:T(8,128)(2,1)S(1)} %pad_maximum_fusion), channel_id=1, source_target_pairs={{0,2},{1,3},{2,0},{3,1},{4,6},{5,7},{6,4},{7,5},{8,10},{9,11},{10,... | collective-permute-start | bytes 2359304 | tf_op jit(solution)/shard_map/ppermute | solution.py:223
  15.2 11.3 %copy-start.8 = (s32[512]{0:T(512)S(1)}, s32[512]{0:T(512)}, u32[]{:S(2)}) copy-start(s32[512]{0:T(512)} %param.18) | copy-start | bytes 6148
  25.2 11.9 %collective-permute-start.3 = (f16[128,1280]{1,0:T(8,128)(2,1)S(1)}, f16[128,1280]{1,0:T(8,128)(2,1)S(1)}, u32[]{:S(2)}, u32[]{:S(2)}) collective-permute-start(f16[128,1280]{1,0:T(8,128)(2,1)S(1)} %multiply_convert_fusion.4), channel_id=1, source_target_pairs={{0,4},{12,8},{1,5},{13,9},{2,6},{14,10},{3,7},{15,11},{16,20},{28,... | collective-permute-start | bytes 983048 | tf_op jit(solution)/shard_map/ppermute | solution.py:284
  37.3 17.6 %slice-start = ((s8[7864320]{0:T(1024)(128)(4,1)}), s8[4194304]{0:T(1024)(128)(4,1)S(1)}, s32[]{:S(2)}) async-start(s8[7864320]{0:T(1024)(128)(4,1)} %bitcast.52), calls=%async_computation | async-start | bytes 8388608
  37.3 17.5 %slice-start.1 = ((s8[7864320]{0:T(1024)(128)(4,1)}), s8[3670016]{0:T(1024)(128)(4,1)S(1)}, s32[]{:S(2)}) async-start(s8[7864320]{0:T(1024)(128)(4,1)} %bitcast.52), calls=%async_computation.1 | async-start | bytes 7340032
  37.4 12.5 %collective-permute-start.6 = (f16[128,1280]{1,0:T(8,128)(2,1)S(1)}, f16[128,1280]{1,0:T(8,128)(2,1)S(1)}, u32[]{:S(2)}, u32[]{:S(2)}) collective-permute-start(f16[128,1280]{1,0:T(8,128)(2,1)S(1)} %multiply_convert_fusion.2), channel_id=1, source_target_pairs={{0,4},{12,8},{1,5},{13,9},{2,6},{14,10},{3,7},{15,11},{16,20},{28,... | collective-permute-start | bytes 983048 | tf_op jit(solution)/shard_map/ppermute | solution.py:295
  38.9 10.9 %collective-permute-start.5 = (f16[128,1280]{1,0:T(8,128)(2,1)S(1)}, f16[128,1280]{1,0:T(8,128)(2,1)S(1)}, u32[]{:S(2)}, u32[]{:S(2)}) collective-permute-start(f16[128,1280]{1,0:T(8,128)(2,1)S(1)} %get-tuple-element.58), channel_id=1, source_target_pairs={{4,8},{8,4},{5,9},{9,5},{6,10},{10,6},{7,11},{11,7},{20,24},{24,20... | collective-permute-start | bytes 983048 | tf_op jit(solution)/shard_map/ppermute | solution.py:294
  49.8 4.1 %copy-start.7 = (bf16[1280]{0:T(1024)(128)(2,1)S(1)}, bf16[1280]{0:T(1024)(128)(2,1)}, u32[]{:S(2)}) copy-start(bf16[1280]{0:T(1024)(128)(2,1)} %param.13) | copy-start | bytes 7684
  49.8 4.2 %copy-start.1 = (bf16[1024,1280]{1,0:T(8,128)(2,1)S(1)}, bf16[1024,1280]{1,0:T(8,128)(2,1)}, u32[]{:S(2)}) copy-start(bf16[1024,1280]{1,0:T(8,128)(2,1)} %from_ref.1) | copy-start | bytes 7864324
  50.1 10.2 %collective-permute-start.9 = (bf16[2,2,384,256]{3,2,1,0:T(8,128)(2,1)S(1)}, bf16[2,2,384,256]{3,2,1,0:T(8,128)(2,1)S(1)}, u32[]{:S(2)}, u32[]{:S(2)}) collective-permute-start(bf16[2,2,384,256]{3,2,1,0:T(8,128)(2,1)S(1)} %pad_maximum_fusion.1), channel_id=1, source_target_pairs={{0,1},{1,0},{2,3},{3,2},{4,5},{5,4},{6,7},{7,6},{8,9},{9,8},{10,11... | collective-permute-start | bytes 2359304 | tf_op jit(solution)/shard_map/ppermute | solution.py:223
  50.2 10.1 %collective-permute-start.8 = (f16[128,1280]{1,0:T(8,128)(2,1)S(1)}, f16[128,1280]{1,0:T(8,128)(2,1)S(1)}, u32[]{:S(2)}, u32[]{:S(2)}) collective-permute-start(f16[128,1280]{1,0:T(8,128)(2,1)S(1)} %multiply_convert_fusion.1), channel_id=1, source_target_pairs={{0,4},{4,0},{8,12},{12,8},{1,5},{5,1},{9,13},{13,9},{2,6},{6,2},{1... | collective-permute-start | bytes 983048 | tf_op jit(solution)/shard_map/ppermute | solution.py:300
  50.4 11.9 %collective-permute-start.7 = (f16[128,1280]{1,0:T(8,128)(2,1)S(1)}, f16[128,1280]{1,0:T(8,128)(2,1)S(1)}, u32[]{:S(2)}, u32[]{:S(2)}) collective-permute-start(f16[128,1280]{1,0:T(8,128)(2,1)S(1)} %multiply_convert_fusion), channel_id=1, source_target_pairs={{4,8},{8,4},{5,9},{9,5},{6,10},{10,6},{7,11},{11,7},{20,24},{24,20... | collective-permute-start | bytes 983048 | tf_op jit(solution)/shard_map/ppermute | solution.py:301
  54.8 1.9 %copy-start.2 = (bf16[1024,1280]{1,0:T(8,128)(2,1)}, bf16[1024,1280]{1,0:T(8,128)(2,1)S(1)}, u32[]{:S(2)}) copy-start(bf16[1024,1280]{1,0:T(8,128)(2,1)S(1)} %select_rows.1) | copy-start | bytes 7864324
  56.7 10.9 %copy-start.5 = (f32[1280]{0:T(1024)S(1)}, f32[1280]{0:T(1024)}, u32[]{:S(2)}) copy-start(f32[1280]{0:T(1024)} %param.15) | copy-start | bytes 15364
  56.7 10.9 %copy-start.6 = (f32[1280]{0:T(1024)S(1)}, f32[1280]{0:T(1024)}, u32[]{:S(2)}) copy-start(f32[1280]{0:T(1024)} %param.14) | copy-start | bytes 15364
  58.5 40.4 %copy-start = (bf16[1280,1536]{1,0:T(8,128)(2,1)}, bf16[1280,1536]{1,0:T(8,128)(2,1)S(1)}, u32[]{:S(2)}) copy-start(bf16[1280,1536]{1,0:T(8,128)(2,1)S(1)} %select_columns.3) | copy-start | bytes 11796484
  60.3 25.6 %copy-start.4 = (bf16[2,2,384,256]{3,2,1,0:T(8,128)(2,1)}, bf16[2,2,384,256]{3,2,1,0:T(8,128)(2,1)S(1)}, u32[]{:S(2)}) copy-start(bf16[2,2,384,256]{3,2,1,0:T(8,128)(2,1)S(1)} %collective-permute-done.9) | copy-start | bytes 2359300
  62.7 1.2 collective-permute-start.10
  63.9 3.6 %collective-permute-start.11 = (f32[2,128]{1,0:T(2,128)S(1)}, f32[2,128]{1,0:T(2,128)S(1)}, u32[]{:S(2)}, u32[]{:S(2)}) collective-permute-start(f32[2,128]{1,0:T(2,128)S(1)} %fusion.22), channel_id=1, source_target_pairs={{0,2},{1,3},{2,0},{3,1},{4,6},{5,7},{6,4},{7,5},{8,10},{9,11},{10,... | collective-permute-start | bytes 3080 | tf_op jit(solution)/shard_map/ppermute | solution.py:223
  68.5 16.8 %collective-permute-start.15 = (f16[128,1536]{1,0:T(8,128)(2,1)S(1)}, f16[128,1536]{1,0:T(8,128)(2,1)S(1)}, u32[]{:S(2)}, u32[]{:S(2)}) collective-permute-start(f16[128,1536]{1,0:T(8,128)(2,1)S(1)} %convolution_convert_fusion.3), channel_id=1, source_target_pairs={{0,1},{1,0},{2,3},{3,2},{4,5},{5,4},{6,7},{7,6},{8,9},{9,8},{10,11... | collective-permute-start | bytes 1179656 | tf_op jit(solution)/shard_map/ppermute | solution.py:223
  68.5 12.0 %collective-permute-start.12 = (bf16[128,1280]{1,0:T(8,128)(2,1)S(1)}, bf16[128,1280]{1,0:T(8,128)(2,1)S(1)}, u32[]{:S(2)}, u32[]{:S(2)}) collective-permute-start(bf16[128,1280]{1,0:T(8,128)(2,1)S(1)} %add_convert_fusion.3), channel_id=1, source_target_pairs={{4,8},{8,4},{5,9},{9,5},{6,10},{10,6},{7,11},{11,7},{20,24},{24,20... | collective-permute-start | bytes 983048 | tf_op jit(solution)/shard_map/ppermute | solution.py:319
  71.7 10.1 %collective-permute-start.14 = (bf16[128,1280]{1,0:T(8,128)(2,1)S(1)}, bf16[128,1280]{1,0:T(8,128)(2,1)S(1)}, u32[]{:S(2)}, u32[]{:S(2)}) collective-permute-start(bf16[128,1280]{1,0:T(8,128)(2,1)S(1)} %add_convert_fusion.3), channel_id=1, source_target_pairs={{0,4},{4,0},{8,12},{12,8},{1,5},{5,1},{9,13},{13,9},{2,6},{6,2},{1... | collective-permute-start | bytes 983048 | tf_op jit(solution)/shard_map/ppermute | solution.py:318
  80.5 11.8 %collective-permute-start.13 = (bf16[128,1280]{1,0:T(8,128)(2,1)S(1)}, bf16[128,1280]{1,0:T(8,128)(2,1)S(1)}, u32[]{:S(2)}, u32[]{:S(2)}) collective-permute-start(bf16[128,1280]{1,0:T(8,128)(2,1)S(1)} %collective-permute-done.12), channel_id=1, source_target_pairs={{4,0},{8,12},{5,1},{9,13},{6,2},{10,14},{7,3},{11,15},{20,16},{24,... | collective-permute-start | bytes 983048 | tf_op jit(solution)/shard_map/ppermute | solution.py:321
  81.8 11.3 %collective-permute-start.16 = (bf16[128,1280]{1,0:T(8,128)(2,1)S(1)}, bf16[128,1280]{1,0:T(8,128)(2,1)S(1)}, u32[]{:S(2)}, u32[]{:S(2)}) collective-permute-start(bf16[128,1280]{1,0:T(8,128)(2,1)S(1)} %collective-permute-done.14), channel_id=1, source_target_pairs={{4,8},{8,4},{5,9},{9,5},{6,10},{10,6},{7,11},{11,7},{20,24},{24,20... | collective-permute-start | bytes 983048 | tf_op jit(solution)/shard_map/ppermute | solution.py:320
  86.0 6.3 %collective-permute-start.18 = (f16[128,768]{1,0:T(8,128)(2,1)S(1)}, f16[128,768]{1,0:T(8,128)(2,1)S(1)}, u32[]{:S(2)}, u32[]{:S(2)}) collective-permute-start(f16[128,768]{1,0:T(8,128)(2,1)S(1)} %slice_convert_fusion.4), channel_id=1, source_target_pairs={{0,2},{1,3},{2,0},{3,1},{4,6},{5,7},{6,4},{7,5},{8,10},{9,11},{10,... | collective-permute-start | bytes 589832 | tf_op jit(solution)/shard_map/ppermute | solution.py:223
  88.2 4.2 %collective-permute-start.17 = (f16[128,1536]{1,0:T(8,128)(2,1)S(1)}, f16[128,1536]{1,0:T(8,128)(2,1)S(1)}, u32[]{:S(2)}, u32[]{:S(2)}) collective-permute-start(f16[128,1536]{1,0:T(8,128)(2,1)S(1)} %convolution_convert_fusion.2), channel_id=1, source_target_pairs={{0,1},{1,0},{2,3},{3,2},{4,5},{5,4},{6,7},{7,6},{8,9},{9,8},{10,11... | collective-permute-start | bytes 1179656 | tf_op jit(solution)/shard_map/ppermute | solution.py:223
  93.2 5.7 %collective-permute-start.19 = (f16[128,768]{1,0:T(8,128)(2,1)S(1)}, f16[128,768]{1,0:T(8,128)(2,1)S(1)}, u32[]{:S(2)}, u32[]{:S(2)}) collective-permute-start(f16[128,768]{1,0:T(8,128)(2,1)S(1)} %slice_convert_fusion.3), channel_id=1, source_target_pairs={{0,2},{1,3},{2,0},{3,1},{4,6},{5,7},{6,4},{7,5},{8,10},{9,11},{10,... | collective-permute-start | bytes 589832 | tf_op jit(solution)/shard_map/ppermute | solution.py:223
  95.4 3.5 %collective-permute-start.20 = (f16[128,1536]{1,0:T(8,128)(2,1)S(1)}, f16[128,1536]{1,0:T(8,128)(2,1)S(1)}, u32[]{:S(2)}, u32[]{:S(2)}) collective-permute-start(f16[128,1536]{1,0:T(8,128)(2,1)S(1)} %convolution_convert_fusion.1), channel_id=1, source_target_pairs={{0,1},{1,0},{2,3},{3,2},{4,5},{5,4},{6,7},{7,6},{8,9},{9,8},{10,11... | collective-permute-start | bytes 1179656 | tf_op jit(solution)/shard_map/ppermute | solution.py:223
  95.5 9.2 %collective-permute-start.21 = (bf16[128,1280]{1,0:T(8,128)(2,1)S(1)}, bf16[128,1280]{1,0:T(8,128)(2,1)S(1)}, u32[]{:S(2)}, u32[]{:S(2)}) collective-permute-start(bf16[128,1280]{1,0:T(8,128)(2,1)S(1)} %collective-permute-done.16), channel_id=1, source_target_pairs={{4,0},{8,12},{5,1},{9,13},{6,2},{10,14},{7,3},{11,15},{20,16},{24,... | collective-permute-start | bytes 983048 | tf_op jit(solution)/shard_map/ppermute | solution.py:322
  99.7 5.7 %collective-permute-start.22 = (f16[128,768]{1,0:T(8,128)(2,1)S(1)}, f16[128,768]{1,0:T(8,128)(2,1)S(1)}, u32[]{:S(2)}, u32[]{:S(2)}) collective-permute-start(f16[128,768]{1,0:T(8,128)(2,1)S(1)} %slice_convert_fusion.2), channel_id=1, source_target_pairs={{0,2},{1,3},{2,0},{3,1},{4,6},{5,7},{6,4},{7,5},{8,10},{9,11},{10,... | collective-permute-start | bytes 589832 | tf_op jit(solution)/shard_map/ppermute | solution.py:223
  106.2 1.8 %collective-permute-start.23 = (f16[128,1536]{1,0:T(8,128)(2,1)S(1)}, f16[128,1536]{1,0:T(8,128)(2,1)S(1)}, u32[]{:S(2)}, u32[]{:S(2)}) collective-permute-start(f16[128,1536]{1,0:T(8,128)(2,1)S(1)} %convolution_convert_fusion), channel_id=1, source_target_pairs={{0,1},{1,0},{2,3},{3,2},{4,5},{5,4},{6,7},{7,6},{8,9},{9,8},{10,11... | collective-permute-start | bytes 1179656 | tf_op jit(solution)/shard_map/ppermute | solution.py:223
  110.8 7.0 %collective-permute-start.24 = (f16[128,768]{1,0:T(8,128)(2,1)S(1)}, f16[128,768]{1,0:T(8,128)(2,1)S(1)}, u32[]{:S(2)}, u32[]{:S(2)}) collective-permute-start(f16[128,768]{1,0:T(8,128)(2,1)S(1)} %slice_convert_fusion.1), channel_id=1, source_target_pairs={{0,2},{1,3},{2,0},{3,1},{4,6},{5,7},{6,4},{7,5},{8,10},{9,11},{10,... | collective-permute-start | bytes 589832 | tf_op jit(solution)/shard_map/ppermute | solution.py:223
  120.3 5.0 %collective-permute-start.25 = (bf16[256,256]{1,0:T(8,128)(2,1)S(1)}, bf16[256,256]{1,0:T(8,128)(2,1)S(1)}, u32[]{:S(2)}, u32[]{:S(2)}) collective-permute-start(bf16[256,256]{1,0:T(8,128)(2,1)S(1)} %attend.2), channel_id=1, source_target_pairs={{0,2},{1,3},{2,0},{3,1},{4,6},{5,7},{6,4},{7,5},{8,10},{9,11},{10,... | collective-permute-start | bytes 393224 | tf_op jit(solution)/shard_map/ppermute | solution.py:223
  125.3 20.4 %copy-start.3 = (bf16[1024,1280]{1,0:T(8,128)(2,1)S(1)}, bf16[1024,1280]{1,0:T(8,128)(2,1)}, u32[]{:S(2)}) copy-start(bf16[1024,1280]{1,0:T(8,128)(2,1)} %copy-done.2) | copy-start | bytes 7864324
  125.3 1.6 collective-permute-start.26
  129.6 11.6 %collective-permute-start.29 = (bf16[128,1280]{1,0:T(8,128)(2,1)S(1)}, bf16[128,1280]{1,0:T(8,128)(2,1)S(1)}, u32[]{:S(2)}, u32[]{:S(2)}) collective-permute-start(bf16[128,1280]{1,0:T(8,128)(2,1)S(1)} %slice.159), channel_id=1, source_target_pairs={{0,4},{12,8},{1,5},{13,9},{2,6},{14,10},{3,7},{15,11},{16,20},{28,... | collective-permute-start | bytes 983048 | tf_op jit(solution)/shard_map/ppermute | solution.py:362
  130.9 5.6 %collective-permute-start.27 = (bf16[256,256]{1,0:T(8,128)(2,1)S(1)}, bf16[256,256]{1,0:T(8,128)(2,1)S(1)}, u32[]{:S(2)}, u32[]{:S(2)}) collective-permute-start(bf16[256,256]{1,0:T(8,128)(2,1)S(1)} %attend.3), channel_id=1, source_target_pairs={{0,2},{1,3},{2,0},{3,1},{4,6},{5,7},{6,4},{7,5},{8,10},{9,11},{10,... | collective-permute-start | bytes 393224 | tf_op jit(solution)/shard_map/ppermute | solution.py:223
  136.5 9.2 %collective-permute-start.28 = (bf16[256,512]{1,0:T(8,128)(2,1)S(1)}, bf16[256,512]{1,0:T(8,128)(2,1)S(1)}, u32[]{:S(2)}, u32[]{:S(2)}) collective-permute-start(bf16[256,512]{1,0:T(8,128)(2,1)S(1)} %pad_maximum_fusion.3), channel_id=1, source_target_pairs={{0,1},{1,0},{2,3},{3,2},{4,5},{5,4},{6,7},{7,6},{8,9},{9,8},{10,11... | collective-permute-start | bytes 786440 | tf_op jit(solution)/shard_map/ppermute | solution.py:223
  141.3 10.8 %collective-permute-start.30 = (bf16[128,1280]{1,0:T(8,128)(2,1)S(1)}, bf16[128,1280]{1,0:T(8,128)(2,1)S(1)}, u32[]{:S(2)}, u32[]{:S(2)}) collective-permute-start(bf16[128,1280]{1,0:T(8,128)(2,1)S(1)} %get-tuple-element.92), channel_id=1, source_target_pairs={{4,8},{8,4},{5,9},{9,5},{6,10},{10,6},{7,11},{11,7},{20,24},{24,20... | collective-permute-start | bytes 983048 | tf_op jit(solution)/shard_map/ppermute | solution.py:368
  144.4 12.2 %collective-permute-start.32 = (bf16[128,1280]{1,0:T(8,128)(2,1)S(1)}, bf16[128,1280]{1,0:T(8,128)(2,1)S(1)}, u32[]{:S(2)}, u32[]{:S(2)}) collective-permute-start(bf16[128,1280]{1,0:T(8,128)(2,1)S(1)} %convert_element_type.164), channel_id=1, source_target_pairs={{0,4},{12,8},{1,5},{13,9},{2,6},{14,10},{3,7},{15,11},{16,20},{28,... | collective-permute-start | bytes 983048 | tf_op jit(solution)/shard_map/ppermute | solution.py:369
  152.2 9.8 %collective-permute-start.31 = (bf16[128,1280]{1,0:T(8,128)(2,1)S(1)}, bf16[128,1280]{1,0:T(8,128)(2,1)S(1)}, u32[]{:S(2)}, u32[]{:S(2)}) collective-permute-start(bf16[128,1280]{1,0:T(8,128)(2,1)S(1)} %fusion), channel_id=1, source_target_pairs={{0,4},{4,0},{8,12},{12,8},{1,5},{5,1},{9,13},{13,9},{2,6},{6,2},{1... | collective-permute-start | bytes 983048 | tf_op jit(solution)/shard_map/ppermute | solution.py:372
  156.7 9.0 %collective-permute-start.33 = (bf16[128,1280]{1,0:T(8,128)(2,1)S(1)}, bf16[128,1280]{1,0:T(8,128)(2,1)S(1)}, u32[]{:S(2)}, u32[]{:S(2)}) collective-permute-start(bf16[128,1280]{1,0:T(8,128)(2,1)S(1)} %add_convert_fusion.1), channel_id=1, source_target_pairs={{4,8},{8,4},{5,9},{9,5},{6,10},{10,6},{7,11},{11,7},{20,24},{24,20... | collective-permute-start | bytes 983048 | tf_op jit(solution)/shard_map/ppermute | solution.py:374

commit v9 on v8

--- a/solution.py
+++ b/solution.py
@@ -367,14 +367,13 @@
     second, mid_far = hold((product_far[rows:], mid_far))
     mid_far = lax.ppermute(mid_far, "lat", MIDDLE)
     in_across = lax.ppermute(second.astype(jnp.bfloat16), "lat", INWARD)
+    product_near, mid_far, in_across = hold((product_near, mid_far, in_across))
     last = (product_near[:rows] + mid_far.astype(jnp.float32)).astype(jnp.bfloat16)
-    second, last = hold((second, last))
     last = lax.ppermute(last, "lat", PAIRS)
     mid_across = (second + in_across.astype(jnp.float32)).astype(jnp.bfloat16)
     mid_across = lax.ppermute(mid_across, "lat", MIDDLE)
-    branch = product_near[rows:] + last.astype(jnp.float32)
-    branch, mid_across = hold((residual + branch, mid_across))
-    return (branch + mid_across.astype(jnp.float32)).astype(jnp.bfloat16)
+    branch = product_near[rows:] + last.astype(jnp.float32) + mid_across.astype(jnp.float32)
+    return (residual + branch).astype(jnp.bfloat16)
 
 
 def attend_block(queries, keys, values, query_pos, key_pos):

time: 167 us -> 165 us (0.988)
  waiting for transfers between devices: 59.6 us -> 57 us
    ppermute x2, waiting for transfers between devices: 5.53 us -> 1.3 us  [line_body(): mid_far = lax.ppermute(mid_far, 'lat', MIDDLE)]
    ppermute x2, waiting for transfers between devices: 4.64 us -> 6.68 us  [line_body(): last = lax.ppermute(last, 'lat', PAIRS)]
where the time goes in v9:
time: 165 us; the launch traced here: 164 us
  waiting for transfers between devices  57 us (35%)
  starting transfers between devices  45.5 us (28%)
  Pallas kernels  32.3 us (20%)
  matrix products  20.9 us (13%)
  other arithmetic  4.41 us (3%)
  local copies, waits for them, and re-layouts  3.5 us (2%)
    ppermute x16, waiting for transfers between devices, swap(): return lax.ppermute(value, 'col', [(i, i ^ distance) for i in range(size)])  22.3 us
    ppermute x16, starting transfers between devices, swap(): return lax.ppermute(value, 'col', [(i, i ^ distance) for i in range(size)])  13 us
    pallas_call x2, Pallas kernels, decode(): pl.pallas_call(decode_kernel, out_shape=jax.ShapeDtypeStruct((rows, colum...  11.7 us
    pallas_call x2, Pallas kernels, densify(): pl.pallas_call(functools.partial(densify_kernel, topk=topk, latents=laten...  11.4 us
    dot_general x1, matrix products, line_body(): far = jnp.dot(codes_far, decoder, preferred_element_type=jnp.float32)  9.88 us
    ppermute x1, waiting for transfers between devices, line_body(): across = lax.ppermute(own, 'lat', MIDDLE)  8.7 us
    ppermute x2, starting transfers between devices, line_body(): mid_far = lax.ppermute(mid_far, 'lat', MIDDLE)  7.02 us
    ppermute x2, waiting for transfers between devices, line_body(): last = lax.ppermute(last, 'lat', PAIRS)  6.68 us
  transfers between devices with their start and end apart: 34, of which 21 were waited for; matrix products, arithmetic and copies ran while one was open for 11% of the time, Pallas kernels for 18%

profile of v9, /device:TPU:8, one launch (start us, length us, event | category | flops | bytes accessed | tf_op | source)
XLA Modules:
  0.0 164.4 jit_solution(5104616971757496868)
XLA Ops:
  1.9 1.6 collective-permute-start
  4.6 1.4 collective-permute-start.2
  6.0 1.5 constant_dynamic-slice_fusion
  7.5 1.6 collective-permute-start.4
  9.5 5.7 %densify.2 = bf16[256,8192]{1,0:T(8,128)(2,1)S(1)} custom-call(s32[1]{0:T(128)} %bitcast.base_ref, f32[16,1024]{1,0:T(8,128)S(1)} %get-tuple-element.111.refs_0_, f32[16,1024]{1,0:T(8,128)S(1)} %get-tuple-element.110.refs_1_), custom_call_target="tpu_custom_call" | custom-call | flops 2147483648 | bytes 4194304 | tf_op jit(solution)/shard_map/densify/pallas_call | solution.py:64
  15.2 9.9 %fusion.24 = f32[256,1280]{1,0:T(8,128)S(1)} fusion(bf16[256,8192]{1,0:T(8,128)(2,1)S(1)} %densify.2, bf16[8192,1280]{1,0:T(8,128)(2,1)} %weights_ref.3), kind=kOutput, calls=%fused_computation.80 | convolution fusion | flops 5368709120 | bytes 26476544 | tf_op jit(solution)/shard_map/dot_general | solution.py:282
  25.2 1.3 collective-permute-start.3
  26.6 5.7 %densify.3.codes_ref = bf16[256,8192]{1,0:T(8,128)(2,1)S(1)} custom-call(s32[1]{0:T(128)} %bitcast.base_ref, f32[16,1024]{1,0:T(8,128)S(1)} %collective-permute-done.2.refs_0_, f32[16,1024]{1,0:T(8,128)S(1)} %constant_dynamic-update-slice_fusion.refs_1_), custom_call_target="tpu_custom_call" | custom-call | flops 2147483648 | bytes 4194304 | tf_op jit(solution)/shard_map/densify/pallas_call | solution.py:64
  32.3 4.8 %decode.2.rest_0_ = f32[256,1280]{1,0:T(8,128)S(1)} custom-call(bf16[256,8192]{1,0:T(8,128)(2,1)S(1)} %densify.3.codes_ref, bf16[8192,1280]{1,0:T(8,128)(2,1)} %weights_ref.3), custom_call_target="tpu_custom_call" | custom-call | flops 1 | bytes 1 | tf_op jit(solution)/shard_map/decode/pallas_call | solution.py:89
  37.4 1.6 collective-permute-start.6
  38.9 4.0 %collective-permute-start.5 = (f16[128,1280]{1,0:T(8,128)(2,1)S(1)}, f16[128,1280]{1,0:T(8,128)(2,1)S(1)}, u32[]{:S(2)}, u32[]{:S(2)}) collective-permute-start(f16[128,1280]{1,0:T(8,128)(2,1)S(1)} %get-tuple-element.57), channel_id=1, source_target_pairs={{4,8},{8,4},{5,9},{9,5},{6,10},{10,6},{7,11},{11,7},{20,24},{24,20... | collective-permute-start | bytes 983048 | tf_op jit(solution)/shard_map/ppermute | solution.py:294
  42.9 6.9 %decode.3 = f32[256,1280]{1,0:T(8,128)S(1)} custom-call(bf16[256,8192]{1,0:T(8,128)(2,1)S(1)} %densify.3.codes_ref, bf16[8192,1280]{1,0:T(8,128)(2,1)} %weights_ref.3, f32[256,1280]{1,0:T(8,128)S(1)} %decode.2.rest_0_), custom_call_target="tpu_custom_call", output_to_operand_aliasing={{}: (2, {})} | custom-call | flops 1 | bytes 1 | tf_op jit(solution)/shard_map/decode/pallas_call | solution.py:89
  50.4 3.5 %collective-permute-start.7 = (f16[128,1280]{1,0:T(8,128)(2,1)S(1)}, f16[128,1280]{1,0:T(8,128)(2,1)S(1)}, u32[]{:S(2)}, u32[]{:S(2)}) collective-permute-start(f16[128,1280]{1,0:T(8,128)(2,1)S(1)} %multiply_convert_fusion), channel_id=1, source_target_pairs={{4,8},{8,4},{5,9},{9,5},{6,10},{10,6},{7,11},{11,7},{20,24},{24,20... | collective-permute-start | bytes 983048 | tf_op jit(solution)/shard_map/ppermute | solution.py:301
  54.9 1.8 %select_columns.2 = bf16[1280,1536]{1,0:T(8,128)(2,1)S(1)} custom-call(s32[2]{0:T(128)S(1)} %get-tuple-element.120.order_ref, bf16[3,1280,1024]{2,1,0:T(8,128)(2,1)S(1)} %bitcast.54), custom_call_target="tpu_custom_call" | custom-call | bytes 7864320 | tf_op jit(solution)/shard_map/select_columns/pallas_call | solution.py:113
  56.7 1.8 %select_columns.3 = bf16[1280,1536]{1,0:T(8,128)(2,1)S(1)} custom-call(s32[2]{0:T(128)S(1)} %get-tuple-element.121.order_ref, bf16[3,1280,1024]{2,1,0:T(8,128)(2,1)S(1)} %bitcast.55), custom_call_target="tpu_custom_call" | custom-call | bytes 7864320 | tf_op jit(solution)/shard_map/select_columns/pallas_call | solution.py:113
  58.5 1.8 %collective-permute-done.8 = f16[128,1280]{1,0:T(8,128)(2,1)S(1)} collective-permute-done((f16[128,1280]{1,0:T(8,128)(2,1)S(1)}, f16[128,1280]{1,0:T(8,128)(2,1)S(1)}, u32[]{:S(2)}, u32[]{:S(2)}) %collective-permute-start.8) | collective-permute-done | bytes 327712 | tf_op jit(solution)/shard_map/ppermute | solution.py:300
  60.3 2.0 %collective-permute-done.7 = f16[128,1280]{1,0:T(8,128)(2,1)S(1)} collective-permute-done((f16[128,1280]{1,0:T(8,128)(2,1)S(1)}, f16[128,1280]{1,0:T(8,128)(2,1)S(1)}, u32[]{:S(2)}, u32[]{:S(2)}) %collective-permute-start.7) | collective-permute-done | bytes 327712 | tf_op jit(solution)/shard_map/ppermute | solution.py:301
  63.9 1.6 collective-permute-start.11
  65.4 2.1 %collective-permute-done.11 = f32[2,128]{1,0:T(2,128)S(1)} collective-permute-done((f32[2,128]{1,0:T(2,128)S(1)}, f32[2,128]{1,0:T(2,128)S(1)}, u32[]{:S(2)}, u32[]{:S(2)}) %collective-permute-start.11) | collective-permute-done | bytes 1056 | tf_op jit(solution)/shard_map/ppermute | solution.py:223
  68.5 3.2 %collective-permute-start.12 = (bf16[128,1280]{1,0:T(8,128)(2,1)S(1)}, bf16[128,1280]{1,0:T(8,128)(2,1)S(1)}, u32[]{:S(2)}, u32[]{:S(2)}) collective-permute-start(bf16[128,1280]{1,0:T(8,128)(2,1)S(1)} %add_convert_fusion.4), channel_id=1, source_target_pairs={{4,8},{8,4},{5,9},{9,5},{6,10},{10,6},{7,11},{11,7},{20,24},{24,20... | collective-permute-start | bytes 983048 | tf_op jit(solution)/shard_map/ppermute | solution.py:319
  71.8 8.7 %collective-permute-done.12 = bf16[128,1280]{1,0:T(8,128)(2,1)S(1)} collective-permute-done((bf16[128,1280]{1,0:T(8,128)(2,1)S(1)}, bf16[128,1280]{1,0:T(8,128)(2,1)S(1)}, u32[]{:S(2)}, u32[]{:S(2)}) %collective-permute-start.12) | collective-permute-done | bytes 327712 | tf_op jit(solution)/shard_map/ppermute | solution.py:319
  80.5 1.3 collective-permute-start.13
  81.8 3.4 %collective-permute-start.16 = (bf16[128,1280]{1,0:T(8,128)(2,1)S(1)}, bf16[128,1280]{1,0:T(8,128)(2,1)S(1)}, u32[]{:S(2)}, u32[]{:S(2)}) collective-permute-start(bf16[128,1280]{1,0:T(8,128)(2,1)S(1)} %collective-permute-done.14), channel_id=1, source_target_pairs={{4,8},{8,4},{5,9},{9,5},{6,10},{10,6},{7,11},{11,7},{20,24},{24,20... | collective-permute-start | bytes 983048 | tf_op jit(solution)/shard_map/ppermute | solution.py:320
  86.0 1.6 collective-permute-start.18
  88.3 4.0 %collective-permute-done.18 = f16[128,768]{1,0:T(8,128)(2,1)S(1)} collective-permute-done((f16[128,768]{1,0:T(8,128)(2,1)S(1)}, f16[128,768]{1,0:T(8,128)(2,1)S(1)}, u32[]{:S(2)}, u32[]{:S(2)}) %collective-permute-start.18) | collective-permute-done | bytes 196640 | tf_op jit(solution)/shard_map/ppermute | solution.py:223
  93.2 1.6 collective-permute-start.19
  95.5 1.3 collective-permute-start.21
  96.8 2.1 %collective-permute-done.19 = f16[128,768]{1,0:T(8,128)(2,1)S(1)} collective-permute-done((f16[128,768]{1,0:T(8,128)(2,1)S(1)}, f16[128,768]{1,0:T(8,128)(2,1)S(1)}, u32[]{:S(2)}, u32[]{:S(2)}) %collective-permute-start.19) | collective-permute-done | bytes 196640 | tf_op jit(solution)/shard_map/ppermute | solution.py:223
  99.7 1.6 collective-permute-start.22
  101.2 3.4 %collective-permute-done.21 = bf16[128,1280]{1,0:T(8,128)(2,1)S(1)} collective-permute-done((bf16[128,1280]{1,0:T(8,128)(2,1)S(1)}, bf16[128,1280]{1,0:T(8,128)(2,1)S(1)}, u32[]{:S(2)}, u32[]{:S(2)}) %collective-permute-start.21) | collective-permute-done | bytes 327712 | tf_op jit(solution)/shard_map/ppermute | solution.py:322
  106.4 1.5 collective-permute-done.23
  107.9 2.8 %convolution_add_fusion = f32[128,1536]{1,0:T(8,128)S(1)} fusion(bf16[128,1280]{1,0:T(8,128)(2,1)S(1)} %broadcast_select_fusion, bf16[1280,1536]{1,0:T(8,128)(2,1)} %copy-done, f16[128,1536]{1,0:T(8,128)(2,1)S(1)} %collective-permute-done.23), kind=kOutput, calls=%fused_computation | convolution fusion | flops 503709696 | bytes 5439488 | tf_op jit(solution)/shard_map/dot_general | solution.py:328
  110.8 1.6 collective-permute-start.24
  113.5 4.3 %collective-permute-done.24 = f16[128,768]{1,0:T(8,128)(2,1)S(1)} collective-permute-done((f16[128,768]{1,0:T(8,128)(2,1)S(1)}, f16[128,768]{1,0:T(8,128)(2,1)S(1)}, u32[]{:S(2)}, u32[]{:S(2)}) %collective-permute-start.24) | collective-permute-done | bytes 196640 | tf_op jit(solution)/shard_map/ppermute | solution.py:223
  117.9 2.4 %attend.2 = bf16[256,256]{1,0:T(8,128)(2,1)S(1)} custom-call(s32[256,1]{1,0:T(8,128)S(1)} %copy.22.refs_0_, s32[1,512]{1,0:T(1,128)S(1)} %bitcast.57, bf16[128,768]{1,0:T(8,128)(2,1)S(1)} %fusion.15.refs_2_, bf16[128,768]{1,0:T(8,128)(2,1)S(1)} %fusion.14.refs_3_, bf16[128,768]{1,0:T(8,128)(2,1)S(1)} %fusion.13.refs_4_, ...), custom_call_target="tpu_custom_call" | custom-call | flops 536870912 | bytes 2097152 | tf_op jit(solution)/shard_map/attend/pallas_call | solution.py:189
  120.3 1.6 collective-permute-start.25
  122.0 2.4 %attend.3 = bf16[256,256]{1,0:T(8,128)(2,1)S(1)} custom-call(s32[256,1]{1,0:T(8,128)S(1)} %copy.23.refs_0_, s32[1,512]{1,0:T(1,128)S(1)} %bitcast.58, bf16[128,768]{1,0:T(8,128)(2,1)S(1)} %fusion.15.refs_2_, bf16[128,768]{1,0:T(8,128)(2,1)S(1)} %fusion.14.refs_3_, bf16[128,768]{1,0:T(8,128)(2,1)S(1)} %fusion.13.refs_4_, ...), custom_call_target="tpu_custom_call" | custom-call | flops 536870912 | bytes 2097152 | tf_op jit(solution)/shard_map/attend/pallas_call | solution.py:189
  125.4 1.5 collective-permute-done.26
  126.9 2.6 %fusion = f32[256,1280]{1,0:T(8,128)S(1)} fusion(bf16[1024,1280]{1,0:T(8,128)(2,1)} %copy-done.2, bf16[256,512]{1,0:T(8,128)(2,1)S(1)} %collective-permute-done.26, bf16[256,256]{1,0:T(8,128)(2,1)S(1)} %collective-permute-done.25, bf16[256,256]{1,0:T(8,128)(2,1)S(1)} %attend.2), kind=kOutput, calls=%fused_computation.23 | convolution fusion | flops 672661504 | bytes 4456448 | tf_op jit(solution)/shard_map/dot_general | solution.py:360
  130.9 1.5 collective-permute-start.27
  132.4 4.1 %collective-permute-done.27 = bf16[256,256]{1,0:T(8,128)(2,1)S(1)} collective-permute-done((bf16[256,256]{1,0:T(8,128)(2,1)S(1)}, bf16[256,256]{1,0:T(8,128)(2,1)S(1)}, u32[]{:S(2)}, u32[]{:S(2)}) %collective-permute-start.27) | collective-permute-done | bytes 131104 | tf_op jit(solution)/shard_map/ppermute | solution.py:223
  136.6 4.6 %collective-permute-done.29 = bf16[128,1280]{1,0:T(8,128)(2,1)S(1)} collective-permute-done((bf16[128,1280]{1,0:T(8,128)(2,1)S(1)}, bf16[128,1280]{1,0:T(8,128)(2,1)S(1)}, u32[]{:S(2)}, u32[]{:S(2)}) %collective-permute-start.29) | collective-permute-done | bytes 327712 | tf_op jit(solution)/shard_map/ppermute | solution.py:362
  142.7 3.1 %collective-permute-start.30 = (bf16[128,1280]{1,0:T(8,128)(2,1)S(1)}, bf16[128,1280]{1,0:T(8,128)(2,1)S(1)}, u32[]{:S(2)}, u32[]{:S(2)}) collective-permute-start(bf16[128,1280]{1,0:T(8,128)(2,1)S(1)} %get-tuple-element.90), channel_id=1, source_target_pairs={{4,8},{8,4},{5,9},{9,5},{6,10},{10,6},{7,11},{11,7},{20,24},{24,20... | collective-permute-start | bytes 983048 | tf_op jit(solution)/shard_map/ppermute | solution.py:368
  146.6 5.6 %collective-permute-done.31 = bf16[128,1280]{1,0:T(8,128)(2,1)S(1)} collective-permute-done((bf16[128,1280]{1,0:T(8,128)(2,1)S(1)}, bf16[128,1280]{1,0:T(8,128)(2,1)S(1)}, u32[]{:S(2)}, u32[]{:S(2)}) %collective-permute-start.31) | collective-permute-done | bytes 327712 | tf_op jit(solution)/shard_map/ppermute | solution.py:369
  152.2 1.3 collective-permute-done.30
  153.7 3.1 %collective-permute-start.33 = (bf16[128,1280]{1,0:T(8,128)(2,1)S(1)}, bf16[128,1280]{1,0:T(8,128)(2,1)S(1)}, u32[]{:S(2)}, u32[]{:S(2)}) collective-permute-start(bf16[128,1280]{1,0:T(8,128)(2,1)S(1)} %add_convert_fusion.1), channel_id=1, source_target_pairs={{4,8},{8,4},{5,9},{9,5},{6,10},{10,6},{7,11},{11,7},{20,24},{24,20... | collective-permute-start | bytes 983048 | tf_op jit(solution)/shard_map/ppermute | solution.py:374
  156.8 4.8 %collective-permute-done.32 = bf16[128,1280]{1,0:T(8,128)(2,1)S(1)} collective-permute-done((bf16[128,1280]{1,0:T(8,128)(2,1)S(1)}, bf16[128,1280]{1,0:T(8,128)(2,1)S(1)}, u32[]{:S(2)}, u32[]{:S(2)}) %collective-permute-start.32) | collective-permute-done | bytes 327712 | tf_op jit(solution)/shard_map/ppermute | solution.py:372
  161.6 2.0 %collective-permute-done.33 = bf16[128,1280]{1,0:T(8,128)(2,1)S(1)} collective-permute-done((bf16[128,1280]{1,0:T(8,128)(2,1)S(1)}, bf16[128,1280]{1,0:T(8,128)(2,1)S(1)}, u32[]{:S(2)}, u32[]{:S(2)}) %collective-permute-start.33) | collective-permute-done | bytes 327712 | tf_op jit(solution)/shard_map/ppermute | solution.py:374
  (117 shorter events, 20.5 us)
Async XLA Ops:
  1.9 7.3 %collective-permute-start = (f32[16,1024]{1,0:T(8,128)S(1)}, f32[16,1024]{1,0:T(8,128)S(1)}, u32[]{:S(2)}, u32[]{:S(2)}) collective-permute-start(f32[16,1024]{1,0:T(8,128)S(1)} %constant_dynamic-update-slice_fusion.refs_1_), channel_id=1, source_target_pairs={{0,12},{4,8},{8,4},{12,0},{1,13},{5,9},{9,5},{13,1},{2,14},{6,10},... | collective-permute-start | bytes 196616 | tf_op jit(solution)/shard_map/ppermute | solution.py:218
  3.5 6.0 %collective-permute-start.1 = (f32[16,1024]{1,0:T(8,128)S(1)}, f32[16,1024]{1,0:T(8,128)S(1)}, u32[]{:S(2)}, u32[]{:S(2)}) collective-permute-start(f32[16,1024]{1,0:T(8,128)S(1)} %constant_dynamic-update-slice_fusion.refs_1_), channel_id=1, source_target_pairs={{0,8},{4,12},{8,0},{12,4},{1,9},{5,13},{9,1},{13,5},{2,10},{6,14},... | collective-permute-start | bytes 196616 | tf_op jit(solution)/shard_map/ppermute | solution.py:217
  4.6 20.6 %collective-permute-start.2 = (f32[16,1024]{1,0:T(8,128)S(1)}, f32[16,1024]{1,0:T(8,128)S(1)}, u32[]{:S(2)}, u32[]{:S(2)}) collective-permute-start(f32[16,1024]{1,0:T(8,128)S(1)} %constant_dynamic-update-slice_fusion.refs_1_), channel_id=1, source_target_pairs={{0,4},{4,0},{8,12},{12,8},{1,5},{5,1},{9,13},{13,9},{2,6},{6,2},{1... | collective-permute-start | bytes 196616 | tf_op jit(solution)/shard_map/ppermute | solution.py:216
  7.5 29.7 %collective-permute-start.4 = (bf16[2,2,384,256]{3,2,1,0:T(8,128)(2,1)S(1)}, bf16[2,2,384,256]{3,2,1,0:T(8,128)(2,1)S(1)}, u32[]{:S(2)}, u32[]{:S(2)}) collective-permute-start(bf16[2,2,384,256]{3,2,1,0:T(8,128)(2,1)S(1)} %pad_maximum_fusion), channel_id=1, source_target_pairs={{0,2},{1,3},{2,0},{3,1},{4,6},{5,7},{6,4},{7,5},{8,10},{9,11},{10,... | collective-permute-start | bytes 2359304 | tf_op jit(solution)/shard_map/ppermute | solution.py:223
  15.2 11.3 %copy-start.8 = (s32[512]{0:T(512)S(1)}, s32[512]{0:T(512)}, u32[]{:S(2)}) copy-start(s32[512]{0:T(512)} %param.18) | copy-start | bytes 6148
  25.2 11.9 %collective-permute-start.3 = (f16[128,1280]{1,0:T(8,128)(2,1)S(1)}, f16[128,1280]{1,0:T(8,128)(2,1)S(1)}, u32[]{:S(2)}, u32[]{:S(2)}) collective-permute-start(f16[128,1280]{1,0:T(8,128)(2,1)S(1)} %multiply_convert_fusion.4), channel_id=1, source_target_pairs={{0,4},{12,8},{1,5},{13,9},{2,6},{14,10},{3,7},{15,11},{16,20},{28,... | collective-permute-start | bytes 983048 | tf_op jit(solution)/shard_map/ppermute | solution.py:284
  37.3 17.6 %slice-start = ((s8[7864320]{0:T(1024)(128)(4,1)}), s8[4194304]{0:T(1024)(128)(4,1)S(1)}, s32[]{:S(2)}) async-start(s8[7864320]{0:T(1024)(128)(4,1)} %bitcast.52), calls=%async_computation | async-start | bytes 8388608
  37.3 17.5 %slice-start.1 = ((s8[7864320]{0:T(1024)(128)(4,1)}), s8[3670016]{0:T(1024)(128)(4,1)S(1)}, s32[]{:S(2)}) async-start(s8[7864320]{0:T(1024)(128)(4,1)} %bitcast.52), calls=%async_computation.1 | async-start | bytes 7340032
  37.4 12.5 %collective-permute-start.6 = (f16[128,1280]{1,0:T(8,128)(2,1)S(1)}, f16[128,1280]{1,0:T(8,128)(2,1)S(1)}, u32[]{:S(2)}, u32[]{:S(2)}) collective-permute-start(f16[128,1280]{1,0:T(8,128)(2,1)S(1)} %multiply_convert_fusion.2), channel_id=1, source_target_pairs={{0,4},{12,8},{1,5},{13,9},{2,6},{14,10},{3,7},{15,11},{16,20},{28,... | collective-permute-start | bytes 983048 | tf_op jit(solution)/shard_map/ppermute | solution.py:295
  38.9 10.9 %collective-permute-start.5 = (f16[128,1280]{1,0:T(8,128)(2,1)S(1)}, f16[128,1280]{1,0:T(8,128)(2,1)S(1)}, u32[]{:S(2)}, u32[]{:S(2)}) collective-permute-start(f16[128,1280]{1,0:T(8,128)(2,1)S(1)} %get-tuple-element.57), channel_id=1, source_target_pairs={{4,8},{8,4},{5,9},{9,5},{6,10},{10,6},{7,11},{11,7},{20,24},{24,20... | collective-permute-start | bytes 983048 | tf_op jit(solution)/shard_map/ppermute | solution.py:294
  49.8 4.1 %copy-start.7 = (bf16[1280]{0:T(1024)(128)(2,1)S(1)}, bf16[1280]{0:T(1024)(128)(2,1)}, u32[]{:S(2)}) copy-start(bf16[1280]{0:T(1024)(128)(2,1)} %param.13) | copy-start | bytes 7684
  49.8 4.2 %copy-start.1 = (bf16[1024,1280]{1,0:T(8,128)(2,1)S(1)}, bf16[1024,1280]{1,0:T(8,128)(2,1)}, u32[]{:S(2)}) copy-start(bf16[1024,1280]{1,0:T(8,128)(2,1)} %from_ref.1) | copy-start | bytes 7864324
  50.1 10.2 %collective-permute-start.9 = (bf16[2,2,384,256]{3,2,1,0:T(8,128)(2,1)S(1)}, bf16[2,2,384,256]{3,2,1,0:T(8,128)(2,1)S(1)}, u32[]{:S(2)}, u32[]{:S(2)}) collective-permute-start(bf16[2,2,384,256]{3,2,1,0:T(8,128)(2,1)S(1)} %pad_maximum_fusion.1), channel_id=1, source_target_pairs={{0,1},{1,0},{2,3},{3,2},{4,5},{5,4},{6,7},{7,6},{8,9},{9,8},{10,11... | collective-permute-start | bytes 2359304 | tf_op jit(solution)/shard_map/ppermute | solution.py:223
  50.2 10.1 %collective-permute-start.8 = (f16[128,1280]{1,0:T(8,128)(2,1)S(1)}, f16[128,1280]{1,0:T(8,128)(2,1)S(1)}, u32[]{:S(2)}, u32[]{:S(2)}) collective-permute-start(f16[128,1280]{1,0:T(8,128)(2,1)S(1)} %multiply_convert_fusion.1), channel_id=1, source_target_pairs={{0,4},{4,0},{8,12},{12,8},{1,5},{5,1},{9,13},{13,9},{2,6},{6,2},{1... | collective-permute-start | bytes 983048 | tf_op jit(solution)/shard_map/ppermute | solution.py:300
  50.4 11.9 %collective-permute-start.7 = (f16[128,1280]{1,0:T(8,128)(2,1)S(1)}, f16[128,1280]{1,0:T(8,128)(2,1)S(1)}, u32[]{:S(2)}, u32[]{:S(2)}) collective-permute-start(f16[128,1280]{1,0:T(8,128)(2,1)S(1)} %multiply_convert_fusion), channel_id=1, source_target_pairs={{4,8},{8,4},{5,9},{9,5},{6,10},{10,6},{7,11},{11,7},{20,24},{24,20... | collective-permute-start | bytes 983048 | tf_op jit(solution)/shard_map/ppermute | solution.py:301
  54.8 1.9 %copy-start.2 = (bf16[1024,1280]{1,0:T(8,128)(2,1)}, bf16[1024,1280]{1,0:T(8,128)(2,1)S(1)}, u32[]{:S(2)}) copy-start(bf16[1024,1280]{1,0:T(8,128)(2,1)S(1)} %select_rows.1) | copy-start | bytes 7864324
  56.7 10.9 %copy-start.5 = (f32[1280]{0:T(1024)S(1)}, f32[1280]{0:T(1024)}, u32[]{:S(2)}) copy-start(f32[1280]{0:T(1024)} %param.15) | copy-start | bytes 15364
  56.7 10.9 %copy-start.6 = (f32[1280]{0:T(1024)S(1)}, f32[1280]{0:T(1024)}, u32[]{:S(2)}) copy-start(f32[1280]{0:T(1024)} %param.14) | copy-start | bytes 15364
  58.5 40.4 %copy-start = (bf16[1280,1536]{1,0:T(8,128)(2,1)}, bf16[1280,1536]{1,0:T(8,128)(2,1)S(1)}, u32[]{:S(2)}) copy-start(bf16[1280,1536]{1,0:T(8,128)(2,1)S(1)} %select_columns.3) | copy-start | bytes 11796484
  60.3 25.6 %copy-start.4 = (bf16[2,2,384,256]{3,2,1,0:T(8,128)(2,1)}, bf16[2,2,384,256]{3,2,1,0:T(8,128)(2,1)S(1)}, u32[]{:S(2)}) copy-start(bf16[2,2,384,256]{3,2,1,0:T(8,128)(2,1)S(1)} %collective-permute-done.9) | copy-start | bytes 2359300
  62.7 1.2 collective-permute-start.10
  63.9 3.6 %collective-permute-start.11 = (f32[2,128]{1,0:T(2,128)S(1)}, f32[2,128]{1,0:T(2,128)S(1)}, u32[]{:S(2)}, u32[]{:S(2)}) collective-permute-start(f32[2,128]{1,0:T(2,128)S(1)} %fusion.20), channel_id=1, source_target_pairs={{0,2},{1,3},{2,0},{3,1},{4,6},{5,7},{6,4},{7,5},{8,10},{9,11},{10,... | collective-permute-start | bytes 3080 | tf_op jit(solution)/shard_map/ppermute | solution.py:223
  68.5 16.8 %collective-permute-start.15 = (f16[128,1536]{1,0:T(8,128)(2,1)S(1)}, f16[128,1536]{1,0:T(8,128)(2,1)S(1)}, u32[]{:S(2)}, u32[]{:S(2)}) collective-permute-start(f16[128,1536]{1,0:T(8,128)(2,1)S(1)} %convolution_convert_fusion.3), channel_id=1, source_target_pairs={{0,1},{1,0},{2,3},{3,2},{4,5},{5,4},{6,7},{7,6},{8,9},{9,8},{10,11... | collective-permute-start | bytes 1179656 | tf_op jit(solution)/shard_map/ppermute | solution.py:223
  68.5 12.0 %collective-permute-start.12 = (bf16[128,1280]{1,0:T(8,128)(2,1)S(1)}, bf16[128,1280]{1,0:T(8,128)(2,1)S(1)}, u32[]{:S(2)}, u32[]{:S(2)}) collective-permute-start(bf16[128,1280]{1,0:T(8,128)(2,1)S(1)} %add_convert_fusion.4), channel_id=1, source_target_pairs={{4,8},{8,4},{5,9},{9,5},{6,10},{10,6},{7,11},{11,7},{20,24},{24,20... | collective-permute-start | bytes 983048 | tf_op jit(solution)/shard_map/ppermute | solution.py:319
  71.7 10.1 %collective-permute-start.14 = (bf16[128,1280]{1,0:T(8,128)(2,1)S(1)}, bf16[128,1280]{1,0:T(8,128)(2,1)S(1)}, u32[]{:S(2)}, u32[]{:S(2)}) collective-permute-start(bf16[128,1280]{1,0:T(8,128)(2,1)S(1)} %add_convert_fusion.4), channel_id=1, source_target_pairs={{0,4},{4,0},{8,12},{12,8},{1,5},{5,1},{9,13},{13,9},{2,6},{6,2},{1... | collective-permute-start | bytes 983048 | tf_op jit(solution)/shard_map/ppermute | solution.py:318
  80.5 11.8 %collective-permute-start.13 = (bf16[128,1280]{1,0:T(8,128)(2,1)S(1)}, bf16[128,1280]{1,0:T(8,128)(2,1)S(1)}, u32[]{:S(2)}, u32[]{:S(2)}) collective-permute-start(bf16[128,1280]{1,0:T(8,128)(2,1)S(1)} %collective-permute-done.12), channel_id=1, source_target_pairs={{4,0},{8,12},{5,1},{9,13},{6,2},{10,14},{7,3},{11,15},{20,16},{24,... | collective-permute-start | bytes 983048 | tf_op jit(solution)/shard_map/ppermute | solution.py:321
  81.8 11.3 %collective-permute-start.16 = (bf16[128,1280]{1,0:T(8,128)(2,1)S(1)}, bf16[128,1280]{1,0:T(8,128)(2,1)S(1)}, u32[]{:S(2)}, u32[]{:S(2)}) collective-permute-start(bf16[128,1280]{1,0:T(8,128)(2,1)S(1)} %collective-permute-done.14), channel_id=1, source_target_pairs={{4,8},{8,4},{5,9},{9,5},{6,10},{10,6},{7,11},{11,7},{20,24},{24,20... | collective-permute-start | bytes 983048 | tf_op jit(solution)/shard_map/ppermute | solution.py:320
  86.0 6.3 %collective-permute-start.18 = (f16[128,768]{1,0:T(8,128)(2,1)S(1)}, f16[128,768]{1,0:T(8,128)(2,1)S(1)}, u32[]{:S(2)}, u32[]{:S(2)}) collective-permute-start(f16[128,768]{1,0:T(8,128)(2,1)S(1)} %slice_convert_fusion.4), channel_id=1, source_target_pairs={{0,2},{1,3},{2,0},{3,1},{4,6},{5,7},{6,4},{7,5},{8,10},{9,11},{10,... | collective-permute-start | bytes 589832 | tf_op jit(solution)/shard_map/ppermute | solution.py:223
  88.2 4.2 %collective-permute-start.17 = (f16[128,1536]{1,0:T(8,128)(2,1)S(1)}, f16[128,1536]{1,0:T(8,128)(2,1)S(1)}, u32[]{:S(2)}, u32[]{:S(2)}) collective-permute-start(f16[128,1536]{1,0:T(8,128)(2,1)S(1)} %convolution_convert_fusion.2), channel_id=1, source_target_pairs={{0,1},{1,0},{2,3},{3,2},{4,5},{5,4},{6,7},{7,6},{8,9},{9,8},{10,11... | collective-permute-start | bytes 1179656 | tf_op jit(solution)/shard_map/ppermute | solution.py:223
  93.2 5.7 %collective-permute-start.19 = (f16[128,768]{1,0:T(8,128)(2,1)S(1)}, f16[128,768]{1,0:T(8,128)(2,1)S(1)}, u32[]{:S(2)}, u32[]{:S(2)}) collective-permute-start(f16[128,768]{1,0:T(8,128)(2,1)S(1)} %slice_convert_fusion.3), channel_id=1, source_target_pairs={{0,2},{1,3},{2,0},{3,1},{4,6},{5,7},{6,4},{7,5},{8,10},{9,11},{10,... | collective-permute-start | bytes 589832 | tf_op jit(solution)/shard_map/ppermute | solution.py:223
  95.4 3.5 %collective-permute-start.20 = (f16[128,1536]{1,0:T(8,128)(2,1)S(1)}, f16[128,1536]{1,0:T(8,128)(2,1)S(1)}, u32[]{:S(2)}, u32[]{:S(2)}) collective-permute-start(f16[128,1536]{1,0:T(8,128)(2,1)S(1)} %convolution_convert_fusion.1), channel_id=1, source_target_pairs={{0,1},{1,0},{2,3},{3,2},{4,5},{5,4},{6,7},{7,6},{8,9},{9,8},{10,11... | collective-permute-start | bytes 1179656 | tf_op jit(solution)/shard_map/ppermute | solution.py:223
  95.5 9.2 %collective-permute-start.21 = (bf16[128,1280]{1,0:T(8,128)(2,1)S(1)}, bf16[128,1280]{1,0:T(8,128)(2,1)S(1)}, u32[]{:S(2)}, u32[]{:S(2)}) collective-permute-start(bf16[128,1280]{1,0:T(8,128)(2,1)S(1)} %collective-permute-done.16), channel_id=1, source_target_pairs={{4,0},{8,12},{5,1},{9,13},{6,2},{10,14},{7,3},{11,15},{20,16},{24,... | collective-permute-start | bytes 983048 | tf_op jit(solution)/shard_map/ppermute | solution.py:322
  99.7 5.7 %collective-permute-start.22 = (f16[128,768]{1,0:T(8,128)(2,1)S(1)}, f16[128,768]{1,0:T(8,128)(2,1)S(1)}, u32[]{:S(2)}, u32[]{:S(2)}) collective-permute-start(f16[128,768]{1,0:T(8,128)(2,1)S(1)} %slice_convert_fusion.2), channel_id=1, source_target_pairs={{0,2},{1,3},{2,0},{3,1},{4,6},{5,7},{6,4},{7,5},{8,10},{9,11},{10,... | collective-permute-start | bytes 589832 | tf_op jit(solution)/shard_map/ppermute | solution.py:223
  106.2 1.8 %collective-permute-start.23 = (f16[128,1536]{1,0:T(8,128)(2,1)S(1)}, f16[128,1536]{1,0:T(8,128)(2,1)S(1)}, u32[]{:S(2)}, u32[]{:S(2)}) collective-permute-start(f16[128,1536]{1,0:T(8,128)(2,1)S(1)} %convolution_convert_fusion), channel_id=1, source_target_pairs={{0,1},{1,0},{2,3},{3,2},{4,5},{5,4},{6,7},{7,6},{8,9},{9,8},{10,11... | collective-permute-start | bytes 1179656 | tf_op jit(solution)/shard_map/ppermute | solution.py:223
  110.8 7.0 %collective-permute-start.24 = (f16[128,768]{1,0:T(8,128)(2,1)S(1)}, f16[128,768]{1,0:T(8,128)(2,1)S(1)}, u32[]{:S(2)}, u32[]{:S(2)}) collective-permute-start(f16[128,768]{1,0:T(8,128)(2,1)S(1)} %slice_convert_fusion.1), channel_id=1, source_target_pairs={{0,2},{1,3},{2,0},{3,1},{4,6},{5,7},{6,4},{7,5},{8,10},{9,11},{10,... | collective-permute-start | bytes 589832 | tf_op jit(solution)/shard_map/ppermute | solution.py:223
  120.3 5.0 %collective-permute-start.25 = (bf16[256,256]{1,0:T(8,128)(2,1)S(1)}, bf16[256,256]{1,0:T(8,128)(2,1)S(1)}, u32[]{:S(2)}, u32[]{:S(2)}) collective-permute-start(bf16[256,256]{1,0:T(8,128)(2,1)S(1)} %attend.2), channel_id=1, source_target_pairs={{0,2},{1,3},{2,0},{3,1},{4,6},{5,7},{6,4},{7,5},{8,10},{9,11},{10,... | collective-permute-start | bytes 393224 | tf_op jit(solution)/shard_map/ppermute | solution.py:223
  125.3 20.4 %copy-start.3 = (bf16[1024,1280]{1,0:T(8,128)(2,1)S(1)}, bf16[1024,1280]{1,0:T(8,128)(2,1)}, u32[]{:S(2)}) copy-start(bf16[1024,1280]{1,0:T(8,128)(2,1)} %copy-done.2) | copy-start | bytes 7864324
  125.3 1.6 collective-permute-start.26
  129.6 11.6 %collective-permute-start.29 = (bf16[128,1280]{1,0:T(8,128)(2,1)S(1)}, bf16[128,1280]{1,0:T(8,128)(2,1)S(1)}, u32[]{:S(2)}, u32[]{:S(2)}) collective-permute-start(bf16[128,1280]{1,0:T(8,128)(2,1)S(1)} %slice.153), channel_id=1, source_target_pairs={{0,4},{12,8},{1,5},{13,9},{2,6},{14,10},{3,7},{15,11},{16,20},{28,... | collective-permute-start | bytes 983048 | tf_op jit(solution)/shard_map/ppermute | solution.py:362
  130.9 5.6 %collective-permute-start.27 = (bf16[256,256]{1,0:T(8,128)(2,1)S(1)}, bf16[256,256]{1,0:T(8,128)(2,1)S(1)}, u32[]{:S(2)}, u32[]{:S(2)}) collective-permute-start(bf16[256,256]{1,0:T(8,128)(2,1)S(1)} %attend.3), channel_id=1, source_target_pairs={{0,2},{1,3},{2,0},{3,1},{4,6},{5,7},{6,4},{7,5},{8,10},{9,11},{10,... | collective-permute-start | bytes 393224 | tf_op jit(solution)/shard_map/ppermute | solution.py:223
  136.5 9.2 %collective-permute-start.28 = (bf16[256,512]{1,0:T(8,128)(2,1)S(1)}, bf16[256,512]{1,0:T(8,128)(2,1)S(1)}, u32[]{:S(2)}, u32[]{:S(2)}) collective-permute-start(bf16[256,512]{1,0:T(8,128)(2,1)S(1)} %pad_maximum_fusion.3), channel_id=1, source_target_pairs={{0,1},{1,0},{2,3},{3,2},{4,5},{5,4},{6,7},{7,6},{8,9},{9,8},{10,11... | collective-permute-start | bytes 786440 | tf_op jit(solution)/shard_map/ppermute | solution.py:223
  141.4 10.8 %collective-permute-start.31 = (bf16[128,1280]{1,0:T(8,128)(2,1)S(1)}, bf16[128,1280]{1,0:T(8,128)(2,1)S(1)}, u32[]{:S(2)}, u32[]{:S(2)}) collective-permute-start(bf16[128,1280]{1,0:T(8,128)(2,1)S(1)} %convert_element_type.161), channel_id=1, source_target_pairs={{0,4},{12,8},{1,5},{13,9},{2,6},{14,10},{3,7},{15,11},{16,20},{28,... | collective-permute-start | bytes 983048 | tf_op jit(solution)/shard_map/ppermute | solution.py:369
  142.7 10.8 %collective-permute-start.30 = (bf16[128,1280]{1,0:T(8,128)(2,1)S(1)}, bf16[128,1280]{1,0:T(8,128)(2,1)S(1)}, u32[]{:S(2)}, u32[]{:S(2)}) collective-permute-start(bf16[128,1280]{1,0:T(8,128)(2,1)S(1)} %get-tuple-element.90), channel_id=1, source_target_pairs={{4,8},{8,4},{5,9},{9,5},{6,10},{10,6},{7,11},{11,7},{20,24},{24,20... | collective-permute-start | bytes 983048 | tf_op jit(solution)/shard_map/ppermute | solution.py:368
  153.5 8.1 %collective-permute-start.32 = (bf16[128,1280]{1,0:T(8,128)(2,1)S(1)}, bf16[128,1280]{1,0:T(8,128)(2,1)S(1)}, u32[]{:S(2)}, u32[]{:S(2)}) collective-permute-start(bf16[128,1280]{1,0:T(8,128)(2,1)S(1)} %add_convert_fusion.2), channel_id=1, source_target_pairs={{0,4},{4,0},{8,12},{12,8},{1,5},{5,1},{9,13},{13,9},{2,6},{6,2},{1... | collective-permute-start | bytes 983048 | tf_op jit(solution)/shard_map/ppermute | solution.py:372
  153.7 9.9 %collective-permute-start.33 = (bf16[128,1280]{1,0:T(8,128)(2,1)S(1)}, bf16[128,1280]{1,0:T(8,128)(2,1)S(1)}, u32[]{:S(2)}, u32[]{:S(2)}) collective-permute-start(bf16[128,1280]{1,0:T(8,128)(2,1)S(1)} %add_convert_fusion.1), channel_id=1, source_target_pairs={{4,8},{8,4},{5,9},{9,5},{6,10},{10,6},{7,11},{11,7},{20,24},{24,20... | collective-permute-start | bytes 983048 | tf_op jit(solution)/shard_map/ppermute | solution.py:374

commit v10 on v9

--- a/solution.py
+++ b/solution.py
@@ -329,6 +329,13 @@
         keep = keep + swap(away, 1, cols).astype(jnp.float32)
         return keep[:, :quarter], keep[:, quarter:].astype(jnp.float16)
 
+    def project_last(block):
+        away = jnp.dot(block, away_weights, preferred_element_type=jnp.float32).astype(jnp.float16)
+        keep = jnp.dot(block, keep_weights, preferred_element_type=jnp.float32)
+        keep, came = hold((keep, swap(away, 1, cols)))
+        keep = keep + came.astype(jnp.float32)
+        return keep[:, :quarter], keep[:, quarter:].astype(jnp.float16)
+
     def finish(keep, payload):
         return (keep + swap(payload, 2, cols).astype(jnp.float32)).astype(jnp.bfloat16)
 
@@ -342,7 +349,7 @@
     second, payload2 = hold((finish(keep1, payload1), payload2))
     third = finish(keep2, payload2)
     fourth, third = hold((jnp.where(outer, far_out, far), third))
-    qkv = [first, second, third, finish(*project(fourth))]
+    qkv = [first, second, third, finish(*project_last(fourth))]
 
     key_row = key_pos.reshape(1, -1)
 

time: 165 us -> 167 us (1.012)
  waiting for transfers between devices: 57 us -> 59 us
    ppermute x16, waiting for transfers between devices: 22.3 us -> 27.1 us  [swap(): return lax.ppermute(value, 'col', [(i, i ^ distance) for i in range(size)])]
    dot_general x0 -> x2, matrix products: none -> 3.48 us  [the longest x1 2.79 us: project_last(): keep = jnp.dot(block, keep_weights, preferred_element_type=jnp.float32)]
    dot_general x4 -> x3, matrix products: 4.86 us -> 2.06 us  [project(): keep = jnp.dot(block, keep_weights, preferred_element_type=jnp.float32)]
    ppermute x1, waiting for transfers between devices: 3.42 us -> 0.74 us  [line_body(): far_out = lax.ppermute(far, 'lat', OUTWARD)]
  transfers between devices with their start and end apart: 34 -> 34, of which waited for: 21 -> 20; matrix products, arithmetic and copies ran while one was open for 11% -> 12% of each run, Pallas kernels for 18% -> 18%
where the time goes in v10:
time: 167 us
  waiting for transfers between devices  59 us (35%)
  starting transfers between devices  45.6 us (27%)
  Pallas kernels  32.3 us (19%)
  matrix products  20.9 us (13%)
  other arithmetic  4.52 us (3%)
  local copies, waits for them, and re-layouts  3.5 us (2%)
    ppermute x16, waiting for transfers between devices, swap(): return lax.ppermute(value, 'col', [(i, i ^ distance) for i in range(size)])  27.1 us
    ppermute x16, starting transfers between devices, swap(): return lax.ppermute(value, 'col', [(i, i ^ distance) for i in range(size)])  13 us
    pallas_call x2, Pallas kernels, decode(): pl.pallas_call(decode_kernel, out_shape=jax.ShapeDtypeStruct((rows, colum...  11.7 us
    pallas_call x2, Pallas kernels, densify(): pl.pallas_call(functools.partial(densify_kernel, topk=topk, latents=laten...  11.4 us
    dot_general x1, matrix products, line_body(): far = jnp.dot(codes_far, decoder, preferred_element_type=jnp.float32)  9.88 us
    ppermute x1, waiting for transfers between devices, line_body(): across = lax.ppermute(own, 'lat', MIDDLE)  8.7 us
    ppermute x2, starting transfers between devices, line_body(): mid_far = lax.ppermute(mid_far, 'lat', MIDDLE)  7.06 us
    ppermute x2, waiting for transfers between devices, line_body(): last = lax.ppermute(last, 'lat', PAIRS)  6.64 us
  transfers between devices with their start and end apart: 34, of which 20 were waited for; matrix products, arithmetic and copies ran while one was open for 12% of the time, Pallas kernels for 18%

profile of v10, /device:TPU:8, one launch (start us, length us, event | category | flops | bytes accessed | tf_op | source)
XLA Modules:
  0.0 166.6 jit_solution(1092112052493921559)
XLA Ops:
  1.9 1.6 collective-permute-start
  4.6 1.4 collective-permute-start.2
  6.0 1.5 constant_dynamic-slice_fusion
  7.5 1.6 collective-permute-start.4
  9.5 5.7 %densify.2 = bf16[256,8192]{1,0:T(8,128)(2,1)S(1)} custom-call(s32[1]{0:T(128)} %bitcast.base_ref, f32[16,1024]{1,0:T(8,128)S(1)} %get-tuple-element.115.refs_0_, f32[16,1024]{1,0:T(8,128)S(1)} %get-tuple-element.114.refs_1_), custom_call_target="tpu_custom_call" | custom-call | flops 2147483648 | bytes 4194304 | tf_op jit(solution)/shard_map/densify/pallas_call | solution.py:64
  15.2 9.9 %fusion.24 = f32[256,1280]{1,0:T(8,128)S(1)} fusion(bf16[256,8192]{1,0:T(8,128)(2,1)S(1)} %densify.2, bf16[8192,1280]{1,0:T(8,128)(2,1)} %weights_ref.3), kind=kOutput, calls=%fused_computation.80 | convolution fusion | flops 5368709120 | bytes 26476544 | tf_op jit(solution)/shard_map/dot_general | solution.py:282
  25.2 1.3 collective-permute-start.3
  26.6 5.7 %densify.3.codes_ref = bf16[256,8192]{1,0:T(8,128)(2,1)S(1)} custom-call(s32[1]{0:T(128)} %bitcast.base_ref, f32[16,1024]{1,0:T(8,128)S(1)} %collective-permute-done.2.refs_0_, f32[16,1024]{1,0:T(8,128)S(1)} %constant_dynamic-update-slice_fusion.refs_1_), custom_call_target="tpu_custom_call" | custom-call | flops 2147483648 | bytes 4194304 | tf_op jit(solution)/shard_map/densify/pallas_call | solution.py:64
  32.3 4.8 %decode.2.rest_0_ = f32[256,1280]{1,0:T(8,128)S(1)} custom-call(bf16[256,8192]{1,0:T(8,128)(2,1)S(1)} %densify.3.codes_ref, bf16[8192,1280]{1,0:T(8,128)(2,1)} %weights_ref.3), custom_call_target="tpu_custom_call" | custom-call | flops 1 | bytes 1 | tf_op jit(solution)/shard_map/decode/pallas_call | solution.py:89
  37.4 1.6 collective-permute-start.6
  38.9 4.0 %collective-permute-start.5 = (f16[128,1280]{1,0:T(8,128)(2,1)S(1)}, f16[128,1280]{1,0:T(8,128)(2,1)S(1)}, u32[]{:S(2)}, u32[]{:S(2)}) collective-permute-start(f16[128,1280]{1,0:T(8,128)(2,1)S(1)} %get-tuple-element.59), channel_id=1, source_target_pairs={{4,8},{8,4},{5,9},{9,5},{6,10},{10,6},{7,11},{11,7},{20,24},{24,20... | collective-permute-start | bytes 983048 | tf_op jit(solution)/shard_map/ppermute | solution.py:294
  42.9 6.9 %decode.3 = f32[256,1280]{1,0:T(8,128)S(1)} custom-call(bf16[256,8192]{1,0:T(8,128)(2,1)S(1)} %densify.3.codes_ref, bf16[8192,1280]{1,0:T(8,128)(2,1)} %weights_ref.3, f32[256,1280]{1,0:T(8,128)S(1)} %decode.2.rest_0_), custom_call_target="tpu_custom_call", output_to_operand_aliasing={{}: (2, {})} | custom-call | flops 1 | bytes 1 | tf_op jit(solution)/shard_map/decode/pallas_call | solution.py:89
  50.4 3.5 %collective-permute-start.7 = (f16[128,1280]{1,0:T(8,128)(2,1)S(1)}, f16[128,1280]{1,0:T(8,128)(2,1)S(1)}, u32[]{:S(2)}, u32[]{:S(2)}) collective-permute-start(f16[128,1280]{1,0:T(8,128)(2,1)S(1)} %multiply_convert_fusion), channel_id=1, source_target_pairs={{4,8},{8,4},{5,9},{9,5},{6,10},{10,6},{7,11},{11,7},{20,24},{24,20... | collective-permute-start | bytes 983048 | tf_op jit(solution)/shard_map/ppermute | solution.py:301
  54.9 1.8 %select_columns.2 = bf16[1280,1536]{1,0:T(8,128)(2,1)S(1)} custom-call(s32[2]{0:T(128)S(1)} %get-tuple-element.124.order_ref, bf16[3,1280,1024]{2,1,0:T(8,128)(2,1)S(1)} %bitcast.54), custom_call_target="tpu_custom_call" | custom-call | bytes 7864320 | tf_op jit(solution)/shard_map/select_columns/pallas_call | solution.py:113
  56.7 1.8 %select_columns.3 = bf16[1280,1536]{1,0:T(8,128)(2,1)S(1)} custom-call(s32[2]{0:T(128)S(1)} %get-tuple-element.125.order_ref, bf16[3,1280,1024]{2,1,0:T(8,128)(2,1)S(1)} %bitcast.55), custom_call_target="tpu_custom_call" | custom-call | bytes 7864320 | tf_op jit(solution)/shard_map/select_columns/pallas_call | solution.py:113
  58.5 1.8 %collective-permute-done.8 = f16[128,1280]{1,0:T(8,128)(2,1)S(1)} collective-permute-done((f16[128,1280]{1,0:T(8,128)(2,1)S(1)}, f16[128,1280]{1,0:T(8,128)(2,1)S(1)}, u32[]{:S(2)}, u32[]{:S(2)}) %collective-permute-start.8) | collective-permute-done | bytes 327712 | tf_op jit(solution)/shard_map/ppermute | solution.py:300
  60.3 2.0 %collective-permute-done.7 = f16[128,1280]{1,0:T(8,128)(2,1)S(1)} collective-permute-done((f16[128,1280]{1,0:T(8,128)(2,1)S(1)}, f16[128,1280]{1,0:T(8,128)(2,1)S(1)}, u32[]{:S(2)}, u32[]{:S(2)}) %collective-permute-start.7) | collective-permute-done | bytes 327712 | tf_op jit(solution)/shard_map/ppermute | solution.py:301
  63.9 1.6 collective-permute-start.11
  65.4 2.1 %collective-permute-done.11 = f32[2,128]{1,0:T(2,128)S(1)} collective-permute-done((f32[2,128]{1,0:T(2,128)S(1)}, f32[2,128]{1,0:T(2,128)S(1)}, u32[]{:S(2)}, u32[]{:S(2)}) %collective-permute-start.11) | collective-permute-done | bytes 1056 | tf_op jit(solution)/shard_map/ppermute | solution.py:223
  68.5 3.2 %collective-permute-start.12 = (bf16[128,1280]{1,0:T(8,128)(2,1)S(1)}, bf16[128,1280]{1,0:T(8,128)(2,1)S(1)}, u32[]{:S(2)}, u32[]{:S(2)}) collective-permute-start(bf16[128,1280]{1,0:T(8,128)(2,1)S(1)} %add_convert_fusion.4), channel_id=1, source_target_pairs={{4,8},{8,4},{5,9},{9,5},{6,10},{10,6},{7,11},{11,7},{20,24},{24,20... | collective-permute-start | bytes 983048 | tf_op jit(solution)/shard_map/ppermute | solution.py:319
  71.8 8.7 %collective-permute-done.12 = bf16[128,1280]{1,0:T(8,128)(2,1)S(1)} collective-permute-done((bf16[128,1280]{1,0:T(8,128)(2,1)S(1)}, bf16[128,1280]{1,0:T(8,128)(2,1)S(1)}, u32[]{:S(2)}, u32[]{:S(2)}) %collective-permute-start.12) | collective-permute-done | bytes 327712 | tf_op jit(solution)/shard_map/ppermute | solution.py:319
  80.5 1.3 collective-permute-start.13
  81.8 3.4 %collective-permute-start.16 = (bf16[128,1280]{1,0:T(8,128)(2,1)S(1)}, bf16[128,1280]{1,0:T(8,128)(2,1)S(1)}, u32[]{:S(2)}, u32[]{:S(2)}) collective-permute-start(bf16[128,1280]{1,0:T(8,128)(2,1)S(1)} %collective-permute-done.14), channel_id=1, source_target_pairs={{4,8},{8,4},{5,9},{9,5},{6,10},{10,6},{7,11},{11,7},{20,24},{24,20... | collective-permute-start | bytes 983048 | tf_op jit(solution)/shard_map/ppermute | solution.py:320
  86.0 1.6 collective-permute-start.18
  88.3 4.0 %collective-permute-done.18 = f16[128,768]{1,0:T(8,128)(2,1)S(1)} collective-permute-done((f16[128,768]{1,0:T(8,128)(2,1)S(1)}, f16[128,768]{1,0:T(8,128)(2,1)S(1)}, u32[]{:S(2)}, u32[]{:S(2)}) %collective-permute-start.18) | collective-permute-done | bytes 196640 | tf_op jit(solution)/shard_map/ppermute | solution.py:223
  93.9 1.6 collective-permute-start.19
  95.5 1.3 collective-permute-start.21
  96.8 4.5 %collective-permute-done.19 = f16[128,768]{1,0:T(8,128)(2,1)S(1)} collective-permute-done((f16[128,768]{1,0:T(8,128)(2,1)S(1)}, f16[128,768]{1,0:T(8,128)(2,1)S(1)}, u32[]{:S(2)}, u32[]{:S(2)}) %collective-permute-start.19) | collective-permute-done | bytes 196640 | tf_op jit(solution)/shard_map/ppermute | solution.py:223
  102.0 1.6 collective-permute-start.22
  104.4 4.2 %collective-permute-done.22 = f16[128,768]{1,0:T(8,128)(2,1)S(1)} collective-permute-done((f16[128,768]{1,0:T(8,128)(2,1)S(1)}, f16[128,768]{1,0:T(8,128)(2,1)S(1)}, u32[]{:S(2)}, u32[]{:S(2)}) %collective-permute-start.22) | collective-permute-done | bytes 196640 | tf_op jit(solution)/shard_map/ppermute | solution.py:223
  109.5 2.8 %fusion.25 = f32[128,1536]{1,0:T(8,128)S(1)} fusion(bf16[128,1280]{1,0:T(8,128)(2,1)S(1)} %broadcast_select_fusion, bf16[1280,1536]{1,0:T(8,128)(2,1)} %copy-done), kind=kOutput, calls=%fused_computation.81 | convolution fusion | flops 503316480 | bytes 5046272 | tf_op jit(solution)/shard_map/dot_general | solution.py:334
  112.5 1.6 collective-permute-start.24
  115.2 4.6 %collective-permute-done.24 = f16[128,768]{1,0:T(8,128)(2,1)S(1)} collective-permute-done((f16[128,768]{1,0:T(8,128)(2,1)S(1)}, f16[128,768]{1,0:T(8,128)(2,1)S(1)}, u32[]{:S(2)}, u32[]{:S(2)}) %collective-permute-start.24) | collective-permute-done | bytes 196640 | tf_op jit(solution)/shard_map/ppermute | solution.py:223
  119.9 2.4 %attend.2 = bf16[256,256]{1,0:T(8,128)(2,1)S(1)} custom-call(s32[256,1]{1,0:T(8,128)S(1)} %copy.22.refs_0_, s32[1,512]{1,0:T(1,128)S(1)} %bitcast.57, bf16[128,768]{1,0:T(8,128)(2,1)S(1)} %fusion.15.refs_2_, bf16[128,768]{1,0:T(8,128)(2,1)S(1)} %fusion.14.refs_3_, bf16[128,768]{1,0:T(8,128)(2,1)S(1)} %fusion.13.refs_4_, ...), custom_call_target="tpu_custom_call" | custom-call | flops 536870912 | bytes 2097152 | tf_op jit(solution)/shard_map/attend/pallas_call | solution.py:189
  122.3 1.6 collective-permute-start.25
  124.0 2.4 %attend.3 = bf16[256,256]{1,0:T(8,128)(2,1)S(1)} custom-call(s32[256,1]{1,0:T(8,128)S(1)} %copy.23.refs_0_, s32[1,512]{1,0:T(1,128)S(1)} %bitcast.58, bf16[128,768]{1,0:T(8,128)(2,1)S(1)} %fusion.15.refs_2_, bf16[128,768]{1,0:T(8,128)(2,1)S(1)} %fusion.14.refs_3_, bf16[128,768]{1,0:T(8,128)(2,1)S(1)} %fusion.13.refs_4_, ...), custom_call_target="tpu_custom_call" | custom-call | flops 536870912 | bytes 2097152 | tf_op jit(solution)/shard_map/attend/pallas_call | solution.py:189
  127.6 1.5 collective-permute-done.26
  129.1 2.6 %fusion = f32[256,1280]{1,0:T(8,128)S(1)} fusion(bf16[1024,1280]{1,0:T(8,128)(2,1)} %copy-done.2, bf16[256,512]{1,0:T(8,128)(2,1)S(1)} %collective-permute-done.26, bf16[256,256]{1,0:T(8,128)(2,1)S(1)} %collective-permute-done.25, bf16[256,256]{1,0:T(8,128)(2,1)S(1)} %attend.2), kind=kOutput, calls=%fused_computation.23 | convolution fusion | flops 672661504 | bytes 4456448 | tf_op jit(solution)/shard_map/dot_general | solution.py:367
  131.8 1.3 collective-permute-start.29
  133.1 1.5 collective-permute-start.27
  134.6 4.1 %collective-permute-done.27 = bf16[256,256]{1,0:T(8,128)(2,1)S(1)} collective-permute-done((bf16[256,256]{1,0:T(8,128)(2,1)S(1)}, bf16[256,256]{1,0:T(8,128)(2,1)S(1)}, u32[]{:S(2)}, u32[]{:S(2)}) %collective-permute-start.27) | collective-permute-done | bytes 131104 | tf_op jit(solution)/shard_map/ppermute | solution.py:223
  138.8 4.6 %collective-permute-done.29 = bf16[128,1280]{1,0:T(8,128)(2,1)S(1)} collective-permute-done((bf16[128,1280]{1,0:T(8,128)(2,1)S(1)}, bf16[128,1280]{1,0:T(8,128)(2,1)S(1)}, u32[]{:S(2)}, u32[]{:S(2)}) %collective-permute-start.29) | collective-permute-done | bytes 327712 | tf_op jit(solution)/shard_map/ppermute | solution.py:369
  144.9 3.1 %collective-permute-start.30 = (bf16[128,1280]{1,0:T(8,128)(2,1)S(1)}, bf16[128,1280]{1,0:T(8,128)(2,1)S(1)}, u32[]{:S(2)}, u32[]{:S(2)}) collective-permute-start(bf16[128,1280]{1,0:T(8,128)(2,1)S(1)} %get-tuple-element.94), channel_id=1, source_target_pairs={{4,8},{8,4},{5,9},{9,5},{6,10},{10,6},{7,11},{11,7},{20,24},{24,20... | collective-permute-start | bytes 983048 | tf_op jit(solution)/shard_map/ppermute | solution.py:375
  148.9 5.5 %collective-permute-done.31 = bf16[128,1280]{1,0:T(8,128)(2,1)S(1)} collective-permute-done((bf16[128,1280]{1,0:T(8,128)(2,1)S(1)}, bf16[128,1280]{1,0:T(8,128)(2,1)S(1)}, u32[]{:S(2)}, u32[]{:S(2)}) %collective-permute-start.31) | collective-permute-done | bytes 327712 | tf_op jit(solution)/shard_map/ppermute | solution.py:376
  154.4 1.3 collective-permute-done.30
  155.9 3.1 %collective-permute-start.33 = (bf16[128,1280]{1,0:T(8,128)(2,1)S(1)}, bf16[128,1280]{1,0:T(8,128)(2,1)S(1)}, u32[]{:S(2)}, u32[]{:S(2)}) collective-permute-start(bf16[128,1280]{1,0:T(8,128)(2,1)S(1)} %add_convert_fusion.1), channel_id=1, source_target_pairs={{4,8},{8,4},{5,9},{9,5},{6,10},{10,6},{7,11},{11,7},{20,24},{24,20... | collective-permute-start | bytes 983048 | tf_op jit(solution)/shard_map/ppermute | solution.py:381
  159.0 4.8 %collective-permute-done.32 = bf16[128,1280]{1,0:T(8,128)(2,1)S(1)} collective-permute-done((bf16[128,1280]{1,0:T(8,128)(2,1)S(1)}, bf16[128,1280]{1,0:T(8,128)(2,1)S(1)}, u32[]{:S(2)}, u32[]{:S(2)}) %collective-permute-start.32) | collective-permute-done | bytes 327712 | tf_op jit(solution)/shard_map/ppermute | solution.py:379
  163.8 2.0 %collective-permute-done.33 = bf16[128,1280]{1,0:T(8,128)(2,1)S(1)} collective-permute-done((bf16[128,1280]{1,0:T(8,128)(2,1)S(1)}, bf16[128,1280]{1,0:T(8,128)(2,1)S(1)}, u32[]{:S(2)}, u32[]{:S(2)}) %collective-permute-start.33) | collective-permute-done | bytes 327712 | tf_op jit(solution)/shard_map/ppermute | solution.py:381
  (118 shorter events, 19.5 us)
Async XLA Ops:
  1.9 7.3 %collective-permute-start = (f32[16,1024]{1,0:T(8,128)S(1)}, f32[16,1024]{1,0:T(8,128)S(1)}, u32[]{:S(2)}, u32[]{:S(2)}) collective-permute-start(f32[16,1024]{1,0:T(8,128)S(1)} %constant_dynamic-update-slice_fusion.refs_1_), channel_id=1, source_target_pairs={{0,12},{4,8},{8,4},{12,0},{1,13},{5,9},{9,5},{13,1},{2,14},{6,10},... | collective-permute-start | bytes 196616 | tf_op jit(solution)/shard_map/ppermute | solution.py:218
  3.5 6.0 %collective-permute-start.1 = (f32[16,1024]{1,0:T(8,128)S(1)}, f32[16,1024]{1,0:T(8,128)S(1)}, u32[]{:S(2)}, u32[]{:S(2)}) collective-permute-start(f32[16,1024]{1,0:T(8,128)S(1)} %constant_dynamic-update-slice_fusion.refs_1_), channel_id=1, source_target_pairs={{0,8},{4,12},{8,0},{12,4},{1,9},{5,13},{9,1},{13,5},{2,10},{6,14},... | collective-permute-start | bytes 196616 | tf_op jit(solution)/shard_map/ppermute | solution.py:217
  4.6 20.6 %collective-permute-start.2 = (f32[16,1024]{1,0:T(8,128)S(1)}, f32[16,1024]{1,0:T(8,128)S(1)}, u32[]{:S(2)}, u32[]{:S(2)}) collective-permute-start(f32[16,1024]{1,0:T(8,128)S(1)} %constant_dynamic-update-slice_fusion.refs_1_), channel_id=1, source_target_pairs={{0,4},{4,0},{8,12},{12,8},{1,5},{5,1},{9,13},{13,9},{2,6},{6,2},{1... | collective-permute-start | bytes 196616 | tf_op jit(solution)/shard_map/ppermute | solution.py:216
  7.5 29.7 %collective-permute-start.4 = (bf16[2,2,384,256]{3,2,1,0:T(8,128)(2,1)S(1)}, bf16[2,2,384,256]{3,2,1,0:T(8,128)(2,1)S(1)}, u32[]{:S(2)}, u32[]{:S(2)}) collective-permute-start(bf16[2,2,384,256]{3,2,1,0:T(8,128)(2,1)S(1)} %pad_maximum_fusion), channel_id=1, source_target_pairs={{0,2},{1,3},{2,0},{3,1},{4,6},{5,7},{6,4},{7,5},{8,10},{9,11},{10,... | collective-permute-start | bytes 2359304 | tf_op jit(solution)/shard_map/ppermute | solution.py:223
  15.2 11.3 %copy-start.8 = (s32[512]{0:T(512)S(1)}, s32[512]{0:T(512)}, u32[]{:S(2)}) copy-start(s32[512]{0:T(512)} %param.18) | copy-start | bytes 6148
  25.2 11.9 %collective-permute-start.3 = (f16[128,1280]{1,0:T(8,128)(2,1)S(1)}, f16[128,1280]{1,0:T(8,128)(2,1)S(1)}, u32[]{:S(2)}, u32[]{:S(2)}) collective-permute-start(f16[128,1280]{1,0:T(8,128)(2,1)S(1)} %multiply_convert_fusion.4), channel_id=1, source_target_pairs={{0,4},{12,8},{1,5},{13,9},{2,6},{14,10},{3,7},{15,11},{16,20},{28,... | collective-permute-start | bytes 983048 | tf_op jit(solution)/shard_map/ppermute | solution.py:284
  37.3 17.6 %slice-start = ((s8[7864320]{0:T(1024)(128)(4,1)}), s8[4194304]{0:T(1024)(128)(4,1)S(1)}, s32[]{:S(2)}) async-start(s8[7864320]{0:T(1024)(128)(4,1)} %bitcast.52), calls=%async_computation | async-start | bytes 8388608
  37.3 17.5 %slice-start.1 = ((s8[7864320]{0:T(1024)(128)(4,1)}), s8[3670016]{0:T(1024)(128)(4,1)S(1)}, s32[]{:S(2)}) async-start(s8[7864320]{0:T(1024)(128)(4,1)} %bitcast.52), calls=%async_computation.1 | async-start | bytes 7340032
  37.4 12.5 %collective-permute-start.6 = (f16[128,1280]{1,0:T(8,128)(2,1)S(1)}, f16[128,1280]{1,0:T(8,128)(2,1)S(1)}, u32[]{:S(2)}, u32[]{:S(2)}) collective-permute-start(f16[128,1280]{1,0:T(8,128)(2,1)S(1)} %multiply_convert_fusion.2), channel_id=1, source_target_pairs={{0,4},{12,8},{1,5},{13,9},{2,6},{14,10},{3,7},{15,11},{16,20},{28,... | collective-permute-start | bytes 983048 | tf_op jit(solution)/shard_map/ppermute | solution.py:295
  38.9 10.9 %collective-permute-start.5 = (f16[128,1280]{1,0:T(8,128)(2,1)S(1)}, f16[128,1280]{1,0:T(8,128)(2,1)S(1)}, u32[]{:S(2)}, u32[]{:S(2)}) collective-permute-start(f16[128,1280]{1,0:T(8,128)(2,1)S(1)} %get-tuple-element.59), channel_id=1, source_target_pairs={{4,8},{8,4},{5,9},{9,5},{6,10},{10,6},{7,11},{11,7},{20,24},{24,20... | collective-permute-start | bytes 983048 | tf_op jit(solution)/shard_map/ppermute | solution.py:294
  49.8 4.1 %copy-start.7 = (bf16[1280]{0:T(1024)(128)(2,1)S(1)}, bf16[1280]{0:T(1024)(128)(2,1)}, u32[]{:S(2)}) copy-start(bf16[1280]{0:T(1024)(128)(2,1)} %param.13) | copy-start | bytes 7684
  49.8 4.2 %copy-start.1 = (bf16[1024,1280]{1,0:T(8,128)(2,1)S(1)}, bf16[1024,1280]{1,0:T(8,128)(2,1)}, u32[]{:S(2)}) copy-start(bf16[1024,1280]{1,0:T(8,128)(2,1)} %from_ref.1) | copy-start | bytes 7864324
  50.1 10.2 %collective-permute-start.9 = (bf16[2,2,384,256]{3,2,1,0:T(8,128)(2,1)S(1)}, bf16[2,2,384,256]{3,2,1,0:T(8,128)(2,1)S(1)}, u32[]{:S(2)}, u32[]{:S(2)}) collective-permute-start(bf16[2,2,384,256]{3,2,1,0:T(8,128)(2,1)S(1)} %pad_maximum_fusion.1), channel_id=1, source_target_pairs={{0,1},{1,0},{2,3},{3,2},{4,5},{5,4},{6,7},{7,6},{8,9},{9,8},{10,11... | collective-permute-start | bytes 2359304 | tf_op jit(solution)/shard_map/ppermute | solution.py:223
  50.2 10.1 %collective-permute-start.8 = (f16[128,1280]{1,0:T(8,128)(2,1)S(1)}, f16[128,1280]{1,0:T(8,128)(2,1)S(1)}, u32[]{:S(2)}, u32[]{:S(2)}) collective-permute-start(f16[128,1280]{1,0:T(8,128)(2,1)S(1)} %multiply_convert_fusion.1), channel_id=1, source_target_pairs={{0,4},{4,0},{8,12},{12,8},{1,5},{5,1},{9,13},{13,9},{2,6},{6,2},{1... | collective-permute-start | bytes 983048 | tf_op jit(solution)/shard_map/ppermute | solution.py:300
  50.4 11.9 %collective-permute-start.7 = (f16[128,1280]{1,0:T(8,128)(2,1)S(1)}, f16[128,1280]{1,0:T(8,128)(2,1)S(1)}, u32[]{:S(2)}, u32[]{:S(2)}) collective-permute-start(f16[128,1280]{1,0:T(8,128)(2,1)S(1)} %multiply_convert_fusion), channel_id=1, source_target_pairs={{4,8},{8,4},{5,9},{9,5},{6,10},{10,6},{7,11},{11,7},{20,24},{24,20... | collective-permute-start | bytes 983048 | tf_op jit(solution)/shard_map/ppermute | solution.py:301
  54.8 1.9 %copy-start.2 = (bf16[1024,1280]{1,0:T(8,128)(2,1)}, bf16[1024,1280]{1,0:T(8,128)(2,1)S(1)}, u32[]{:S(2)}) copy-start(bf16[1024,1280]{1,0:T(8,128)(2,1)S(1)} %select_rows.1) | copy-start | bytes 7864324
  56.7 10.9 %copy-start.5 = (f32[1280]{0:T(1024)S(1)}, f32[1280]{0:T(1024)}, u32[]{:S(2)}) copy-start(f32[1280]{0:T(1024)} %param.15) | copy-start | bytes 15364
  56.7 10.9 %copy-start.6 = (f32[1280]{0:T(1024)S(1)}, f32[1280]{0:T(1024)}, u32[]{:S(2)}) copy-start(f32[1280]{0:T(1024)} %param.14) | copy-start | bytes 15364
  58.5 42.8 %copy-start = (bf16[1280,1536]{1,0:T(8,128)(2,1)}, bf16[1280,1536]{1,0:T(8,128)(2,1)S(1)}, u32[]{:S(2)}) copy-start(bf16[1280,1536]{1,0:T(8,128)(2,1)S(1)} %select_columns.3) | copy-start | bytes 11796484
  60.3 25.6 %copy-start.4 = (bf16[2,2,384,256]{3,2,1,0:T(8,128)(2,1)}, bf16[2,2,384,256]{3,2,1,0:T(8,128)(2,1)S(1)}, u32[]{:S(2)}) copy-start(bf16[2,2,384,256]{3,2,1,0:T(8,128)(2,1)S(1)} %collective-permute-done.9) | copy-start | bytes 2359300
  62.7 1.2 collective-permute-start.10
  63.9 3.6 %collective-permute-start.11 = (f32[2,128]{1,0:T(2,128)S(1)}, f32[2,128]{1,0:T(2,128)S(1)}, u32[]{:S(2)}, u32[]{:S(2)}) collective-permute-start(f32[2,128]{1,0:T(2,128)S(1)} %fusion.20), channel_id=1, source_target_pairs={{0,2},{1,3},{2,0},{3,1},{4,6},{5,7},{6,4},{7,5},{8,10},{9,11},{10,... | collective-permute-start | bytes 3080 | tf_op jit(solution)/shard_map/ppermute | solution.py:223
  68.5 16.8 %collective-permute-start.15 = (f16[128,1536]{1,0:T(8,128)(2,1)S(1)}, f16[128,1536]{1,0:T(8,128)(2,1)S(1)}, u32[]{:S(2)}, u32[]{:S(2)}) collective-permute-start(f16[128,1536]{1,0:T(8,128)(2,1)S(1)} %convolution_convert_fusion.3), channel_id=1, source_target_pairs={{0,1},{1,0},{2,3},{3,2},{4,5},{5,4},{6,7},{7,6},{8,9},{9,8},{10,11... | collective-permute-start | bytes 1179656 | tf_op jit(solution)/shard_map/ppermute | solution.py:223
  68.5 12.0 %collective-permute-start.12 = (bf16[128,1280]{1,0:T(8,128)(2,1)S(1)}, bf16[128,1280]{1,0:T(8,128)(2,1)S(1)}, u32[]{:S(2)}, u32[]{:S(2)}) collective-permute-start(bf16[128,1280]{1,0:T(8,128)(2,1)S(1)} %add_convert_fusion.4), channel_id=1, source_target_pairs={{4,8},{8,4},{5,9},{9,5},{6,10},{10,6},{7,11},{11,7},{20,24},{24,20... | collective-permute-start | bytes 983048 | tf_op jit(solution)/shard_map/ppermute | solution.py:319
  71.7 10.1 %collective-permute-start.14 = (bf16[128,1280]{1,0:T(8,128)(2,1)S(1)}, bf16[128,1280]{1,0:T(8,128)(2,1)S(1)}, u32[]{:S(2)}, u32[]{:S(2)}) collective-permute-start(bf16[128,1280]{1,0:T(8,128)(2,1)S(1)} %add_convert_fusion.4), channel_id=1, source_target_pairs={{0,4},{4,0},{8,12},{12,8},{1,5},{5,1},{9,13},{13,9},{2,6},{6,2},{1... | collective-permute-start | bytes 983048 | tf_op jit(solution)/shard_map/ppermute | solution.py:318
  80.5 11.8 %collective-permute-start.13 = (bf16[128,1280]{1,0:T(8,128)(2,1)S(1)}, bf16[128,1280]{1,0:T(8,128)(2,1)S(1)}, u32[]{:S(2)}, u32[]{:S(2)}) collective-permute-start(bf16[128,1280]{1,0:T(8,128)(2,1)S(1)} %collective-permute-done.12), channel_id=1, source_target_pairs={{4,0},{8,12},{5,1},{9,13},{6,2},{10,14},{7,3},{11,15},{20,16},{24,... | collective-permute-start | bytes 983048 | tf_op jit(solution)/shard_map/ppermute | solution.py:321
  81.8 11.3 %collective-permute-start.16 = (bf16[128,1280]{1,0:T(8,128)(2,1)S(1)}, bf16[128,1280]{1,0:T(8,128)(2,1)S(1)}, u32[]{:S(2)}, u32[]{:S(2)}) collective-permute-start(bf16[128,1280]{1,0:T(8,128)(2,1)S(1)} %collective-permute-done.14), channel_id=1, source_target_pairs={{4,8},{8,4},{5,9},{9,5},{6,10},{10,6},{7,11},{11,7},{20,24},{24,20... | collective-permute-start | bytes 983048 | tf_op jit(solution)/shard_map/ppermute | solution.py:320
  86.0 6.3 %collective-permute-start.18 = (f16[128,768]{1,0:T(8,128)(2,1)S(1)}, f16[128,768]{1,0:T(8,128)(2,1)S(1)}, u32[]{:S(2)}, u32[]{:S(2)}) collective-permute-start(f16[128,768]{1,0:T(8,128)(2,1)S(1)} %slice_convert_fusion.4), channel_id=1, source_target_pairs={{0,2},{1,3},{2,0},{3,1},{4,6},{5,7},{6,4},{7,5},{8,10},{9,11},{10,... | collective-permute-start | bytes 589832 | tf_op jit(solution)/shard_map/ppermute | solution.py:223
  88.2 4.2 %collective-permute-start.17 = (f16[128,1536]{1,0:T(8,128)(2,1)S(1)}, f16[128,1536]{1,0:T(8,128)(2,1)S(1)}, u32[]{:S(2)}, u32[]{:S(2)}) collective-permute-start(f16[128,1536]{1,0:T(8,128)(2,1)S(1)} %convolution_convert_fusion.2), channel_id=1, source_target_pairs={{0,1},{1,0},{2,3},{3,2},{4,5},{5,4},{6,7},{7,6},{8,9},{9,8},{10,11... | collective-permute-start | bytes 1179656 | tf_op jit(solution)/shard_map/ppermute | solution.py:223
  93.8 7.4 %collective-permute-start.20 = (f16[128,1536]{1,0:T(8,128)(2,1)S(1)}, f16[128,1536]{1,0:T(8,128)(2,1)S(1)}, u32[]{:S(2)}, u32[]{:S(2)}) collective-permute-start(f16[128,1536]{1,0:T(8,128)(2,1)S(1)} %convolution_convert_fusion.1), channel_id=1, source_target_pairs={{0,1},{1,0},{2,3},{3,2},{4,5},{5,4},{6,7},{7,6},{8,9},{9,8},{10,11... | collective-permute-start | bytes 1179656 | tf_op jit(solution)/shard_map/ppermute | solution.py:223
  93.9 7.3 %collective-permute-start.19 = (f16[128,768]{1,0:T(8,128)(2,1)S(1)}, f16[128,768]{1,0:T(8,128)(2,1)S(1)}, u32[]{:S(2)}, u32[]{:S(2)}) collective-permute-start(f16[128,768]{1,0:T(8,128)(2,1)S(1)} %slice_convert_fusion.3), channel_id=1, source_target_pairs={{0,2},{1,3},{2,0},{3,1},{4,6},{5,7},{6,4},{7,5},{8,10},{9,11},{10,... | collective-permute-start | bytes 589832 | tf_op jit(solution)/shard_map/ppermute | solution.py:223
  95.5 8.8 %collective-permute-start.21 = (bf16[128,1280]{1,0:T(8,128)(2,1)S(1)}, bf16[128,1280]{1,0:T(8,128)(2,1)S(1)}, u32[]{:S(2)}, u32[]{:S(2)}) collective-permute-start(bf16[128,1280]{1,0:T(8,128)(2,1)S(1)} %collective-permute-done.16), channel_id=1, source_target_pairs={{4,0},{8,12},{5,1},{9,13},{6,2},{10,14},{7,3},{11,15},{20,16},{24,... | collective-permute-start | bytes 983048 | tf_op jit(solution)/shard_map/ppermute | solution.py:322
  102.0 6.5 %collective-permute-start.22 = (f16[128,768]{1,0:T(8,128)(2,1)S(1)}, f16[128,768]{1,0:T(8,128)(2,1)S(1)}, u32[]{:S(2)}, u32[]{:S(2)}) collective-permute-start(f16[128,768]{1,0:T(8,128)(2,1)S(1)} %slice_convert_fusion.2), channel_id=1, source_target_pairs={{0,2},{1,3},{2,0},{3,1},{4,6},{5,7},{6,4},{7,5},{8,10},{9,11},{10,... | collective-permute-start | bytes 589832 | tf_op jit(solution)/shard_map/ppermute | solution.py:223
  109.3 3.0 %collective-permute-start.23 = (f16[128,1536]{1,0:T(8,128)(2,1)S(1)}, f16[128,1536]{1,0:T(8,128)(2,1)S(1)}, u32[]{:S(2)}, u32[]{:S(2)}) collective-permute-start(f16[128,1536]{1,0:T(8,128)(2,1)S(1)} %convolution_convert_fusion), channel_id=1, source_target_pairs={{0,1},{1,0},{2,3},{3,2},{4,5},{5,4},{6,7},{7,6},{8,9},{9,8},{10,11... | collective-permute-start | bytes 1179656 | tf_op jit(solution)/shard_map/ppermute | solution.py:223
  112.5 7.4 %collective-permute-start.24 = (f16[128,768]{1,0:T(8,128)(2,1)S(1)}, f16[128,768]{1,0:T(8,128)(2,1)S(1)}, u32[]{:S(2)}, u32[]{:S(2)}) collective-permute-start(f16[128,768]{1,0:T(8,128)(2,1)S(1)} %slice_convert_fusion.1), channel_id=1, source_target_pairs={{0,2},{1,3},{2,0},{3,1},{4,6},{5,7},{6,4},{7,5},{8,10},{9,11},{10,... | collective-permute-start | bytes 589832 | tf_op jit(solution)/shard_map/ppermute | solution.py:223
  122.3 5.2 %collective-permute-start.25 = (bf16[256,256]{1,0:T(8,128)(2,1)S(1)}, bf16[256,256]{1,0:T(8,128)(2,1)S(1)}, u32[]{:S(2)}, u32[]{:S(2)}) collective-permute-start(bf16[256,256]{1,0:T(8,128)(2,1)S(1)} %attend.2), channel_id=1, source_target_pairs={{0,2},{1,3},{2,0},{3,1},{4,6},{5,7},{6,4},{7,5},{8,10},{9,11},{10,... | collective-permute-start | bytes 393224 | tf_op jit(solution)/shard_map/ppermute | solution.py:223
  127.5 20.5 %copy-start.3 = (bf16[1024,1280]{1,0:T(8,128)(2,1)S(1)}, bf16[1024,1280]{1,0:T(8,128)(2,1)}, u32[]{:S(2)}) copy-start(bf16[1024,1280]{1,0:T(8,128)(2,1)} %copy-done.2) | copy-start | bytes 7864324
  127.5 1.6 collective-permute-start.26
  131.8 11.6 %collective-permute-start.29 = (bf16[128,1280]{1,0:T(8,128)(2,1)S(1)}, bf16[128,1280]{1,0:T(8,128)(2,1)S(1)}, u32[]{:S(2)}, u32[]{:S(2)}) collective-permute-start(bf16[128,1280]{1,0:T(8,128)(2,1)S(1)} %slice.153), channel_id=1, source_target_pairs={{0,4},{12,8},{1,5},{13,9},{2,6},{14,10},{3,7},{15,11},{16,20},{28,... | collective-permute-start | bytes 983048 | tf_op jit(solution)/shard_map/ppermute | solution.py:369
  133.1 5.6 %collective-permute-start.27 = (bf16[256,256]{1,0:T(8,128)(2,1)S(1)}, bf16[256,256]{1,0:T(8,128)(2,1)S(1)}, u32[]{:S(2)}, u32[]{:S(2)}) collective-permute-start(bf16[256,256]{1,0:T(8,128)(2,1)S(1)} %attend.3), channel_id=1, source_target_pairs={{0,2},{1,3},{2,0},{3,1},{4,6},{5,7},{6,4},{7,5},{8,10},{9,11},{10,... | collective-permute-start | bytes 393224 | tf_op jit(solution)/shard_map/ppermute | solution.py:223
  138.7 9.3 %collective-permute-start.28 = (bf16[256,512]{1,0:T(8,128)(2,1)S(1)}, bf16[256,512]{1,0:T(8,128)(2,1)S(1)}, u32[]{:S(2)}, u32[]{:S(2)}) collective-permute-start(bf16[256,512]{1,0:T(8,128)(2,1)S(1)} %pad_maximum_fusion.3), channel_id=1, source_target_pairs={{0,1},{1,0},{2,3},{3,2},{4,5},{5,4},{6,7},{7,6},{8,9},{9,8},{10,11... | collective-permute-start | bytes 786440 | tf_op jit(solution)/shard_map/ppermute | solution.py:223
  143.6 10.8 %collective-permute-start.31 = (bf16[128,1280]{1,0:T(8,128)(2,1)S(1)}, bf16[128,1280]{1,0:T(8,128)(2,1)S(1)}, u32[]{:S(2)}, u32[]{:S(2)}) collective-permute-start(bf16[128,1280]{1,0:T(8,128)(2,1)S(1)} %convert_element_type.161), channel_id=1, source_target_pairs={{0,4},{12,8},{1,5},{13,9},{2,6},{14,10},{3,7},{15,11},{16,20},{28,... | collective-permute-start | bytes 983048 | tf_op jit(solution)/shard_map/ppermute | solution.py:376
  144.9 10.8 %collective-permute-start.30 = (bf16[128,1280]{1,0:T(8,128)(2,1)S(1)}, bf16[128,1280]{1,0:T(8,128)(2,1)S(1)}, u32[]{:S(2)}, u32[]{:S(2)}) collective-permute-start(bf16[128,1280]{1,0:T(8,128)(2,1)S(1)} %get-tuple-element.94), channel_id=1, source_target_pairs={{4,8},{8,4},{5,9},{9,5},{6,10},{10,6},{7,11},{11,7},{20,24},{24,20... | collective-permute-start | bytes 983048 | tf_op jit(solution)/shard_map/ppermute | solution.py:375
  155.7 8.1 %collective-permute-start.32 = (bf16[128,1280]{1,0:T(8,128)(2,1)S(1)}, bf16[128,1280]{1,0:T(8,128)(2,1)S(1)}, u32[]{:S(2)}, u32[]{:S(2)}) collective-permute-start(bf16[128,1280]{1,0:T(8,128)(2,1)S(1)} %add_convert_fusion.2), channel_id=1, source_target_pairs={{0,4},{4,0},{8,12},{12,8},{1,5},{5,1},{9,13},{13,9},{2,6},{6,2},{1... | collective-permute-start | bytes 983048 | tf_op jit(solution)/shard_map/ppermute | solution.py:379
  155.9 9.9 %collective-permute-start.33 = (bf16[128,1280]{1,0:T(8,128)(2,1)S(1)}, bf16[128,1280]{1,0:T(8,128)(2,1)S(1)}, u32[]{:S(2)}, u32[]{:S(2)}) collective-permute-start(bf16[128,1280]{1,0:T(8,128)(2,1)S(1)} %add_convert_fusion.1), channel_id=1, source_target_pairs={{4,8},{8,4},{5,9},{9,5},{6,10},{10,6},{7,11},{11,7},{20,24},{24,20... | collective-permute-start | bytes 983048 | tf_op jit(solution)/shard_map/ppermute | solution.py:381
